TPU v7x, 256 devices: a whole 4x4x8 slice. The times are simulated.
256 devices in a mesh: gx: 8 (over x, core), gy: 32 (over y, z).
Axes of the slice: x: 4, y: 4, z: 8, core: 2. Of those that a mesh axis runs over, the one named last changes fastest.
Arguments:
- state: float32 [2, 8, 512, 1024], P(None, None, 'gy', 'gx'), may hold values from 0 to 1, as said below
- previous: float32 [2, 8, 512, 1024], P(None, None, 'gy', 'gx'), may hold values from 0 to 1
- feed: float32 [8, 512, 1024], P(None, 'gy', 'gx'), may hold values from 0.01 to 0.1
- kill: float32 [8, 512, 1024], P(None, 'gy', 'gx'), may hold values from 0.03 to 0.1
Outputs:
- correction: float32 [2, 8, 512, 1024], P(None, None, 'gy', 'gx')
Inputs may be any that keep to these rules, and one draw needn't show every extreme that they name: `state`: u and v of every cell lie in the stated range.
All inputs are finite; a program needn't handle non-finite values.
Results may differ from a plain program's by a relative error of at most 0.0001.
Values sent between devices are 32-bit elements; how exact they have to be, the bound alone decides.
A program may use at most 128 MiB of HBM per device.

v0:
```python
import jax
import jax.numpy as jnp
from jax import lax
from jax.sharding import PartitionSpec as P

substrate_diffusion = 40.0
catalyst_diffusion = 20.0
inverse_step = 2.0
lower_fraction = 0.25
coarsenings = 2


def padded(cells, width):
    for axis, dim in (("gx", 3), ("gy", 2)):
        count = lax.axis_size(axis)
        size = cells.shape[dim]
        head = lax.slice_in_dim(cells, 0, width, axis=dim)
        tail = lax.slice_in_dim(cells, size - width, size, axis=dim)
        cells = jnp.concatenate(
            [
                lax.ppermute(tail, axis, [(i, (i + 1) % count) for i in range(count)]),
                cells,
                lax.ppermute(head, axis, [((i + 1) % count, i) for i in range(count)]),
            ],
            axis=dim,
        )
    return cells


def crop(cells, have, want):
    cut = have - want
    if cut == 0:
        return cells
    return cells[..., cut:cells.shape[-2] - cut, cut:cells.shape[-1] - cut]


def shrunk_neighbours(cells):
    centre = cells[:, :, 1:-1, 1:-1]
    along_x = cells[:, :, 1:-1, :-2] + cells[:, :, 1:-1, 2:]
    along_y = cells[:, :, :-2, 1:-1] + cells[:, :, 2:, 1:-1]
    along_z = jnp.roll(centre, 1, 1) + jnp.roll(centre, -1, 1)
    return along_x + along_y + along_z


def global_max(value):
    for axis in ("gx", "gy"):
        count = lax.axis_size(axis)
        step = 1
        while step < count:
            other = lax.ppermute(value, axis, [(i, i ^ step) for i in range(count)])
            value = jnp.maximum(value, other)
            step *= 2
    return value


def restrict(field):
    lead, depth, rows, cols = field.shape
    blocks = field.reshape(lead, depth // 2, 2, rows // 2, 2, cols // 2, 2)
    return jnp.mean(blocks, axis=(2, 4, 6))


def prolong(field):
    return jnp.repeat(jnp.repeat(jnp.repeat(field, 2, 1), 2, 2), 2, 3)


def diffusions(level):
    scale = 0.25**level
    return jnp.array(
        [substrate_diffusion * scale, catalyst_diffusion * scale], jnp.float32
    ).reshape(2, 1, 1, 1)


def coefficients(fields, level):
    scale = 0.25**level
    diff_first = substrate_diffusion * scale
    diff_second = catalyst_diffusion * scale
    substrate, catalyst, feed_rate, kill_rate = (fields[0], fields[1], fields[2], fields[3])
    product = substrate * catalyst
    squared = catalyst * catalyst
    self_first = inverse_step + squared + feed_rate + 6.0 * diff_first
    cross_first = 2.0 * product
    cross_second = -squared
    self_second = inverse_step + feed_rate + kill_rate - 2.0 * product + 6.0 * diff_second
    coeff = jnp.stack([self_first, cross_first, cross_second, self_second])
    return coeff, (6.0 * diff_first + cross_first) / self_first, (6.0 * diff_second + squared) / self_second


class Level:
    def __init__(self, coeff, halo, level):
        self.coeff = coeff
        self.halo = halo
        self.level = level

    def at(self, halo):
        return crop(self.coeff, self.halo, halo)

    def operate(self, field, halo):
        coeff = self.at(halo - 1)
        centre = crop(field, halo, halo - 1)
        first = coeff[0] * centre[0] + coeff[1] * centre[1]
        second = coeff[2] * centre[0] + coeff[3] * centre[1]
        return jnp.stack([first, second]) - diffusions(self.level) * shrunk_neighbours(field)

    def diagonal(self, halo):
        coeff = self.at(halo)
        return jnp.stack([coeff[0], coeff[3]])


def chebyshev(ops, source, source_halo, start, start_halo, spread):
    upper = 1.0 + spread
    lower = lower_fraction * upper
    centre = (upper + lower) / 2.0
    half_width = (upper - lower) / 2.0
    ratio = centre / half_width
    damping = 1.0 / ratio
    if start is None:
        halo = source_halo
        resid = source / ops.diagonal(halo)
        update = resid / centre
        iterate = update
    else:
        halo = min(source_halo, start_halo - 1)
        applied = ops.operate(start, start_halo)
        resid = (crop(source, source_halo, halo) - crop(applied, start_halo - 1, halo)) / ops.diagonal(halo)
        update = resid / centre
        iterate = crop(start, start_halo, halo) + update
    for sweep in range(2):
        applied = ops.operate(iterate, halo)
        halo = halo - 1
        resid = (crop(source, source_halo, halo) - applied) / ops.diagonal(halo)
        damping_next = 1.0 / (2.0 * ratio - damping)
        update = damping_next * damping * crop(update, halo + 1, halo) + 2.0 * damping_next / half_width * resid
        iterate = crop(iterate, halo + 1, halo) + update
        damping = damping_next
    return iterate, halo


def body(state, previous, feed, kill):
    deep = 3
    fields = jnp.concatenate([state, feed[None], kill[None]], 0)
    fields_1 = restrict(fields)
    fields_2 = restrict(fields_1)
    local = []
    for level, level_fields in enumerate((fields, fields_1, fields_2)):
        _, first, second = coefficients(level_fields, level)
        local.extend([jnp.max(first), jnp.max(second)])
    local = jnp.stack(local).reshape(3, 2)
    spreads = global_max(jnp.maximum(local[:, 0], local[:, 1]))

    wide = padded(jnp.concatenate([fields, previous], 0), deep + 1)
    ops_0 = Level(coefficients(crop(wide[:4], deep + 1, deep), 0)[0], deep, 0)
    state_w = wide[:2]
    substrate, catalyst = crop(state_w[0], deep + 1, deep), crop(state_w[1], deep + 1, deep)
    centre = crop(state_w, deep + 1, deep)
    reaction = substrate * catalyst * catalyst
    laplace = shrunk_neighbours(state_w) - 6.0 * centre
    feed_w = crop(wide[2], deep + 1, deep)
    kill_w = crop(wide[3], deep + 1, deep)
    previous_w = crop(wide[4:6], deep + 1, deep)
    local_terms = jnp.stack(
        [reaction - feed_w * (1.0 - substrate), -reaction + (feed_w + kill_w) * catalyst]
    )
    nonlinear = inverse_step * (centre - previous_w) - diffusions(0) * laplace + local_terms
    source_0 = -nonlinear
    pre_0, pre_0_halo = chebyshev(ops_0, source_0, deep, None, None, spreads[0])
    resid_0 = crop(source_0, deep, 0) - ops_0.operate(crop(pre_0, pre_0_halo, 1), 1)

    wide_1 = padded(jnp.concatenate([restrict(resid_0), fields_1], 0), deep)
    ops_1 = Level(coefficients(wide_1[2:], 1)[0], deep, 1)
    source_1 = wide_1[:2]
    pre_1, pre_1_halo = chebyshev(ops_1, source_1, deep, None, None, spreads[1])
    resid_1 = crop(source_1, deep, 0) - ops_1.operate(crop(pre_1, pre_1_halo, 1), 1)

    wide_2 = padded(jnp.concatenate([restrict(resid_1), fields_2], 0), deep)
    ops_2 = Level(coefficients(wide_2[2:], 2)[0], deep, 2)
    source_2 = wide_2[:2]
    first_2, first_2_halo = chebyshev(ops_2, source_2, deep, None, None, spreads[2])
    start_2 = padded(crop(first_2, first_2_halo, 0), deep)
    coarse_2, coarse_2_halo = chebyshev(ops_2, source_2, deep, start_2, deep, spreads[2])

    start_1 = padded(crop(pre_1, pre_1_halo, 0) + prolong(crop(coarse_2, coarse_2_halo, 0)), deep)
    post_1, post_1_halo = chebyshev(ops_1, source_1, deep, start_1, deep, spreads[1])

    start_0 = padded(crop(pre_0, pre_0_halo, 0) + prolong(crop(post_1, post_1_halo, 0)), deep)
    post_0, post_0_halo = chebyshev(ops_0, source_0, deep, start_0, deep, spreads[0])
    return crop(post_0, post_0_halo, 0)


def solution(mesh):
    placed = (
        P(None, None, "gy", "gx"),
        P(None, None, "gy", "gx"),
        P(None, "gy", "gx"),
        P(None, "gy", "gx"),
    )
    return jax.shard_map(
        body, mesh=mesh, in_specs=placed, out_specs=P(None, None, "gy", "gx"), check_vma=False
    )
```

profile of v0, /device:TPU:0, one launch (start us, length us, event | category | flops | bytes accessed | tf_op | source)
XLA Modules:
  0.0 180.7 jit_solution(16749268596301550648)
XLA Ops:
  0.0 1.1 pad_maximum_fusion.1
  1.3 2.9 %collective-permute-start.1 = (f32[6,8,16,4]{3,2,1,0:T(8,128)S(1)}, f32[6,8,16,4]{3,2,1,0:T(8,128)S(1)}, u32[]{:S(2)}, u32[]{:S(2)}) collective-permute-start(f32[6,8,16,4]{3,2,1,0:T(8,128)S(1)} %get-tuple-element.90), channel_id=1, source_target_pairs={{32,0},{64,32},{96,64},{128,96},{160,128},{192,160},{224,192},{0,2... | collective-permute-start | bytes 36872 | tf_op jit(solution)/shard_map/ppermute | solution.py:23
  4.3 9.8 %concatenate.179 = f32[2,4,2,8,2,64,2]{6,5,4,3,2,1,0:T(8,128)} reshape(f32[2,8,16,128]{3,2,1,0:T(8,128)S(1)} %copy-done) | data formatting | bytes 262144 | tf_op jit(solution)/shard_map/concatenate | solution.py:140
  14.0 5.5 %concatenate.180 = f32[1,4,2,8,2,64,2]{6,5,4,3,2,1,0:T(8,128)} reshape(f32[8,16,128]{2,1,0:T(8,128)S(1)} %copy-done.6) | data formatting | bytes 131072 | tf_op jit(solution)/shard_map/concatenate | solution.py:140
  19.6 5.6 %concatenate.181 = f32[1,4,2,8,2,64,2]{6,5,4,3,2,1,0:T(8,128)} reshape(f32[8,16,128]{2,1,0:T(8,128)S(1)} %copy-done.5) | data formatting | bytes 131072 | tf_op jit(solution)/shard_map/concatenate | solution.py:140
  25.1 6.9 %maximum_reduce_fusion = f32[4,4,8,64]{3,2,1,0:T(8,128)S(1)} fusion(f32[1,4,2,8,2,64,2]{6,5,4,3,2,1,0:T(8,128)} %concatenate.181, f32[1,4,2,8,2,64,2]{6,5,4,3,2,1,0:T(8,128)} %concatenate.180, f32[2,4,2,8,2,64,2]{6,5,4,3,2,1,0:T(8,128)} %concatenate.179), kind=kLoop, calls=%fused_computation | loop fusion | flops 188416 | bytes 294912 | tf_op jit(solution)/shard_map/reduce_sum | solution.py:59
  35.3 4.0 %stack.88 = f32[6]{0:T(128)S(1)} concatenate(f32[1]{0:T(128)} %bitcast.10, f32[1]{0:T(128)} %bitcast.12, f32[1]{0:T(128)} %bitcast.13, f32[1]{0:T(128)} %bitcast.14, f32[1]{0:T(128)} %bitcast.16, f32[1]{0:T(128)} %bitcast.17), dimensions={0} | concatenate | bytes 48 | tf_op jit(solution)/shard_map/stack | solution.py:147
  39.6 1.1 collective-permute-done.4
  40.7 3.5 %collective-permute-done.5 = f32[3]{0:T(128)S(1)} collective-permute-done((f32[3]{0:T(128)S(1)}, f32[3]{0:T(128)S(1)}, u32[]{:S(2)}, u32[]{:S(2)}) %collective-permute-start.5) | collective-permute-done | bytes 44 | tf_op jit(solution)/shard_map/ppermute | solution.py:50
  44.3 5.0 %collective-permute-done.6 = f32[3]{0:T(128)S(1)} collective-permute-done((f32[3]{0:T(128)S(1)}, f32[3]{0:T(128)S(1)}, u32[]{:S(2)}, u32[]{:S(2)}) %collective-permute-start.6) | collective-permute-done | bytes 44 | tf_op jit(solution)/shard_map/ppermute | solution.py:50
  49.5 3.4 %collective-permute-done.7 = f32[3]{0:T(128)S(1)} collective-permute-done((f32[3]{0:T(128)S(1)}, f32[3]{0:T(128)S(1)}, u32[]{:S(2)}, u32[]{:S(2)}) %collective-permute-start.7) | collective-permute-done | bytes 44 | tf_op jit(solution)/shard_map/ppermute | solution.py:50
  52.9 1.5 collective-permute-start.8
  54.4 2.9 %collective-permute-done.8 = f32[3]{0:T(128)S(1)} collective-permute-done((f32[3]{0:T(128)S(1)}, f32[3]{0:T(128)S(1)}, u32[]{:S(2)}, u32[]{:S(2)}) %collective-permute-start.8) | collective-permute-done | bytes 44 | tf_op jit(solution)/shard_map/ppermute | solution.py:50
  57.3 5.5 %collective-permute-start.9 = (f32[3]{0:T(128)S(1)}, f32[3]{0:T(128)S(1)}, u32[]{:S(2)}, u32[]{:S(2)}) collective-permute-start(f32[3]{0:T(128)S(1)} %max.36), channel_id=1, source_target_pairs={{0,4},{1,5},{2,6},{3,7},{4,0},{5,1},{6,2},{7,3},{8,12},{9,13},{10,... | collective-permute-start | bytes 44 | tf_op jit(solution)/shard_map/ppermute | solution.py:50
  62.8 2.0 %collective-permute-done.9 = f32[3]{0:T(128)S(1)} collective-permute-done((f32[3]{0:T(128)S(1)}, f32[3]{0:T(128)S(1)}, u32[]{:S(2)}, u32[]{:S(2)}) %collective-permute-start.9) | collective-permute-done | bytes 44 | tf_op jit(solution)/shard_map/ppermute | solution.py:50
  64.8 1.1 collective-permute-start.10
  65.9 2.4 %collective-permute-done.10 = f32[3]{0:T(128)S(1)} collective-permute-done((f32[3]{0:T(128)S(1)}, f32[3]{0:T(128)S(1)}, u32[]{:S(2)}, u32[]{:S(2)}) %collective-permute-start.10) | collective-permute-done | bytes 44 | tf_op jit(solution)/shard_map/ppermute | solution.py:50
  68.3 2.7 %collective-permute-start.11 = (f32[3]{0:T(128)S(1)}, f32[3]{0:T(128)S(1)}, u32[]{:S(2)}, u32[]{:S(2)}) collective-permute-start(f32[3]{0:T(128)S(1)} %max.38), channel_id=1, source_target_pairs={{0,16},{1,17},{2,18},{3,19},{4,20},{5,21},{6,22},{7,23},{8,24},{9,... | collective-permute-start | bytes 44 | tf_op jit(solution)/shard_map/ppermute | solution.py:50
  71.0 2.3 %collective-permute-done.11 = f32[3]{0:T(128)S(1)} collective-permute-done((f32[3]{0:T(128)S(1)}, f32[3]{0:T(128)S(1)}, u32[]{:S(2)}, u32[]{:S(2)}) %collective-permute-start.11) | collective-permute-done | bytes 44 | tf_op jit(solution)/shard_map/ppermute | solution.py:50
  74.5 6.3 %collective-permute-start.3 = (f32[6,8,4,136]{3,1,2,0:T(8,128)S(1)}, f32[6,8,4,136]{3,1,2,0:T(8,128)S(1)}, u32[]{:S(2)}, u32[]{:S(2)}) collective-permute-start(f32[6,8,4,136]{3,1,2,0:T(8,128)S(1)} %copy.510), channel_id=1, source_target_pairs={{1,0},{2,1},{3,2},{4,3},{5,4},{6,5},{7,6},{8,7},{9,8},{10,9},{11,1... | collective-permute-start | bytes 313352 | tf_op jit(solution)/shard_map/ppermute | solution.py:23
  82.3 1.8 collective-permute-done.2
  88.7 0.7 fusion.20
  89.5 0.8 multiply_add_fusion.13
  90.6 9.8 %reshape.117 = f32[2,4,2,8,2,64,2]{6,5,4,3,2,1,0:T(8,128)} reshape(f32[2,8,16,128]{3,2,1,0:T(8,128)S(1)} %fusion.55) | data formatting | bytes 262144 | tf_op jit(solution)/shard_map/reshape | solution.py:58
  100.4 4.0 %reduce_sum.38 = f32[2,4,8,64]{3,2,1,0:T(8,128)S(1)} reduce(f32[2,4,2,8,2,64,2]{6,5,4,3,2,1,0:T(8,128)} %reshape.117, f32[]{:T(128)} %constant.24.clone.1), dimensions={2,4,6}, to_apply=%region_8.9 | reduce | flops 28672 | bytes 147460 | tf_op jit(solution)/shard_map/reduce_sum | solution.py:59
  104.6 2.9 %collective-permute-start.13 = (f32[6,4,8,3]{3,2,1,0:T(8,128)S(1)}, f32[6,4,8,3]{3,2,1,0:T(8,128)S(1)}, u32[]{:S(2)}, u32[]{:S(2)}) collective-permute-start(f32[6,4,8,3]{3,2,1,0:T(8,128)S(1)} %get-tuple-element.106), channel_id=1, source_target_pairs={{32,0},{64,32},{96,64},{128,96},{160,128},{192,160},{224,192},{0,2... | collective-permute-start | bytes 6920 | tf_op jit(solution)/shard_map/ppermute | solution.py:23
  107.5 2.3 %collective-permute-done.12 = f32[6,4,8,3]{3,2,1,0:T(8,128)S(1)} collective-permute-done((f32[6,4,8,3]{3,2,1,0:T(8,128)S(1)}, f32[6,4,8,3]{3,2,1,0:T(8,128)S(1)}, u32[]{:S(2)}, u32[]{:S(2)}) %collective-permute-start.12) | collective-permute-done | bytes 2336 | tf_op jit(solution)/shard_map/ppermute | solution.py:21
  110.1 5.6 %collective-permute-start.15 = (f32[6,4,3,70]{3,1,2,0:T(4,128)S(1)}, f32[6,4,3,70]{3,1,2,0:T(4,128)S(1)}, u32[]{:S(2)}, u32[]{:S(2)}) collective-permute-start(f32[6,4,3,70]{3,1,2,0:T(4,128)S(1)} %copy.512), channel_id=1, source_target_pairs={{1,0},{2,1},{3,2},{4,3},{5,4},{6,5},{7,6},{8,7},{9,8},{10,9},{11,1... | collective-permute-start | bytes 60488 | tf_op jit(solution)/shard_map/ppermute | solution.py:23
  116.7 0.9 collective-permute-done.14
  119.9 1.1 reshape.118
  121.3 2.9 %collective-permute-start.17 = (f32[6,2,4,3]{3,2,1,0:T(4,128)S(1)}, f32[6,2,4,3]{3,2,1,0:T(4,128)S(1)}, u32[]{:S(2)}, u32[]{:S(2)}) collective-permute-start(f32[6,2,4,3]{3,2,1,0:T(4,128)S(1)} %get-tuple-element.164), channel_id=1, source_target_pairs={{32,0},{64,32},{96,64},{128,96},{160,128},{192,160},{224,192},{0,2... | collective-permute-start | bytes 1736 | tf_op jit(solution)/shard_map/ppermute | solution.py:23
  124.3 1.5 collective-permute-done.16
  126.0 5.7 %collective-permute-start.19 = (f32[6,2,3,38]{3,2,1,0:T(4,128)S(1)}, f32[6,2,3,38]{3,2,1,0:T(4,128)S(1)}, u32[]{:S(2)}, u32[]{:S(2)}) collective-permute-start(f32[6,2,3,38]{3,2,1,0:T(4,128)S(1)} %get-tuple-element.162), channel_id=1, source_target_pairs={{1,0},{2,1},{3,2},{4,3},{5,4},{6,5},{7,6},{8,7},{9,8},{10,9},{11,1... | collective-permute-start | bytes 16424 | tf_op jit(solution)/shard_map/ppermute | solution.py:23
  133.6 0.8 slice_add_fusion.49
  134.7 3.0 %collective-permute-start.21 = (f32[2,2,4,3]{3,2,1,0:T(4,128)S(1)}, f32[2,2,4,3]{3,2,1,0:T(4,128)S(1)}, u32[]{:S(2)}, u32[]{:S(2)}) collective-permute-start(f32[2,2,4,3]{3,2,1,0:T(4,128)S(1)} %get-tuple-element.177), channel_id=1, source_target_pairs={{32,0},{64,32},{96,64},{128,96},{160,128},{192,160},{224,192},{0,2... | collective-permute-start | bytes 584 | tf_op jit(solution)/shard_map/ppermute | solution.py:23
  137.7 1.3 collective-permute-done.20
  139.2 5.7 %collective-permute-start.23 = (f32[2,2,3,38]{3,2,1,0:T(4,128)S(1)}, f32[2,2,3,38]{3,2,1,0:T(4,128)S(1)}, u32[]{:S(2)}, u32[]{:S(2)}) collective-permute-start(f32[2,2,3,38]{3,2,1,0:T(4,128)S(1)} %get-tuple-element.186), channel_id=1, source_target_pairs={{1,0},{2,1},{3,2},{4,3},{5,4},{6,5},{7,6},{8,7},{9,8},{10,9},{11,1... | collective-permute-start | bytes 5480 | tf_op jit(solution)/shard_map/ppermute | solution.py:23
  144.9 1.5 collective-permute-done.22
  147.8 3.0 %collective-permute-start.25 = (f32[2,4,8,3]{3,2,1,0:T(8,128)S(1)}, f32[2,4,8,3]{3,2,1,0:T(8,128)S(1)}, u32[]{:S(2)}, u32[]{:S(2)}) collective-permute-start(f32[2,4,8,3]{3,2,1,0:T(8,128)S(1)} %get-tuple-element.150), channel_id=1, source_target_pairs={{32,0},{64,32},{96,64},{128,96},{160,128},{192,160},{224,192},{0,2... | collective-permute-start | bytes 2312 | tf_op jit(solution)/shard_map/ppermute | solution.py:23
  150.8 1.6 collective-permute-done.24
  152.6 5.5 %collective-permute-start.27 = (f32[2,4,3,70]{3,2,1,0:T(4,128)S(1)}, f32[2,4,3,70]{3,2,1,0:T(4,128)S(1)}, u32[]{:S(2)}, u32[]{:S(2)}) collective-permute-start(f32[2,4,3,70]{3,2,1,0:T(4,128)S(1)} %get-tuple-element.148), channel_id=1, source_target_pairs={{1,0},{2,1},{3,2},{4,3},{5,4},{6,5},{7,6},{8,7},{9,8},{10,9},{11,1... | collective-permute-start | bytes 20168 | tf_op jit(solution)/shard_map/ppermute | solution.py:23
  158.1 1.6 collective-permute-done.26
  162.2 2.9 %collective-permute-start.29 = (f32[2,8,16,3]{3,2,1,0:T(8,128)S(1)}, f32[2,8,16,3]{3,2,1,0:T(8,128)S(1)}, u32[]{:S(2)}, u32[]{:S(2)}) collective-permute-start(f32[2,8,16,3]{3,2,1,0:T(8,128)S(1)} %get-tuple-element.100), channel_id=1, source_target_pairs={{32,0},{64,32},{96,64},{128,96},{160,128},{192,160},{224,192},{0,2... | collective-permute-start | bytes 9224 | tf_op jit(solution)/shard_map/ppermute | solution.py:23
  165.1 2.6 %collective-permute-done.28 = f32[2,8,16,3]{3,2,1,0:T(8,128)S(1)} collective-permute-done((f32[2,8,16,3]{3,2,1,0:T(8,128)S(1)}, f32[2,8,16,3]{3,2,1,0:T(8,128)S(1)}, u32[]{:S(2)}, u32[]{:S(2)}) %collective-permute-start.28) | collective-permute-done | bytes 3104 | tf_op jit(solution)/shard_map/ppermute | solution.py:21
  168.1 5.5 %collective-permute-start.31 = (f32[2,8,3,134]{3,1,2,0:T(8,128)S(1)}, f32[2,8,3,134]{3,1,2,0:T(8,128)S(1)}, u32[]{:S(2)}, u32[]{:S(2)}) collective-permute-start(f32[2,8,3,134]{3,1,2,0:T(8,128)S(1)} %copy.506), channel_id=1, source_target_pairs={{1,0},{2,1},{3,2},{4,3},{5,4},{6,5},{7,6},{8,7},{9,8},{10,9},{11,1... | collective-permute-start | bytes 77192 | tf_op jit(solution)/shard_map/ppermute | solution.py:23
  173.6 2.0 %collective-permute-done.30 = f32[2,8,3,134]{3,1,2,0:T(8,128)S(1)} collective-permute-done((f32[2,8,3,134]{3,1,2,0:T(8,128)S(1)}, f32[2,8,3,134]{3,1,2,0:T(8,128)S(1)}, u32[]{:S(2)}, u32[]{:S(2)}) %collective-permute-start.30) | collective-permute-done | bytes 25760 | tf_op jit(solution)/shard_map/ppermute | solution.py:21
  178.6 0.7 slice_add_fusion.2
  179.7 0.9 fusion.50
  (214 shorter events, 22.7 us)
Async XLA Ops:
  0.0 4.3 %copy-start = (f32[2,8,16,128]{3,2,1,0:T(8,128)S(1)}, f32[2,8,16,128]{3,2,1,0:T(8,128)}, u32[]{:S(2)}) copy-start(f32[2,8,16,128]{3,2,1,0:T(8,128)} %param.22) | copy-start | bytes 393220
  1.3 72.1 %collective-permute-start = (f32[6,8,16,4]{3,2,1,0:T(8,128)S(1)}, f32[6,8,16,4]{3,2,1,0:T(8,128)S(1)}, u32[]{:S(2)}, u32[]{:S(2)}) collective-permute-start(f32[6,8,16,4]{3,2,1,0:T(8,128)S(1)} %get-tuple-element.89), channel_id=1, source_target_pairs={{0,32},{32,64},{64,96},{96,128},{128,160},{160,192},{192,224},{224... | collective-permute-start | bytes 36872 | tf_op jit(solution)/shard_map/ppermute | solution.py:21
  1.3 12.7 %copy-start.6 = (f32[8,16,128]{2,1,0:T(8,128)S(1)}, f32[8,16,128]{2,1,0:T(8,128)}, u32[]{:S(2)}) copy-start(f32[8,16,128]{2,1,0:T(8,128)} %param.24) | copy-start | bytes 196612
  1.3 72.0 %collective-permute-start.1 = (f32[6,8,16,4]{3,2,1,0:T(8,128)S(1)}, f32[6,8,16,4]{3,2,1,0:T(8,128)S(1)}, u32[]{:S(2)}, u32[]{:S(2)}) collective-permute-start(f32[6,8,16,4]{3,2,1,0:T(8,128)S(1)} %get-tuple-element.90), channel_id=1, source_target_pairs={{32,0},{64,32},{96,64},{128,96},{160,128},{192,160},{224,192},{0,2... | collective-permute-start | bytes 36872 | tf_op jit(solution)/shard_map/ppermute | solution.py:23
  14.0 5.5 %copy-start.5 = (f32[8,16,128]{2,1,0:T(8,128)S(1)}, f32[8,16,128]{2,1,0:T(8,128)}, u32[]{:S(2)}) copy-start(f32[8,16,128]{2,1,0:T(8,128)} %param.25) | copy-start | bytes 196612
  32.0 41.3 %copy-start.7 = (f32[2,8,16,128]{3,2,1,0:T(8,128)S(1)}, f32[2,8,16,128]{3,2,1,0:T(8,128)}, u32[]{:S(2)}) copy-start(f32[2,8,16,128]{3,2,1,0:T(8,128)} %param.23) | copy-start | bytes 393220
  39.5 1.2 collective-permute-start.4
  40.7 3.5 %collective-permute-start.5 = (f32[3]{0:T(128)S(1)}, f32[3]{0:T(128)S(1)}, u32[]{:S(2)}, u32[]{:S(2)}) collective-permute-start(f32[3]{0:T(128)S(1)} %max.32), channel_id=1, source_target_pairs={{0,64},{32,96},{64,0},{96,32},{128,192},{160,224},{192,128},{224,1... | collective-permute-start | bytes 44 | tf_op jit(solution)/shard_map/ppermute | solution.py:50
  44.3 5.0 %collective-permute-start.6 = (f32[3]{0:T(128)S(1)}, f32[3]{0:T(128)S(1)}, u32[]{:S(2)}, u32[]{:S(2)}) collective-permute-start(f32[3]{0:T(128)S(1)} %max.33), channel_id=1, source_target_pairs={{0,128},{32,160},{64,192},{96,224},{128,0},{160,32},{192,64},{224,... | collective-permute-start | bytes 44 | tf_op jit(solution)/shard_map/ppermute | solution.py:50
  49.3 3.5 %collective-permute-start.7 = (f32[3]{0:T(128)S(1)}, f32[3]{0:T(128)S(1)}, u32[]{:S(2)}, u32[]{:S(2)}) collective-permute-start(f32[3]{0:T(128)S(1)} %max.34), channel_id=1, source_target_pairs={{0,1},{1,0},{2,3},{3,2},{4,5},{5,4},{6,7},{7,6},{8,9},{9,8},{10,11... | collective-permute-start | bytes 44 | tf_op jit(solution)/shard_map/ppermute | solution.py:50
  52.9 4.4 %collective-permute-start.8 = (f32[3]{0:T(128)S(1)}, f32[3]{0:T(128)S(1)}, u32[]{:S(2)}, u32[]{:S(2)}) collective-permute-start(f32[3]{0:T(128)S(1)} %max.35), channel_id=1, source_target_pairs={{0,2},{1,3},{2,0},{3,1},{4,6},{5,7},{6,4},{7,5},{8,10},{9,11},{10,... | collective-permute-start | bytes 44 | tf_op jit(solution)/shard_map/ppermute | solution.py:50
  57.3 7.4 %collective-permute-start.9 = (f32[3]{0:T(128)S(1)}, f32[3]{0:T(128)S(1)}, u32[]{:S(2)}, u32[]{:S(2)}) collective-permute-start(f32[3]{0:T(128)S(1)} %max.36), channel_id=1, source_target_pairs={{0,4},{1,5},{2,6},{3,7},{4,0},{5,1},{6,2},{7,3},{8,12},{9,13},{10,... | collective-permute-start | bytes 44 | tf_op jit(solution)/shard_map/ppermute | solution.py:50
  64.8 3.5 %collective-permute-start.10 = (f32[3]{0:T(128)S(1)}, f32[3]{0:T(128)S(1)}, u32[]{:S(2)}, u32[]{:S(2)}) collective-permute-start(f32[3]{0:T(128)S(1)} %max.37), channel_id=1, source_target_pairs={{0,8},{1,9},{2,10},{3,11},{4,12},{5,13},{6,14},{7,15},{8,0},{9,1},... | collective-permute-start | bytes 44 | tf_op jit(solution)/shard_map/ppermute | solution.py:50
  68.3 5.0 %collective-permute-start.11 = (f32[3]{0:T(128)S(1)}, f32[3]{0:T(128)S(1)}, u32[]{:S(2)}, u32[]{:S(2)}) collective-permute-start(f32[3]{0:T(128)S(1)} %max.38), channel_id=1, source_target_pairs={{0,16},{1,17},{2,18},{3,19},{4,20},{5,21},{6,22},{7,23},{8,24},{9,... | collective-permute-start | bytes 44 | tf_op jit(solution)/shard_map/ppermute | solution.py:50
  73.8 10.3 %collective-permute-start.2 = (f32[6,8,4,136]{3,1,2,0:T(8,128)S(1)}, f32[6,8,4,136]{3,1,2,0:T(8,128)S(1)}, u32[]{:S(2)}, u32[]{:S(2)}) collective-permute-start(f32[6,8,4,136]{3,1,2,0:T(8,128)S(1)} %copy.509), channel_id=1, source_target_pairs={{0,1},{1,2},{2,3},{3,4},{4,5},{5,6},{6,7},{7,8},{8,9},{9,10},{10,1... | collective-permute-start | bytes 313352 | tf_op jit(solution)/shard_map/ppermute | solution.py:21
  74.5 9.7 %collective-permute-start.3 = (f32[6,8,4,136]{3,1,2,0:T(8,128)S(1)}, f32[6,8,4,136]{3,1,2,0:T(8,128)S(1)}, u32[]{:S(2)}, u32[]{:S(2)}) collective-permute-start(f32[6,8,4,136]{3,1,2,0:T(8,128)S(1)} %copy.510), channel_id=1, source_target_pairs={{1,0},{2,1},{3,2},{4,3},{5,4},{6,5},{7,6},{8,7},{9,8},{10,9},{11,1... | collective-permute-start | bytes 313352 | tf_op jit(solution)/shard_map/ppermute | solution.py:23
  104.5 15.4 %copy-start.8 = (f32[2,4,8,64]{3,2,1,0:T(8,128)}, f32[2,4,8,64]{3,2,1,0:T(8,128)S(1)}, u32[]{:S(2)}) copy-start(f32[2,4,8,64]{3,2,1,0:T(8,128)S(1)} %reduce_sum.38) | copy-start | bytes 49156
  104.6 5.3 %collective-permute-start.12 = (f32[6,4,8,3]{3,2,1,0:T(8,128)S(1)}, f32[6,4,8,3]{3,2,1,0:T(8,128)S(1)}, u32[]{:S(2)}, u32[]{:S(2)}) collective-permute-start(f32[6,4,8,3]{3,2,1,0:T(8,128)S(1)} %get-tuple-element.105), channel_id=1, source_target_pairs={{0,32},{32,64},{64,96},{96,128},{128,160},{160,192},{192,224},{224... | collective-permute-start | bytes 6920 | tf_op jit(solution)/shard_map/ppermute | solution.py:21
  104.6 5.2 %collective-permute-start.13 = (f32[6,4,8,3]{3,2,1,0:T(8,128)S(1)}, f32[6,4,8,3]{3,2,1,0:T(8,128)S(1)}, u32[]{:S(2)}, u32[]{:S(2)}) collective-permute-start(f32[6,4,8,3]{3,2,1,0:T(8,128)S(1)} %get-tuple-element.106), channel_id=1, source_target_pairs={{32,0},{64,32},{96,64},{128,96},{160,128},{192,160},{224,192},{0,2... | collective-permute-start | bytes 6920 | tf_op jit(solution)/shard_map/ppermute | solution.py:23
  110.0 8.2 %copy-start.21 = (f32[2]{0:T(128)S(1)}, f32[2]{0:T(128)}, u32[]{:S(2)}) copy-start(f32[2]{0:T(128)} %constant.17.clone) | copy-start | bytes 28
  110.0 7.6 %collective-permute-start.14 = (f32[6,4,3,70]{3,1,2,0:T(4,128)S(1)}, f32[6,4,3,70]{3,1,2,0:T(4,128)S(1)}, u32[]{:S(2)}, u32[]{:S(2)}) collective-permute-start(f32[6,4,3,70]{3,1,2,0:T(4,128)S(1)} %copy.511), channel_id=1, source_target_pairs={{0,1},{1,2},{2,3},{3,4},{4,5},{5,6},{6,7},{7,8},{8,9},{9,10},{10,1... | collective-permute-start | bytes 60488 | tf_op jit(solution)/shard_map/ppermute | solution.py:21
  110.1 7.5 %collective-permute-start.15 = (f32[6,4,3,70]{3,1,2,0:T(4,128)S(1)}, f32[6,4,3,70]{3,1,2,0:T(4,128)S(1)}, u32[]{:S(2)}, u32[]{:S(2)}) collective-permute-start(f32[6,4,3,70]{3,1,2,0:T(4,128)S(1)} %copy.512), channel_id=1, source_target_pairs={{1,0},{2,1},{3,2},{4,3},{5,4},{6,5},{7,6},{8,7},{9,8},{10,9},{11,1... | collective-permute-start | bytes 60488 | tf_op jit(solution)/shard_map/ppermute | solution.py:23
  118.5 1.3 copy-start.10
  118.5 1.3 copy-start.12
  121.2 13.3 %copy-start.22 = (f32[2]{0:T(128)S(1)}, f32[2]{0:T(128)}, u32[]{:S(2)}) copy-start(f32[2]{0:T(128)} %constant.66.clone) | copy-start | bytes 28
  121.3 4.5 %collective-permute-start.16 = (f32[6,2,4,3]{3,2,1,0:T(4,128)S(1)}, f32[6,2,4,3]{3,2,1,0:T(4,128)S(1)}, u32[]{:S(2)}, u32[]{:S(2)}) collective-permute-start(f32[6,2,4,3]{3,2,1,0:T(4,128)S(1)} %get-tuple-element.163), channel_id=1, source_target_pairs={{0,32},{32,64},{64,96},{96,128},{128,160},{160,192},{192,224},{224... | collective-permute-start | bytes 1736 | tf_op jit(solution)/shard_map/ppermute | solution.py:21
  121.3 4.5 %collective-permute-start.17 = (f32[6,2,4,3]{3,2,1,0:T(4,128)S(1)}, f32[6,2,4,3]{3,2,1,0:T(4,128)S(1)}, u32[]{:S(2)}, u32[]{:S(2)}) collective-permute-start(f32[6,2,4,3]{3,2,1,0:T(4,128)S(1)} %get-tuple-element.164), channel_id=1, source_target_pairs={{32,0},{64,32},{96,64},{128,96},{160,128},{192,160},{224,192},{0,2... | collective-permute-start | bytes 1736 | tf_op jit(solution)/shard_map/ppermute | solution.py:23
  125.9 7.3 %collective-permute-start.18 = (f32[6,2,3,38]{3,2,1,0:T(4,128)S(1)}, f32[6,2,3,38]{3,2,1,0:T(4,128)S(1)}, u32[]{:S(2)}, u32[]{:S(2)}) collective-permute-start(f32[6,2,3,38]{3,2,1,0:T(4,128)S(1)} %get-tuple-element.161), channel_id=1, source_target_pairs={{0,1},{1,2},{2,3},{3,4},{4,5},{5,6},{6,7},{7,8},{8,9},{9,10},{10,1... | collective-permute-start | bytes 16424 | tf_op jit(solution)/shard_map/ppermute | solution.py:21
  126.0 7.2 %collective-permute-start.19 = (f32[6,2,3,38]{3,2,1,0:T(4,128)S(1)}, f32[6,2,3,38]{3,2,1,0:T(4,128)S(1)}, u32[]{:S(2)}, u32[]{:S(2)}) collective-permute-start(f32[6,2,3,38]{3,2,1,0:T(4,128)S(1)} %get-tuple-element.162), channel_id=1, source_target_pairs={{1,0},{2,1},{3,2},{4,3},{5,4},{6,5},{7,6},{8,7},{9,8},{10,9},{11,1... | collective-permute-start | bytes 16424 | tf_op jit(solution)/shard_map/ppermute | solution.py:23
  134.7 4.3 %collective-permute-start.20 = (f32[2,2,4,3]{3,2,1,0:T(4,128)S(1)}, f32[2,2,4,3]{3,2,1,0:T(4,128)S(1)}, u32[]{:S(2)}, u32[]{:S(2)}) collective-permute-start(f32[2,2,4,3]{3,2,1,0:T(4,128)S(1)} %get-tuple-element.176), channel_id=1, source_target_pairs={{0,32},{32,64},{64,96},{96,128},{128,160},{160,192},{192,224},{224... | collective-permute-start | bytes 584 | tf_op jit(solution)/shard_map/ppermute | solution.py:21
  134.7 4.3 %collective-permute-start.21 = (f32[2,2,4,3]{3,2,1,0:T(4,128)S(1)}, f32[2,2,4,3]{3,2,1,0:T(4,128)S(1)}, u32[]{:S(2)}, u32[]{:S(2)}) collective-permute-start(f32[2,2,4,3]{3,2,1,0:T(4,128)S(1)} %get-tuple-element.177), channel_id=1, source_target_pairs={{32,0},{64,32},{96,64},{128,96},{160,128},{192,160},{224,192},{0,2... | collective-permute-start | bytes 584 | tf_op jit(solution)/shard_map/ppermute | solution.py:23
  139.1 7.3 %collective-permute-start.22 = (f32[2,2,3,38]{3,2,1,0:T(4,128)S(1)}, f32[2,2,3,38]{3,2,1,0:T(4,128)S(1)}, u32[]{:S(2)}, u32[]{:S(2)}) collective-permute-start(f32[2,2,3,38]{3,2,1,0:T(4,128)S(1)} %get-tuple-element.185), channel_id=1, source_target_pairs={{0,1},{1,2},{2,3},{3,4},{4,5},{5,6},{6,7},{7,8},{8,9},{9,10},{10,1... | collective-permute-start | bytes 5480 | tf_op jit(solution)/shard_map/ppermute | solution.py:21
  139.2 7.2 %collective-permute-start.23 = (f32[2,2,3,38]{3,2,1,0:T(4,128)S(1)}, f32[2,2,3,38]{3,2,1,0:T(4,128)S(1)}, u32[]{:S(2)}, u32[]{:S(2)}) collective-permute-start(f32[2,2,3,38]{3,2,1,0:T(4,128)S(1)} %get-tuple-element.186), channel_id=1, source_target_pairs={{1,0},{2,1},{3,2},{4,3},{5,4},{6,5},{7,6},{8,7},{9,8},{10,9},{11,1... | collective-permute-start | bytes 5480 | tf_op jit(solution)/shard_map/ppermute | solution.py:23
  147.0 13.1 %copy-start.15 = (f32[1,4,12,68]{3,2,1,0:T(8,128)S(1)}, f32[1,4,12,68]{3,2,1,0:T(8,128)}, u32[]{:S(2)}) copy-start(f32[1,4,12,68]{3,2,1,0:T(8,128)} %copy-done.14) | copy-start | bytes 39172
  147.0 13.1 %copy-start.17 = (f32[1,4,12,68]{3,2,1,0:T(8,128)S(1)}, f32[1,4,12,68]{3,2,1,0:T(8,128)}, u32[]{:S(2)}) copy-start(f32[1,4,12,68]{3,2,1,0:T(8,128)} %copy-done.16) | copy-start | bytes 39172
  147.7 12.9 %copy-start.11 = (f32[1,4,10,66]{3,2,1,0:T(8,128)S(1)}, f32[1,4,10,66]{3,2,1,0:T(8,128)}, u32[]{:S(2)}) copy-start(f32[1,4,10,66]{3,2,1,0:T(8,128)} %copy-done.10) | copy-start | bytes 31684
  147.7 12.9 %copy-start.13 = (f32[1,4,10,66]{3,2,1,0:T(8,128)S(1)}, f32[1,4,10,66]{3,2,1,0:T(8,128)}, u32[]{:S(2)}) copy-start(f32[1,4,10,66]{3,2,1,0:T(8,128)} %copy-done.12) | copy-start | bytes 31684
  147.8 4.6 %collective-permute-start.24 = (f32[2,4,8,3]{3,2,1,0:T(8,128)S(1)}, f32[2,4,8,3]{3,2,1,0:T(8,128)S(1)}, u32[]{:S(2)}, u32[]{:S(2)}) collective-permute-start(f32[2,4,8,3]{3,2,1,0:T(8,128)S(1)} %get-tuple-element.149), channel_id=1, source_target_pairs={{0,32},{32,64},{64,96},{96,128},{128,160},{160,192},{192,224},{224... | collective-permute-start | bytes 2312 | tf_op jit(solution)/shard_map/ppermute | solution.py:21
  147.8 4.6 %collective-permute-start.25 = (f32[2,4,8,3]{3,2,1,0:T(8,128)S(1)}, f32[2,4,8,3]{3,2,1,0:T(8,128)S(1)}, u32[]{:S(2)}, u32[]{:S(2)}) collective-permute-start(f32[2,4,8,3]{3,2,1,0:T(8,128)S(1)} %get-tuple-element.150), channel_id=1, source_target_pairs={{32,0},{64,32},{96,64},{128,96},{160,128},{192,160},{224,192},{0,2... | collective-permute-start | bytes 2312 | tf_op jit(solution)/shard_map/ppermute | solution.py:23
  152.5 7.2 %collective-permute-start.26 = (f32[2,4,3,70]{3,2,1,0:T(4,128)S(1)}, f32[2,4,3,70]{3,2,1,0:T(4,128)S(1)}, u32[]{:S(2)}, u32[]{:S(2)}) collective-permute-start(f32[2,4,3,70]{3,2,1,0:T(4,128)S(1)} %get-tuple-element.147), channel_id=1, source_target_pairs={{0,1},{1,2},{2,3},{3,4},{4,5},{5,6},{6,7},{7,8},{8,9},{9,10},{10,1... | collective-permute-start | bytes 20168 | tf_op jit(solution)/shard_map/ppermute | solution.py:21
  152.6 7.1 %collective-permute-start.27 = (f32[2,4,3,70]{3,2,1,0:T(4,128)S(1)}, f32[2,4,3,70]{3,2,1,0:T(4,128)S(1)}, u32[]{:S(2)}, u32[]{:S(2)}) collective-permute-start(f32[2,4,3,70]{3,2,1,0:T(4,128)S(1)} %get-tuple-element.148), channel_id=1, source_target_pairs={{1,0},{2,1},{3,2},{4,3},{5,4},{6,5},{7,6},{8,7},{9,8},{10,9},{11,1... | collective-permute-start | bytes 20168 | tf_op jit(solution)/shard_map/ppermute | solution.py:23
  160.1 0.9 copy-start.9
  162.1 5.6 %collective-permute-start.28 = (f32[2,8,16,3]{3,2,1,0:T(8,128)S(1)}, f32[2,8,16,3]{3,2,1,0:T(8,128)S(1)}, u32[]{:S(2)}, u32[]{:S(2)}) collective-permute-start(f32[2,8,16,3]{3,2,1,0:T(8,128)S(1)} %get-tuple-element.99), channel_id=1, source_target_pairs={{0,32},{32,64},{64,96},{96,128},{128,160},{160,192},{192,224},{224... | collective-permute-start | bytes 9224 | tf_op jit(solution)/shard_map/ppermute | solution.py:21
  162.2 5.6 %collective-permute-start.29 = (f32[2,8,16,3]{3,2,1,0:T(8,128)S(1)}, f32[2,8,16,3]{3,2,1,0:T(8,128)S(1)}, u32[]{:S(2)}, u32[]{:S(2)}) collective-permute-start(f32[2,8,16,3]{3,2,1,0:T(8,128)S(1)} %get-tuple-element.100), channel_id=1, source_target_pairs={{32,0},{64,32},{96,64},{128,96},{160,128},{192,160},{224,192},{0,2... | collective-permute-start | bytes 9224 | tf_op jit(solution)/shard_map/ppermute | solution.py:23
  167.9 7.6 %collective-permute-start.30 = (f32[2,8,3,134]{3,1,2,0:T(8,128)S(1)}, f32[2,8,3,134]{3,1,2,0:T(8,128)S(1)}, u32[]{:S(2)}, u32[]{:S(2)}) collective-permute-start(f32[2,8,3,134]{3,1,2,0:T(8,128)S(1)} %copy.505), channel_id=1, source_target_pairs={{0,1},{1,2},{2,3},{3,4},{4,5},{5,6},{6,7},{7,8},{8,9},{9,10},{10,1... | collective-permute-start | bytes 77192 | tf_op jit(solution)/shard_map/ppermute | solution.py:21
  168.1 7.5 %collective-permute-start.31 = (f32[2,8,3,134]{3,1,2,0:T(8,128)S(1)}, f32[2,8,3,134]{3,1,2,0:T(8,128)S(1)}, u32[]{:S(2)}, u32[]{:S(2)}) collective-permute-start(f32[2,8,3,134]{3,1,2,0:T(8,128)S(1)} %copy.506), channel_id=1, source_target_pairs={{1,0},{2,1},{3,2},{4,3},{5,4},{6,5},{7,6},{8,7},{9,8},{10,9},{11,1... | collective-permute-start | bytes 77192 | tf_op jit(solution)/shard_map/ppermute | solution.py:23
  176.2 1.0 copy-start.4
  178.6 1.1 copy-start.18
  (7 other events, 5.1 us)
where the time goes:
time: 183 us; the launch traced here: 181 us
  starting transfers between devices  64.3 us (35%)
  local copies, waits for them, and re-layouts  43.3 us (24%)
  waiting for transfers between devices  40.5 us (22%)
  other arithmetic  28.9 us (16%)
  between operations  3.74 us (2%)
    ppermute x12, starting transfers between devices, padded(): lax.ppermute(head, axis, [((i + 1) % count, i) for i in range(count)])  52 us
    ppermute x8, waiting for transfers between devices, global_max(): other = lax.ppermute(value, axis, [(i, i ^ step) for i in range(count)])  22.6 us
    concatenate x3, local copies, waits for them, and re-layouts, body(): fields = jnp.concatenate([state, feed[None], kill[None]], 0)  20.9 us
    ppermute x12, waiting for transfers between devices, padded(): lax.ppermute(tail, axis, [(i, (i + 1) % count) for i in range(count)])  17.7 us
    reduce_sum x4, other arithmetic, restrict(): return jnp.mean(blocks, axis=(2, 4, 6))  11.7 us
    ppermute x8, starting transfers between devices, global_max(): other = lax.ppermute(value, axis, [(i, i ^ step) for i in range(count)])  11.2 us
    reshape x2, local copies, waits for them, and re-layouts, restrict(): blocks = field.reshape(lead, depth // 2, 2, rows // 2, 2, cols // 2, 2)  10.9 us
    add x12, other arithmetic, chebyshev(): iterate = crop(iterate, halo + 1, halo) + update  4.68 us
  transfers between devices with their start and end apart: 32, of which 19 were waited for; matrix products, arithmetic and copies ran while one was open for 20% of the time, Pallas kernels for 0%

commit v1 on v0

--- a/solution.py
+++ b/solution.py
@@ -55,8 +55,15 @@
 
 def restrict(field):
     lead, depth, rows, cols = field.shape
-    blocks = field.reshape(lead, depth // 2, 2, rows // 2, 2, cols // 2, 2)
-    return jnp.mean(blocks, axis=(2, 4, 6))
+    count = lead * depth * rows
+    pick_x = (lax.broadcasted_iota(jnp.int32, (cols, cols // 2), 0) // 2
+              == lax.broadcasted_iota(jnp.int32, (cols, cols // 2), 1)).astype(jnp.float32)
+    row = lax.broadcasted_iota(jnp.int32, (count // 4, count), 1)
+    target = ((row // (depth * rows)) * (depth // 2) + (row // rows) % depth // 2) * (rows // 2) + row % rows // 2
+    pick_rows = (lax.broadcasted_iota(jnp.int32, (count // 4, count), 0) == target).astype(jnp.float32)
+    pairs = jnp.dot(field.reshape(count, cols), pick_x, precision=lax.Precision.HIGHEST)
+    blocks = jnp.dot(pick_rows, pairs, precision=lax.Precision.HIGHEST)
+    return (blocks * 0.125).reshape(lead, depth // 2, rows // 2, cols // 2)
 
 
 def prolong(field):

time: 183 us -> 142 us (0.78)
  local copies, waits for them, and re-layouts: 43.3 us -> 10.5 us
  other arithmetic: 28.9 us -> 17.1 us
  starting transfers between devices: 64.3 us -> 71.2 us
  waiting for transfers between devices: 40.5 us -> 35.2 us
  matrix products: 0 us -> 2.06 us
    concatenate x3 -> x0, local copies, waits for them, and re-layouts: 20.9 us -> none  [body(): fields = jnp.concatenate([state, feed[None], kill[None]], 0)]
    reduce_sum x4 -> x0, other arithmetic: 11.7 us -> none  [restrict(): return jnp.mean(blocks, axis=(2, 4, 6))]
    reshape x2 -> x0, local copies, waits for them, and re-layouts: 10.9 us -> none  [restrict(): blocks = field.reshape(lead, depth // 2, 2, rows // 2, 2, cols // 2, 2)]
    ppermute x8, starting transfers between devices: 11.2 us -> 17.6 us  [global_max(): other = lax.ppermute(value, axis, [(i, i ^ step) for i in range(count)])]
    ppermute x8, waiting for transfers between devices: 22.6 us -> 17 us  [global_max(): other = lax.ppermute(value, axis, [(i, i ^ step) for i in range(count)])]
    dot_general x0 -> x8, matrix products: none -> 2.06 us  [the longest x4 1.26 us: restrict(): jnp.dot(field.reshape(count, cols), pick_x, precision=lax.Precision.HIGHEST)]
  transfers between devices with their start and end apart: 32 -> 32, of which waited for: 19 -> 18; matrix products, arithmetic and copies ran while one was open for 20% -> 1% of each run, Pallas kernels for 0% -> 0%
where the time goes in v1:
time: 142 us; the launch traced here: 140 us
  starting transfers between devices  71.2 us (50%)
  waiting for transfers between devices  35.2 us (25%)
  other arithmetic  17.1 us (12%)
  local copies, waits for them, and re-layouts  10.5 us (7%)
  between operations  3.69 us (3%)
  matrix products  2.06 us (1%)
    ppermute x12, starting transfers between devices, padded(): lax.ppermute(head, axis, [((i + 1) % count, i) for i in range(count)])  51.6 us
    ppermute x12, waiting for transfers between devices, padded(): lax.ppermute(tail, axis, [(i, (i + 1) % count) for i in range(count)])  18.1 us
    ppermute x8, starting transfers between devices, global_max(): other = lax.ppermute(value, axis, [(i, i ^ step) for i in range(count)])  17.6 us
    ppermute x8, waiting for transfers between devices, global_max(): other = lax.ppermute(value, axis, [(i, i ^ step) for i in range(count)])  17 us
    add x12, other arithmetic, chebyshev(): iterate = crop(iterate, halo + 1, halo) + update  4.03 us
    another operation x1, local copies, waits for them, and re-layouts, body(): local = jnp.stack(local).reshape(3, 2)  3.81 us
    add x16, other arithmetic, operate(): first = coeff[0] * centre[0] + coeff[1] * centre[1]  3.52 us
    slice x31, local copies, waits for them, and re-layouts, shrunk_neighbours(): along_z = jnp.roll(centre, 1, 1) + jnp.roll(centre, -1, 1)  3.43 us
  transfers between devices with their start and end apart: 32, of which 18 were waited for; matrix products, arithmetic and copies ran while one was open for 1% of the time, Pallas kernels for 0%

profile of v1, /device:TPU:0, one launch (start us, length us, event | category | flops | bytes accessed | tf_op | source)
XLA Modules:
  0.0 139.7 jit_solution(10788093562873671295)
XLA Ops:
  0.2 1.7 %fusion.127 = (f32[]{:T(128)}, f32[]{:T(128)}) fusion(f32[8,16,128]{2,1,0:T(8,128)} %param.25, f32[8,16,128]{2,1,0:T(8,128)} %param.24, f32[2,8,16,128]{3,2,1,0:T(8,128)} %param.22), kind=kLoop, calls=%fused_computation.266 | loop fusion | flops 262142 | bytes 262152 | tf_op jit(solution)/shard_map/reduce_max | solution.py:153
  1.8 1.0 pad_maximum_fusion.5
  3.5 0.8 fusion.173
  4.7 0.7 fusion.303
  5.4 3.8 %stack.88 = f32[6]{0:T(128)S(1)} concatenate(f32[1]{0:T(128)} %bitcast.10, f32[1]{0:T(128)} %bitcast.12, f32[1]{0:T(128)} %bitcast.14, f32[1]{0:T(128)} %bitcast.15, f32[1]{0:T(128)} %bitcast.16, f32[1]{0:T(128)} %bitcast.17), dimensions={0} | concatenate | bytes 48 | tf_op jit(solution)/shard_map/stack | solution.py:154
  10.4 2.5 %collective-permute-start.1 = (f32[6,8,16,4]{3,2,1,0:T(8,128)S(1)}, f32[6,8,16,4]{3,2,1,0:T(8,128)S(1)}, u32[]{:S(2)}, u32[]{:S(2)}) collective-permute-start(f32[6,8,16,4]{3,2,1,0:T(8,128)S(1)} %get-tuple-element.90), channel_id=1, source_target_pairs={{32,0},{64,32},{96,64},{128,96},{160,128},{192,160},{224,192},{0,2... | collective-permute-start | bytes 36872 | tf_op jit(solution)/shard_map/ppermute | solution.py:23
  13.1 4.6 %collective-permute-done.5 = f32[3]{0:T(128)S(1)} collective-permute-done((f32[3]{0:T(128)S(1)}, f32[3]{0:T(128)S(1)}, u32[]{:S(2)}, u32[]{:S(2)}) %collective-permute-start.5) | collective-permute-done | bytes 44 | tf_op jit(solution)/shard_map/ppermute | solution.py:50
  17.8 2.1 %collective-permute-start.6 = (f32[3]{0:T(128)S(1)}, f32[3]{0:T(128)S(1)}, u32[]{:S(2)}, u32[]{:S(2)}) collective-permute-start(f32[3]{0:T(128)S(1)} %max.33), channel_id=1, source_target_pairs={{0,128},{32,160},{64,192},{96,224},{128,0},{160,32},{192,64},{224,... | collective-permute-start | bytes 44 | tf_op jit(solution)/shard_map/ppermute | solution.py:50
  19.9 2.9 %collective-permute-done.6 = f32[3]{0:T(128)S(1)} collective-permute-done((f32[3]{0:T(128)S(1)}, f32[3]{0:T(128)S(1)}, u32[]{:S(2)}, u32[]{:S(2)}) %collective-permute-start.6) | collective-permute-done | bytes 44 | tf_op jit(solution)/shard_map/ppermute | solution.py:50
  22.8 1.3 collective-permute-start.7
  24.1 2.2 %collective-permute-done.7 = f32[3]{0:T(128)S(1)} collective-permute-done((f32[3]{0:T(128)S(1)}, f32[3]{0:T(128)S(1)}, u32[]{:S(2)}, u32[]{:S(2)}) %collective-permute-start.7) | collective-permute-done | bytes 44 | tf_op jit(solution)/shard_map/ppermute | solution.py:50
  26.3 2.6 %collective-permute-start.8 = (f32[3]{0:T(128)S(1)}, f32[3]{0:T(128)S(1)}, u32[]{:S(2)}, u32[]{:S(2)}) collective-permute-start(f32[3]{0:T(128)S(1)} %max.35), channel_id=1, source_target_pairs={{0,2},{1,3},{2,0},{3,1},{4,6},{5,7},{6,4},{7,5},{8,10},{9,11},{10,... | collective-permute-start | bytes 44 | tf_op jit(solution)/shard_map/ppermute | solution.py:50
  29.0 1.8 %collective-permute-done.8 = f32[3]{0:T(128)S(1)} collective-permute-done((f32[3]{0:T(128)S(1)}, f32[3]{0:T(128)S(1)}, u32[]{:S(2)}, u32[]{:S(2)}) %collective-permute-start.8) | collective-permute-done | bytes 44 | tf_op jit(solution)/shard_map/ppermute | solution.py:50
  30.8 6.6 %collective-permute-start.9 = (f32[3]{0:T(128)S(1)}, f32[3]{0:T(128)S(1)}, u32[]{:S(2)}, u32[]{:S(2)}) collective-permute-start(f32[3]{0:T(128)S(1)} %max.36), channel_id=1, source_target_pairs={{0,4},{1,5},{2,6},{3,7},{4,0},{5,1},{6,2},{7,3},{8,12},{9,13},{10,... | collective-permute-start | bytes 44 | tf_op jit(solution)/shard_map/ppermute | solution.py:50
  37.4 1.5 %collective-permute-done.9 = f32[3]{0:T(128)S(1)} collective-permute-done((f32[3]{0:T(128)S(1)}, f32[3]{0:T(128)S(1)}, u32[]{:S(2)}, u32[]{:S(2)}) %collective-permute-start.9) | collective-permute-done | bytes 44 | tf_op jit(solution)/shard_map/ppermute | solution.py:50
  38.9 1.6 %collective-permute-start.10 = (f32[3]{0:T(128)S(1)}, f32[3]{0:T(128)S(1)}, u32[]{:S(2)}, u32[]{:S(2)}) collective-permute-start(f32[3]{0:T(128)S(1)} %max.37), channel_id=1, source_target_pairs={{0,8},{1,9},{2,10},{3,11},{4,12},{5,13},{6,14},{7,15},{8,0},{9,1},... | collective-permute-start | bytes 44 | tf_op jit(solution)/shard_map/ppermute | solution.py:50
  40.4 2.0 %collective-permute-done.10 = f32[3]{0:T(128)S(1)} collective-permute-done((f32[3]{0:T(128)S(1)}, f32[3]{0:T(128)S(1)}, u32[]{:S(2)}, u32[]{:S(2)}) %collective-permute-start.10) | collective-permute-done | bytes 44 | tf_op jit(solution)/shard_map/ppermute | solution.py:50
  42.4 3.2 %collective-permute-start.11 = (f32[3]{0:T(128)S(1)}, f32[3]{0:T(128)S(1)}, u32[]{:S(2)}, u32[]{:S(2)}) collective-permute-start(f32[3]{0:T(128)S(1)} %max.38), channel_id=1, source_target_pairs={{0,16},{1,17},{2,18},{3,19},{4,20},{5,21},{6,22},{7,23},{8,24},{9,... | collective-permute-start | bytes 44 | tf_op jit(solution)/shard_map/ppermute | solution.py:50
  45.6 1.9 %collective-permute-done.11 = f32[3]{0:T(128)S(1)} collective-permute-done((f32[3]{0:T(128)S(1)}, f32[3]{0:T(128)S(1)}, u32[]{:S(2)}, u32[]{:S(2)}) %collective-permute-start.11) | collective-permute-done | bytes 44 | tf_op jit(solution)/shard_map/ppermute | solution.py:50
  47.9 1.0 collective-permute-start.2
  48.9 6.3 %collective-permute-start.3 = (f32[6,8,4,136]{3,2,1,0:T(4,128)S(1)}, f32[6,8,4,136]{3,2,1,0:T(4,128)S(1)}, u32[]{:S(2)}, u32[]{:S(2)}) collective-permute-start(f32[6,8,4,136]{3,2,1,0:T(4,128)S(1)} %get-tuple-element.48), channel_id=1, source_target_pairs={{1,0},{2,1},{3,2},{4,3},{5,4},{6,5},{7,6},{8,7},{9,8},{10,9},{11,1... | collective-permute-start | bytes 313352 | tf_op jit(solution)/shard_map/ppermute | solution.py:23
  55.2 0.7 fusion.396
  56.8 1.8 %collective-permute-done.2 = f32[6,8,4,136]{3,2,1,0:T(4,128)S(1)} collective-permute-done((f32[6,8,4,136]{3,2,1,0:T(4,128)S(1)}, f32[6,8,4,136]{3,2,1,0:T(4,128)S(1)}, u32[]{:S(2)}, u32[]{:S(2)}) %collective-permute-start.2) | collective-permute-done | bytes 104480 | tf_op jit(solution)/shard_map/ppermute | solution.py:21
  61.6 0.6 slice_add_fusion.12
  63.1 0.7 fusion.20
  63.9 0.8 multiply_add_fusion.13
  65.7 2.9 %collective-permute-start.13 = (f32[6,4,8,3]{3,2,1,0:T(8,128)S(1)}, f32[6,4,8,3]{3,2,1,0:T(8,128)S(1)}, u32[]{:S(2)}, u32[]{:S(2)}) collective-permute-start(f32[6,4,8,3]{3,2,1,0:T(8,128)S(1)} %get-tuple-element.106), channel_id=1, source_target_pairs={{32,0},{64,32},{96,64},{128,96},{160,128},{192,160},{224,192},{0,2... | collective-permute-start | bytes 6920 | tf_op jit(solution)/shard_map/ppermute | solution.py:23
  68.6 2.3 %collective-permute-done.12 = f32[6,4,8,3]{3,2,1,0:T(8,128)S(1)} collective-permute-done((f32[6,4,8,3]{3,2,1,0:T(8,128)S(1)}, f32[6,4,8,3]{3,2,1,0:T(8,128)S(1)}, u32[]{:S(2)}, u32[]{:S(2)}) %collective-permute-start.12) | collective-permute-done | bytes 2336 | tf_op jit(solution)/shard_map/ppermute | solution.py:21
  71.2 5.7 %collective-permute-start.15 = (f32[6,4,3,70]{3,2,1,0:T(4,128)S(1)}, f32[6,4,3,70]{3,2,1,0:T(4,128)S(1)}, u32[]{:S(2)}, u32[]{:S(2)}) collective-permute-start(f32[6,4,3,70]{3,2,1,0:T(4,128)S(1)} %get-tuple-element.104), channel_id=1, source_target_pairs={{1,0},{2,1},{3,2},{4,3},{5,4},{6,5},{7,6},{8,7},{9,8},{10,9},{11,1... | collective-permute-start | bytes 60488 | tf_op jit(solution)/shard_map/ppermute | solution.py:23
  77.8 1.0 collective-permute-done.14
  81.0 2.9 %collective-permute-start.17 = (f32[6,2,4,3]{3,2,1,0:T(4,128)S(1)}, f32[6,2,4,3]{3,2,1,0:T(4,128)S(1)}, u32[]{:S(2)}, u32[]{:S(2)}) collective-permute-start(f32[6,2,4,3]{3,2,1,0:T(4,128)S(1)} %get-tuple-element.164), channel_id=1, source_target_pairs={{32,0},{64,32},{96,64},{128,96},{160,128},{192,160},{224,192},{0,2... | collective-permute-start | bytes 1736 | tf_op jit(solution)/shard_map/ppermute | solution.py:23
  83.9 1.5 %collective-permute-done.16 = f32[6,2,4,3]{3,2,1,0:T(4,128)S(1)} collective-permute-done((f32[6,2,4,3]{3,2,1,0:T(4,128)S(1)}, f32[6,2,4,3]{3,2,1,0:T(4,128)S(1)}, u32[]{:S(2)}, u32[]{:S(2)}) %collective-permute-start.16) | collective-permute-done | bytes 608 | tf_op jit(solution)/shard_map/ppermute | solution.py:21
  85.6 5.5 %collective-permute-start.19 = (f32[6,2,3,38]{3,2,1,0:T(4,128)S(1)}, f32[6,2,3,38]{3,2,1,0:T(4,128)S(1)}, u32[]{:S(2)}, u32[]{:S(2)}) collective-permute-start(f32[6,2,3,38]{3,2,1,0:T(4,128)S(1)} %get-tuple-element.162), channel_id=1, source_target_pairs={{1,0},{2,1},{3,2},{4,3},{5,4},{6,5},{7,6},{8,7},{9,8},{10,9},{11,1... | collective-permute-start | bytes 16424 | tf_op jit(solution)/shard_map/ppermute | solution.py:23
  92.0 0.8 collective-permute-done.18
  93.6 3.0 %collective-permute-start.21 = (f32[2,2,4,3]{3,2,1,0:T(4,128)S(1)}, f32[2,2,4,3]{3,2,1,0:T(4,128)S(1)}, u32[]{:S(2)}, u32[]{:S(2)}) collective-permute-start(f32[2,2,4,3]{3,2,1,0:T(4,128)S(1)} %get-tuple-element.177), channel_id=1, source_target_pairs={{32,0},{64,32},{96,64},{128,96},{160,128},{192,160},{224,192},{0,2... | collective-permute-start | bytes 584 | tf_op jit(solution)/shard_map/ppermute | solution.py:23
  96.7 1.3 collective-permute-done.20
  98.1 5.7 %collective-permute-start.23 = (f32[2,2,3,38]{3,2,1,0:T(4,128)S(1)}, f32[2,2,3,38]{3,2,1,0:T(4,128)S(1)}, u32[]{:S(2)}, u32[]{:S(2)}) collective-permute-start(f32[2,2,3,38]{3,2,1,0:T(4,128)S(1)} %get-tuple-element.186), channel_id=1, source_target_pairs={{1,0},{2,1},{3,2},{4,3},{5,4},{6,5},{7,6},{8,7},{9,8},{10,9},{11,1... | collective-permute-start | bytes 5480 | tf_op jit(solution)/shard_map/ppermute | solution.py:23
  103.9 1.3 collective-permute-done.22
  106.6 3.0 %collective-permute-start.25 = (f32[2,4,8,3]{3,2,1,0:T(8,128)S(1)}, f32[2,4,8,3]{3,2,1,0:T(8,128)S(1)}, u32[]{:S(2)}, u32[]{:S(2)}) collective-permute-start(f32[2,4,8,3]{3,2,1,0:T(8,128)S(1)} %get-tuple-element.150), channel_id=1, source_target_pairs={{32,0},{64,32},{96,64},{128,96},{160,128},{192,160},{224,192},{0,2... | collective-permute-start | bytes 2312 | tf_op jit(solution)/shard_map/ppermute | solution.py:23
  109.6 1.6 %collective-permute-done.24 = f32[2,4,8,3]{3,2,1,0:T(8,128)S(1)} collective-permute-done((f32[2,4,8,3]{3,2,1,0:T(8,128)S(1)}, f32[2,4,8,3]{3,2,1,0:T(8,128)S(1)}, u32[]{:S(2)}, u32[]{:S(2)}) %collective-permute-start.24) | collective-permute-done | bytes 800 | tf_op jit(solution)/shard_map/ppermute | solution.py:21
  111.4 5.7 %collective-permute-start.27 = (f32[2,4,3,70]{3,2,1,0:T(4,128)S(1)}, f32[2,4,3,70]{3,2,1,0:T(4,128)S(1)}, u32[]{:S(2)}, u32[]{:S(2)}) collective-permute-start(f32[2,4,3,70]{3,2,1,0:T(4,128)S(1)} %get-tuple-element.148), channel_id=1, source_target_pairs={{1,0},{2,1},{3,2},{4,3},{5,4},{6,5},{7,6},{8,7},{9,8},{10,9},{11,1... | collective-permute-start | bytes 20168 | tf_op jit(solution)/shard_map/ppermute | solution.py:23
  117.0 1.6 %collective-permute-done.26 = f32[2,4,3,70]{3,2,1,0:T(4,128)S(1)} collective-permute-done((f32[2,4,3,70]{3,2,1,0:T(4,128)S(1)}, f32[2,4,3,70]{3,2,1,0:T(4,128)S(1)}, u32[]{:S(2)}, u32[]{:S(2)}) %collective-permute-start.26) | collective-permute-done | bytes 6752 | tf_op jit(solution)/shard_map/ppermute | solution.py:21
  121.1 2.9 %collective-permute-start.29 = (f32[2,8,16,3]{3,2,1,0:T(8,128)S(1)}, f32[2,8,16,3]{3,2,1,0:T(8,128)S(1)}, u32[]{:S(2)}, u32[]{:S(2)}) collective-permute-start(f32[2,8,16,3]{3,2,1,0:T(8,128)S(1)} %get-tuple-element.100), channel_id=1, source_target_pairs={{32,0},{64,32},{96,64},{128,96},{160,128},{192,160},{224,192},{0,2... | collective-permute-start | bytes 9224 | tf_op jit(solution)/shard_map/ppermute | solution.py:23
  124.0 2.6 %collective-permute-done.28 = f32[2,8,16,3]{3,2,1,0:T(8,128)S(1)} collective-permute-done((f32[2,8,16,3]{3,2,1,0:T(8,128)S(1)}, f32[2,8,16,3]{3,2,1,0:T(8,128)S(1)}, u32[]{:S(2)}, u32[]{:S(2)}) %collective-permute-start.28) | collective-permute-done | bytes 3104 | tf_op jit(solution)/shard_map/ppermute | solution.py:21
  126.9 5.5 %collective-permute-start.31 = (f32[2,8,3,134]{3,2,1,0:T(4,128)S(1)}, f32[2,8,3,134]{3,2,1,0:T(4,128)S(1)}, u32[]{:S(2)}, u32[]{:S(2)}) collective-permute-start(f32[2,8,3,134]{3,2,1,0:T(4,128)S(1)} %get-tuple-element.70), channel_id=1, source_target_pairs={{1,0},{2,1},{3,2},{4,3},{5,4},{6,5},{7,6},{8,7},{9,8},{10,9},{11,1... | collective-permute-start | bytes 77192 | tf_op jit(solution)/shard_map/ppermute | solution.py:23
  132.4 2.2 %collective-permute-done.30 = f32[2,8,3,134]{3,2,1,0:T(4,128)S(1)} collective-permute-done((f32[2,8,3,134]{3,2,1,0:T(4,128)S(1)}, f32[2,8,3,134]{3,2,1,0:T(4,128)S(1)}, u32[]{:S(2)}, u32[]{:S(2)}) %collective-permute-start.30) | collective-permute-done | bytes 25760 | tf_op jit(solution)/shard_map/ppermute | solution.py:21
  137.6 0.7 slice_add_fusion.2
  138.7 0.9 fusion.63
  (199 shorter events, 18.5 us)
Async XLA Ops:
  3.2 6.4 %copy-start = (f32[2,8,16,128]{3,2,1,0:T(8,128)S(1)}, f32[2,8,16,128]{3,2,1,0:T(8,128)}, u32[]{:S(2)}) copy-start(f32[2,8,16,128]{3,2,1,0:T(8,128)} %param.22) | copy-start | bytes 393220
  3.2 6.4 %copy-start.5 = (f32[8,16,128]{2,1,0:T(8,128)S(1)}, f32[8,16,128]{2,1,0:T(8,128)}, u32[]{:S(2)}) copy-start(f32[8,16,128]{2,1,0:T(8,128)} %param.25) | copy-start | bytes 196612
  3.2 6.4 %copy-start.6 = (f32[8,16,128]{2,1,0:T(8,128)S(1)}, f32[8,16,128]{2,1,0:T(8,128)}, u32[]{:S(2)}) copy-start(f32[8,16,128]{2,1,0:T(8,128)} %param.24) | copy-start | bytes 196612
  3.2 6.4 %copy-start.7 = (f32[2,8,16,128]{3,2,1,0:T(8,128)S(1)}, f32[2,8,16,128]{3,2,1,0:T(8,128)}, u32[]{:S(2)}) copy-start(f32[2,8,16,128]{3,2,1,0:T(8,128)} %param.23) | copy-start | bytes 393220
  9.5 3.5 %collective-permute-start.4 = (f32[3]{0:T(128)S(1)}, f32[3]{0:T(128)S(1)}, u32[]{:S(2)}, u32[]{:S(2)}) collective-permute-start(f32[3]{0:T(128)S(1)} %maximum_reduce_fusion), channel_id=1, source_target_pairs={{0,32},{32,0},{64,96},{96,64},{128,160},{160,128},{192,224},{224,1... | collective-permute-start | bytes 44 | tf_op jit(solution)/shard_map/ppermute | solution.py:50
  9.9 37.6 %collective-permute-start = (f32[6,8,16,4]{3,2,1,0:T(8,128)S(1)}, f32[6,8,16,4]{3,2,1,0:T(8,128)S(1)}, u32[]{:S(2)}, u32[]{:S(2)}) collective-permute-start(f32[6,8,16,4]{3,2,1,0:T(8,128)S(1)} %get-tuple-element.89), channel_id=1, source_target_pairs={{0,32},{32,64},{64,96},{96,128},{128,160},{160,192},{192,224},{224... | collective-permute-start | bytes 36872 | tf_op jit(solution)/shard_map/ppermute | solution.py:21
  10.4 37.2 %collective-permute-start.1 = (f32[6,8,16,4]{3,2,1,0:T(8,128)S(1)}, f32[6,8,16,4]{3,2,1,0:T(8,128)S(1)}, u32[]{:S(2)}, u32[]{:S(2)}) collective-permute-start(f32[6,8,16,4]{3,2,1,0:T(8,128)S(1)} %get-tuple-element.90), channel_id=1, source_target_pairs={{32,0},{64,32},{96,64},{128,96},{160,128},{192,160},{224,192},{0,2... | collective-permute-start | bytes 36872 | tf_op jit(solution)/shard_map/ppermute | solution.py:23
  13.0 4.7 %collective-permute-start.5 = (f32[3]{0:T(128)S(1)}, f32[3]{0:T(128)S(1)}, u32[]{:S(2)}, u32[]{:S(2)}) collective-permute-start(f32[3]{0:T(128)S(1)} %max.32), channel_id=1, source_target_pairs={{0,64},{32,96},{64,0},{96,32},{128,192},{160,224},{192,128},{224,1... | collective-permute-start | bytes 44 | tf_op jit(solution)/shard_map/ppermute | solution.py:50
  17.8 5.0 %collective-permute-start.6 = (f32[3]{0:T(128)S(1)}, f32[3]{0:T(128)S(1)}, u32[]{:S(2)}, u32[]{:S(2)}) collective-permute-start(f32[3]{0:T(128)S(1)} %max.33), channel_id=1, source_target_pairs={{0,128},{32,160},{64,192},{96,224},{128,0},{160,32},{192,64},{224,... | collective-permute-start | bytes 44 | tf_op jit(solution)/shard_map/ppermute | solution.py:50
  22.8 3.5 %collective-permute-start.7 = (f32[3]{0:T(128)S(1)}, f32[3]{0:T(128)S(1)}, u32[]{:S(2)}, u32[]{:S(2)}) collective-permute-start(f32[3]{0:T(128)S(1)} %max.34), channel_id=1, source_target_pairs={{0,1},{1,0},{2,3},{3,2},{4,5},{5,4},{6,7},{7,6},{8,9},{9,8},{10,11... | collective-permute-start | bytes 44 | tf_op jit(solution)/shard_map/ppermute | solution.py:50
  26.3 4.4 %collective-permute-start.8 = (f32[3]{0:T(128)S(1)}, f32[3]{0:T(128)S(1)}, u32[]{:S(2)}, u32[]{:S(2)}) collective-permute-start(f32[3]{0:T(128)S(1)} %max.35), channel_id=1, source_target_pairs={{0,2},{1,3},{2,0},{3,1},{4,6},{5,7},{6,4},{7,5},{8,10},{9,11},{10,... | collective-permute-start | bytes 44 | tf_op jit(solution)/shard_map/ppermute | solution.py:50
  30.8 8.1 %collective-permute-start.9 = (f32[3]{0:T(128)S(1)}, f32[3]{0:T(128)S(1)}, u32[]{:S(2)}, u32[]{:S(2)}) collective-permute-start(f32[3]{0:T(128)S(1)} %max.36), channel_id=1, source_target_pairs={{0,4},{1,5},{2,6},{3,7},{4,0},{5,1},{6,2},{7,3},{8,12},{9,13},{10,... | collective-permute-start | bytes 44 | tf_op jit(solution)/shard_map/ppermute | solution.py:50
  38.9 3.5 %collective-permute-start.10 = (f32[3]{0:T(128)S(1)}, f32[3]{0:T(128)S(1)}, u32[]{:S(2)}, u32[]{:S(2)}) collective-permute-start(f32[3]{0:T(128)S(1)} %max.37), channel_id=1, source_target_pairs={{0,8},{1,9},{2,10},{3,11},{4,12},{5,13},{6,14},{7,15},{8,0},{9,1},... | collective-permute-start | bytes 44 | tf_op jit(solution)/shard_map/ppermute | solution.py:50
  42.4 5.1 %collective-permute-start.11 = (f32[3]{0:T(128)S(1)}, f32[3]{0:T(128)S(1)}, u32[]{:S(2)}, u32[]{:S(2)}) collective-permute-start(f32[3]{0:T(128)S(1)} %max.38), channel_id=1, source_target_pairs={{0,16},{1,17},{2,18},{3,19},{4,20},{5,21},{6,22},{7,23},{8,24},{9,... | collective-permute-start | bytes 44 | tf_op jit(solution)/shard_map/ppermute | solution.py:50
  47.9 10.7 %collective-permute-start.2 = (f32[6,8,4,136]{3,2,1,0:T(4,128)S(1)}, f32[6,8,4,136]{3,2,1,0:T(4,128)S(1)}, u32[]{:S(2)}, u32[]{:S(2)}) collective-permute-start(f32[6,8,4,136]{3,2,1,0:T(4,128)S(1)} %get-tuple-element.47), channel_id=1, source_target_pairs={{0,1},{1,2},{2,3},{3,4},{4,5},{5,6},{6,7},{7,8},{8,9},{9,10},{10,1... | collective-permute-start | bytes 313352 | tf_op jit(solution)/shard_map/ppermute | solution.py:21
  48.9 9.7 %collective-permute-start.3 = (f32[6,8,4,136]{3,2,1,0:T(4,128)S(1)}, f32[6,8,4,136]{3,2,1,0:T(4,128)S(1)}, u32[]{:S(2)}, u32[]{:S(2)}) collective-permute-start(f32[6,8,4,136]{3,2,1,0:T(4,128)S(1)} %get-tuple-element.48), channel_id=1, source_target_pairs={{1,0},{2,1},{3,2},{4,3},{5,4},{6,5},{7,6},{8,7},{9,8},{10,9},{11,1... | collective-permute-start | bytes 313352 | tf_op jit(solution)/shard_map/ppermute | solution.py:23
  59.5 0.7 copy-start.9
  61.5 0.7 copy-start.1
  61.5 0.8 copy-start.3
  65.6 13.7 %copy-start.10 = (f32[2]{0:T(128)S(1)}, f32[2]{0:T(128)}, u32[]{:S(2)}) copy-start(f32[2]{0:T(128)} %constant.330.clone) | copy-start | bytes 28
  65.7 5.3 %collective-permute-start.12 = (f32[6,4,8,3]{3,2,1,0:T(8,128)S(1)}, f32[6,4,8,3]{3,2,1,0:T(8,128)S(1)}, u32[]{:S(2)}, u32[]{:S(2)}) collective-permute-start(f32[6,4,8,3]{3,2,1,0:T(8,128)S(1)} %get-tuple-element.105), channel_id=1, source_target_pairs={{0,32},{32,64},{64,96},{96,128},{128,160},{160,192},{192,224},{224... | collective-permute-start | bytes 6920 | tf_op jit(solution)/shard_map/ppermute | solution.py:21
  65.7 5.2 %collective-permute-start.13 = (f32[6,4,8,3]{3,2,1,0:T(8,128)S(1)}, f32[6,4,8,3]{3,2,1,0:T(8,128)S(1)}, u32[]{:S(2)}, u32[]{:S(2)}) collective-permute-start(f32[6,4,8,3]{3,2,1,0:T(8,128)S(1)} %get-tuple-element.106), channel_id=1, source_target_pairs={{32,0},{64,32},{96,64},{128,96},{160,128},{192,160},{224,192},{0,2... | collective-permute-start | bytes 6920 | tf_op jit(solution)/shard_map/ppermute | solution.py:23
  71.1 7.8 %collective-permute-start.14 = (f32[6,4,3,70]{3,2,1,0:T(4,128)S(1)}, f32[6,4,3,70]{3,2,1,0:T(4,128)S(1)}, u32[]{:S(2)}, u32[]{:S(2)}) collective-permute-start(f32[6,4,3,70]{3,2,1,0:T(4,128)S(1)} %get-tuple-element.103), channel_id=1, source_target_pairs={{0,1},{1,2},{2,3},{3,4},{4,5},{5,6},{6,7},{7,8},{8,9},{9,10},{10,1... | collective-permute-start | bytes 60488 | tf_op jit(solution)/shard_map/ppermute | solution.py:21
  71.2 7.7 %collective-permute-start.15 = (f32[6,4,3,70]{3,2,1,0:T(4,128)S(1)}, f32[6,4,3,70]{3,2,1,0:T(4,128)S(1)}, u32[]{:S(2)}, u32[]{:S(2)}) collective-permute-start(f32[6,4,3,70]{3,2,1,0:T(4,128)S(1)} %get-tuple-element.104), channel_id=1, source_target_pairs={{1,0},{2,1},{3,2},{4,3},{5,4},{6,5},{7,6},{8,7},{9,8},{10,9},{11,1... | collective-permute-start | bytes 60488 | tf_op jit(solution)/shard_map/ppermute | solution.py:23
  79.8 13.3 %copy-start.11 = (f32[2]{0:T(128)S(1)}, f32[2]{0:T(128)}, u32[]{:S(2)}) copy-start(f32[2]{0:T(128)} %constant.331.clone) | copy-start | bytes 28
  80.9 4.5 %collective-permute-start.16 = (f32[6,2,4,3]{3,2,1,0:T(4,128)S(1)}, f32[6,2,4,3]{3,2,1,0:T(4,128)S(1)}, u32[]{:S(2)}, u32[]{:S(2)}) collective-permute-start(f32[6,2,4,3]{3,2,1,0:T(4,128)S(1)} %get-tuple-element.163), channel_id=1, source_target_pairs={{0,32},{32,64},{64,96},{96,128},{128,160},{160,192},{192,224},{224... | collective-permute-start | bytes 1736 | tf_op jit(solution)/shard_map/ppermute | solution.py:21
  81.0 4.5 %collective-permute-start.17 = (f32[6,2,4,3]{3,2,1,0:T(4,128)S(1)}, f32[6,2,4,3]{3,2,1,0:T(4,128)S(1)}, u32[]{:S(2)}, u32[]{:S(2)}) collective-permute-start(f32[6,2,4,3]{3,2,1,0:T(4,128)S(1)} %get-tuple-element.164), channel_id=1, source_target_pairs={{32,0},{64,32},{96,64},{128,96},{160,128},{192,160},{224,192},{0,2... | collective-permute-start | bytes 1736 | tf_op jit(solution)/shard_map/ppermute | solution.py:23
  85.5 7.3 %collective-permute-start.18 = (f32[6,2,3,38]{3,2,1,0:T(4,128)S(1)}, f32[6,2,3,38]{3,2,1,0:T(4,128)S(1)}, u32[]{:S(2)}, u32[]{:S(2)}) collective-permute-start(f32[6,2,3,38]{3,2,1,0:T(4,128)S(1)} %get-tuple-element.161), channel_id=1, source_target_pairs={{0,1},{1,2},{2,3},{3,4},{4,5},{5,6},{6,7},{7,8},{8,9},{9,10},{10,1... | collective-permute-start | bytes 16424 | tf_op jit(solution)/shard_map/ppermute | solution.py:21
  85.6 7.2 %collective-permute-start.19 = (f32[6,2,3,38]{3,2,1,0:T(4,128)S(1)}, f32[6,2,3,38]{3,2,1,0:T(4,128)S(1)}, u32[]{:S(2)}, u32[]{:S(2)}) collective-permute-start(f32[6,2,3,38]{3,2,1,0:T(4,128)S(1)} %get-tuple-element.162), channel_id=1, source_target_pairs={{1,0},{2,1},{3,2},{4,3},{5,4},{6,5},{7,6},{8,7},{9,8},{10,9},{11,1... | collective-permute-start | bytes 16424 | tf_op jit(solution)/shard_map/ppermute | solution.py:23
  93.6 4.3 %collective-permute-start.20 = (f32[2,2,4,3]{3,2,1,0:T(4,128)S(1)}, f32[2,2,4,3]{3,2,1,0:T(4,128)S(1)}, u32[]{:S(2)}, u32[]{:S(2)}) collective-permute-start(f32[2,2,4,3]{3,2,1,0:T(4,128)S(1)} %get-tuple-element.176), channel_id=1, source_target_pairs={{0,32},{32,64},{64,96},{96,128},{128,160},{160,192},{192,224},{224... | collective-permute-start | bytes 584 | tf_op jit(solution)/shard_map/ppermute | solution.py:21
  93.6 4.3 %collective-permute-start.21 = (f32[2,2,4,3]{3,2,1,0:T(4,128)S(1)}, f32[2,2,4,3]{3,2,1,0:T(4,128)S(1)}, u32[]{:S(2)}, u32[]{:S(2)}) collective-permute-start(f32[2,2,4,3]{3,2,1,0:T(4,128)S(1)} %get-tuple-element.177), channel_id=1, source_target_pairs={{32,0},{64,32},{96,64},{128,96},{160,128},{192,160},{224,192},{0,2... | collective-permute-start | bytes 584 | tf_op jit(solution)/shard_map/ppermute | solution.py:23
  98.0 7.1 %collective-permute-start.22 = (f32[2,2,3,38]{3,2,1,0:T(4,128)S(1)}, f32[2,2,3,38]{3,2,1,0:T(4,128)S(1)}, u32[]{:S(2)}, u32[]{:S(2)}) collective-permute-start(f32[2,2,3,38]{3,2,1,0:T(4,128)S(1)} %get-tuple-element.185), channel_id=1, source_target_pairs={{0,1},{1,2},{2,3},{3,4},{4,5},{5,6},{6,7},{7,8},{8,9},{9,10},{10,1... | collective-permute-start | bytes 5480 | tf_op jit(solution)/shard_map/ppermute | solution.py:21
  98.1 7.1 %collective-permute-start.23 = (f32[2,2,3,38]{3,2,1,0:T(4,128)S(1)}, f32[2,2,3,38]{3,2,1,0:T(4,128)S(1)}, u32[]{:S(2)}, u32[]{:S(2)}) collective-permute-start(f32[2,2,3,38]{3,2,1,0:T(4,128)S(1)} %get-tuple-element.186), channel_id=1, source_target_pairs={{1,0},{2,1},{3,2},{4,3},{5,4},{6,5},{7,6},{8,7},{9,8},{10,9},{11,1... | collective-permute-start | bytes 5480 | tf_op jit(solution)/shard_map/ppermute | solution.py:23
  106.6 4.6 %collective-permute-start.24 = (f32[2,4,8,3]{3,2,1,0:T(8,128)S(1)}, f32[2,4,8,3]{3,2,1,0:T(8,128)S(1)}, u32[]{:S(2)}, u32[]{:S(2)}) collective-permute-start(f32[2,4,8,3]{3,2,1,0:T(8,128)S(1)} %get-tuple-element.149), channel_id=1, source_target_pairs={{0,32},{32,64},{64,96},{96,128},{128,160},{160,192},{192,224},{224... | collective-permute-start | bytes 2312 | tf_op jit(solution)/shard_map/ppermute | solution.py:21
  106.6 4.6 %collective-permute-start.25 = (f32[2,4,8,3]{3,2,1,0:T(8,128)S(1)}, f32[2,4,8,3]{3,2,1,0:T(8,128)S(1)}, u32[]{:S(2)}, u32[]{:S(2)}) collective-permute-start(f32[2,4,8,3]{3,2,1,0:T(8,128)S(1)} %get-tuple-element.150), channel_id=1, source_target_pairs={{32,0},{64,32},{96,64},{128,96},{160,128},{192,160},{224,192},{0,2... | collective-permute-start | bytes 2312 | tf_op jit(solution)/shard_map/ppermute | solution.py:23
  111.3 7.4 %collective-permute-start.26 = (f32[2,4,3,70]{3,2,1,0:T(4,128)S(1)}, f32[2,4,3,70]{3,2,1,0:T(4,128)S(1)}, u32[]{:S(2)}, u32[]{:S(2)}) collective-permute-start(f32[2,4,3,70]{3,2,1,0:T(4,128)S(1)} %get-tuple-element.147), channel_id=1, source_target_pairs={{0,1},{1,2},{2,3},{3,4},{4,5},{5,6},{6,7},{7,8},{8,9},{9,10},{10,1... | collective-permute-start | bytes 20168 | tf_op jit(solution)/shard_map/ppermute | solution.py:21
  111.4 7.3 %collective-permute-start.27 = (f32[2,4,3,70]{3,2,1,0:T(4,128)S(1)}, f32[2,4,3,70]{3,2,1,0:T(4,128)S(1)}, u32[]{:S(2)}, u32[]{:S(2)}) collective-permute-start(f32[2,4,3,70]{3,2,1,0:T(4,128)S(1)} %get-tuple-element.148), channel_id=1, source_target_pairs={{1,0},{2,1},{3,2},{4,3},{5,4},{6,5},{7,6},{8,7},{9,8},{10,9},{11,1... | collective-permute-start | bytes 20168 | tf_op jit(solution)/shard_map/ppermute | solution.py:23
  121.1 5.6 %collective-permute-start.28 = (f32[2,8,16,3]{3,2,1,0:T(8,128)S(1)}, f32[2,8,16,3]{3,2,1,0:T(8,128)S(1)}, u32[]{:S(2)}, u32[]{:S(2)}) collective-permute-start(f32[2,8,16,3]{3,2,1,0:T(8,128)S(1)} %get-tuple-element.99), channel_id=1, source_target_pairs={{0,32},{32,64},{64,96},{96,128},{128,160},{160,192},{192,224},{224... | collective-permute-start | bytes 9224 | tf_op jit(solution)/shard_map/ppermute | solution.py:21
  121.1 5.6 %collective-permute-start.29 = (f32[2,8,16,3]{3,2,1,0:T(8,128)S(1)}, f32[2,8,16,3]{3,2,1,0:T(8,128)S(1)}, u32[]{:S(2)}, u32[]{:S(2)}) collective-permute-start(f32[2,8,16,3]{3,2,1,0:T(8,128)S(1)} %get-tuple-element.100), channel_id=1, source_target_pairs={{32,0},{64,32},{96,64},{128,96},{160,128},{192,160},{224,192},{0,2... | collective-permute-start | bytes 9224 | tf_op jit(solution)/shard_map/ppermute | solution.py:23
  126.8 7.7 %collective-permute-start.30 = (f32[2,8,3,134]{3,2,1,0:T(4,128)S(1)}, f32[2,8,3,134]{3,2,1,0:T(4,128)S(1)}, u32[]{:S(2)}, u32[]{:S(2)}) collective-permute-start(f32[2,8,3,134]{3,2,1,0:T(4,128)S(1)} %get-tuple-element.69), channel_id=1, source_target_pairs={{0,1},{1,2},{2,3},{3,4},{4,5},{5,6},{6,7},{7,8},{8,9},{9,10},{10,1... | collective-permute-start | bytes 77192 | tf_op jit(solution)/shard_map/ppermute | solution.py:21
  126.9 7.7 %collective-permute-start.31 = (f32[2,8,3,134]{3,2,1,0:T(4,128)S(1)}, f32[2,8,3,134]{3,2,1,0:T(4,128)S(1)}, u32[]{:S(2)}, u32[]{:S(2)}) collective-permute-start(f32[2,8,3,134]{3,2,1,0:T(4,128)S(1)} %get-tuple-element.70), channel_id=1, source_target_pairs={{1,0},{2,1},{3,2},{4,3},{5,4},{6,5},{7,6},{8,7},{9,8},{10,9},{11,1... | collective-permute-start | bytes 77192 | tf_op jit(solution)/shard_map/ppermute | solution.py:23
  135.2 0.9 copy-start.2
  135.2 1.0 copy-start.4
  137.6 1.1 copy-start.8

commit v2 on v1

--- a/solution.py
+++ b/solution.py
@@ -2,6 +2,8 @@
 import jax.numpy as jnp
 from jax import lax
 from jax.sharding import PartitionSpec as P
+from jax.experimental import pallas as pl
+from jax.experimental.pallas import tpu as pltpu
 
 substrate_diffusion = 40.0
 catalyst_diffusion = 20.0
@@ -42,15 +44,72 @@
     return along_x + along_y + along_z
 
 
-def global_max(value):
-    for axis in ("gx", "gy"):
-        count = lax.axis_size(axis)
-        step = 1
-        while step < count:
-            other = lax.ppermute(value, axis, [(i, i ^ step) for i in range(count)])
-            value = jnp.maximum(value, other)
-            step *= 2
-    return value
+def gather_kernel(axis, value, out, land, send_sem, recv_sem, own_sem):
+    count = lax.axis_size(axis)
+    me = lax.axis_index(axis)
+    other = lax.axis_index("gy" if axis == "gx" else "gx")
+    mesh_ids = pl.DeviceIdType.MESH
+
+    def device(index):
+        return (index, other) if axis == "gx" else (other, index)
+
+    barrier = pltpu.get_barrier_semaphore()
+    for step in range(1, count):
+        pl.semaphore_signal(barrier, 1, device_id=device(lax.rem(me + step, count)),
+                            device_id_type=mesh_ids)
+    pl.semaphore_wait(barrier, count - 1)
+    copies = []
+    for step in range(1, count):
+        copy = pltpu.make_async_remote_copy(
+            src_ref=value,
+            dst_ref=land.at[me],
+            send_sem=send_sem.at[step],
+            recv_sem=recv_sem.at[me],
+            device_id=device(lax.rem(me + step, count)),
+            device_id_type=mesh_ids,
+        )
+        copy.start()
+        copies.append(copy)
+    own = pltpu.make_async_copy(value, land.at[me], own_sem)
+    own.start()
+    for step in range(1, count):
+        copies[step - 1].wait_send()
+        source = lax.rem(me + count - step, count)
+        pltpu.make_async_remote_copy(
+            src_ref=value,
+            dst_ref=land.at[source],
+            send_sem=send_sem.at[step],
+            recv_sem=recv_sem.at[source],
+            device_id=device(source),
+            device_id_type=mesh_ids,
+        ).wait_recv()
+    own.wait()
+    out[...] = land[...]
+
+
+def gather_axis(block, axis, tag):
+    count = lax.axis_size(axis)
+    vmem = pl.BlockSpec(memory_space=pltpu.VMEM)
+    shape = (count,) + block.shape
+    return pl.pallas_call(
+        lambda *refs: gather_kernel(axis, *refs),
+        out_shape=jax.ShapeDtypeStruct(shape, jnp.float32),
+        in_specs=[vmem],
+        out_specs=vmem,
+        scratch_shapes=[
+            pltpu.VMEM(shape, jnp.float32),
+            pltpu.SemaphoreType.DMA((count,)),
+            pltpu.SemaphoreType.DMA((count,)),
+            pltpu.SemaphoreType.DMA(()),
+        ],
+        compiler_params=pltpu.CompilerParams(collective_id=tag, has_side_effects=True),
+    )(block)
+
+
+def global_max(block):
+    for tag, axis in enumerate(("gx", "gy")):
+        block = jnp.max(gather_axis(block, axis, tag), axis=0)
+    return block
 
 
 def restrict(field):
@@ -147,12 +206,12 @@
     fields = jnp.concatenate([state, feed[None], kill[None]], 0)
     fields_1 = restrict(fields)
     fields_2 = restrict(fields_1)
-    local = []
+    lane = lax.broadcasted_iota(jnp.int32, (8, 128), 1)
+    local = jnp.zeros((8, 128), jnp.float32)
     for level, level_fields in enumerate((fields, fields_1, fields_2)):
         _, first, second = coefficients(level_fields, level)
-        local.extend([jnp.max(first), jnp.max(second)])
-    local = jnp.stack(local).reshape(3, 2)
-    spreads = global_max(jnp.maximum(local[:, 0], local[:, 1]))
+        local = jnp.where(lane == level, jnp.maximum(jnp.max(first), jnp.max(second)), local)
+    spreads = global_max(local)[0]
 
     wide = padded(jnp.concatenate([fields, previous], 0), deep + 1)
     ops_0 = Level(coefficients(crop(wide[:4], deep + 1, deep), 0)[0], deep, 0)

time: 142 us -> 130 us (0.915)
  Pallas kernels: 0 us -> 22 us
  starting transfers between devices: 71.2 us -> 51.1 us
  waiting for transfers between devices: 35.2 us -> 20.4 us
  local copies, waits for them, and re-layouts: 10.5 us -> 6.59 us
  between operations: 3.69 us -> 7.51 us
  other arithmetic: 17.1 us -> 18.8 us
    pallas_call x0 -> x2, Pallas kernels: none -> 22 us  [gather_axis(): pl.pallas_call(lambda *refs: gather_kernel(axis, *refs), out_shape=jax.Sh...]
    ppermute x8 -> x0, starting transfers between devices: 17.6 us -> none  [global_max(): other = lax.ppermute(value, axis, [(i, i ^ step) for i in range(count)])]
    ppermute x8 -> x0, waiting for transfers between devices: 17 us -> none  [global_max(): other = lax.ppermute(value, axis, [(i, i ^ step) for i in range(count)])]
    another operation x1 -> x0, local copies, waits for them, and re-layouts: 3.81 us -> none  [body(): local = jnp.stack(local).reshape(3, 2)]
    ppermute x12, waiting for transfers between devices: 18.1 us -> 20.3 us  [padded(): lax.ppermute(tail, axis, [(i, (i + 1) % count) for i in range(count)])]
    ppermute x12, starting transfers between devices: 51.6 us -> 49.8 us  [padded(): lax.ppermute(head, axis, [((i + 1) % count, i) for i in range(count)])]
    reduce_max x3 -> x5, other arithmetic: 3.13 us -> 4.45 us  [the longest x2 2.3 us: global_max(): block = jnp.max(gather_axis(block, axis, tag), axis=0)]
  transfers between devices with their start and end apart: 32 -> 24, of which waited for: 18 -> 11; matrix products, arithmetic and copies ran while one was open for 1% -> 6% of each run, Pallas kernels for 0% -> 17%
where the time goes in v2:
time: 130 us; the launch traced here: 129 us
  starting transfers between devices  51.1 us (39%)
  Pallas kernels  22 us (17%)
  waiting for transfers between devices  20.4 us (16%)
  other arithmetic  18.8 us (14%)
  between operations  7.51 us (6%)
  local copies, waits for them, and re-layouts  6.59 us (5%)
  matrix products  2.06 us (2%)
    ppermute x12, starting transfers between devices, padded(): lax.ppermute(head, axis, [((i + 1) % count, i) for i in range(count)])  49.8 us
    pallas_call x2, Pallas kernels, gather_axis(): pl.pallas_call(lambda *refs: gather_kernel(axis, *refs), out_shape=jax.Sh...  22 us
    ppermute x12, waiting for transfers between devices, padded(): lax.ppermute(tail, axis, [(i, (i + 1) % count) for i in range(count)])  20.3 us
    add x12, other arithmetic, chebyshev(): iterate = crop(iterate, halo + 1, halo) + update  3.99 us
    add x16, other arithmetic, operate(): first = coeff[0] * centre[0] + coeff[1] * centre[1]  3.51 us
    slice x31, local copies, waits for them, and re-layouts, shrunk_neighbours(): along_z = jnp.roll(centre, 1, 1) + jnp.roll(centre, -1, 1)  3.43 us
  transfers between devices with their start and end apart: 24, of which 11 were waited for; matrix products, arithmetic and copies ran while one was open for 6% of the time, Pallas kernels for 17%

profile of v2, /device:TPU:0, one launch (start us, length us, event | category | flops | bytes accessed | tf_op | source)
XLA Modules:
  0.0 128.5 jit_solution(11854697013771118995)
XLA Ops:
  0.0 1.1 pad_maximum_fusion.1
  1.3 2.9 %collective-permute-start.1 = (f32[6,8,16,4]{3,2,1,0:T(8,128)S(1)}, f32[6,8,16,4]{3,2,1,0:T(8,128)S(1)}, u32[]{:S(2)}, u32[]{:S(2)}) collective-permute-start(f32[6,8,16,4]{3,2,1,0:T(8,128)S(1)} %get-tuple-element.90), channel_id=1, source_target_pairs={{32,0},{64,32},{96,64},{128,96},{160,128},{192,160},{224,192},{0,2... | collective-permute-start | bytes 36872 | tf_op jit(solution)/shard_map/ppermute | solution.py:25
  4.5 0.7 fusion.127
  5.2 0.4 fusion.125
  5.9 0.7 fusion.173
  7.1 0.7 fusion.303
  11.6 0.6 select_select_fusion.8.refs_0_
  12.2 6.7 %shard_map.208 = f32[8,8,128]{2,1,0:T(8,128)} custom-call(f32[8,128]{1,0:T(8,128)} %select_select_fusion.8.refs_0_), custom_call_target="tpu_custom_call" | custom-call | tf_op jit(solution)/shard_map/pallas_call | solution.py:94
  18.9 1.4 %reduce_max.78.refs_0_ = f32[8,128]{1,0:T(8,128)} reduce(f32[8,8,128]{2,1,0:T(8,128)} %shard_map.208, f32[]{:T(128)} %constant.326.clone.1), dimensions={0}, to_apply=%region_6.7 | reduce | flops 7168 | bytes 36868 | tf_op jit(solution)/shard_map/reduce_max | solution.py:111
  20.2 15.4 %shard_map.209 = f32[32,8,128]{2,1,0:T(8,128)} custom-call(f32[8,128]{1,0:T(8,128)} %reduce_max.78.refs_0_), custom_call_target="tpu_custom_call" | custom-call | tf_op jit(solution)/shard_map/pallas_call | solution.py:94
  35.6 0.9 reduce_max.79
  36.6 0.7 fusion.396
  38.6 0.8 collective-permute-start.2
  39.4 4.6 %collective-permute-start.3 = (f32[6,8,4,136]{3,2,1,0:T(4,128)S(1)}, f32[6,8,4,136]{3,2,1,0:T(4,128)S(1)}, u32[]{:S(2)}, u32[]{:S(2)}) collective-permute-start(f32[6,8,4,136]{3,2,1,0:T(4,128)S(1)} %get-tuple-element.48), channel_id=1, source_target_pairs={{1,0},{2,1},{3,2},{4,3},{5,4},{6,5},{7,6},{8,7},{9,8},{10,9},{11,1... | collective-permute-start | bytes 313352 | tf_op jit(solution)/shard_map/ppermute | solution.py:25
  44.1 4.1 %collective-permute-done.2 = f32[6,8,4,136]{3,2,1,0:T(4,128)S(1)} collective-permute-done((f32[6,8,4,136]{3,2,1,0:T(4,128)S(1)}, f32[6,8,4,136]{3,2,1,0:T(4,128)S(1)}, u32[]{:S(2)}, u32[]{:S(2)}) %collective-permute-start.2) | collective-permute-done | bytes 104480 | tf_op jit(solution)/shard_map/ppermute | solution.py:23
  48.1 0.5 pad_maximum_fusion
  49.7 0.6 fusion.35
  50.6 0.4 multiply_add_fusion.8
  51.0 0.6 slice_add_fusion.12
  51.8 0.4 multiply_add_fusion.6
  52.5 0.7 fusion.20
  53.4 0.8 multiply_add_fusion.13
  55.1 2.9 %collective-permute-start.5 = (f32[6,4,8,3]{3,2,1,0:T(8,128)S(1)}, f32[6,4,8,3]{3,2,1,0:T(8,128)S(1)}, u32[]{:S(2)}, u32[]{:S(2)}) collective-permute-start(f32[6,4,8,3]{3,2,1,0:T(8,128)S(1)} %get-tuple-element.106), channel_id=1, source_target_pairs={{32,0},{64,32},{96,64},{128,96},{160,128},{192,160},{224,192},{0,2... | collective-permute-start | bytes 6920 | tf_op jit(solution)/shard_map/ppermute | solution.py:25
  58.1 2.3 %collective-permute-done.4 = f32[6,4,8,3]{3,2,1,0:T(8,128)S(1)} collective-permute-done((f32[6,4,8,3]{3,2,1,0:T(8,128)S(1)}, f32[6,4,8,3]{3,2,1,0:T(8,128)S(1)}, u32[]{:S(2)}, u32[]{:S(2)}) %collective-permute-start.4) | collective-permute-done | bytes 2336 | tf_op jit(solution)/shard_map/ppermute | solution.py:23
  60.6 5.3 %collective-permute-start.7 = (f32[6,4,3,70]{3,2,1,0:T(4,128)S(1)}, f32[6,4,3,70]{3,2,1,0:T(4,128)S(1)}, u32[]{:S(2)}, u32[]{:S(2)}) collective-permute-start(f32[6,4,3,70]{3,2,1,0:T(4,128)S(1)} %get-tuple-element.104), channel_id=1, source_target_pairs={{1,0},{2,1},{3,2},{4,3},{5,4},{6,5},{7,6},{8,7},{9,8},{10,9},{11,1... | collective-permute-start | bytes 60488 | tf_op jit(solution)/shard_map/ppermute | solution.py:25
  66.9 1.1 collective-permute-done.6
  70.1 2.9 %collective-permute-start.9 = (f32[6,2,4,3]{3,2,1,0:T(4,128)S(1)}, f32[6,2,4,3]{3,2,1,0:T(4,128)S(1)}, u32[]{:S(2)}, u32[]{:S(2)}) collective-permute-start(f32[6,2,4,3]{3,2,1,0:T(4,128)S(1)} %get-tuple-element.164), channel_id=1, source_target_pairs={{32,0},{64,32},{96,64},{128,96},{160,128},{192,160},{224,192},{0,2... | collective-permute-start | bytes 1736 | tf_op jit(solution)/shard_map/ppermute | solution.py:25
  73.1 1.5 %collective-permute-done.8 = f32[6,2,4,3]{3,2,1,0:T(4,128)S(1)} collective-permute-done((f32[6,2,4,3]{3,2,1,0:T(4,128)S(1)}, f32[6,2,4,3]{3,2,1,0:T(4,128)S(1)}, u32[]{:S(2)}, u32[]{:S(2)}) %collective-permute-start.8) | collective-permute-done | bytes 608 | tf_op jit(solution)/shard_map/ppermute | solution.py:23
  74.8 5.4 %collective-permute-start.11 = (f32[6,2,3,38]{3,2,1,0:T(4,128)S(1)}, f32[6,2,3,38]{3,2,1,0:T(4,128)S(1)}, u32[]{:S(2)}, u32[]{:S(2)}) collective-permute-start(f32[6,2,3,38]{3,2,1,0:T(4,128)S(1)} %get-tuple-element.162), channel_id=1, source_target_pairs={{1,0},{2,1},{3,2},{4,3},{5,4},{6,5},{7,6},{8,7},{9,8},{10,9},{11,1... | collective-permute-start | bytes 16424 | tf_op jit(solution)/shard_map/ppermute | solution.py:25
  81.1 0.8 collective-permute-done.10
  82.7 3.0 %collective-permute-start.13 = (f32[2,2,4,3]{3,2,1,0:T(4,128)S(1)}, f32[2,2,4,3]{3,2,1,0:T(4,128)S(1)}, u32[]{:S(2)}, u32[]{:S(2)}) collective-permute-start(f32[2,2,4,3]{3,2,1,0:T(4,128)S(1)} %get-tuple-element.177), channel_id=1, source_target_pairs={{32,0},{64,32},{96,64},{128,96},{160,128},{192,160},{224,192},{0,2... | collective-permute-start | bytes 584 | tf_op jit(solution)/shard_map/ppermute | solution.py:25
  85.7 1.3 collective-permute-done.12
  87.2 5.5 %collective-permute-start.15 = (f32[2,2,3,38]{3,2,1,0:T(4,128)S(1)}, f32[2,2,3,38]{3,2,1,0:T(4,128)S(1)}, u32[]{:S(2)}, u32[]{:S(2)}) collective-permute-start(f32[2,2,3,38]{3,2,1,0:T(4,128)S(1)} %get-tuple-element.186), channel_id=1, source_target_pairs={{1,0},{2,1},{3,2},{4,3},{5,4},{6,5},{7,6},{8,7},{9,8},{10,9},{11,1... | collective-permute-start | bytes 5480 | tf_op jit(solution)/shard_map/ppermute | solution.py:25
  92.7 1.5 %collective-permute-done.14 = f32[2,2,3,38]{3,2,1,0:T(4,128)S(1)} collective-permute-done((f32[2,2,3,38]{3,2,1,0:T(4,128)S(1)}, f32[2,2,3,38]{3,2,1,0:T(4,128)S(1)}, u32[]{:S(2)}, u32[]{:S(2)}) %collective-permute-start.14) | collective-permute-done | bytes 1856 | tf_op jit(solution)/shard_map/ppermute | solution.py:23
  95.6 3.0 %collective-permute-start.17 = (f32[2,4,8,3]{3,2,1,0:T(8,128)S(1)}, f32[2,4,8,3]{3,2,1,0:T(8,128)S(1)}, u32[]{:S(2)}, u32[]{:S(2)}) collective-permute-start(f32[2,4,8,3]{3,2,1,0:T(8,128)S(1)} %get-tuple-element.150), channel_id=1, source_target_pairs={{32,0},{64,32},{96,64},{128,96},{160,128},{192,160},{224,192},{0,2... | collective-permute-start | bytes 2312 | tf_op jit(solution)/shard_map/ppermute | solution.py:25
  98.6 1.6 %collective-permute-done.16 = f32[2,4,8,3]{3,2,1,0:T(8,128)S(1)} collective-permute-done((f32[2,4,8,3]{3,2,1,0:T(8,128)S(1)}, f32[2,4,8,3]{3,2,1,0:T(8,128)S(1)}, u32[]{:S(2)}, u32[]{:S(2)}) %collective-permute-start.16) | collective-permute-done | bytes 800 | tf_op jit(solution)/shard_map/ppermute | solution.py:23
  100.4 5.5 %collective-permute-start.19 = (f32[2,4,3,70]{3,2,1,0:T(4,128)S(1)}, f32[2,4,3,70]{3,2,1,0:T(4,128)S(1)}, u32[]{:S(2)}, u32[]{:S(2)}) collective-permute-start(f32[2,4,3,70]{3,2,1,0:T(4,128)S(1)} %get-tuple-element.148), channel_id=1, source_target_pairs={{1,0},{2,1},{3,2},{4,3},{5,4},{6,5},{7,6},{8,7},{9,8},{10,9},{11,1... | collective-permute-start | bytes 20168 | tf_op jit(solution)/shard_map/ppermute | solution.py:25
  105.9 1.6 %collective-permute-done.18 = f32[2,4,3,70]{3,2,1,0:T(4,128)S(1)} collective-permute-done((f32[2,4,3,70]{3,2,1,0:T(4,128)S(1)}, f32[2,4,3,70]{3,2,1,0:T(4,128)S(1)}, u32[]{:S(2)}, u32[]{:S(2)}) %collective-permute-start.18) | collective-permute-done | bytes 6752 | tf_op jit(solution)/shard_map/ppermute | solution.py:23
  109.9 2.9 %collective-permute-start.21 = (f32[2,8,16,3]{3,2,1,0:T(8,128)S(1)}, f32[2,8,16,3]{3,2,1,0:T(8,128)S(1)}, u32[]{:S(2)}, u32[]{:S(2)}) collective-permute-start(f32[2,8,16,3]{3,2,1,0:T(8,128)S(1)} %get-tuple-element.100), channel_id=1, source_target_pairs={{32,0},{64,32},{96,64},{128,96},{160,128},{192,160},{224,192},{0,2... | collective-permute-start | bytes 9224 | tf_op jit(solution)/shard_map/ppermute | solution.py:25
  112.9 2.6 %collective-permute-done.20 = f32[2,8,16,3]{3,2,1,0:T(8,128)S(1)} collective-permute-done((f32[2,8,16,3]{3,2,1,0:T(8,128)S(1)}, f32[2,8,16,3]{3,2,1,0:T(8,128)S(1)}, u32[]{:S(2)}, u32[]{:S(2)}) %collective-permute-start.20) | collective-permute-done | bytes 3104 | tf_op jit(solution)/shard_map/ppermute | solution.py:23
  115.8 5.7 %collective-permute-start.23 = (f32[2,8,3,134]{3,2,1,0:T(4,128)S(1)}, f32[2,8,3,134]{3,2,1,0:T(4,128)S(1)}, u32[]{:S(2)}, u32[]{:S(2)}) collective-permute-start(f32[2,8,3,134]{3,2,1,0:T(4,128)S(1)} %get-tuple-element.70), channel_id=1, source_target_pairs={{1,0},{2,1},{3,2},{4,3},{5,4},{6,5},{7,6},{8,7},{9,8},{10,9},{11,1... | collective-permute-start | bytes 77192 | tf_op jit(solution)/shard_map/ppermute | solution.py:25
  121.5 1.9 %collective-permute-done.22 = f32[2,8,3,134]{3,2,1,0:T(4,128)S(1)} collective-permute-done((f32[2,8,3,134]{3,2,1,0:T(4,128)S(1)}, f32[2,8,3,134]{3,2,1,0:T(4,128)S(1)}, u32[]{:S(2)}, u32[]{:S(2)}) %collective-permute-start.22) | collective-permute-done | bytes 25760 | tf_op jit(solution)/shard_map/ppermute | solution.py:23
  123.7 0.4 multiply_add_fusion.4
  124.4 0.6 copy-done.2
  125.1 0.6 slice_add_fusion.5
  125.7 0.4 multiply_add_fusion.2
  126.5 0.7 slice_add_fusion.2
  127.6 0.9 fusion.63
  (179 shorter events, 13.2 us)
Async XLA Ops:
  0.0 4.3 %copy-start = (f32[2,8,16,128]{3,2,1,0:T(8,128)S(1)}, f32[2,8,16,128]{3,2,1,0:T(8,128)}, u32[]{:S(2)}) copy-start(f32[2,8,16,128]{3,2,1,0:T(8,128)} %param.22) | copy-start | bytes 393220
  0.0 4.3 %copy-start.5 = (f32[8,16,128]{2,1,0:T(8,128)S(1)}, f32[8,16,128]{2,1,0:T(8,128)}, u32[]{:S(2)}) copy-start(f32[8,16,128]{2,1,0:T(8,128)} %param.25) | copy-start | bytes 196612
  0.0 4.3 %copy-start.6 = (f32[8,16,128]{2,1,0:T(8,128)S(1)}, f32[8,16,128]{2,1,0:T(8,128)}, u32[]{:S(2)}) copy-start(f32[8,16,128]{2,1,0:T(8,128)} %param.24) | copy-start | bytes 196612
  1.3 36.9 %collective-permute-start = (f32[6,8,16,4]{3,2,1,0:T(8,128)S(1)}, f32[6,8,16,4]{3,2,1,0:T(8,128)S(1)}, u32[]{:S(2)}, u32[]{:S(2)}) collective-permute-start(f32[6,8,16,4]{3,2,1,0:T(8,128)S(1)} %get-tuple-element.89), channel_id=1, source_target_pairs={{0,32},{32,64},{64,96},{96,128},{128,160},{160,192},{192,224},{224... | collective-permute-start | bytes 36872 | tf_op jit(solution)/shard_map/ppermute | solution.py:23
  1.3 36.9 %collective-permute-start.1 = (f32[6,8,16,4]{3,2,1,0:T(8,128)S(1)}, f32[6,8,16,4]{3,2,1,0:T(8,128)S(1)}, u32[]{:S(2)}, u32[]{:S(2)}) collective-permute-start(f32[6,8,16,4]{3,2,1,0:T(8,128)S(1)} %get-tuple-element.90), channel_id=1, source_target_pairs={{32,0},{64,32},{96,64},{128,96},{160,128},{192,160},{224,192},{0,2... | collective-permute-start | bytes 36872 | tf_op jit(solution)/shard_map/ppermute | solution.py:25
  5.9 32.3 %copy-start.7 = (f32[2,8,16,128]{3,2,1,0:T(8,128)S(1)}, f32[2,8,16,128]{3,2,1,0:T(8,128)}, u32[]{:S(2)}) copy-start(f32[2,8,16,128]{3,2,1,0:T(8,128)} %param.23) | copy-start | bytes 393220
  38.6 9.5 %collective-permute-start.2 = (f32[6,8,4,136]{3,2,1,0:T(4,128)S(1)}, f32[6,8,4,136]{3,2,1,0:T(4,128)S(1)}, u32[]{:S(2)}, u32[]{:S(2)}) collective-permute-start(f32[6,8,4,136]{3,2,1,0:T(4,128)S(1)} %get-tuple-element.47), channel_id=1, source_target_pairs={{0,1},{1,2},{2,3},{3,4},{4,5},{5,6},{6,7},{7,8},{8,9},{9,10},{10,1... | collective-permute-start | bytes 313352 | tf_op jit(solution)/shard_map/ppermute | solution.py:23
  39.4 8.7 %collective-permute-start.3 = (f32[6,8,4,136]{3,2,1,0:T(4,128)S(1)}, f32[6,8,4,136]{3,2,1,0:T(4,128)S(1)}, u32[]{:S(2)}, u32[]{:S(2)}) collective-permute-start(f32[6,8,4,136]{3,2,1,0:T(4,128)S(1)} %get-tuple-element.48), channel_id=1, source_target_pairs={{1,0},{2,1},{3,2},{4,3},{5,4},{6,5},{7,6},{8,7},{9,8},{10,9},{11,1... | collective-permute-start | bytes 313352 | tf_op jit(solution)/shard_map/ppermute | solution.py:25
  49.0 0.7 copy-start.9
  51.0 0.7 copy-start.1
  51.0 0.7 copy-start.3
  55.1 13.5 %copy-start.10 = (f32[2]{0:T(128)S(1)}, f32[2]{0:T(128)}, u32[]{:S(2)}) copy-start(f32[2]{0:T(128)} %constant.335.clone) | copy-start | bytes 28
  55.1 5.3 %collective-permute-start.4 = (f32[6,4,8,3]{3,2,1,0:T(8,128)S(1)}, f32[6,4,8,3]{3,2,1,0:T(8,128)S(1)}, u32[]{:S(2)}, u32[]{:S(2)}) collective-permute-start(f32[6,4,8,3]{3,2,1,0:T(8,128)S(1)} %get-tuple-element.105), channel_id=1, source_target_pairs={{0,32},{32,64},{64,96},{96,128},{128,160},{160,192},{192,224},{224... | collective-permute-start | bytes 6920 | tf_op jit(solution)/shard_map/ppermute | solution.py:23
  55.1 5.2 %collective-permute-start.5 = (f32[6,4,8,3]{3,2,1,0:T(8,128)S(1)}, f32[6,4,8,3]{3,2,1,0:T(8,128)S(1)}, u32[]{:S(2)}, u32[]{:S(2)}) collective-permute-start(f32[6,4,8,3]{3,2,1,0:T(8,128)S(1)} %get-tuple-element.106), channel_id=1, source_target_pairs={{32,0},{64,32},{96,64},{128,96},{160,128},{192,160},{224,192},{0,2... | collective-permute-start | bytes 6920 | tf_op jit(solution)/shard_map/ppermute | solution.py:25
  60.5 7.5 %collective-permute-start.6 = (f32[6,4,3,70]{3,2,1,0:T(4,128)S(1)}, f32[6,4,3,70]{3,2,1,0:T(4,128)S(1)}, u32[]{:S(2)}, u32[]{:S(2)}) collective-permute-start(f32[6,4,3,70]{3,2,1,0:T(4,128)S(1)} %get-tuple-element.103), channel_id=1, source_target_pairs={{0,1},{1,2},{2,3},{3,4},{4,5},{5,6},{6,7},{7,8},{8,9},{9,10},{10,1... | collective-permute-start | bytes 60488 | tf_op jit(solution)/shard_map/ppermute | solution.py:23
  60.6 7.4 %collective-permute-start.7 = (f32[6,4,3,70]{3,2,1,0:T(4,128)S(1)}, f32[6,4,3,70]{3,2,1,0:T(4,128)S(1)}, u32[]{:S(2)}, u32[]{:S(2)}) collective-permute-start(f32[6,4,3,70]{3,2,1,0:T(4,128)S(1)} %get-tuple-element.104), channel_id=1, source_target_pairs={{1,0},{2,1},{3,2},{4,3},{5,4},{6,5},{7,6},{8,7},{9,8},{10,9},{11,1... | collective-permute-start | bytes 60488 | tf_op jit(solution)/shard_map/ppermute | solution.py:25
  69.0 13.3 %copy-start.11 = (f32[2]{0:T(128)S(1)}, f32[2]{0:T(128)}, u32[]{:S(2)}) copy-start(f32[2]{0:T(128)} %constant.336.clone) | copy-start | bytes 28
  70.1 4.5 %collective-permute-start.8 = (f32[6,2,4,3]{3,2,1,0:T(4,128)S(1)}, f32[6,2,4,3]{3,2,1,0:T(4,128)S(1)}, u32[]{:S(2)}, u32[]{:S(2)}) collective-permute-start(f32[6,2,4,3]{3,2,1,0:T(4,128)S(1)} %get-tuple-element.163), channel_id=1, source_target_pairs={{0,32},{32,64},{64,96},{96,128},{128,160},{160,192},{192,224},{224... | collective-permute-start | bytes 1736 | tf_op jit(solution)/shard_map/ppermute | solution.py:23
  70.1 4.5 %collective-permute-start.9 = (f32[6,2,4,3]{3,2,1,0:T(4,128)S(1)}, f32[6,2,4,3]{3,2,1,0:T(4,128)S(1)}, u32[]{:S(2)}, u32[]{:S(2)}) collective-permute-start(f32[6,2,4,3]{3,2,1,0:T(4,128)S(1)} %get-tuple-element.164), channel_id=1, source_target_pairs={{32,0},{64,32},{96,64},{128,96},{160,128},{192,160},{224,192},{0,2... | collective-permute-start | bytes 1736 | tf_op jit(solution)/shard_map/ppermute | solution.py:25
  74.7 7.2 %collective-permute-start.10 = (f32[6,2,3,38]{3,2,1,0:T(4,128)S(1)}, f32[6,2,3,38]{3,2,1,0:T(4,128)S(1)}, u32[]{:S(2)}, u32[]{:S(2)}) collective-permute-start(f32[6,2,3,38]{3,2,1,0:T(4,128)S(1)} %get-tuple-element.161), channel_id=1, source_target_pairs={{0,1},{1,2},{2,3},{3,4},{4,5},{5,6},{6,7},{7,8},{8,9},{9,10},{10,1... | collective-permute-start | bytes 16424 | tf_op jit(solution)/shard_map/ppermute | solution.py:23
  74.8 7.1 %collective-permute-start.11 = (f32[6,2,3,38]{3,2,1,0:T(4,128)S(1)}, f32[6,2,3,38]{3,2,1,0:T(4,128)S(1)}, u32[]{:S(2)}, u32[]{:S(2)}) collective-permute-start(f32[6,2,3,38]{3,2,1,0:T(4,128)S(1)} %get-tuple-element.162), channel_id=1, source_target_pairs={{1,0},{2,1},{3,2},{4,3},{5,4},{6,5},{7,6},{8,7},{9,8},{10,9},{11,1... | collective-permute-start | bytes 16424 | tf_op jit(solution)/shard_map/ppermute | solution.py:25
  82.7 4.3 %collective-permute-start.12 = (f32[2,2,4,3]{3,2,1,0:T(4,128)S(1)}, f32[2,2,4,3]{3,2,1,0:T(4,128)S(1)}, u32[]{:S(2)}, u32[]{:S(2)}) collective-permute-start(f32[2,2,4,3]{3,2,1,0:T(4,128)S(1)} %get-tuple-element.176), channel_id=1, source_target_pairs={{0,32},{32,64},{64,96},{96,128},{128,160},{160,192},{192,224},{224... | collective-permute-start | bytes 584 | tf_op jit(solution)/shard_map/ppermute | solution.py:23
  82.7 4.3 %collective-permute-start.13 = (f32[2,2,4,3]{3,2,1,0:T(4,128)S(1)}, f32[2,2,4,3]{3,2,1,0:T(4,128)S(1)}, u32[]{:S(2)}, u32[]{:S(2)}) collective-permute-start(f32[2,2,4,3]{3,2,1,0:T(4,128)S(1)} %get-tuple-element.177), channel_id=1, source_target_pairs={{32,0},{64,32},{96,64},{128,96},{160,128},{192,160},{224,192},{0,2... | collective-permute-start | bytes 584 | tf_op jit(solution)/shard_map/ppermute | solution.py:25
  87.1 7.1 %collective-permute-start.14 = (f32[2,2,3,38]{3,2,1,0:T(4,128)S(1)}, f32[2,2,3,38]{3,2,1,0:T(4,128)S(1)}, u32[]{:S(2)}, u32[]{:S(2)}) collective-permute-start(f32[2,2,3,38]{3,2,1,0:T(4,128)S(1)} %get-tuple-element.185), channel_id=1, source_target_pairs={{0,1},{1,2},{2,3},{3,4},{4,5},{5,6},{6,7},{7,8},{8,9},{9,10},{10,1... | collective-permute-start | bytes 5480 | tf_op jit(solution)/shard_map/ppermute | solution.py:23
  87.2 7.0 %collective-permute-start.15 = (f32[2,2,3,38]{3,2,1,0:T(4,128)S(1)}, f32[2,2,3,38]{3,2,1,0:T(4,128)S(1)}, u32[]{:S(2)}, u32[]{:S(2)}) collective-permute-start(f32[2,2,3,38]{3,2,1,0:T(4,128)S(1)} %get-tuple-element.186), channel_id=1, source_target_pairs={{1,0},{2,1},{3,2},{4,3},{5,4},{6,5},{7,6},{8,7},{9,8},{10,9},{11,1... | collective-permute-start | bytes 5480 | tf_op jit(solution)/shard_map/ppermute | solution.py:25
  95.6 4.6 %collective-permute-start.16 = (f32[2,4,8,3]{3,2,1,0:T(8,128)S(1)}, f32[2,4,8,3]{3,2,1,0:T(8,128)S(1)}, u32[]{:S(2)}, u32[]{:S(2)}) collective-permute-start(f32[2,4,8,3]{3,2,1,0:T(8,128)S(1)} %get-tuple-element.149), channel_id=1, source_target_pairs={{0,32},{32,64},{64,96},{96,128},{128,160},{160,192},{192,224},{224... | collective-permute-start | bytes 2312 | tf_op jit(solution)/shard_map/ppermute | solution.py:23
  95.6 4.6 %collective-permute-start.17 = (f32[2,4,8,3]{3,2,1,0:T(8,128)S(1)}, f32[2,4,8,3]{3,2,1,0:T(8,128)S(1)}, u32[]{:S(2)}, u32[]{:S(2)}) collective-permute-start(f32[2,4,8,3]{3,2,1,0:T(8,128)S(1)} %get-tuple-element.150), channel_id=1, source_target_pairs={{32,0},{64,32},{96,64},{128,96},{160,128},{192,160},{224,192},{0,2... | collective-permute-start | bytes 2312 | tf_op jit(solution)/shard_map/ppermute | solution.py:25
  100.3 7.2 %collective-permute-start.18 = (f32[2,4,3,70]{3,2,1,0:T(4,128)S(1)}, f32[2,4,3,70]{3,2,1,0:T(4,128)S(1)}, u32[]{:S(2)}, u32[]{:S(2)}) collective-permute-start(f32[2,4,3,70]{3,2,1,0:T(4,128)S(1)} %get-tuple-element.147), channel_id=1, source_target_pairs={{0,1},{1,2},{2,3},{3,4},{4,5},{5,6},{6,7},{7,8},{8,9},{9,10},{10,1... | collective-permute-start | bytes 20168 | tf_op jit(solution)/shard_map/ppermute | solution.py:23
  100.4 7.1 %collective-permute-start.19 = (f32[2,4,3,70]{3,2,1,0:T(4,128)S(1)}, f32[2,4,3,70]{3,2,1,0:T(4,128)S(1)}, u32[]{:S(2)}, u32[]{:S(2)}) collective-permute-start(f32[2,4,3,70]{3,2,1,0:T(4,128)S(1)} %get-tuple-element.148), channel_id=1, source_target_pairs={{1,0},{2,1},{3,2},{4,3},{5,4},{6,5},{7,6},{8,7},{9,8},{10,9},{11,1... | collective-permute-start | bytes 20168 | tf_op jit(solution)/shard_map/ppermute | solution.py:25
  109.9 5.6 %collective-permute-start.20 = (f32[2,8,16,3]{3,2,1,0:T(8,128)S(1)}, f32[2,8,16,3]{3,2,1,0:T(8,128)S(1)}, u32[]{:S(2)}, u32[]{:S(2)}) collective-permute-start(f32[2,8,16,3]{3,2,1,0:T(8,128)S(1)} %get-tuple-element.99), channel_id=1, source_target_pairs={{0,32},{32,64},{64,96},{96,128},{128,160},{160,192},{192,224},{224... | collective-permute-start | bytes 9224 | tf_op jit(solution)/shard_map/ppermute | solution.py:23
  109.9 5.6 %collective-permute-start.21 = (f32[2,8,16,3]{3,2,1,0:T(8,128)S(1)}, f32[2,8,16,3]{3,2,1,0:T(8,128)S(1)}, u32[]{:S(2)}, u32[]{:S(2)}) collective-permute-start(f32[2,8,16,3]{3,2,1,0:T(8,128)S(1)} %get-tuple-element.100), channel_id=1, source_target_pairs={{32,0},{64,32},{96,64},{128,96},{160,128},{192,160},{224,192},{0,2... | collective-permute-start | bytes 9224 | tf_op jit(solution)/shard_map/ppermute | solution.py:25
  115.7 7.7 %collective-permute-start.22 = (f32[2,8,3,134]{3,2,1,0:T(4,128)S(1)}, f32[2,8,3,134]{3,2,1,0:T(4,128)S(1)}, u32[]{:S(2)}, u32[]{:S(2)}) collective-permute-start(f32[2,8,3,134]{3,2,1,0:T(4,128)S(1)} %get-tuple-element.69), channel_id=1, source_target_pairs={{0,1},{1,2},{2,3},{3,4},{4,5},{5,6},{6,7},{7,8},{8,9},{9,10},{10,1... | collective-permute-start | bytes 77192 | tf_op jit(solution)/shard_map/ppermute | solution.py:23
  115.8 7.7 %collective-permute-start.23 = (f32[2,8,3,134]{3,2,1,0:T(4,128)S(1)}, f32[2,8,3,134]{3,2,1,0:T(4,128)S(1)}, u32[]{:S(2)}, u32[]{:S(2)}) collective-permute-start(f32[2,8,3,134]{3,2,1,0:T(4,128)S(1)} %get-tuple-element.70), channel_id=1, source_target_pairs={{1,0},{2,1},{3,2},{4,3},{5,4},{6,5},{7,6},{8,7},{9,8},{10,9},{11,1... | collective-permute-start | bytes 77192 | tf_op jit(solution)/shard_map/ppermute | solution.py:25
  124.1 0.9 copy-start.2
  124.1 1.0 copy-start.4
  126.4 1.1 copy-start.8

commit v3 on v2

--- a/solution.py
+++ b/solution.py
@@ -31,6 +31,7 @@
 
 def crop(cells, have, want):
     cut = have - want
+    assert cut >= 0
     if cut == 0:
         return cells
     return cells[..., cut:cells.shape[-2] - cut, cut:cells.shape[-1] - cut]
@@ -213,29 +214,28 @@
         local = jnp.where(lane == level, jnp.maximum(jnp.max(first), jnp.max(second)), local)
     spreads = global_max(local)[0]
 
-    wide = padded(jnp.concatenate([fields, previous], 0), deep + 1)
-    ops_0 = Level(coefficients(crop(wide[:4], deep + 1, deep), 0)[0], deep, 0)
+    wide = padded(jnp.concatenate([fields, previous], 0), 14)
+    ops_0 = Level(coefficients(crop(wide[:4], 14, 13), 0)[0], 13, 0)
     state_w = wide[:2]
-    substrate, catalyst = crop(state_w[0], deep + 1, deep), crop(state_w[1], deep + 1, deep)
-    centre = crop(state_w, deep + 1, deep)
+    substrate, catalyst = crop(state_w[0], 14, 13), crop(state_w[1], 14, 13)
+    centre = crop(state_w, 14, 13)
     reaction = substrate * catalyst * catalyst
     laplace = shrunk_neighbours(state_w) - 6.0 * centre
-    feed_w = crop(wide[2], deep + 1, deep)
-    kill_w = crop(wide[3], deep + 1, deep)
-    previous_w = crop(wide[4:6], deep + 1, deep)
+    feed_w = crop(wide[2], 14, 13)
+    kill_w = crop(wide[3], 14, 13)
+    previous_w = crop(wide[4:6], 14, 13)
     local_terms = jnp.stack(
         [reaction - feed_w * (1.0 - substrate), -reaction + (feed_w + kill_w) * catalyst]
     )
     nonlinear = inverse_step * (centre - previous_w) - diffusions(0) * laplace + local_terms
     source_0 = -nonlinear
-    pre_0, pre_0_halo = chebyshev(ops_0, source_0, deep, None, None, spreads[0])
-    resid_0 = crop(source_0, deep, 0) - ops_0.operate(crop(pre_0, pre_0_halo, 1), 1)
-
-    wide_1 = padded(jnp.concatenate([restrict(resid_0), fields_1], 0), deep)
-    ops_1 = Level(coefficients(wide_1[2:], 1)[0], deep, 1)
-    source_1 = wide_1[:2]
-    pre_1, pre_1_halo = chebyshev(ops_1, source_1, deep, None, None, spreads[1])
-    resid_1 = crop(source_1, deep, 0) - ops_1.operate(crop(pre_1, pre_1_halo, 1), 1)
+    pre_0, pre_0_halo = chebyshev(ops_0, source_0, 13, None, None, spreads[0])
+    resid_0 = crop(source_0, 13, 10) - ops_0.operate(crop(pre_0, pre_0_halo, 11), 11)
+
+    source_1 = restrict(resid_0)
+    ops_1 = Level(coefficients(restrict(crop(wide[:4], 14, 10)), 1)[0], 5, 1)
+    pre_1, pre_1_halo = chebyshev(ops_1, source_1, 5, None, None, spreads[1])
+    resid_1 = crop(source_1, 5, 0) - ops_1.operate(crop(pre_1, pre_1_halo, 1), 1)
 
     wide_2 = padded(jnp.concatenate([restrict(resid_1), fields_2], 0), deep)
     ops_2 = Level(coefficients(wide_2[2:], 2)[0], deep, 2)
@@ -244,11 +244,11 @@
     start_2 = padded(crop(first_2, first_2_halo, 0), deep)
     coarse_2, coarse_2_halo = chebyshev(ops_2, source_2, deep, start_2, deep, spreads[2])
 
-    start_1 = padded(crop(pre_1, pre_1_halo, 0) + prolong(crop(coarse_2, coarse_2_halo, 0)), deep)
-    post_1, post_1_halo = chebyshev(ops_1, source_1, deep, start_1, deep, spreads[1])
-
-    start_0 = padded(crop(pre_0, pre_0_halo, 0) + prolong(crop(post_1, post_1_halo, 0)), deep)
-    post_0, post_0_halo = chebyshev(ops_0, source_0, deep, start_0, deep, spreads[0])
+    start_1 = padded(crop(pre_1, pre_1_halo, 0) + prolong(crop(coarse_2, coarse_2_halo, 0)), 5)
+    post_1, post_1_halo = chebyshev(ops_1, source_1, 5, start_1, 5, spreads[1])
+
+    start_0 = crop(pre_0, pre_0_halo, 3) + crop(prolong(post_1), 2 * post_1_halo, 3)
+    post_0, post_0_halo = chebyshev(ops_0, source_0, 13, start_0, 3, spreads[0])
     return crop(post_0, post_0_halo, 0)
 
 

time: 130 us -> 152 us (1.17)
  starting transfers between devices: 51.1 us -> 33.1 us
  local copies, waits for them, and re-layouts: 6.59 us -> 23.3 us
  other arithmetic: 18.8 us -> 30.2 us
  waiting for transfers between devices: 20.4 us -> 27.3 us
  matrix products: 2.06 us -> 6.3 us
    ppermute x12 -> x8, starting transfers between devices: 49.8 us -> 32.9 us  [padded(): lax.ppermute(head, axis, [((i + 1) % count, i) for i in range(count)])]
    ppermute x12 -> x8, waiting for transfers between devices: 0.08 us -> 13.3 us  [padded(): lax.ppermute(head, axis, [((i + 1) % count, i) for i in range(count)])]
    ppermute x12 -> x8, waiting for transfers between devices: 20.3 us -> 13.9 us  [padded(): lax.ppermute(tail, axis, [(i, (i + 1) % count) for i in range(count)])]
    reshape x0 -> x3, local copies, waits for them, and re-layouts: none -> 4.4 us  [the longest x2 4.39 us: restrict(): field.reshape(count, cols)]
    dot_general x4 -> x5, matrix products: 1.26 us -> 4.54 us  [restrict(): jnp.dot(field.reshape(count, cols), pick_x, precision=lax.Precision.HIGHEST)]
    slice x1 -> x3, local copies, waits for them, and re-layouts: 0.07 us -> 2.91 us  [crop(): return cells[..., cut:cells.shape[-2] - cut, cut:cells.shape[-1] - cut]]
    sub x2, other arithmetic: 0.31 us -> 3.14 us  [the longest x1 3.02 us: body(): crop(source_0, 13, 10) - ops_0.operate(crop(pre_0, pre_0_halo, 11), 11)]
    add x12, other arithmetic: 3.99 us -> 6.73 us  [chebyshev(): iterate = crop(iterate, halo + 1, halo) + update]
  transfers between devices with their start and end apart: 24 -> 16, of which waited for: 11 -> 9; matrix products, arithmetic and copies ran while one was open for 6% -> 7% of each run, Pallas kernels for 17% -> 15%
where the time goes in v3:
time: 152 us; the launch traced here: 150 us
  starting transfers between devices  33.1 us (22%)
  other arithmetic  30.2 us (20%)
  waiting for transfers between devices  27.3 us (18%)
  local copies, waits for them, and re-layouts  23.3 us (15%)
  Pallas kernels  22 us (14%)
  between operations  7.61 us (5%)
  matrix products  6.3 us (4%)
    ppermute x8, starting transfers between devices, padded(): lax.ppermute(head, axis, [((i + 1) % count, i) for i in range(count)])  32.9 us
    pallas_call x2, Pallas kernels, gather_axis(): pl.pallas_call(lambda *refs: gather_kernel(axis, *refs), out_shape=jax.Sh...  22 us
    ppermute x8, waiting for transfers between devices, padded(): lax.ppermute(tail, axis, [(i, (i + 1) % count) for i in range(count)])  13.9 us
    ppermute x8, waiting for transfers between devices, padded(): lax.ppermute(head, axis, [((i + 1) % count, i) for i in range(count)])  13.3 us
    add x12, other arithmetic, chebyshev(): iterate = crop(iterate, halo + 1, halo) + update  6.73 us
    slice x31, local copies, waits for them, and re-layouts, shrunk_neighbours(): along_z = jnp.roll(centre, 1, 1) + jnp.roll(centre, -1, 1)  5.15 us
    add x16, other arithmetic, operate(): first = coeff[0] * centre[0] + coeff[1] * centre[1]  4.65 us
    dot_general x5, matrix products, restrict(): jnp.dot(field.reshape(count, cols), pick_x, precision=lax.Precision.HIGHEST)  4.54 us
  transfers between devices with their start and end apart: 16, of which 9 were waited for; matrix products, arithmetic and copies ran while one was open for 7% of the time, Pallas kernels for 15%

profile of v3, /device:TPU:0, one launch (start us, length us, event | category | flops | bytes accessed | tf_op | source)
XLA Modules:
  0.0 149.7 jit_solution(5725205341162002115)
XLA Ops:
  0.0 1.1 pad_maximum_fusion.2
  1.3 2.9 %collective-permute-start.1 = (f32[6,8,16,14]{3,2,1,0:T(8,128)S(1)}, f32[6,8,16,14]{3,2,1,0:T(8,128)S(1)}, u32[]{:S(2)}, u32[]{:S(2)}) collective-permute-start(f32[6,8,16,14]{3,2,1,0:T(8,128)S(1)} %get-tuple-element.96), channel_id=1, source_target_pairs={{32,0},{64,32},{96,64},{128,96},{160,128},{192,160},{224,192},{0,2... | collective-permute-start | bytes 129032 | tf_op jit(solution)/shard_map/ppermute | solution.py:25
  9.5 0.7 fusion.225
  10.6 0.7 fusion.369
  14.5 6.7 %shard_map.208 = f32[8,8,128]{2,1,0:T(8,128)} custom-call(f32[8,128]{1,0:T(8,128)} %select_select_fusion.10.refs_0_), custom_call_target="tpu_custom_call" | custom-call | tf_op jit(solution)/shard_map/pallas_call | solution.py:95
  21.2 1.4 reduce_max.78.refs_0_
  22.5 15.4 %shard_map.209 = f32[32,8,128]{2,1,0:T(8,128)} custom-call(f32[8,128]{1,0:T(8,128)} %reduce_max.78.refs_0_), custom_call_target="tpu_custom_call" | custom-call | tf_op jit(solution)/shard_map/pallas_call | solution.py:95
  37.9 0.9 reduce_max.79
  42.6 4.7 %collective-permute-start.3 = (f32[6,8,14,156]{3,1,2,0:T(8,128)S(1)}, f32[6,8,14,156]{3,1,2,0:T(8,128)S(1)}, u32[]{:S(2)}, u32[]{:S(2)}) collective-permute-start(f32[6,8,14,156]{3,1,2,0:T(8,128)S(1)} %copy.160), channel_id=1, source_target_pairs={{1,0},{2,1},{3,2},{4,3},{5,4},{6,5},{7,6},{8,7},{9,8},{10,9},{11,1... | collective-permute-start | bytes 1257992 | tf_op jit(solution)/shard_map/ppermute | solution.py:25
  47.9 13.2 %collective-permute-done.3 = f32[6,8,14,156]{3,1,2,0:T(8,128)S(1)} collective-permute-done((f32[6,8,14,156]{3,1,2,0:T(8,128)S(1)}, f32[6,8,14,156]{3,1,2,0:T(8,128)S(1)}, u32[]{:S(2)}, u32[]{:S(2)}) %collective-permute-start.3) | collective-permute-done | bytes 419360 | tf_op jit(solution)/shard_map/ppermute | solution.py:25
  61.4 5.3 %collective-permute-done.2 = f32[6,8,14,156]{3,1,2,0:T(8,128)S(1)} collective-permute-done((f32[6,8,14,156]{3,1,2,0:T(8,128)S(1)}, f32[6,8,14,156]{3,1,2,0:T(8,128)S(1)}, u32[]{:S(2)}, u32[]{:S(2)}) %collective-permute-start.2) | collective-permute-done | bytes 419360 | tf_op jit(solution)/shard_map/ppermute | solution.py:23
  67.6 1.5 slice.1815
  70.9 1.1 fusion.25
  73.1 1.0 slice_add_fusion.8
  75.1 1.1 fusion.54
  76.3 1.5 fusion.95
  77.8 1.4 fusion.430
  79.2 2.4 %reshape.224 = f32[1152,148]{1,0:T(8,128)} reshape(f32[4,8,36,148]{3,2,1,0:T(8,128)} %slice.1815) | data formatting | bytes 1363968 | tf_op jit(solution)/shard_map/reshape | solution.py:124
  81.6 2.0 %fusion.157 = f32[1152,74]{0,1:T(8,128)S(1)} fusion(f32[1152,148]{1,0:T(8,128)} %reshape.224, s32[148]{0:T(256)S(1)} %get-tuple-element.208, s32[148]{0:T(256)S(1)} %get-tuple-element.209, pred[148]{0:T(512)(128)(4,1)S(1)} %compare_and_fusion.2), kind=kOutput, calls=%fused_computation.270 | convolution fusion | flops 151422352 | bytes 1024308 | tf_op jit(solution)/shard_map/dot_general | solution.py:124
  83.6 0.8 fusion.14
  85.1 3.0 %fusion.46 = f32[2,8,36,148]{3,2,1,0:T(8,128)} fusion(f32[2,8,38,150]{3,2,1,0:T(8,128)S(1)} %fusion.54, f32[2,8,42,154]{3,2,1,0:T(8,128)S(1)} %get-tuple-element.32, f32[1,8,36,148]{3,2,1,0:T(8,128)} %get-tuple-element.60, f32[1,8,36,148]{3,2,1,0:T(8,128)} %get-tuple-element.59, f32[2,7,36,148]{3,2,1,0:T(8,128)} %get-tuple-element.56, ...), kind=kLoop, calls=%fused_computation.79 | loop fusion | flops 937728 | bytes 3068936 | tf_op jit(solution)/shard_map/sub | solution.py:233
  88.1 2.0 %reshape.222 = f32[576,148]{1,0:T(8,128)} reshape(f32[2,8,36,148]{3,2,1,0:T(8,128)} %fusion.46) | data formatting | bytes 681984 | tf_op jit(solution)/shard_map/reshape | solution.py:124
  90.1 1.6 %fusion.158 = f32[576,74]{0,1:T(8,128)S(1)} fusion(f32[576,148]{1,0:T(8,128)} %reshape.222, s32[148]{0:T(256)S(1)} %get-tuple-element.208, s32[148]{0:T(256)S(1)} %get-tuple-element.209, pred[148]{0:T(512)(128)(4,1)S(1)} %compare_and_fusion.2), kind=kOutput, calls=%fused_computation.271 | convolution fusion | flops 75722128 | bytes 512820 | tf_op jit(solution)/shard_map/dot_general | solution.py:124
  92.3 0.8 neg.31
  93.3 0.8 slice_add_fusion.32
  96.1 2.9 %collective-permute-start.5 = (f32[6,2,4,3]{3,2,1,0:T(4,128)S(1)}, f32[6,2,4,3]{3,2,1,0:T(4,128)S(1)}, u32[]{:S(2)}, u32[]{:S(2)}) collective-permute-start(f32[6,2,4,3]{3,2,1,0:T(4,128)S(1)} %get-tuple-element.160), channel_id=1, source_target_pairs={{32,0},{64,32},{96,64},{128,96},{160,128},{192,160},{224,192},{0,2... | collective-permute-start | bytes 1736 | tf_op jit(solution)/shard_map/ppermute | solution.py:25
  99.0 1.5 %collective-permute-done.4 = f32[6,2,4,3]{3,2,1,0:T(4,128)S(1)} collective-permute-done((f32[6,2,4,3]{3,2,1,0:T(4,128)S(1)}, f32[6,2,4,3]{3,2,1,0:T(4,128)S(1)}, u32[]{:S(2)}, u32[]{:S(2)}) %collective-permute-start.4) | collective-permute-done | bytes 608 | tf_op jit(solution)/shard_map/ppermute | solution.py:23
  101.3 5.3 %collective-permute-start.7 = (f32[6,2,3,38]{3,2,1,0:T(4,128)S(1)}, f32[6,2,3,38]{3,2,1,0:T(4,128)S(1)}, u32[]{:S(2)}, u32[]{:S(2)}) collective-permute-start(f32[6,2,3,38]{3,2,1,0:T(4,128)S(1)} %get-tuple-element.158), channel_id=1, source_target_pairs={{1,0},{2,1},{3,2},{4,3},{5,4},{6,5},{7,6},{8,7},{9,8},{10,9},{11,1... | collective-permute-start | bytes 16424 | tf_op jit(solution)/shard_map/ppermute | solution.py:25
  107.5 1.1 collective-permute-done.6
  109.0 0.8 slice_add_fusion.49
  109.9 0.8 fusion.260
  110.7 3.0 %collective-permute-start.9 = (f32[2,2,4,3]{3,2,1,0:T(4,128)S(1)}, f32[2,2,4,3]{3,2,1,0:T(4,128)S(1)}, u32[]{:S(2)}, u32[]{:S(2)}) collective-permute-start(f32[2,2,4,3]{3,2,1,0:T(4,128)S(1)} %get-tuple-element.173), channel_id=1, source_target_pairs={{32,0},{64,32},{96,64},{128,96},{160,128},{192,160},{224,192},{0,2... | collective-permute-start | bytes 584 | tf_op jit(solution)/shard_map/ppermute | solution.py:25
  113.8 1.3 collective-permute-done.8
  115.2 5.3 %collective-permute-start.11 = (f32[2,2,3,38]{3,2,1,0:T(4,128)S(1)}, f32[2,2,3,38]{3,2,1,0:T(4,128)S(1)}, u32[]{:S(2)}, u32[]{:S(2)}) collective-permute-start(f32[2,2,3,38]{3,2,1,0:T(4,128)S(1)} %get-tuple-element.182), channel_id=1, source_target_pairs={{1,0},{2,1},{3,2},{4,3},{5,4},{6,5},{7,6},{8,7},{9,8},{10,9},{11,1... | collective-permute-start | bytes 5480 | tf_op jit(solution)/shard_map/ppermute | solution.py:25
  120.6 1.6 %collective-permute-done.10 = f32[2,2,3,38]{3,2,1,0:T(4,128)S(1)} collective-permute-done((f32[2,2,3,38]{3,2,1,0:T(4,128)S(1)}, f32[2,2,3,38]{3,2,1,0:T(4,128)S(1)}, u32[]{:S(2)}, u32[]{:S(2)}) %collective-permute-start.10) | collective-permute-done | bytes 1856 | tf_op jit(solution)/shard_map/ppermute | solution.py:23
  123.2 0.8 broadcast_in_dim.45
  124.0 1.1 copy.154
  125.2 3.0 %collective-permute-start.13 = (f32[2,4,8,5]{3,2,1,0:T(8,128)S(1)}, f32[2,4,8,5]{3,2,1,0:T(8,128)S(1)}, u32[]{:S(2)}, u32[]{:S(2)}) collective-permute-start(f32[2,4,8,5]{3,2,1,0:T(8,128)S(1)} %get-tuple-element.148), channel_id=1, source_target_pairs={{32,0},{64,32},{96,64},{128,96},{160,128},{192,160},{224,192},{0,2... | collective-permute-start | bytes 3848 | tf_op jit(solution)/shard_map/ppermute | solution.py:25
  128.2 1.6 %collective-permute-done.12 = f32[2,4,8,5]{3,2,1,0:T(8,128)S(1)} collective-permute-done((f32[2,4,8,5]{3,2,1,0:T(8,128)S(1)}, f32[2,4,8,5]{3,2,1,0:T(8,128)S(1)}, u32[]{:S(2)}, u32[]{:S(2)}) %collective-permute-start.12) | collective-permute-done | bytes 1312 | tf_op jit(solution)/shard_map/ppermute | solution.py:23
  130.0 5.7 %collective-permute-start.15 = (f32[2,4,5,74]{3,2,1,0:T(8,128)S(1)}, f32[2,4,5,74]{3,2,1,0:T(8,128)S(1)}, u32[]{:S(2)}, u32[]{:S(2)}) collective-permute-start(f32[2,4,5,74]{3,2,1,0:T(8,128)S(1)} %get-tuple-element.146), channel_id=1, source_target_pairs={{1,0},{2,1},{3,2},{4,3},{5,4},{6,5},{7,6},{8,7},{9,8},{10,9},{11,1... | collective-permute-start | bytes 35528 | tf_op jit(solution)/shard_map/ppermute | solution.py:25
  135.7 1.5 %collective-permute-done.14 = f32[2,4,5,74]{3,2,1,0:T(8,128)S(1)} collective-permute-done((f32[2,4,5,74]{3,2,1,0:T(8,128)S(1)}, f32[2,4,5,74]{3,2,1,0:T(8,128)S(1)}, u32[]{:S(2)}, u32[]{:S(2)}) %collective-permute-start.14) | collective-permute-done | bytes 11872 | tf_op jit(solution)/shard_map/ppermute | solution.py:23
  137.7 0.9 slice_add_fusion.27
  139.7 1.1 copy.156
  140.8 1.1 broadcast_in_dim.48
  141.9 1.3 slice.1989
  143.3 1.9 %copy.161 = f32[2,8,22,134]{3,2,1,0:T(8,128)S(1)} copy(f32[2,8,22,134]{2,1,3,0:T(8,128)} %slice.1989) | data formatting | bytes 377344
  147.7 0.7 slice_add_fusion.11
  148.8 0.9 fusion.140
  (215 shorter events, 23.0 us)
Async XLA Ops:
  0.0 4.3 %copy-start = (f32[2,8,16,128]{3,2,1,0:T(8,128)S(1)}, f32[2,8,16,128]{3,2,1,0:T(8,128)}, u32[]{:S(2)}) copy-start(f32[2,8,16,128]{3,2,1,0:T(8,128)} %param.22) | copy-start | bytes 393220
  0.0 4.3 %copy-start.1 = (f32[8,16,128]{2,1,0:T(8,128)S(1)}, f32[8,16,128]{2,1,0:T(8,128)}, u32[]{:S(2)}) copy-start(f32[8,16,128]{2,1,0:T(8,128)} %param.25) | copy-start | bytes 196612
  0.0 4.3 %copy-start.2 = (f32[8,16,128]{2,1,0:T(8,128)S(1)}, f32[8,16,128]{2,1,0:T(8,128)}, u32[]{:S(2)}) copy-start(f32[8,16,128]{2,1,0:T(8,128)} %param.24) | copy-start | bytes 196612
  1.3 40.0 %collective-permute-start = (f32[6,8,16,14]{3,2,1,0:T(8,128)S(1)}, f32[6,8,16,14]{3,2,1,0:T(8,128)S(1)}, u32[]{:S(2)}, u32[]{:S(2)}) collective-permute-start(f32[6,8,16,14]{3,2,1,0:T(8,128)S(1)} %get-tuple-element.95), channel_id=1, source_target_pairs={{0,32},{32,64},{64,96},{96,128},{128,160},{160,192},{192,224},{224... | collective-permute-start | bytes 129032 | tf_op jit(solution)/shard_map/ppermute | solution.py:23
  1.3 39.9 %collective-permute-start.1 = (f32[6,8,16,14]{3,2,1,0:T(8,128)S(1)}, f32[6,8,16,14]{3,2,1,0:T(8,128)S(1)}, u32[]{:S(2)}, u32[]{:S(2)}) collective-permute-start(f32[6,8,16,14]{3,2,1,0:T(8,128)S(1)} %get-tuple-element.96), channel_id=1, source_target_pairs={{32,0},{64,32},{96,64},{128,96},{160,128},{192,160},{224,192},{0,2... | collective-permute-start | bytes 129032 | tf_op jit(solution)/shard_map/ppermute | solution.py:25
  4.3 6.0 %copy-start.27 = (pred[64]{0:T(512)(128)(4,1)}, pred[64]{0:T(512)(128)(4,1)S(1)}, u32[]{:S(2)}) copy-start(pred[64]{0:T(512)(128)(4,1)S(1)} %compare_and_fusion.3) | copy-start | bytes 196
  5.6 4.6 %copy-start.21 = (s32[64]{0:T(128)}, s32[64]{0:T(128)S(1)}, u32[]{:S(2)}) copy-start(s32[64]{0:T(128)S(1)} %get-tuple-element.196) | copy-start | bytes 772
  5.6 4.6 %copy-start.23 = (s32[64]{0:T(128)}, s32[64]{0:T(128)S(1)}, u32[]{:S(2)}) copy-start(s32[64]{0:T(128)S(1)} %get-tuple-element.197) | copy-start | bytes 772
  9.2 32.1 %copy-start.3 = (f32[2,8,16,128]{3,2,1,0:T(8,128)S(1)}, f32[2,8,16,128]{3,2,1,0:T(8,128)}, u32[]{:S(2)}) copy-start(f32[2,8,16,128]{3,2,1,0:T(8,128)} %param.23) | copy-start | bytes 393220
  42.6 18.5 %collective-permute-start.3 = (f32[6,8,14,156]{3,1,2,0:T(8,128)S(1)}, f32[6,8,14,156]{3,1,2,0:T(8,128)S(1)}, u32[]{:S(2)}, u32[]{:S(2)}) collective-permute-start(f32[6,8,14,156]{3,1,2,0:T(8,128)S(1)} %copy.160), channel_id=1, source_target_pairs={{1,0},{2,1},{3,2},{4,3},{5,4},{6,5},{7,6},{8,7},{9,8},{10,9},{11,1... | collective-permute-start | bytes 1257992 | tf_op jit(solution)/shard_map/ppermute | solution.py:25
  47.3 19.4 %collective-permute-start.2 = (f32[6,8,14,156]{3,1,2,0:T(8,128)S(1)}, f32[6,8,14,156]{3,1,2,0:T(8,128)S(1)}, u32[]{:S(2)}, u32[]{:S(2)}) collective-permute-start(f32[6,8,14,156]{3,1,2,0:T(8,128)S(1)} %copy.159), channel_id=1, source_target_pairs={{0,1},{1,2},{2,3},{3,4},{4,5},{5,6},{6,7},{7,8},{8,9},{9,10},{10,1... | collective-permute-start | bytes 1257992 | tf_op jit(solution)/shard_map/ppermute | solution.py:23
  70.2 0.7 copy-start.10
  93.0 1.4 copy-start.12
  93.2 1.0 copy-start.8
  93.2 2.2 %copy-start.9 = (f32[1,4,16,72]{3,2,1,0:T(8,128)}, f32[1,4,16,72]{3,2,1,0:T(8,128)S(1)}, u32[]{:S(2)}) copy-start(f32[1,4,16,72]{3,2,1,0:T(8,128)S(1)} %get-tuple-element.144) | copy-start | bytes 55300
  93.2 2.2 %copy-start.22 = (s32[64]{0:T(128)S(1)}, s32[64]{0:T(128)}, u32[]{:S(2)}) copy-start(s32[64]{0:T(128)} %copy-done.21) | copy-start | bytes 772
  93.2 2.2 %copy-start.24 = (s32[64]{0:T(128)S(1)}, s32[64]{0:T(128)}, u32[]{:S(2)}) copy-start(s32[64]{0:T(128)} %copy-done.23) | copy-start | bytes 772
  93.2 2.2 %copy-start.28 = (pred[64]{0:T(512)(128)(4,1)S(1)}, pred[64]{0:T(512)(128)(4,1)}, u32[]{:S(2)}) copy-start(pred[64]{0:T(512)(128)(4,1)} %copy-done.27) | copy-start | bytes 196
  93.2 2.5 %copy-start.15 = (s32[64]{0:T(128)S(1)}, s32[64]{0:T(128)}, u32[]{:S(2)}) copy-start(s32[64]{0:T(128)} %get-tuple-element.232) | copy-start | bytes 772
  93.2 2.5 %copy-start.16 = (s32[64]{0:T(128)S(1)}, s32[64]{0:T(128)}, u32[]{:S(2)}) copy-start(s32[64]{0:T(128)} %get-tuple-element.233) | copy-start | bytes 772
  93.2 2.5 %copy-start.17 = (s32[64]{0:T(128)S(1)}, s32[64]{0:T(128)}, u32[]{:S(2)}) copy-start(s32[64]{0:T(128)} %get-tuple-element.230) | copy-start | bytes 772
  93.2 2.5 %copy-start.18 = (s32[64]{0:T(128)S(1)}, s32[64]{0:T(128)}, u32[]{:S(2)}) copy-start(s32[64]{0:T(128)} %get-tuple-element.231) | copy-start | bytes 772
  93.2 2.5 %copy-start.19 = (s32[64]{0:T(128)S(1)}, s32[64]{0:T(128)}, u32[]{:S(2)}) copy-start(s32[64]{0:T(128)} %get-tuple-element.228) | copy-start | bytes 772
  93.3 2.5 %copy-start.20 = (s32[64]{0:T(128)S(1)}, s32[64]{0:T(128)}, u32[]{:S(2)}) copy-start(s32[64]{0:T(128)} %get-tuple-element.229) | copy-start | bytes 772
  93.3 2.5 %copy-start.25 = (pred[64]{0:T(512)(128)(4,1)S(1)}, pred[64]{0:T(512)(128)(4,1)}, u32[]{:S(2)}) copy-start(pred[64]{0:T(512)(128)(4,1)} %get-tuple-element.226) | copy-start | bytes 196
  93.3 2.5 %copy-start.26 = (pred[64]{0:T(512)(128)(4,1)S(1)}, pred[64]{0:T(512)(128)(4,1)}, u32[]{:S(2)}) copy-start(pred[64]{0:T(512)(128)(4,1)} %get-tuple-element.227) | copy-start | bytes 196
  93.3 2.5 %copy-start.29 = (pred[64]{0:T(512)(128)(4,1)S(1)}, pred[64]{0:T(512)(128)(4,1)}, u32[]{:S(2)}) copy-start(pred[64]{0:T(512)(128)(4,1)} %compare_and_fusion.7) | copy-start | bytes 196
  94.4 0.6 copy-start.6
  94.4 14.5 %copy-start.4 = (f32[1,4,14,70]{3,2,1,0:T(8,128)}, f32[1,4,14,70]{3,2,1,0:T(8,128)S(1)}, u32[]{:S(2)}) copy-start(f32[1,4,14,70]{3,2,1,0:T(8,128)S(1)} %get-tuple-element.139) | copy-start | bytes 47044
  96.1 4.5 %collective-permute-start.4 = (f32[6,2,4,3]{3,2,1,0:T(4,128)S(1)}, f32[6,2,4,3]{3,2,1,0:T(4,128)S(1)}, u32[]{:S(2)}, u32[]{:S(2)}) collective-permute-start(f32[6,2,4,3]{3,2,1,0:T(4,128)S(1)} %get-tuple-element.159), channel_id=1, source_target_pairs={{0,32},{32,64},{64,96},{96,128},{128,160},{160,192},{192,224},{224... | collective-permute-start | bytes 1736 | tf_op jit(solution)/shard_map/ppermute | solution.py:23
  96.1 4.5 %collective-permute-start.5 = (f32[6,2,4,3]{3,2,1,0:T(4,128)S(1)}, f32[6,2,4,3]{3,2,1,0:T(4,128)S(1)}, u32[]{:S(2)}, u32[]{:S(2)}) collective-permute-start(f32[6,2,4,3]{3,2,1,0:T(4,128)S(1)} %get-tuple-element.160), channel_id=1, source_target_pairs={{32,0},{64,32},{96,64},{128,96},{160,128},{192,160},{224,192},{0,2... | collective-permute-start | bytes 1736 | tf_op jit(solution)/shard_map/ppermute | solution.py:25
  101.3 7.4 %collective-permute-start.6 = (f32[6,2,3,38]{3,2,1,0:T(4,128)}, f32[6,2,3,38]{3,2,1,0:T(4,128)S(1)}, u32[]{:S(2)}, u32[]{:S(2)}) collective-permute-start(f32[6,2,3,38]{3,2,1,0:T(4,128)} %get-tuple-element.157), channel_id=1, source_target_pairs={{0,1},{1,2},{2,3},{3,4},{4,5},{5,6},{6,7},{7,8},{8,9},{9,10},{10,1... | collective-permute-start | bytes 16424 | tf_op jit(solution)/shard_map/ppermute | solution.py:23
  101.3 7.4 %collective-permute-start.7 = (f32[6,2,3,38]{3,2,1,0:T(4,128)S(1)}, f32[6,2,3,38]{3,2,1,0:T(4,128)S(1)}, u32[]{:S(2)}, u32[]{:S(2)}) collective-permute-start(f32[6,2,3,38]{3,2,1,0:T(4,128)S(1)} %get-tuple-element.158), channel_id=1, source_target_pairs={{1,0},{2,1},{3,2},{4,3},{5,4},{6,5},{7,6},{8,7},{9,8},{10,9},{11,1... | collective-permute-start | bytes 16424 | tf_op jit(solution)/shard_map/ppermute | solution.py:25
  107.5 15.0 %copy-start.14 = (f32[2]{0:T(128)S(1)}, f32[2]{0:T(128)}, u32[]{:S(2)}) copy-start(f32[2]{0:T(128)} %constant.378.clone) | copy-start | bytes 28
  110.7 4.3 %collective-permute-start.8 = (f32[2,2,4,3]{3,2,1,0:T(4,128)S(1)}, f32[2,2,4,3]{3,2,1,0:T(4,128)S(1)}, u32[]{:S(2)}, u32[]{:S(2)}) collective-permute-start(f32[2,2,4,3]{3,2,1,0:T(4,128)S(1)} %get-tuple-element.172), channel_id=1, source_target_pairs={{0,32},{32,64},{64,96},{96,128},{128,160},{160,192},{192,224},{224... | collective-permute-start | bytes 584 | tf_op jit(solution)/shard_map/ppermute | solution.py:23
  110.7 4.3 %collective-permute-start.9 = (f32[2,2,4,3]{3,2,1,0:T(4,128)S(1)}, f32[2,2,4,3]{3,2,1,0:T(4,128)S(1)}, u32[]{:S(2)}, u32[]{:S(2)}) collective-permute-start(f32[2,2,4,3]{3,2,1,0:T(4,128)S(1)} %get-tuple-element.173), channel_id=1, source_target_pairs={{32,0},{64,32},{96,64},{128,96},{160,128},{192,160},{224,192},{0,2... | collective-permute-start | bytes 584 | tf_op jit(solution)/shard_map/ppermute | solution.py:25
  115.1 7.0 %collective-permute-start.10 = (f32[2,2,3,38]{3,2,1,0:T(4,128)S(1)}, f32[2,2,3,38]{3,2,1,0:T(4,128)S(1)}, u32[]{:S(2)}, u32[]{:S(2)}) collective-permute-start(f32[2,2,3,38]{3,2,1,0:T(4,128)S(1)} %get-tuple-element.181), channel_id=1, source_target_pairs={{0,1},{1,2},{2,3},{3,4},{4,5},{5,6},{6,7},{7,8},{8,9},{9,10},{10,1... | collective-permute-start | bytes 5480 | tf_op jit(solution)/shard_map/ppermute | solution.py:23
  115.2 7.0 %collective-permute-start.11 = (f32[2,2,3,38]{3,2,1,0:T(4,128)S(1)}, f32[2,2,3,38]{3,2,1,0:T(4,128)S(1)}, u32[]{:S(2)}, u32[]{:S(2)}) collective-permute-start(f32[2,2,3,38]{3,2,1,0:T(4,128)S(1)} %get-tuple-element.182), channel_id=1, source_target_pairs={{1,0},{2,1},{3,2},{4,3},{5,4},{6,5},{7,6},{8,7},{9,8},{10,9},{11,1... | collective-permute-start | bytes 5480 | tf_op jit(solution)/shard_map/ppermute | solution.py:25
  122.6 15.1 %copy-start.13 = (f32[2]{0:T(128)S(1)}, f32[2]{0:T(128)}, u32[]{:S(2)}) copy-start(f32[2]{0:T(128)} %constant.377.clone) | copy-start | bytes 28
  125.1 13.9 %copy-start.5 = (f32[1,4,14,70]{3,2,1,0:T(8,128)S(1)}, f32[1,4,14,70]{3,2,1,0:T(8,128)}, u32[]{:S(2)}) copy-start(f32[1,4,14,70]{3,2,1,0:T(8,128)} %copy-done.4) | copy-start | bytes 47044
  125.1 13.9 %copy-start.7 = (f32[1,4,14,70]{3,2,1,0:T(8,128)S(1)}, f32[1,4,14,70]{3,2,1,0:T(8,128)}, u32[]{:S(2)}) copy-start(f32[1,4,14,70]{3,2,1,0:T(8,128)} %copy-done.6) | copy-start | bytes 47044
  125.2 4.6 %collective-permute-start.12 = (f32[2,4,8,5]{3,2,1,0:T(8,128)S(1)}, f32[2,4,8,5]{3,2,1,0:T(8,128)S(1)}, u32[]{:S(2)}, u32[]{:S(2)}) collective-permute-start(f32[2,4,8,5]{3,2,1,0:T(8,128)S(1)} %get-tuple-element.147), channel_id=1, source_target_pairs={{0,32},{32,64},{64,96},{96,128},{128,160},{160,192},{192,224},{224... | collective-permute-start | bytes 3848 | tf_op jit(solution)/shard_map/ppermute | solution.py:23
  125.2 4.6 %collective-permute-start.13 = (f32[2,4,8,5]{3,2,1,0:T(8,128)S(1)}, f32[2,4,8,5]{3,2,1,0:T(8,128)S(1)}, u32[]{:S(2)}, u32[]{:S(2)}) collective-permute-start(f32[2,4,8,5]{3,2,1,0:T(8,128)S(1)} %get-tuple-element.148), channel_id=1, source_target_pairs={{32,0},{64,32},{96,64},{128,96},{160,128},{192,160},{224,192},{0,2... | collective-permute-start | bytes 3848 | tf_op jit(solution)/shard_map/ppermute | solution.py:25
  129.9 7.3 %collective-permute-start.14 = (f32[2,4,5,74]{3,2,1,0:T(8,128)S(1)}, f32[2,4,5,74]{3,2,1,0:T(8,128)S(1)}, u32[]{:S(2)}, u32[]{:S(2)}) collective-permute-start(f32[2,4,5,74]{3,2,1,0:T(8,128)S(1)} %get-tuple-element.145), channel_id=1, source_target_pairs={{0,1},{1,2},{2,3},{3,4},{4,5},{5,6},{6,7},{7,8},{8,9},{9,10},{10,1... | collective-permute-start | bytes 35528 | tf_op jit(solution)/shard_map/ppermute | solution.py:23
  130.0 7.3 %collective-permute-start.15 = (f32[2,4,5,74]{3,2,1,0:T(8,128)S(1)}, f32[2,4,5,74]{3,2,1,0:T(8,128)S(1)}, u32[]{:S(2)}, u32[]{:S(2)}) collective-permute-start(f32[2,4,5,74]{3,2,1,0:T(8,128)S(1)} %get-tuple-element.146), channel_id=1, source_target_pairs={{1,0},{2,1},{3,2},{4,3},{5,4},{6,5},{7,6},{8,7},{9,8},{10,9},{11,1... | collective-permute-start | bytes 35528 | tf_op jit(solution)/shard_map/ppermute | solution.py:25
  145.7 0.7 copy-start.11

commit v4 on v3

--- a/solution.py
+++ b/solution.py
@@ -214,26 +214,27 @@
         local = jnp.where(lane == level, jnp.maximum(jnp.max(first), jnp.max(second)), local)
     spreads = global_max(local)[0]
 
-    wide = padded(jnp.concatenate([fields, previous], 0), 14)
-    ops_0 = Level(coefficients(crop(wide[:4], 14, 13), 0)[0], 13, 0)
+    wide = padded(jnp.concatenate([fields, previous], 0), 6)
+    ops_0 = Level(coefficients(crop(wide[:4], 6, 5), 0)[0], 5, 0)
     state_w = wide[:2]
-    substrate, catalyst = crop(state_w[0], 14, 13), crop(state_w[1], 14, 13)
-    centre = crop(state_w, 14, 13)
+    substrate, catalyst = crop(state_w[0], 6, 5), crop(state_w[1], 6, 5)
+    centre = crop(state_w, 6, 5)
     reaction = substrate * catalyst * catalyst
     laplace = shrunk_neighbours(state_w) - 6.0 * centre
-    feed_w = crop(wide[2], 14, 13)
-    kill_w = crop(wide[3], 14, 13)
-    previous_w = crop(wide[4:6], 14, 13)
+    feed_w = crop(wide[2], 6, 5)
+    kill_w = crop(wide[3], 6, 5)
+    previous_w = crop(wide[4:6], 6, 5)
     local_terms = jnp.stack(
         [reaction - feed_w * (1.0 - substrate), -reaction + (feed_w + kill_w) * catalyst]
     )
     nonlinear = inverse_step * (centre - previous_w) - diffusions(0) * laplace + local_terms
     source_0 = -nonlinear
-    pre_0, pre_0_halo = chebyshev(ops_0, source_0, 13, None, None, spreads[0])
-    resid_0 = crop(source_0, 13, 10) - ops_0.operate(crop(pre_0, pre_0_halo, 11), 11)
-
-    source_1 = restrict(resid_0)
-    ops_1 = Level(coefficients(restrict(crop(wide[:4], 14, 10)), 1)[0], 5, 1)
+    pre_0, pre_0_halo = chebyshev(ops_0, source_0, 5, None, None, spreads[0])
+    resid_0 = crop(source_0, 5, 0) - ops_0.operate(crop(pre_0, pre_0_halo, 1), 1)
+
+    wide_1 = padded(jnp.concatenate([restrict(resid_0), fields_1], 0), 5)
+    ops_1 = Level(coefficients(wide_1[2:], 1)[0], 5, 1)
+    source_1 = wide_1[:2]
     pre_1, pre_1_halo = chebyshev(ops_1, source_1, 5, None, None, spreads[1])
     resid_1 = crop(source_1, 5, 0) - ops_1.operate(crop(pre_1, pre_1_halo, 1), 1)
 
@@ -248,7 +249,7 @@
     post_1, post_1_halo = chebyshev(ops_1, source_1, 5, start_1, 5, spreads[1])
 
     start_0 = crop(pre_0, pre_0_halo, 3) + crop(prolong(post_1), 2 * post_1_halo, 3)
-    post_0, post_0_halo = chebyshev(ops_0, source_0, 13, start_0, 3, spreads[0])
+    post_0, post_0_halo = chebyshev(ops_0, source_0, 5, start_0, 3, spreads[0])
     return crop(post_0, post_0_halo, 0)
 
 

time: 152 us -> 123 us (0.81); the launches traced: 150 us -> 123 us
  waiting for transfers between devices: 27.3 us -> 48.7 us
  starting transfers between devices: 33.1 us -> 15.7 us
  local copies, waits for them, and re-layouts: 23.3 us -> 6.66 us
  other arithmetic: 30.2 us -> 18.2 us
  matrix products: 6.3 us -> 2.06 us
  Pallas kernels: 22 us -> 24.6 us
    ppermute x8 -> x10, starting transfers between devices: 32.9 us -> 5.83 us  [padded(): lax.ppermute(head, axis, [((i + 1) % count, i) for i in range(count)])]
    ppermute x8 -> x10, waiting for transfers between devices: 13.9 us -> 31.5 us  [padded(): lax.ppermute(tail, axis, [(i, (i + 1) % count) for i in range(count)])]
    ppermute x8 -> x10, starting transfers between devices: 0.21 us -> 9.85 us  [padded(): lax.ppermute(tail, axis, [(i, (i + 1) % count) for i in range(count)])]
    reshape x3 -> x0, local copies, waits for them, and re-layouts: 4.4 us -> none  [the longest x2 4.39 us: restrict(): field.reshape(count, cols)]
    ppermute x8 -> x10, waiting for transfers between devices: 13.3 us -> 17.2 us  [padded(): lax.ppermute(head, axis, [((i + 1) % count, i) for i in range(count)])]
    dot_general x5 -> x4, matrix products: 4.54 us -> 1.26 us  [restrict(): jnp.dot(field.reshape(count, cols), pick_x, precision=lax.Precision.HIGHEST)]
    unnamed x63 -> x15, local copies, waits for them, and re-layouts: 3.55 us -> 0.71 us
    sub x1, other arithmetic: 3.02 us -> 0.24 us  [body(): crop(source_0, 5, 0) - ops_0.operate(crop(pre_0, pre_0_halo, 1), 1)]
  transfers between devices with their start and end apart: 16 -> 20, of which waited for: 9 -> 18; matrix products, arithmetic and copies ran while one was open for 7% -> 6% of each run, Pallas kernels for 15% -> 20%
where the time goes in v4:
time: 123 us
  waiting for transfers between devices  48.7 us (40%)
  Pallas kernels  24.6 us (20%)
  other arithmetic  18.2 us (15%)
  starting transfers between devices  15.7 us (13%)
  between operations  7.23 us (6%)
  local copies, waits for them, and re-layouts  6.66 us (5%)
  matrix products  2.06 us (2%)
    ppermute x10, waiting for transfers between devices, padded(): lax.ppermute(tail, axis, [(i, (i + 1) % count) for i in range(count)])  31.5 us
    pallas_call x2, Pallas kernels, gather_axis(): pl.pallas_call(lambda *refs: gather_kernel(axis, *refs), out_shape=jax.Sh...  24.6 us
    ppermute x10, waiting for transfers between devices, padded(): lax.ppermute(head, axis, [((i + 1) % count, i) for i in range(count)])  17.2 us
    ppermute x10, starting transfers between devices, padded(): lax.ppermute(tail, axis, [(i, (i + 1) % count) for i in range(count)])  9.85 us
    ppermute x10, starting transfers between devices, padded(): lax.ppermute(head, axis, [((i + 1) % count, i) for i in range(count)])  5.83 us
    add x12, other arithmetic, chebyshev(): iterate = crop(iterate, halo + 1, halo) + update  4.09 us
    slice x31, local copies, waits for them, and re-layouts, shrunk_neighbours(): along_z = jnp.roll(centre, 1, 1) + jnp.roll(centre, -1, 1)  3.5 us
    add x16, other arithmetic, operate(): first = coeff[0] * centre[0] + coeff[1] * centre[1]  2.93 us
  transfers between devices with their start and end apart: 20, of which 18 were waited for; matrix products, arithmetic and copies ran while one was open for 6% of the time, Pallas kernels for 20%

profile of v4, /device:TPU:0, one launch (start us, length us, event | category | flops | bytes accessed | tf_op | source)
XLA Modules:
  0.0 123.1 jit_solution(10288934674758854934)
XLA Ops:
  0.0 1.1 pad_maximum_fusion.2
  1.3 0.5 collective-permute-start.1
  1.8 0.6 fusion.143
  4.6 0.7 fusion.184
  5.8 0.7 fusion.315
  9.0 0.6 select_select_fusion.8.refs_0_
  9.6 7.5 %shard_map.208 = f32[8,8,128]{2,1,0:T(8,128)} custom-call(f32[8,128]{1,0:T(8,128)} %select_select_fusion.8.refs_0_), custom_call_target="tpu_custom_call" | custom-call | tf_op jit(solution)/shard_map/pallas_call | solution.py:95
  17.1 1.4 %reduce_max.78.refs_0_ = f32[8,128]{1,0:T(8,128)} reduce(f32[8,8,128]{2,1,0:T(8,128)} %shard_map.208, f32[]{:T(128)} %constant.326.clone.1), dimensions={0}, to_apply=%region_6.7 | reduce | flops 7168 | bytes 36868 | tf_op jit(solution)/shard_map/reduce_max | solution.py:112
  18.4 17.1 %shard_map.209 = f32[32,8,128]{2,1,0:T(8,128)} custom-call(f32[8,128]{1,0:T(8,128)} %reduce_max.78.refs_0_), custom_call_target="tpu_custom_call" | custom-call | tf_op jit(solution)/shard_map/pallas_call | solution.py:95
  35.6 0.9 reduce_max.79
  36.5 0.7 fusion.408
  37.6 4.7 %collective-permute-start.3 = (f32[6,8,6,140]{3,2,1,0:T(8,128)S(1)}, f32[6,8,6,140]{3,2,1,0:T(8,128)S(1)}, u32[]{:S(2)}, u32[]{:S(2)}) collective-permute-start(f32[6,8,6,140]{3,2,1,0:T(8,128)S(1)} %get-tuple-element.50), channel_id=1, source_target_pairs={{1,0},{2,1},{3,2},{4,3},{5,4},{6,5},{7,6},{8,7},{9,8},{10,9},{11,1... | collective-permute-start | bytes 483848 | tf_op jit(solution)/shard_map/ppermute | solution.py:25
  43.4 6.4 %collective-permute-done.3 = f32[6,8,6,140]{3,2,1,0:T(8,128)S(1)} collective-permute-done((f32[6,8,6,140]{3,2,1,0:T(8,128)S(1)}, f32[6,8,6,140]{3,2,1,0:T(8,128)S(1)}, u32[]{:S(2)}, u32[]{:S(2)}) %collective-permute-start.3) | collective-permute-done | bytes 161312 | tf_op jit(solution)/shard_map/ppermute | solution.py:25
  49.9 5.5 %collective-permute-done.2 = f32[6,8,6,140]{3,2,1,0:T(8,128)S(1)} collective-permute-done((f32[6,8,6,140]{3,2,1,0:T(8,128)S(1)}, f32[6,8,6,140]{3,2,1,0:T(8,128)S(1)}, u32[]{:S(2)}, u32[]{:S(2)}) %collective-permute-start.2) | collective-permute-done | bytes 161312 | tf_op jit(solution)/shard_map/ppermute | solution.py:23
  55.4 0.6 pad_maximum_fusion
  57.2 0.8 fusion.8
  58.3 0.4 fusion.63
  58.7 0.6 slice_add_fusion.12
  59.4 0.4 fusion.61
  60.1 0.7 fusion.29
  62.1 0.5 collective-permute-start.4
  62.6 1.7 %collective-permute-done.5 = f32[6,4,8,5]{3,2,1,0:T(8,128)S(1)} collective-permute-done((f32[6,4,8,5]{3,2,1,0:T(8,128)S(1)}, f32[6,4,8,5]{3,2,1,0:T(8,128)S(1)}, u32[]{:S(2)}, u32[]{:S(2)}) %collective-permute-start.5) | collective-permute-done | bytes 3872 | tf_op jit(solution)/shard_map/ppermute | solution.py:25
  64.3 3.1 %collective-permute-done.4 = f32[6,4,8,5]{3,2,1,0:T(8,128)S(1)} collective-permute-done((f32[6,4,8,5]{3,2,1,0:T(8,128)S(1)}, f32[6,4,8,5]{3,2,1,0:T(8,128)S(1)}, u32[]{:S(2)}, u32[]{:S(2)}) %collective-permute-start.4) | collective-permute-done | bytes 3872 | tf_op jit(solution)/shard_map/ppermute | solution.py:23
  67.9 1.7 %collective-permute-start.6 = (f32[6,4,5,74]{3,2,1,0:T(8,128)S(1)}, f32[6,4,5,74]{3,2,1,0:T(8,128)S(1)}, u32[]{:S(2)}, u32[]{:S(2)}) collective-permute-start(f32[6,4,5,74]{3,2,1,0:T(8,128)S(1)} %get-tuple-element.115), channel_id=1, source_target_pairs={{0,1},{1,2},{2,3},{3,4},{4,5},{5,6},{6,7},{7,8},{8,9},{9,10},{10,1... | collective-permute-start | bytes 106568 | tf_op jit(solution)/shard_map/ppermute | solution.py:23
  70.5 1.8 %collective-permute-done.7 = f32[6,4,5,74]{3,2,1,0:T(8,128)S(1)} collective-permute-done((f32[6,4,5,74]{3,2,1,0:T(8,128)S(1)}, f32[6,4,5,74]{3,2,1,0:T(8,128)S(1)}, u32[]{:S(2)}, u32[]{:S(2)}) %collective-permute-start.7) | collective-permute-done | bytes 35552 | tf_op jit(solution)/shard_map/ppermute | solution.py:25
  72.2 3.6 %collective-permute-done.6 = f32[6,4,5,74]{3,2,1,0:T(8,128)S(1)} collective-permute-done((f32[6,4,5,74]{3,2,1,0:T(8,128)S(1)}, f32[6,4,5,74]{3,2,1,0:T(8,128)S(1)}, u32[]{:S(2)}, u32[]{:S(2)}) %collective-permute-start.6) | collective-permute-done | bytes 35552 | tf_op jit(solution)/shard_map/ppermute | solution.py:23
  78.0 0.5 collective-permute-start.8
  78.5 1.0 collective-permute-done.9
  79.5 3.0 %collective-permute-done.8 = f32[6,2,4,3]{3,2,1,0:T(4,128)S(1)} collective-permute-done((f32[6,2,4,3]{3,2,1,0:T(4,128)S(1)}, f32[6,2,4,3]{3,2,1,0:T(4,128)S(1)}, u32[]{:S(2)}, u32[]{:S(2)}) %collective-permute-start.8) | collective-permute-done | bytes 608 | tf_op jit(solution)/shard_map/ppermute | solution.py:23
  82.7 2.0 %collective-permute-start.10 = (f32[6,2,3,38]{3,2,1,0:T(4,128)S(1)}, f32[6,2,3,38]{3,2,1,0:T(4,128)S(1)}, u32[]{:S(2)}, u32[]{:S(2)}) collective-permute-start(f32[6,2,3,38]{3,2,1,0:T(4,128)S(1)} %get-tuple-element.161), channel_id=1, source_target_pairs={{0,1},{1,2},{2,3},{3,4},{4,5},{5,6},{6,7},{7,8},{8,9},{9,10},{10,1... | collective-permute-start | bytes 16424 | tf_op jit(solution)/shard_map/ppermute | solution.py:23
  85.6 0.9 collective-permute-done.11
  86.5 3.4 %collective-permute-done.10 = f32[6,2,3,38]{3,2,1,0:T(4,128)S(1)} collective-permute-done((f32[6,2,3,38]{3,2,1,0:T(4,128)S(1)}, f32[6,2,3,38]{3,2,1,0:T(4,128)S(1)}, u32[]{:S(2)}, u32[]{:S(2)}) %collective-permute-start.10) | collective-permute-done | bytes 5504 | tf_op jit(solution)/shard_map/ppermute | solution.py:23
  90.7 0.5 collective-permute-start.12
  91.3 0.8 collective-permute-done.13
  92.0 2.9 %collective-permute-done.12 = f32[2,2,4,3]{3,2,1,0:T(4,128)S(1)} collective-permute-done((f32[2,2,4,3]{3,2,1,0:T(4,128)S(1)}, f32[2,2,4,3]{3,2,1,0:T(4,128)S(1)}, u32[]{:S(2)}, u32[]{:S(2)}) %collective-permute-start.12) | collective-permute-done | bytes 224 | tf_op jit(solution)/shard_map/ppermute | solution.py:23
  95.1 2.0 %collective-permute-start.14 = (f32[2,2,3,38]{3,2,1,0:T(4,128)S(1)}, f32[2,2,3,38]{3,2,1,0:T(4,128)S(1)}, u32[]{:S(2)}, u32[]{:S(2)}) collective-permute-start(f32[2,2,3,38]{3,2,1,0:T(4,128)S(1)} %get-tuple-element.185), channel_id=1, source_target_pairs={{0,1},{1,2},{2,3},{3,4},{4,5},{5,6},{6,7},{7,8},{8,9},{9,10},{10,1... | collective-permute-start | bytes 5480 | tf_op jit(solution)/shard_map/ppermute | solution.py:23
  97.2 1.6 %collective-permute-done.15 = f32[2,2,3,38]{3,2,1,0:T(4,128)S(1)} collective-permute-done((f32[2,2,3,38]{3,2,1,0:T(4,128)S(1)}, f32[2,2,3,38]{3,2,1,0:T(4,128)S(1)}, u32[]{:S(2)}, u32[]{:S(2)}) %collective-permute-start.15) | collective-permute-done | bytes 1856 | tf_op jit(solution)/shard_map/ppermute | solution.py:25
  98.8 3.4 %collective-permute-done.14 = f32[2,2,3,38]{3,2,1,0:T(4,128)S(1)} collective-permute-done((f32[2,2,3,38]{3,2,1,0:T(4,128)S(1)}, f32[2,2,3,38]{3,2,1,0:T(4,128)S(1)}, u32[]{:S(2)}, u32[]{:S(2)}) %collective-permute-start.14) | collective-permute-done | bytes 1856 | tf_op jit(solution)/shard_map/ppermute | solution.py:23
  103.6 0.5 collective-permute-start.16
  104.1 1.1 collective-permute-done.17
  105.2 3.0 %collective-permute-done.16 = f32[2,4,8,5]{3,2,1,0:T(8,128)S(1)} collective-permute-done((f32[2,4,8,5]{3,2,1,0:T(8,128)S(1)}, f32[2,4,8,5]{3,2,1,0:T(8,128)S(1)}, u32[]{:S(2)}, u32[]{:S(2)}) %collective-permute-start.16) | collective-permute-done | bytes 1312 | tf_op jit(solution)/shard_map/ppermute | solution.py:23
  108.3 2.0 %collective-permute-start.18 = (f32[2,4,5,74]{3,2,1,0:T(8,128)S(1)}, f32[2,4,5,74]{3,2,1,0:T(8,128)S(1)}, u32[]{:S(2)}, u32[]{:S(2)}) collective-permute-start(f32[2,4,5,74]{3,2,1,0:T(8,128)S(1)} %get-tuple-element.149), channel_id=1, source_target_pairs={{0,1},{1,2},{2,3},{3,4},{4,5},{5,6},{6,7},{7,8},{8,9},{9,10},{10,1... | collective-permute-start | bytes 35528 | tf_op jit(solution)/shard_map/ppermute | solution.py:23
  110.3 1.9 %collective-permute-done.19 = f32[2,4,5,74]{3,2,1,0:T(8,128)S(1)} collective-permute-done((f32[2,4,5,74]{3,2,1,0:T(8,128)S(1)}, f32[2,4,5,74]{3,2,1,0:T(8,128)S(1)}, u32[]{:S(2)}, u32[]{:S(2)}) %collective-permute-start.19) | collective-permute-done | bytes 11872 | tf_op jit(solution)/shard_map/ppermute | solution.py:25
  112.2 3.6 %collective-permute-done.18 = f32[2,4,5,74]{3,2,1,0:T(8,128)S(1)} collective-permute-done((f32[2,4,5,74]{3,2,1,0:T(8,128)S(1)}, f32[2,4,5,74]{3,2,1,0:T(8,128)S(1)}, u32[]{:S(2)}, u32[]{:S(2)}) %collective-permute-start.18) | collective-permute-done | bytes 11872 | tf_op jit(solution)/shard_map/ppermute | solution.py:23
  118.2 0.7 copy.42
  119.7 0.6 slice_add_fusion.7
  121.1 0.7 slice_add_fusion.4
  122.2 0.9 fusion.71
  (160 shorter events, 14.5 us)
Async XLA Ops:
  0.0 1.8 %copy-start.1 = (f32[8,16,128]{2,1,0:T(8,128)S(1)}, f32[8,16,128]{2,1,0:T(8,128)}, u32[]{:S(2)}) copy-start(f32[8,16,128]{2,1,0:T(8,128)} %param.25) | copy-start | bytes 196612
  0.0 1.8 %copy-start.2 = (f32[8,16,128]{2,1,0:T(8,128)S(1)}, f32[8,16,128]{2,1,0:T(8,128)}, u32[]{:S(2)}) copy-start(f32[8,16,128]{2,1,0:T(8,128)} %param.24) | copy-start | bytes 196612
  0.0 1.8 %copy-start = (f32[2,8,16,128]{3,2,1,0:T(8,128)S(1)}, f32[2,8,16,128]{3,2,1,0:T(8,128)}, u32[]{:S(2)}) copy-start(f32[2,8,16,128]{3,2,1,0:T(8,128)} %param.22) | copy-start | bytes 393220
  1.3 35.9 %collective-permute-start.1 = (f32[6,8,16,6]{3,2,1,0:T(8,128)S(1)}, f32[6,8,16,6]{3,2,1,0:T(8,128)S(1)}, u32[]{:S(2)}, u32[]{:S(2)}) collective-permute-start(f32[6,8,16,6]{3,2,1,0:T(8,128)S(1)} %get-tuple-element.88), channel_id=1, source_target_pairs={{32,0},{64,32},{96,64},{128,96},{160,128},{192,160},{224,192},{0,2... | collective-permute-start | bytes 55304 | tf_op jit(solution)/shard_map/ppermute | solution.py:25
  1.8 35.4 %collective-permute-start = (f32[6,8,16,6]{3,2,1,0:T(8,128)S(1)}, f32[6,8,16,6]{3,2,1,0:T(8,128)S(1)}, u32[]{:S(2)}, u32[]{:S(2)}) collective-permute-start(f32[6,8,16,6]{3,2,1,0:T(8,128)S(1)} %get-tuple-element.87), channel_id=1, source_target_pairs={{0,32},{32,64},{64,96},{96,128},{128,160},{160,192},{192,224},{224... | collective-permute-start | bytes 55304 | tf_op jit(solution)/shard_map/ppermute | solution.py:23
  4.3 32.9 %copy-start.3 = (f32[2,8,16,128]{3,2,1,0:T(8,128)S(1)}, f32[2,8,16,128]{3,2,1,0:T(8,128)}, u32[]{:S(2)}) copy-start(f32[2,8,16,128]{3,2,1,0:T(8,128)} %param.23) | copy-start | bytes 393220
  37.6 12.2 %collective-permute-start.3 = (f32[6,8,6,140]{3,2,1,0:T(8,128)S(1)}, f32[6,8,6,140]{3,2,1,0:T(8,128)S(1)}, u32[]{:S(2)}, u32[]{:S(2)}) collective-permute-start(f32[6,8,6,140]{3,2,1,0:T(8,128)S(1)} %get-tuple-element.50), channel_id=1, source_target_pairs={{1,0},{2,1},{3,2},{4,3},{5,4},{6,5},{7,6},{8,7},{9,8},{10,9},{11,1... | collective-permute-start | bytes 483848 | tf_op jit(solution)/shard_map/ppermute | solution.py:25
  42.4 13.0 %collective-permute-start.2 = (f32[6,8,6,140]{3,2,1,0:T(8,128)S(1)}, f32[6,8,6,140]{3,2,1,0:T(8,128)S(1)}, u32[]{:S(2)}, u32[]{:S(2)}) collective-permute-start(f32[6,8,6,140]{3,2,1,0:T(8,128)S(1)} %get-tuple-element.49), channel_id=1, source_target_pairs={{0,1},{1,2},{2,3},{3,4},{4,5},{5,6},{6,7},{7,8},{8,9},{9,10},{10,1... | collective-permute-start | bytes 483848 | tf_op jit(solution)/shard_map/ppermute | solution.py:23
  56.5 0.7 copy-start.4
  62.0 14.4 %copy-start.5 = (f32[2]{0:T(128)S(1)}, f32[2]{0:T(128)}, u32[]{:S(2)}) copy-start(f32[2]{0:T(128)} %constant.335.clone) | copy-start | bytes 28
  62.1 2.2 %collective-permute-start.5 = (f32[6,4,8,5]{3,2,1,0:T(8,128)S(1)}, f32[6,4,8,5]{3,2,1,0:T(8,128)S(1)}, u32[]{:S(2)}, u32[]{:S(2)}) collective-permute-start(f32[6,4,8,5]{3,2,1,0:T(8,128)S(1)} %get-tuple-element.118), channel_id=1, source_target_pairs={{32,0},{64,32},{96,64},{128,96},{160,128},{192,160},{224,192},{0,2... | collective-permute-start | bytes 11528 | tf_op jit(solution)/shard_map/ppermute | solution.py:25
  62.1 5.3 %collective-permute-start.4 = (f32[6,4,8,5]{3,2,1,0:T(8,128)S(1)}, f32[6,4,8,5]{3,2,1,0:T(8,128)S(1)}, u32[]{:S(2)}, u32[]{:S(2)}) collective-permute-start(f32[6,4,8,5]{3,2,1,0:T(8,128)S(1)} %get-tuple-element.117), channel_id=1, source_target_pairs={{0,32},{32,64},{64,96},{96,128},{128,160},{160,192},{192,224},{224... | collective-permute-start | bytes 11528 | tf_op jit(solution)/shard_map/ppermute | solution.py:23
  67.5 4.7 %collective-permute-start.7 = (f32[6,4,5,74]{3,2,1,0:T(8,128)S(1)}, f32[6,4,5,74]{3,2,1,0:T(8,128)S(1)}, u32[]{:S(2)}, u32[]{:S(2)}) collective-permute-start(f32[6,4,5,74]{3,2,1,0:T(8,128)S(1)} %get-tuple-element.116), channel_id=1, source_target_pairs={{1,0},{2,1},{3,2},{4,3},{5,4},{6,5},{7,6},{8,7},{9,8},{10,9},{11,1... | collective-permute-start | bytes 106568 | tf_op jit(solution)/shard_map/ppermute | solution.py:25
  67.9 7.9 %collective-permute-start.6 = (f32[6,4,5,74]{3,2,1,0:T(8,128)S(1)}, f32[6,4,5,74]{3,2,1,0:T(8,128)S(1)}, u32[]{:S(2)}, u32[]{:S(2)}) collective-permute-start(f32[6,4,5,74]{3,2,1,0:T(8,128)S(1)} %get-tuple-element.115), channel_id=1, source_target_pairs={{0,1},{1,2},{2,3},{3,4},{4,5},{5,6},{6,7},{7,8},{8,9},{9,10},{10,1... | collective-permute-start | bytes 106568 | tf_op jit(solution)/shard_map/ppermute | solution.py:23
  76.6 13.6 %copy-start.6 = (f32[2]{0:T(128)S(1)}, f32[2]{0:T(128)}, u32[]{:S(2)}) copy-start(f32[2]{0:T(128)} %constant.336.clone) | copy-start | bytes 28
  78.0 1.5 %collective-permute-start.9 = (f32[6,2,4,3]{3,2,1,0:T(4,128)S(1)}, f32[6,2,4,3]{3,2,1,0:T(4,128)S(1)}, u32[]{:S(2)}, u32[]{:S(2)}) collective-permute-start(f32[6,2,4,3]{3,2,1,0:T(4,128)S(1)} %get-tuple-element.164), channel_id=1, source_target_pairs={{32,0},{64,32},{96,64},{128,96},{160,128},{192,160},{224,192},{0,2... | collective-permute-start | bytes 1736 | tf_op jit(solution)/shard_map/ppermute | solution.py:25
  78.0 4.5 %collective-permute-start.8 = (f32[6,2,4,3]{3,2,1,0:T(4,128)S(1)}, f32[6,2,4,3]{3,2,1,0:T(4,128)S(1)}, u32[]{:S(2)}, u32[]{:S(2)}) collective-permute-start(f32[6,2,4,3]{3,2,1,0:T(4,128)S(1)} %get-tuple-element.163), channel_id=1, source_target_pairs={{0,32},{32,64},{64,96},{96,128},{128,160},{160,192},{192,224},{224... | collective-permute-start | bytes 1736 | tf_op jit(solution)/shard_map/ppermute | solution.py:23
  82.6 3.9 %collective-permute-start.11 = (f32[6,2,3,38]{3,2,1,0:T(4,128)S(1)}, f32[6,2,3,38]{3,2,1,0:T(4,128)S(1)}, u32[]{:S(2)}, u32[]{:S(2)}) collective-permute-start(f32[6,2,3,38]{3,2,1,0:T(4,128)S(1)} %get-tuple-element.162), channel_id=1, source_target_pairs={{1,0},{2,1},{3,2},{4,3},{5,4},{6,5},{7,6},{8,7},{9,8},{10,9},{11,1... | collective-permute-start | bytes 16424 | tf_op jit(solution)/shard_map/ppermute | solution.py:25
  82.7 7.2 %collective-permute-start.10 = (f32[6,2,3,38]{3,2,1,0:T(4,128)S(1)}, f32[6,2,3,38]{3,2,1,0:T(4,128)S(1)}, u32[]{:S(2)}, u32[]{:S(2)}) collective-permute-start(f32[6,2,3,38]{3,2,1,0:T(4,128)S(1)} %get-tuple-element.161), channel_id=1, source_target_pairs={{0,1},{1,2},{2,3},{3,4},{4,5},{5,6},{6,7},{7,8},{8,9},{9,10},{10,1... | collective-permute-start | bytes 16424 | tf_op jit(solution)/shard_map/ppermute | solution.py:23
  90.7 1.4 %collective-permute-start.13 = (f32[2,2,4,3]{3,2,1,0:T(4,128)S(1)}, f32[2,2,4,3]{3,2,1,0:T(4,128)S(1)}, u32[]{:S(2)}, u32[]{:S(2)}) collective-permute-start(f32[2,2,4,3]{3,2,1,0:T(4,128)S(1)} %get-tuple-element.177), channel_id=1, source_target_pairs={{32,0},{64,32},{96,64},{128,96},{160,128},{192,160},{224,192},{0,2... | collective-permute-start | bytes 584 | tf_op jit(solution)/shard_map/ppermute | solution.py:25
  90.7 4.3 %collective-permute-start.12 = (f32[2,2,4,3]{3,2,1,0:T(4,128)S(1)}, f32[2,2,4,3]{3,2,1,0:T(4,128)S(1)}, u32[]{:S(2)}, u32[]{:S(2)}) collective-permute-start(f32[2,2,4,3]{3,2,1,0:T(4,128)S(1)} %get-tuple-element.176), channel_id=1, source_target_pairs={{0,32},{32,64},{64,96},{96,128},{128,160},{160,192},{192,224},{224... | collective-permute-start | bytes 584 | tf_op jit(solution)/shard_map/ppermute | solution.py:23
  95.1 3.7 %collective-permute-start.15 = (f32[2,2,3,38]{3,2,1,0:T(4,128)S(1)}, f32[2,2,3,38]{3,2,1,0:T(4,128)S(1)}, u32[]{:S(2)}, u32[]{:S(2)}) collective-permute-start(f32[2,2,3,38]{3,2,1,0:T(4,128)S(1)} %get-tuple-element.186), channel_id=1, source_target_pairs={{1,0},{2,1},{3,2},{4,3},{5,4},{6,5},{7,6},{8,7},{9,8},{10,9},{11,1... | collective-permute-start | bytes 5480 | tf_op jit(solution)/shard_map/ppermute | solution.py:25
  95.1 7.0 %collective-permute-start.14 = (f32[2,2,3,38]{3,2,1,0:T(4,128)S(1)}, f32[2,2,3,38]{3,2,1,0:T(4,128)S(1)}, u32[]{:S(2)}, u32[]{:S(2)}) collective-permute-start(f32[2,2,3,38]{3,2,1,0:T(4,128)S(1)} %get-tuple-element.185), channel_id=1, source_target_pairs={{0,1},{1,2},{2,3},{3,4},{4,5},{5,6},{6,7},{7,8},{8,9},{9,10},{10,1... | collective-permute-start | bytes 5480 | tf_op jit(solution)/shard_map/ppermute | solution.py:23
  103.6 1.6 %collective-permute-start.17 = (f32[2,4,8,5]{3,2,1,0:T(8,128)S(1)}, f32[2,4,8,5]{3,2,1,0:T(8,128)S(1)}, u32[]{:S(2)}, u32[]{:S(2)}) collective-permute-start(f32[2,4,8,5]{3,2,1,0:T(8,128)S(1)} %get-tuple-element.152), channel_id=1, source_target_pairs={{32,0},{64,32},{96,64},{128,96},{160,128},{192,160},{224,192},{0,2... | collective-permute-start | bytes 3848 | tf_op jit(solution)/shard_map/ppermute | solution.py:25
  103.6 4.6 %collective-permute-start.16 = (f32[2,4,8,5]{3,2,1,0:T(8,128)S(1)}, f32[2,4,8,5]{3,2,1,0:T(8,128)S(1)}, u32[]{:S(2)}, u32[]{:S(2)}) collective-permute-start(f32[2,4,8,5]{3,2,1,0:T(8,128)S(1)} %get-tuple-element.151), channel_id=1, source_target_pairs={{0,32},{32,64},{64,96},{96,128},{128,160},{160,192},{192,224},{224... | collective-permute-start | bytes 3848 | tf_op jit(solution)/shard_map/ppermute | solution.py:23
  108.2 4.0 %collective-permute-start.19 = (f32[2,4,5,74]{3,2,1,0:T(8,128)S(1)}, f32[2,4,5,74]{3,2,1,0:T(8,128)S(1)}, u32[]{:S(2)}, u32[]{:S(2)}) collective-permute-start(f32[2,4,5,74]{3,2,1,0:T(8,128)S(1)} %get-tuple-element.150), channel_id=1, source_target_pairs={{1,0},{2,1},{3,2},{4,3},{5,4},{6,5},{7,6},{8,7},{9,8},{10,9},{11,1... | collective-permute-start | bytes 35528 | tf_op jit(solution)/shard_map/ppermute | solution.py:25
  108.3 7.5 %collective-permute-start.18 = (f32[2,4,5,74]{3,2,1,0:T(8,128)S(1)}, f32[2,4,5,74]{3,2,1,0:T(8,128)S(1)}, u32[]{:S(2)}, u32[]{:S(2)}) collective-permute-start(f32[2,4,5,74]{3,2,1,0:T(8,128)S(1)} %get-tuple-element.149), channel_id=1, source_target_pairs={{0,1},{1,2},{2,3},{3,4},{4,5},{5,6},{6,7},{7,8},{8,9},{9,10},{10,1... | collective-permute-start | bytes 35528 | tf_op jit(solution)/shard_map/ppermute | solution.py:23

commit v5 on v4

--- a/solution.py
+++ b/solution.py
@@ -16,16 +16,17 @@
     for axis, dim in (("gx", 3), ("gy", 2)):
         count = lax.axis_size(axis)
         size = cells.shape[dim]
-        head = lax.slice_in_dim(cells, 0, width, axis=dim)
-        tail = lax.slice_in_dim(cells, size - width, size, axis=dim)
-        cells = jnp.concatenate(
-            [
-                lax.ppermute(tail, axis, [(i, (i + 1) % count) for i in range(count)]),
-                cells,
-                lax.ppermute(head, axis, [((i + 1) % count, i) for i in range(count)]),
-            ],
-            axis=dim,
-        )
+        below, above = [], []
+        remaining, distance = width, 1
+        while remaining > 0:
+            take = min(remaining, size)
+            tail = lax.slice_in_dim(cells, size - take, size, axis=dim)
+            head = lax.slice_in_dim(cells, 0, take, axis=dim)
+            below.insert(0, lax.ppermute(tail, axis, [(i, (i + distance) % count) for i in range(count)]))
+            above.append(lax.ppermute(head, axis, [((i + distance) % count, i) for i in range(count)]))
+            remaining -= take
+            distance += 1
+        cells = jnp.concatenate(below + [cells] + above, axis=dim)
     return cells
 
 
@@ -232,21 +233,20 @@
     pre_0, pre_0_halo = chebyshev(ops_0, source_0, 5, None, None, spreads[0])
     resid_0 = crop(source_0, 5, 0) - ops_0.operate(crop(pre_0, pre_0_halo, 1), 1)
 
-    wide_1 = padded(jnp.concatenate([restrict(resid_0), fields_1], 0), 5)
-    ops_1 = Level(coefficients(wide_1[2:], 1)[0], 5, 1)
+    wide_1 = padded(jnp.concatenate([restrict(resid_0), fields_1], 0), 7)
+    ops_1 = Level(coefficients(wide_1[2:], 1)[0], 7, 1)
     source_1 = wide_1[:2]
-    pre_1, pre_1_halo = chebyshev(ops_1, source_1, 5, None, None, spreads[1])
-    resid_1 = crop(source_1, 5, 0) - ops_1.operate(crop(pre_1, pre_1_halo, 1), 1)
-
-    wide_2 = padded(jnp.concatenate([restrict(resid_1), fields_2], 0), deep)
-    ops_2 = Level(coefficients(wide_2[2:], 2)[0], deep, 2)
+    pre_1, pre_1_halo = chebyshev(ops_1, source_1, 7, None, None, spreads[1])
+    resid_1 = crop(source_1, 7, 0) - ops_1.operate(crop(pre_1, pre_1_halo, 1), 1)
+
+    wide_2 = padded(jnp.concatenate([restrict(resid_1), fields_2], 0), 8)
+    ops_2 = Level(coefficients(wide_2[2:], 2)[0], 8, 2)
     source_2 = wide_2[:2]
-    first_2, first_2_halo = chebyshev(ops_2, source_2, deep, None, None, spreads[2])
-    start_2 = padded(crop(first_2, first_2_halo, 0), deep)
-    coarse_2, coarse_2_halo = chebyshev(ops_2, source_2, deep, start_2, deep, spreads[2])
-
-    start_1 = padded(crop(pre_1, pre_1_halo, 0) + prolong(crop(coarse_2, coarse_2_halo, 0)), 5)
-    post_1, post_1_halo = chebyshev(ops_1, source_1, 5, start_1, 5, spreads[1])
+    first_2, first_2_halo = chebyshev(ops_2, source_2, 8, None, None, spreads[2])
+    coarse_2, coarse_2_halo = chebyshev(ops_2, source_2, 8, first_2, first_2_halo, spreads[2])
+
+    start_1 = crop(pre_1, pre_1_halo, 5) + crop(prolong(coarse_2), 2 * coarse_2_halo, 5)
+    post_1, post_1_halo = chebyshev(ops_1, source_1, 7, start_1, 5, spreads[1])
 
     start_0 = crop(pre_0, pre_0_halo, 3) + crop(prolong(post_1), 2 * post_1_halo, 3)
     post_0, post_0_halo = chebyshev(ops_0, source_0, 5, start_0, 3, spreads[0])

time: 123 us -> 103 us (0.84)
  waiting for transfers between devices: 48.7 us -> 27.1 us
    ppermute x20 -> x14, waiting for transfers between devices: 48.7 us -> 27.1 us  [the longest x7 15.1 us: padded(): lax.ppermute(tail, axis, [(i, (i + distance) % count) for i in range(coun...]
    ppermute x20 -> x14, starting transfers between devices: 15.7 us -> 16.7 us  [the longest x7 13.7 us: padded(): lax.ppermute(head, axis, [((i + distance) % count, i) for i in range(coun...]
    add x16 -> x17, other arithmetic: 2.93 us -> 3.13 us  [operate(): first = coeff[0] * centre[0] + coeff[1] * centre[1]]
  transfers between devices with their start and end apart: 20 -> 14, of which waited for: 18 -> 9; matrix products, arithmetic and copies ran while one was open for 6% -> 7% of each run, Pallas kernels for 20% -> 24%
where the time goes in v5:
time: 103 us
  waiting for transfers between devices  27.1 us (26%)
  Pallas kernels  24.6 us (24%)
  other arithmetic  18.2 us (18%)
  starting transfers between devices  16.7 us (16%)
  between operations  7.35 us (7%)
  local copies, waits for them, and re-layouts  6.83 us (7%)
  matrix products  2.05 us (2%)
    pallas_call x2, Pallas kernels, gather_axis(): pl.pallas_call(lambda *refs: gather_kernel(axis, *refs), out_shape=jax.Sh...  24.6 us
    ppermute x7, waiting for transfers between devices, padded(): lax.ppermute(tail, axis, [(i, (i + distance) % count) for i in range(coun...  15.1 us
    ppermute x7, starting transfers between devices, padded(): lax.ppermute(head, axis, [((i + distance) % count, i) for i in range(coun...  13.7 us
    ppermute x7, waiting for transfers between devices, padded(): lax.ppermute(head, axis, [((i + distance) % count, i) for i in range(coun...  12 us
    add x12, other arithmetic, chebyshev(): iterate = crop(iterate, halo + 1, halo) + update  4.34 us
    slice x31, local copies, waits for them, and re-layouts, shrunk_neighbours(): along_z = jnp.roll(centre, 1, 1) + jnp.roll(centre, -1, 1)  3.55 us
    add x17, other arithmetic, operate(): first = coeff[0] * centre[0] + coeff[1] * centre[1]  3.13 us
    ppermute x7, starting transfers between devices, padded(): lax.ppermute(tail, axis, [(i, (i + distance) % count) for i in range(coun...  2.95 us
  transfers between devices with their start and end apart: 14, of which 9 were waited for; matrix products, arithmetic and copies ran while one was open for 7% of the time, Pallas kernels for 24%

profile of v5, /device:TPU:0, one launch (start us, length us, event | category | flops | bytes accessed | tf_op | source)
XLA Modules:
  0.0 102.9 jit_solution(662023785750963689)
XLA Ops:
  0.0 1.1 %pad_maximum_fusion.2 = f32[6,8,16,128]{3,2,1,0:T(8,128)S(1)} fusion(f32[2,8,16,128]{3,2,1,0:T(8,128)} %param.23, f32[1,8,16,128]{3,2,1,0:T(8,128)} %bitcast.64, f32[1,8,16,128]{3,2,1,0:T(8,128)} %bitcast.68, f32[2,8,16,128]{3,2,1,0:T(8,128)} %param.22), kind=kLoop, calls=%fused_computation.66 | loop fusion | flops 294912 | bytes 786432 | tf_op jit(solution)/shard_map/concatenate | solution.py:218
  1.3 0.5 collective-permute-start.1
  1.8 0.7 fusion.143
  4.1 0.4 fusion.141
  4.5 0.3 convolution_multiply_fusion.1
  4.8 0.8 fusion.227
  6.0 0.7 fusion.327
  9.2 0.6 select_select_fusion.8.refs_0_
  9.8 7.5 %shard_map.208 = f32[8,8,128]{2,1,0:T(8,128)} custom-call(f32[8,128]{1,0:T(8,128)} %select_select_fusion.8.refs_0_), custom_call_target="tpu_custom_call" | custom-call | tf_op jit(solution)/shard_map/pallas_call | solution.py:96
  17.3 1.4 %reduce_max.78.refs_0_ = f32[8,128]{1,0:T(8,128)} reduce(f32[8,8,128]{2,1,0:T(8,128)} %shard_map.208, f32[]{:T(128)} %constant.326.clone.1), dimensions={0}, to_apply=%region_6.7 | reduce | flops 7168 | bytes 36868 | tf_op jit(solution)/shard_map/reduce_max | solution.py:113
  18.7 17.1 %shard_map.209 = f32[32,8,128]{2,1,0:T(8,128)} custom-call(f32[8,128]{1,0:T(8,128)} %reduce_max.78.refs_0_), custom_call_target="tpu_custom_call" | custom-call | tf_op jit(solution)/shard_map/pallas_call | solution.py:96
  35.8 0.9 reduce_max.79
  36.8 0.6 fusion.413
  37.4 0.4 pad_maximum_fusion.1
  37.9 4.7 %collective-permute-start.3 = (f32[6,8,6,140]{3,2,1,0:T(8,128)S(1)}, f32[6,8,6,140]{3,2,1,0:T(8,128)S(1)}, u32[]{:S(2)}, u32[]{:S(2)}) collective-permute-start(f32[6,8,6,140]{3,2,1,0:T(8,128)S(1)} %get-tuple-element.50), channel_id=1, source_target_pairs={{1,0},{2,1},{3,2},{4,3},{5,4},{6,5},{7,6},{8,7},{9,8},{10,9},{11,1... | collective-permute-start | bytes 483848 | tf_op jit(solution)/shard_map/ppermute | solution.py:26
  43.6 6.5 %collective-permute-done.3 = f32[6,8,6,140]{3,2,1,0:T(8,128)S(1)} collective-permute-done((f32[6,8,6,140]{3,2,1,0:T(8,128)S(1)}, f32[6,8,6,140]{3,2,1,0:T(8,128)S(1)}, u32[]{:S(2)}, u32[]{:S(2)}) %collective-permute-start.3) | collective-permute-done | bytes 161312 | tf_op jit(solution)/shard_map/ppermute | solution.py:26
  50.1 5.5 %collective-permute-done.2 = f32[6,8,6,140]{3,2,1,0:T(8,128)S(1)} collective-permute-done((f32[6,8,6,140]{3,2,1,0:T(8,128)S(1)}, f32[6,8,6,140]{3,2,1,0:T(8,128)S(1)}, u32[]{:S(2)}, u32[]{:S(2)}) %collective-permute-start.2) | collective-permute-done | bytes 161312 | tf_op jit(solution)/shard_map/ppermute | solution.py:25
  55.6 0.6 pad_maximum_fusion
  56.2 0.4 fusion.48
  56.8 0.3 fusion.380
  57.1 0.4 subtract_bitcast_fusion
  57.4 0.8 fusion.8
  58.6 0.4 fusion.63
  59.0 0.6 slice_add_fusion.12
  59.6 0.4 fusion.61
  60.3 0.7 fusion.29
  61.7 0.3 fusion.140
  62.3 0.5 collective-permute-start.4
  62.8 1.7 %collective-permute-done.5 = f32[6,4,8,7]{3,2,1,0:T(8,128)S(1)} collective-permute-done((f32[6,4,8,7]{3,2,1,0:T(8,128)S(1)}, f32[6,4,8,7]{3,2,1,0:T(8,128)S(1)}, u32[]{:S(2)}, u32[]{:S(2)}) %collective-permute-start.5) | collective-permute-done | bytes 5408 | tf_op jit(solution)/shard_map/ppermute | solution.py:26
  64.5 3.1 %collective-permute-done.4 = f32[6,4,8,7]{3,2,1,0:T(8,128)S(1)} collective-permute-done((f32[6,4,8,7]{3,2,1,0:T(8,128)S(1)}, f32[6,4,8,7]{3,2,1,0:T(8,128)S(1)}, u32[]{:S(2)}, u32[]{:S(2)}) %collective-permute-start.4) | collective-permute-done | bytes 5408 | tf_op jit(solution)/shard_map/ppermute | solution.py:25
  67.7 0.4 collective-permute-start.7
  68.1 1.7 %collective-permute-start.6 = (f32[6,4,7,78]{3,2,1,0:T(8,128)S(1)}, f32[6,4,7,78]{3,2,1,0:T(8,128)S(1)}, u32[]{:S(2)}, u32[]{:S(2)}) collective-permute-start(f32[6,4,7,78]{3,2,1,0:T(8,128)S(1)} %get-tuple-element.127), channel_id=1, source_target_pairs={{0,1},{1,2},{2,3},{3,4},{4,5},{5,6},{6,7},{7,8},{8,9},{9,10},{10,1... | collective-permute-start | bytes 157256 | tf_op jit(solution)/shard_map/ppermute | solution.py:25
  70.7 1.7 %collective-permute-done.7 = f32[6,4,7,78]{3,2,1,0:T(8,128)S(1)} collective-permute-done((f32[6,4,7,78]{3,2,1,0:T(8,128)S(1)}, f32[6,4,7,78]{3,2,1,0:T(8,128)S(1)}, u32[]{:S(2)}, u32[]{:S(2)}) %collective-permute-start.7) | collective-permute-done | bytes 52448 | tf_op jit(solution)/shard_map/ppermute | solution.py:26
  72.4 3.6 %collective-permute-done.6 = f32[6,4,7,78]{3,2,1,0:T(8,128)S(1)} collective-permute-done((f32[6,4,7,78]{3,2,1,0:T(8,128)S(1)}, f32[6,4,7,78]{3,2,1,0:T(8,128)S(1)}, u32[]{:S(2)}, u32[]{:S(2)}) %collective-permute-start.6) | collective-permute-done | bytes 52448 | tf_op jit(solution)/shard_map/ppermute | solution.py:25
  78.3 0.5 collective-permute-start.8
  78.8 1.0 collective-permute-done.9
  79.9 3.0 %collective-permute-done.8 = f32[6,2,4,8]{3,2,1,0:T(4,128)S(1)} collective-permute-done((f32[6,2,4,8]{3,2,1,0:T(4,128)S(1)}, f32[6,2,4,8]{3,2,1,0:T(4,128)S(1)}, u32[]{:S(2)}, u32[]{:S(2)}) %collective-permute-start.8) | collective-permute-done | bytes 1568 | tf_op jit(solution)/shard_map/ppermute | solution.py:25
  83.1 5.3 %collective-permute-start.12 = (f32[6,2,4,48]{3,2,1,0:T(4,128)S(1)}, f32[6,2,4,48]{3,2,1,0:T(4,128)S(1)}, u32[]{:S(2)}, u32[]{:S(2)}) collective-permute-start(f32[6,2,4,48]{3,2,1,0:T(4,128)S(1)} %pad_maximum_fusion.13), channel_id=1, source_target_pairs={{1,0},{2,1},{3,2},{4,3},{5,4},{6,5},{7,6},{8,7},{9,8},{10,9},{11,1... | collective-permute-start | bytes 27656 | tf_op jit(solution)/shard_map/ppermute | solution.py:26
  88.4 2.8 %collective-permute-start.13 = (f32[6,2,4,48]{3,2,1,0:T(4,128)S(1)}, f32[6,2,4,48]{3,2,1,0:T(4,128)S(1)}, u32[]{:S(2)}, u32[]{:S(2)}) collective-permute-start(f32[6,2,4,48]{3,2,1,0:T(4,128)S(1)} %pad_maximum_fusion.13), channel_id=1, source_target_pairs={{2,0},{3,1},{4,2},{5,3},{6,4},{7,5},{8,6},{9,7},{10,8},{11,9},{12,... | collective-permute-start | bytes 27656 | tf_op jit(solution)/shard_map/ppermute | solution.py:26
  92.2 1.1 %collective-permute-done.13 = f32[6,2,4,48]{3,2,1,0:T(4,128)S(1)} collective-permute-done((f32[6,2,4,48]{3,2,1,0:T(4,128)S(1)}, f32[6,2,4,48]{3,2,1,0:T(4,128)S(1)}, u32[]{:S(2)}, u32[]{:S(2)}) %collective-permute-start.13) | collective-permute-done | bytes 9248 | tf_op jit(solution)/shard_map/ppermute | solution.py:26
  97.3 0.3 copy.43
  97.6 0.3 slice.2061
  98.0 0.7 copy.46
  98.7 0.4 fusion.59
  99.5 0.6 slice_add_fusion.7
  100.1 0.4 fusion.57
  100.8 0.7 slice_add_fusion.4
  101.9 0.9 fusion.71
  (140 shorter events, 10.3 us)
Async XLA Ops:
  0.0 1.8 %copy-start.1 = (f32[8,16,128]{2,1,0:T(8,128)S(1)}, f32[8,16,128]{2,1,0:T(8,128)}, u32[]{:S(2)}) copy-start(f32[8,16,128]{2,1,0:T(8,128)} %param.25) | copy-start | bytes 196612
  0.0 1.8 %copy-start.2 = (f32[8,16,128]{2,1,0:T(8,128)S(1)}, f32[8,16,128]{2,1,0:T(8,128)}, u32[]{:S(2)}) copy-start(f32[8,16,128]{2,1,0:T(8,128)} %param.24) | copy-start | bytes 196612
  0.0 1.8 %copy-start = (f32[2,8,16,128]{3,2,1,0:T(8,128)S(1)}, f32[2,8,16,128]{3,2,1,0:T(8,128)}, u32[]{:S(2)}) copy-start(f32[2,8,16,128]{3,2,1,0:T(8,128)} %param.22) | copy-start | bytes 393220
  1.3 36.1 %collective-permute-start.1 = (f32[6,8,16,6]{3,2,1,0:T(8,128)S(1)}, f32[6,8,16,6]{3,2,1,0:T(8,128)S(1)}, u32[]{:S(2)}, u32[]{:S(2)}) collective-permute-start(f32[6,8,16,6]{3,2,1,0:T(8,128)S(1)} %get-tuple-element.88), channel_id=1, source_target_pairs={{32,0},{64,32},{96,64},{128,96},{160,128},{192,160},{224,192},{0,2... | collective-permute-start | bytes 55304 | tf_op jit(solution)/shard_map/ppermute | solution.py:26
  1.8 35.7 %collective-permute-start = (f32[6,8,16,6]{3,2,1,0:T(8,128)S(1)}, f32[6,8,16,6]{3,2,1,0:T(8,128)S(1)}, u32[]{:S(2)}, u32[]{:S(2)}) collective-permute-start(f32[6,8,16,6]{3,2,1,0:T(8,128)S(1)} %get-tuple-element.87), channel_id=1, source_target_pairs={{0,32},{32,64},{64,96},{96,128},{128,160},{160,192},{192,224},{224... | collective-permute-start | bytes 55304 | tf_op jit(solution)/shard_map/ppermute | solution.py:25
  4.5 33.0 %copy-start.3 = (f32[2,8,16,128]{3,2,1,0:T(8,128)S(1)}, f32[2,8,16,128]{3,2,1,0:T(8,128)}, u32[]{:S(2)}) copy-start(f32[2,8,16,128]{3,2,1,0:T(8,128)} %param.23) | copy-start | bytes 393220
  37.9 12.2 %collective-permute-start.3 = (f32[6,8,6,140]{3,2,1,0:T(8,128)S(1)}, f32[6,8,6,140]{3,2,1,0:T(8,128)S(1)}, u32[]{:S(2)}, u32[]{:S(2)}) collective-permute-start(f32[6,8,6,140]{3,2,1,0:T(8,128)S(1)} %get-tuple-element.50), channel_id=1, source_target_pairs={{1,0},{2,1},{3,2},{4,3},{5,4},{6,5},{7,6},{8,7},{9,8},{10,9},{11,1... | collective-permute-start | bytes 483848 | tf_op jit(solution)/shard_map/ppermute | solution.py:26
  42.6 13.0 %collective-permute-start.2 = (f32[6,8,6,140]{3,2,1,0:T(8,128)S(1)}, f32[6,8,6,140]{3,2,1,0:T(8,128)S(1)}, u32[]{:S(2)}, u32[]{:S(2)}) collective-permute-start(f32[6,8,6,140]{3,2,1,0:T(8,128)S(1)} %get-tuple-element.49), channel_id=1, source_target_pairs={{0,1},{1,2},{2,3},{3,4},{4,5},{5,6},{6,7},{7,8},{8,9},{9,10},{10,1... | collective-permute-start | bytes 483848 | tf_op jit(solution)/shard_map/ppermute | solution.py:25
  56.8 0.7 copy-start.4
  62.3 2.2 %collective-permute-start.5 = (f32[6,4,8,7]{3,2,1,0:T(8,128)S(1)}, f32[6,4,8,7]{3,2,1,0:T(8,128)S(1)}, u32[]{:S(2)}, u32[]{:S(2)}) collective-permute-start(f32[6,4,8,7]{3,2,1,0:T(8,128)S(1)} %get-tuple-element.130), channel_id=1, source_target_pairs={{32,0},{64,32},{96,64},{128,96},{160,128},{192,160},{224,192},{0,2... | collective-permute-start | bytes 16136 | tf_op jit(solution)/shard_map/ppermute | solution.py:26
  62.3 5.3 %collective-permute-start.4 = (f32[6,4,8,7]{3,2,1,0:T(8,128)S(1)}, f32[6,4,8,7]{3,2,1,0:T(8,128)S(1)}, u32[]{:S(2)}, u32[]{:S(2)}) collective-permute-start(f32[6,4,8,7]{3,2,1,0:T(8,128)S(1)} %get-tuple-element.129), channel_id=1, source_target_pairs={{0,32},{32,64},{64,96},{96,128},{128,160},{160,192},{192,224},{224... | collective-permute-start | bytes 16136 | tf_op jit(solution)/shard_map/ppermute | solution.py:25
  62.8 13.8 %copy-start.5 = (f32[2]{0:T(128)S(1)}, f32[2]{0:T(128)}, u32[]{:S(2)}) copy-start(f32[2]{0:T(128)} %constant.335.clone) | copy-start | bytes 28
  67.7 4.7 %collective-permute-start.7 = (f32[6,4,7,78]{3,2,1,0:T(8,128)S(1)}, f32[6,4,7,78]{3,2,1,0:T(8,128)S(1)}, u32[]{:S(2)}, u32[]{:S(2)}) collective-permute-start(f32[6,4,7,78]{3,2,1,0:T(8,128)S(1)} %get-tuple-element.128), channel_id=1, source_target_pairs={{1,0},{2,1},{3,2},{4,3},{5,4},{6,5},{7,6},{8,7},{9,8},{10,9},{11,1... | collective-permute-start | bytes 157256 | tf_op jit(solution)/shard_map/ppermute | solution.py:26
  68.1 7.9 %collective-permute-start.6 = (f32[6,4,7,78]{3,2,1,0:T(8,128)S(1)}, f32[6,4,7,78]{3,2,1,0:T(8,128)S(1)}, u32[]{:S(2)}, u32[]{:S(2)}) collective-permute-start(f32[6,4,7,78]{3,2,1,0:T(8,128)S(1)} %get-tuple-element.127), channel_id=1, source_target_pairs={{0,1},{1,2},{2,3},{3,4},{4,5},{5,6},{6,7},{7,8},{8,9},{9,10},{10,1... | collective-permute-start | bytes 157256 | tf_op jit(solution)/shard_map/ppermute | solution.py:25
  77.2 16.4 %copy-start.6 = (f32[2]{0:T(128)S(1)}, f32[2]{0:T(128)}, u32[]{:S(2)}) copy-start(f32[2]{0:T(128)} %constant.336.clone) | copy-start | bytes 28
  78.3 1.5 %collective-permute-start.9 = (f32[6,2,4,8]{3,2,1,0:T(4,128)S(1)}, f32[6,2,4,8]{3,2,1,0:T(4,128)S(1)}, u32[]{:S(2)}, u32[]{:S(2)}) collective-permute-start(f32[6,2,4,8]{3,2,1,0:T(4,128)S(1)} %get-tuple-element.184), channel_id=1, source_target_pairs={{32,0},{64,32},{96,64},{128,96},{160,128},{192,160},{224,192},{0,2... | collective-permute-start | bytes 4616 | tf_op jit(solution)/shard_map/ppermute | solution.py:26
  78.3 4.5 %collective-permute-start.8 = (f32[6,2,4,8]{3,2,1,0:T(4,128)S(1)}, f32[6,2,4,8]{3,2,1,0:T(4,128)S(1)}, u32[]{:S(2)}, u32[]{:S(2)}) collective-permute-start(f32[6,2,4,8]{3,2,1,0:T(4,128)S(1)} %get-tuple-element.183), channel_id=1, source_target_pairs={{0,32},{32,64},{64,96},{96,128},{128,160},{160,192},{192,224},{224... | collective-permute-start | bytes 4616 | tf_op jit(solution)/shard_map/ppermute | solution.py:25
  82.9 9.3 %collective-permute-start.10 = (f32[6,2,4,48]{3,2,1,0:T(4,128)S(1)}, f32[6,2,4,48]{3,2,1,0:T(4,128)S(1)}, u32[]{:S(2)}, u32[]{:S(2)}) collective-permute-start(f32[6,2,4,48]{3,2,1,0:T(4,128)S(1)} %pad_maximum_fusion.13), channel_id=1, source_target_pairs={{0,2},{1,3},{2,4},{3,5},{4,6},{5,7},{6,8},{7,9},{8,10},{9,11},{10,... | collective-permute-start | bytes 27656 | tf_op jit(solution)/shard_map/ppermute | solution.py:25
  83.0 9.2 %collective-permute-start.11 = (f32[6,2,4,48]{3,2,1,0:T(4,128)S(1)}, f32[6,2,4,48]{3,2,1,0:T(4,128)S(1)}, u32[]{:S(2)}, u32[]{:S(2)}) collective-permute-start(f32[6,2,4,48]{3,2,1,0:T(4,128)S(1)} %pad_maximum_fusion.13), channel_id=1, source_target_pairs={{0,1},{1,2},{2,3},{3,4},{4,5},{5,6},{6,7},{7,8},{8,9},{9,10},{10,1... | collective-permute-start | bytes 27656 | tf_op jit(solution)/shard_map/ppermute | solution.py:25
  83.1 9.1 %collective-permute-start.12 = (f32[6,2,4,48]{3,2,1,0:T(4,128)S(1)}, f32[6,2,4,48]{3,2,1,0:T(4,128)S(1)}, u32[]{:S(2)}, u32[]{:S(2)}) collective-permute-start(f32[6,2,4,48]{3,2,1,0:T(4,128)S(1)} %pad_maximum_fusion.13), channel_id=1, source_target_pairs={{1,0},{2,1},{3,2},{4,3},{5,4},{6,5},{7,6},{8,7},{9,8},{10,9},{11,1... | collective-permute-start | bytes 27656 | tf_op jit(solution)/shard_map/ppermute | solution.py:26
  88.4 4.8 %collective-permute-start.13 = (f32[6,2,4,48]{3,2,1,0:T(4,128)S(1)}, f32[6,2,4,48]{3,2,1,0:T(4,128)S(1)}, u32[]{:S(2)}, u32[]{:S(2)}) collective-permute-start(f32[6,2,4,48]{3,2,1,0:T(4,128)S(1)} %pad_maximum_fusion.13), channel_id=1, source_target_pairs={{2,0},{3,1},{4,2},{5,3},{6,4},{7,5},{8,6},{9,7},{10,8},{11,9},{12,... | collective-permute-start | bytes 27656 | tf_op jit(solution)/shard_map/ppermute | solution.py:26

commit v6 on v5

--- a/solution.py
+++ b/solution.py
@@ -12,22 +12,24 @@
 coarsenings = 2
 
 
+def padded_along(cells, width, axis, dim):
+    count = lax.axis_size(axis)
+    size = cells.shape[dim]
+    below, above = [], []
+    remaining, distance = width, 1
+    while remaining > 0:
+        take = min(remaining, size)
+        tail = lax.slice_in_dim(cells, size - take, size, axis=dim)
+        head = lax.slice_in_dim(cells, 0, take, axis=dim)
+        below.insert(0, lax.ppermute(tail, axis, [(i, (i + distance) % count) for i in range(count)]))
+        above.append(lax.ppermute(head, axis, [((i + distance) % count, i) for i in range(count)]))
+        remaining -= take
+        distance += 1
+    return jnp.concatenate(below + [cells] + above, axis=dim)
+
+
 def padded(cells, width):
-    for axis, dim in (("gx", 3), ("gy", 2)):
-        count = lax.axis_size(axis)
-        size = cells.shape[dim]
-        below, above = [], []
-        remaining, distance = width, 1
-        while remaining > 0:
-            take = min(remaining, size)
-            tail = lax.slice_in_dim(cells, size - take, size, axis=dim)
-            head = lax.slice_in_dim(cells, 0, take, axis=dim)
-            below.insert(0, lax.ppermute(tail, axis, [(i, (i + distance) % count) for i in range(count)]))
-            above.append(lax.ppermute(head, axis, [((i + distance) % count, i) for i in range(count)]))
-            remaining -= take
-            distance += 1
-        cells = jnp.concatenate(below + [cells] + above, axis=dim)
-    return cells
+    return padded_along(padded_along(cells, width, "gx", 3), width, "gy", 2)
 
 
 def crop(cells, have, want):
@@ -213,9 +215,11 @@
     for level, level_fields in enumerate((fields, fields_1, fields_2)):
         _, first, second = coefficients(level_fields, level)
         local = jnp.where(lane == level, jnp.maximum(jnp.max(first), jnp.max(second)), local)
+    wide_x = padded_along(jnp.concatenate([fields, previous], 0), 6, "gx", 3)
+    local, wide_x = lax.optimization_barrier((local, wide_x))
     spreads = global_max(local)[0]
 
-    wide = padded(jnp.concatenate([fields, previous], 0), 6)
+    wide = padded_along(wide_x, 6, "gy", 2)
     ops_0 = Level(coefficients(crop(wide[:4], 6, 5), 0)[0], 5, 0)
     state_w = wide[:2]
     substrate, catalyst = crop(state_w[0], 6, 5), crop(state_w[1], 6, 5)

time: 103 us -> 99.9 us (0.970)
  waiting for transfers between devices: 27.1 us -> 17.4 us
  starting transfers between devices: 16.7 us -> 22.7 us
  other arithmetic: 18.2 us -> 22 us
  Pallas kernels: 24.6 us -> 21 us
    ppermute x14, waiting for transfers between devices: 27.1 us -> 17.4 us  [the longest x7 11.7 us: padded_along(): lax.ppermute(tail, axis, [(i, (i + distance) % count) for i in range(coun...]
    ppermute x14, starting transfers between devices: 16.7 us -> 22.7 us  [the longest x7 22 us: padded_along(): lax.ppermute(head, axis, [((i + distance) % count, i) for i in range(coun...]
    pallas_call x2, Pallas kernels: 24.6 us -> 21 us  [gather_axis(): pl.pallas_call(lambda *refs: gather_kernel(axis, *refs), out_shape=jax.Sh...]
    sub x4, other arithmetic: 0.02 us -> 1.2 us  [restrict(): row // rows]
    slice x31 -> x30, local copies, waits for them, and re-layouts: 3.55 us -> 3.45 us  [shrunk_neighbours(): along_z = jnp.roll(centre, 1, 1) + jnp.roll(centre, -1, 1)]
  transfers between devices with their start and end apart: 14 -> 14, of which waited for: 9 -> 7; matrix products, arithmetic and copies ran while one was open for 7% -> 11% of each run, Pallas kernels for 24% -> 21%
where the time goes in v6:
time: 99.9 us; the launch traced here: 99.6 us
  starting transfers between devices  22.7 us (23%)
  other arithmetic  22 us (22%)
  Pallas kernels  21 us (21%)
  waiting for transfers between devices  17.4 us (17%)
  between operations  7.57 us (8%)
  local copies, waits for them, and re-layouts  6.81 us (7%)
  matrix products  2.06 us (2%)
    ppermute x7, starting transfers between devices, padded_along(): lax.ppermute(head, axis, [((i + distance) % count, i) for i in range(coun...  22 us
    pallas_call x2, Pallas kernels, gather_axis(): pl.pallas_call(lambda *refs: gather_kernel(axis, *refs), out_shape=jax.Sh...  21 us
    ppermute x7, waiting for transfers between devices, padded_along(): lax.ppermute(tail, axis, [(i, (i + distance) % count) for i in range(coun...  11.7 us
    ppermute x7, waiting for transfers between devices, padded_along(): lax.ppermute(head, axis, [((i + distance) % count, i) for i in range(coun...  5.64 us
    add x12, other arithmetic, chebyshev(): iterate = crop(iterate, halo + 1, halo) + update  4.36 us
    add x17, other arithmetic, operate(): first = coeff[0] * centre[0] + coeff[1] * centre[1]  3.79 us
    slice x30, local copies, waits for them, and re-layouts, shrunk_neighbours(): along_z = jnp.roll(centre, 1, 1) + jnp.roll(centre, -1, 1)  3.45 us
    reduce_max x2, other arithmetic, global_max(): block = jnp.max(gather_axis(block, axis, tag), axis=0)  2.3 us
  transfers between devices with their start and end apart: 14, of which 7 were waited for; matrix products, arithmetic and copies ran while one was open for 11% of the time, Pallas kernels for 21%

profile of v6, /device:TPU:0, one launch (start us, length us, event | category | flops | bytes accessed | tf_op | source)
XLA Modules:
  0.0 99.6 jit_solution(4148733349126439800)
XLA Ops:
  0.0 1.1 %pad_maximum_fusion.6 = f32[6,8,16,128]{3,2,1,0:T(8,128)S(1)} fusion(f32[2,8,16,128]{3,2,1,0:T(8,128)} %param.23, f32[1,8,16,128]{3,2,1,0:T(8,128)} %bitcast.69, f32[1,8,16,128]{3,2,1,0:T(8,128)} %bitcast.72, f32[2,8,16,128]{3,2,1,0:T(8,128)} %param.22), kind=kLoop, calls=%fused_computation.72 | loop fusion | flops 294912 | bytes 786432 | tf_op jit(solution)/shard_map/concatenate | solution.py:218
  1.3 0.5 collective-permute-start.1
  1.8 0.7 fusion.146
  2.8 0.6 broadcast_add_fusion.2
  3.4 0.6 compare_and_fusion.2
  4.0 0.6 iota_shift-right-logical_fusion.6
  4.5 0.6 iota_shift-right-logical_fusion.7
  6.5 0.4 fusion.144
  7.2 0.8 fusion.230
  8.4 0.7 fusion.330
  11.5 0.6 select_select_fusion.8.refs_0_
  12.1 0.6 broadcast_add_fusion.5
  12.8 0.4 pad_maximum_fusion.1
  13.2 8.4 %collective-permute-start.3 = (f32[6,8,6,140]{3,2,1,0:T(8,128)S(1)}, f32[6,8,6,140]{3,2,1,0:T(8,128)S(1)}, u32[]{:S(2)}, u32[]{:S(2)}) collective-permute-start(f32[6,8,6,140]{3,2,1,0:T(8,128)S(1)} %get-tuple-element.52), channel_id=1, source_target_pairs={{1,0},{2,1},{3,2},{4,3},{5,4},{6,5},{7,6},{8,7},{9,8},{10,9},{11,1... | collective-permute-start | bytes 483848 | tf_op jit(solution)/shard_map/ppermute | solution.py:25
  21.6 0.5 fusion.343
  22.2 7.4 %shard_map.208 = f32[8,8,128]{2,1,0:T(8,128)} custom-call(f32[8,128]{1,0:T(8,128)} %select_select_fusion.8.refs_0_), custom_call_target="tpu_custom_call" | custom-call | tf_op jit(solution)/shard_map/pallas_call | solution.py:98
  29.6 1.4 %reduce_max.78.refs_0_ = f32[8,128]{1,0:T(8,128)} reduce(f32[8,8,128]{2,1,0:T(8,128)} %shard_map.208, f32[]{:T(128)} %constant.322.clone.1), dimensions={0}, to_apply=%region_6.7 | reduce | flops 7168 | bytes 36868 | tf_op jit(solution)/shard_map/reduce_max | solution.py:115
  30.9 13.7 %shard_map.209 = f32[32,8,128]{2,1,0:T(8,128)} custom-call(f32[8,128]{1,0:T(8,128)} %reduce_max.78.refs_0_), custom_call_target="tpu_custom_call" | custom-call | tf_op jit(solution)/shard_map/pallas_call | solution.py:98
  44.6 0.9 reduce_max.79
  45.5 0.7 fusion.415
  47.4 0.4 fusion.51
  48.1 0.4 subtract_bitcast_fusion
  48.5 0.8 fusion.11
  49.7 0.4 fusion.66
  50.1 0.6 slice_add_fusion.12
  50.7 0.4 fusion.64
  51.5 0.7 fusion.32
  52.3 0.8 multiply_add_fusion.5
  53.5 0.3 fusion.143
  54.2 0.6 collective-permute-start.5
  54.8 2.2 %collective-permute-done.5 = f32[6,4,8,7]{3,2,1,0:T(8,128)S(1)} collective-permute-done((f32[6,4,8,7]{3,2,1,0:T(8,128)S(1)}, f32[6,4,8,7]{3,2,1,0:T(8,128)S(1)}, u32[]{:S(2)}, u32[]{:S(2)}) %collective-permute-start.5) | collective-permute-done | bytes 5408 | tf_op jit(solution)/shard_map/ppermute | solution.py:25
  57.0 3.0 %collective-permute-done.4 = f32[6,4,8,7]{3,2,1,0:T(8,128)S(1)} collective-permute-done((f32[6,4,8,7]{3,2,1,0:T(8,128)S(1)}, f32[6,4,8,7]{3,2,1,0:T(8,128)S(1)}, u32[]{:S(2)}, u32[]{:S(2)}) %collective-permute-start.4) | collective-permute-done | bytes 5408 | tf_op jit(solution)/shard_map/ppermute | solution.py:24
  60.2 4.4 %collective-permute-start.7 = (f32[6,4,7,78]{3,2,1,0:T(8,128)S(1)}, f32[6,4,7,78]{3,2,1,0:T(8,128)S(1)}, u32[]{:S(2)}, u32[]{:S(2)}) collective-permute-start(f32[6,4,7,78]{3,2,1,0:T(8,128)S(1)} %get-tuple-element.130), channel_id=1, source_target_pairs={{1,0},{2,1},{3,2},{4,3},{5,4},{6,5},{7,6},{8,7},{9,8},{10,9},{11,1... | collective-permute-start | bytes 157256 | tf_op jit(solution)/shard_map/ppermute | solution.py:25
  65.4 1.4 %collective-permute-done.7 = f32[6,4,7,78]{3,2,1,0:T(8,128)S(1)} collective-permute-done((f32[6,4,7,78]{3,2,1,0:T(8,128)S(1)}, f32[6,4,7,78]{3,2,1,0:T(8,128)S(1)}, u32[]{:S(2)}, u32[]{:S(2)}) %collective-permute-start.7) | collective-permute-done | bytes 52448 | tf_op jit(solution)/shard_map/ppermute | solution.py:25
  66.8 5.7 %collective-permute-done.6 = f32[6,4,7,78]{3,2,1,0:T(8,128)S(1)} collective-permute-done((f32[6,4,7,78]{3,2,1,0:T(8,128)S(1)}, f32[6,4,7,78]{3,2,1,0:T(8,128)S(1)}, u32[]{:S(2)}, u32[]{:S(2)}) %collective-permute-start.6) | collective-permute-done | bytes 52448 | tf_op jit(solution)/shard_map/ppermute | solution.py:24
  75.0 0.5 collective-permute-start.8
  75.5 1.0 %collective-permute-done.9 = f32[6,2,4,8]{3,2,1,0:T(4,128)S(1)} collective-permute-done((f32[6,2,4,8]{3,2,1,0:T(4,128)S(1)}, f32[6,2,4,8]{3,2,1,0:T(4,128)S(1)}, u32[]{:S(2)}, u32[]{:S(2)}) %collective-permute-start.9) | collective-permute-done | bytes 1568 | tf_op jit(solution)/shard_map/ppermute | solution.py:25
  76.5 3.0 %collective-permute-done.8 = f32[6,2,4,8]{3,2,1,0:T(4,128)S(1)} collective-permute-done((f32[6,2,4,8]{3,2,1,0:T(4,128)S(1)}, f32[6,2,4,8]{3,2,1,0:T(4,128)S(1)}, u32[]{:S(2)}, u32[]{:S(2)}) %collective-permute-start.8) | collective-permute-done | bytes 1568 | tf_op jit(solution)/shard_map/ppermute | solution.py:24
  79.7 5.3 %collective-permute-start.12 = (f32[6,2,4,48]{3,2,1,0:T(4,128)S(1)}, f32[6,2,4,48]{3,2,1,0:T(4,128)S(1)}, u32[]{:S(2)}, u32[]{:S(2)}) collective-permute-start(f32[6,2,4,48]{3,2,1,0:T(4,128)S(1)} %pad_maximum_fusion.17), channel_id=1, source_target_pairs={{1,0},{2,1},{3,2},{4,3},{5,4},{6,5},{7,6},{8,7},{9,8},{10,9},{11,1... | collective-permute-start | bytes 27656 | tf_op jit(solution)/shard_map/ppermute | solution.py:25
  85.1 2.8 %collective-permute-start.13 = (f32[6,2,4,48]{3,2,1,0:T(4,128)S(1)}, f32[6,2,4,48]{3,2,1,0:T(4,128)S(1)}, u32[]{:S(2)}, u32[]{:S(2)}) collective-permute-start(f32[6,2,4,48]{3,2,1,0:T(4,128)S(1)} %pad_maximum_fusion.17), channel_id=1, source_target_pairs={{2,0},{3,1},{4,2},{5,3},{6,4},{7,5},{8,6},{9,7},{10,8},{11,9},{12,... | collective-permute-start | bytes 27656 | tf_op jit(solution)/shard_map/ppermute | solution.py:25
  88.9 1.0 %collective-permute-done.13 = f32[6,2,4,48]{3,2,1,0:T(4,128)S(1)} collective-permute-done((f32[6,2,4,48]{3,2,1,0:T(4,128)S(1)}, f32[6,2,4,48]{3,2,1,0:T(4,128)S(1)}, u32[]{:S(2)}, u32[]{:S(2)}) %collective-permute-start.13) | collective-permute-done | bytes 9248 | tf_op jit(solution)/shard_map/ppermute | solution.py:25
  94.3 0.3 slice.2057
  94.6 0.7 copy.46
  95.4 0.4 fusion.62
  96.1 0.6 slice_add_fusion.7
  96.7 0.4 fusion.60
  97.5 0.7 slice_add_fusion.4
  98.6 0.9 fusion.74
  (175 shorter events, 11.2 us)
Async XLA Ops:
  0.0 1.8 %copy-start = (f32[2,8,16,128]{3,2,1,0:T(8,128)S(1)}, f32[2,8,16,128]{3,2,1,0:T(8,128)}, u32[]{:S(2)}) copy-start(f32[2,8,16,128]{3,2,1,0:T(8,128)} %param.22) | copy-start | bytes 393220
  0.0 1.8 %copy-start.1 = (f32[8,16,128]{2,1,0:T(8,128)S(1)}, f32[8,16,128]{2,1,0:T(8,128)}, u32[]{:S(2)}) copy-start(f32[8,16,128]{2,1,0:T(8,128)} %param.25) | copy-start | bytes 196612
  0.0 1.8 %copy-start.2 = (f32[8,16,128]{2,1,0:T(8,128)S(1)}, f32[8,16,128]{2,1,0:T(8,128)}, u32[]{:S(2)}) copy-start(f32[8,16,128]{2,1,0:T(8,128)} %param.24) | copy-start | bytes 196612
  1.3 11.5 %collective-permute-start.1 = (f32[6,8,16,6]{3,2,1,0:T(8,128)S(1)}, f32[6,8,16,6]{3,2,1,0:T(8,128)S(1)}, u32[]{:S(2)}, u32[]{:S(2)}) collective-permute-start(f32[6,8,16,6]{3,2,1,0:T(8,128)S(1)} %get-tuple-element.90), channel_id=1, source_target_pairs={{32,0},{64,32},{96,64},{128,96},{160,128},{192,160},{224,192},{0,2... | collective-permute-start | bytes 55304 | tf_op jit(solution)/shard_map/ppermute | solution.py:25
  1.8 11.0 %collective-permute-start = (f32[6,8,16,6]{3,2,1,0:T(8,128)S(1)}, f32[6,8,16,6]{3,2,1,0:T(8,128)S(1)}, u32[]{:S(2)}, u32[]{:S(2)}) collective-permute-start(f32[6,8,16,6]{3,2,1,0:T(8,128)S(1)} %get-tuple-element.89), channel_id=1, source_target_pairs={{0,32},{32,64},{64,96},{96,128},{128,160},{160,192},{192,224},{224... | collective-permute-start | bytes 55304 | tf_op jit(solution)/shard_map/ppermute | solution.py:24
  2.6 5.3 %copy-start.10 = (s32[64]{0:T(128)}, s32[64]{0:T(128)S(1)}, u32[]{:S(2)}) copy-start(s32[64]{0:T(128)S(1)} %get-tuple-element.200) | copy-start | bytes 772
  2.7 5.3 %copy-start.12 = (s32[64]{0:T(128)}, s32[64]{0:T(128)S(1)}, u32[]{:S(2)}) copy-start(s32[64]{0:T(128)S(1)} %get-tuple-element.201) | copy-start | bytes 772
  2.7 5.3 %copy-start.22 = (pred[64]{0:T(512)(128)(4,1)}, pred[64]{0:T(512)(128)(4,1)S(1)}, u32[]{:S(2)}) copy-start(pred[64]{0:T(512)(128)(4,1)S(1)} %compare_and_fusion.4) | copy-start | bytes 196
  6.9 5.9 %copy-start.3 = (f32[2,8,16,128]{3,2,1,0:T(8,128)S(1)}, f32[2,8,16,128]{3,2,1,0:T(8,128)}, u32[]{:S(2)}) copy-start(f32[2,8,16,128]{3,2,1,0:T(8,128)} %param.23) | copy-start | bytes 393220
  13.2 33.9 %collective-permute-start.3 = (f32[6,8,6,140]{3,2,1,0:T(8,128)S(1)}, f32[6,8,6,140]{3,2,1,0:T(8,128)S(1)}, u32[]{:S(2)}, u32[]{:S(2)}) collective-permute-start(f32[6,8,6,140]{3,2,1,0:T(8,128)S(1)} %get-tuple-element.52), channel_id=1, source_target_pairs={{1,0},{2,1},{3,2},{4,3},{5,4},{6,5},{7,6},{8,7},{9,8},{10,9},{11,1... | collective-permute-start | bytes 483848 | tf_op jit(solution)/shard_map/ppermute | solution.py:25
  21.6 25.6 %collective-permute-start.2 = (f32[6,8,6,140]{3,2,1,0:T(8,128)S(1)}, f32[6,8,6,140]{3,2,1,0:T(8,128)S(1)}, u32[]{:S(2)}, u32[]{:S(2)}) collective-permute-start(f32[6,8,6,140]{3,2,1,0:T(8,128)S(1)} %get-tuple-element.51), channel_id=1, source_target_pairs={{0,1},{1,2},{2,3},{3,4},{4,5},{5,6},{6,7},{7,8},{8,9},{9,10},{10,1... | collective-permute-start | bytes 483848 | tf_op jit(solution)/shard_map/ppermute | solution.py:24
  47.8 0.7 copy-start.5
  52.2 1.6 %copy-start.8 = (s32[256]{0:T(256)S(1)}, s32[256]{0:T(256)}, u32[]{:S(2)}) copy-start(s32[256]{0:T(256)} %get-tuple-element.218) | copy-start | bytes 3076
  52.2 1.6 %copy-start.9 = (s32[256]{0:T(256)S(1)}, s32[256]{0:T(256)}, u32[]{:S(2)}) copy-start(s32[256]{0:T(256)} %get-tuple-element.219) | copy-start | bytes 3076
  52.2 1.6 %copy-start.20 = (pred[256]{0:T(512)(128)(4,1)S(1)}, pred[256]{0:T(512)(128)(4,1)}, u32[]{:S(2)}) copy-start(pred[256]{0:T(512)(128)(4,1)} %get-tuple-element.216) | copy-start | bytes 772
  52.2 1.6 %copy-start.21 = (pred[256]{0:T(512)(128)(4,1)S(1)}, pred[256]{0:T(512)(128)(4,1)}, u32[]{:S(2)}) copy-start(pred[256]{0:T(512)(128)(4,1)} %get-tuple-element.217) | copy-start | bytes 772
  52.2 1.6 %copy-start.24 = (pred[256]{0:T(512)(128)(4,1)S(1)}, pred[256]{0:T(512)(128)(4,1)}, u32[]{:S(2)}) copy-start(pred[256]{0:T(512)(128)(4,1)} %fusion.343) | copy-start | bytes 772
  54.2 2.8 %collective-permute-start.5 = (f32[6,4,8,7]{3,2,1,0:T(8,128)S(1)}, f32[6,4,8,7]{3,2,1,0:T(8,128)S(1)}, u32[]{:S(2)}, u32[]{:S(2)}) collective-permute-start(f32[6,4,8,7]{3,2,1,0:T(8,128)S(1)} %get-tuple-element.132), channel_id=1, source_target_pairs={{32,0},{64,32},{96,64},{128,96},{160,128},{192,160},{224,192},{0,2... | collective-permute-start | bytes 16136 | tf_op jit(solution)/shard_map/ppermute | solution.py:25
  54.8 5.3 %collective-permute-start.4 = (f32[6,4,8,7]{3,2,1,0:T(8,128)S(1)}, f32[6,4,8,7]{3,2,1,0:T(8,128)S(1)}, u32[]{:S(2)}, u32[]{:S(2)}) collective-permute-start(f32[6,4,8,7]{3,2,1,0:T(8,128)S(1)} %get-tuple-element.131), channel_id=1, source_target_pairs={{0,32},{32,64},{64,96},{96,128},{128,160},{160,192},{192,224},{224... | collective-permute-start | bytes 16136 | tf_op jit(solution)/shard_map/ppermute | solution.py:24
  54.8 18.3 %copy-start.6 = (f32[2]{0:T(128)S(1)}, f32[2]{0:T(128)}, u32[]{:S(2)}) copy-start(f32[2]{0:T(128)} %constant.335.clone) | copy-start | bytes 28
  60.2 6.6 %collective-permute-start.7 = (f32[6,4,7,78]{3,2,1,0:T(8,128)S(1)}, f32[6,4,7,78]{3,2,1,0:T(8,128)S(1)}, u32[]{:S(2)}, u32[]{:S(2)}) collective-permute-start(f32[6,4,7,78]{3,2,1,0:T(8,128)S(1)} %get-tuple-element.130), channel_id=1, source_target_pairs={{1,0},{2,1},{3,2},{4,3},{5,4},{6,5},{7,6},{8,7},{9,8},{10,9},{11,1... | collective-permute-start | bytes 157256 | tf_op jit(solution)/shard_map/ppermute | solution.py:25
  64.6 7.9 %collective-permute-start.6 = (f32[6,4,7,78]{3,2,1,0:T(8,128)S(1)}, f32[6,4,7,78]{3,2,1,0:T(8,128)S(1)}, u32[]{:S(2)}, u32[]{:S(2)}) collective-permute-start(f32[6,4,7,78]{3,2,1,0:T(8,128)S(1)} %get-tuple-element.129), channel_id=1, source_target_pairs={{0,1},{1,2},{2,3},{3,4},{4,5},{5,6},{6,7},{7,8},{8,9},{9,10},{10,1... | collective-permute-start | bytes 157256 | tf_op jit(solution)/shard_map/ppermute | solution.py:24
  73.3 1.1 %copy-start.11 = (s32[64]{0:T(128)S(1)}, s32[64]{0:T(128)}, u32[]{:S(2)}) copy-start(s32[64]{0:T(128)} %copy-done.10) | copy-start | bytes 772
  73.3 1.1 %copy-start.13 = (s32[64]{0:T(128)S(1)}, s32[64]{0:T(128)}, u32[]{:S(2)}) copy-start(s32[64]{0:T(128)} %copy-done.12) | copy-start | bytes 772
  73.3 1.1 %copy-start.23 = (pred[64]{0:T(512)(128)(4,1)S(1)}, pred[64]{0:T(512)(128)(4,1)}, u32[]{:S(2)}) copy-start(pred[64]{0:T(512)(128)(4,1)} %copy-done.22) | copy-start | bytes 196
  73.3 1.3 %copy-start.14 = (s32[64]{0:T(128)S(1)}, s32[64]{0:T(128)}, u32[]{:S(2)}) copy-start(s32[64]{0:T(128)} %get-tuple-element.222) | copy-start | bytes 772
  73.3 1.3 %copy-start.15 = (s32[64]{0:T(128)S(1)}, s32[64]{0:T(128)}, u32[]{:S(2)}) copy-start(s32[64]{0:T(128)} %get-tuple-element.223) | copy-start | bytes 772
  73.4 1.3 %copy-start.16 = (s32[64]{0:T(128)S(1)}, s32[64]{0:T(128)}, u32[]{:S(2)}) copy-start(s32[64]{0:T(128)} %get-tuple-element.224) | copy-start | bytes 772
  73.4 1.3 %copy-start.17 = (s32[64]{0:T(128)S(1)}, s32[64]{0:T(128)}, u32[]{:S(2)}) copy-start(s32[64]{0:T(128)} %get-tuple-element.225) | copy-start | bytes 772
  73.4 1.3 %copy-start.18 = (s32[64]{0:T(128)S(1)}, s32[64]{0:T(128)}, u32[]{:S(2)}) copy-start(s32[64]{0:T(128)} %get-tuple-element.226) | copy-start | bytes 772
  73.4 1.3 %copy-start.19 = (s32[64]{0:T(128)S(1)}, s32[64]{0:T(128)}, u32[]{:S(2)}) copy-start(s32[64]{0:T(128)} %get-tuple-element.227) | copy-start | bytes 772
  73.7 16.5 %copy-start.7 = (f32[2]{0:T(128)S(1)}, f32[2]{0:T(128)}, u32[]{:S(2)}) copy-start(f32[2]{0:T(128)} %constant.336.clone) | copy-start | bytes 28
  75.0 1.5 %collective-permute-start.9 = (f32[6,2,4,8]{3,2,1,0:T(4,128)S(1)}, f32[6,2,4,8]{3,2,1,0:T(4,128)S(1)}, u32[]{:S(2)}, u32[]{:S(2)}) collective-permute-start(f32[6,2,4,8]{3,2,1,0:T(4,128)S(1)} %get-tuple-element.186), channel_id=1, source_target_pairs={{32,0},{64,32},{96,64},{128,96},{160,128},{192,160},{224,192},{0,2... | collective-permute-start | bytes 4616 | tf_op jit(solution)/shard_map/ppermute | solution.py:25
  75.0 4.5 %collective-permute-start.8 = (f32[6,2,4,8]{3,2,1,0:T(4,128)S(1)}, f32[6,2,4,8]{3,2,1,0:T(4,128)S(1)}, u32[]{:S(2)}, u32[]{:S(2)}) collective-permute-start(f32[6,2,4,8]{3,2,1,0:T(4,128)S(1)} %get-tuple-element.185), channel_id=1, source_target_pairs={{0,32},{32,64},{64,96},{96,128},{128,160},{160,192},{192,224},{224... | collective-permute-start | bytes 4616 | tf_op jit(solution)/shard_map/ppermute | solution.py:24
  79.6 9.3 %collective-permute-start.10 = (f32[6,2,4,48]{3,2,1,0:T(4,128)S(1)}, f32[6,2,4,48]{3,2,1,0:T(4,128)S(1)}, u32[]{:S(2)}, u32[]{:S(2)}) collective-permute-start(f32[6,2,4,48]{3,2,1,0:T(4,128)S(1)} %pad_maximum_fusion.17), channel_id=1, source_target_pairs={{0,2},{1,3},{2,4},{3,5},{4,6},{5,7},{6,8},{7,9},{8,10},{9,11},{10,... | collective-permute-start | bytes 27656 | tf_op jit(solution)/shard_map/ppermute | solution.py:24
  79.7 9.2 %collective-permute-start.11 = (f32[6,2,4,48]{3,2,1,0:T(4,128)S(1)}, f32[6,2,4,48]{3,2,1,0:T(4,128)S(1)}, u32[]{:S(2)}, u32[]{:S(2)}) collective-permute-start(f32[6,2,4,48]{3,2,1,0:T(4,128)S(1)} %pad_maximum_fusion.17), channel_id=1, source_target_pairs={{0,1},{1,2},{2,3},{3,4},{4,5},{5,6},{6,7},{7,8},{8,9},{9,10},{10,1... | collective-permute-start | bytes 27656 | tf_op jit(solution)/shard_map/ppermute | solution.py:24
  79.7 9.1 %collective-permute-start.12 = (f32[6,2,4,48]{3,2,1,0:T(4,128)S(1)}, f32[6,2,4,48]{3,2,1,0:T(4,128)S(1)}, u32[]{:S(2)}, u32[]{:S(2)}) collective-permute-start(f32[6,2,4,48]{3,2,1,0:T(4,128)S(1)} %pad_maximum_fusion.17), channel_id=1, source_target_pairs={{1,0},{2,1},{3,2},{4,3},{5,4},{6,5},{7,6},{8,7},{9,8},{10,9},{11,1... | collective-permute-start | bytes 27656 | tf_op jit(solution)/shard_map/ppermute | solution.py:25
  85.1 4.8 %collective-permute-start.13 = (f32[6,2,4,48]{3,2,1,0:T(4,128)S(1)}, f32[6,2,4,48]{3,2,1,0:T(4,128)S(1)}, u32[]{:S(2)}, u32[]{:S(2)}) collective-permute-start(f32[6,2,4,48]{3,2,1,0:T(4,128)S(1)} %pad_maximum_fusion.17), channel_id=1, source_target_pairs={{2,0},{3,1},{4,2},{5,3},{6,4},{7,5},{8,6},{9,7},{10,8},{11,9},{12,... | collective-permute-start | bytes 27656 | tf_op jit(solution)/shard_map/ppermute | solution.py:25
  97.5 1.1 %copy-start.4 = (f32[1,8,16,128]{3,2,1,0:T(8,128)S(1)}, f32[1,8,16,128]{3,2,1,0:T(8,128)}, u32[]{:S(2)}) copy-start(f32[1,8,16,128]{3,2,1,0:T(8,128)} %get-tuple-element.94) | copy-start | bytes 196612

commit v7 on v6

--- a/solution.py
+++ b/solution.py
@@ -26,6 +26,81 @@
         remaining -= take
         distance += 1
     return jnp.concatenate(below + [cells] + above, axis=dim)
+
+
+def halo_kernel(offsets, *refs):
+    count = len(offsets)
+    pieces, got, land = refs[:count], refs[count:2 * count], refs[2 * count:3 * count]
+    send_sem, recv_sem = refs[3 * count], refs[3 * count + 1]
+    count_x = lax.axis_size("gx")
+    count_y = lax.axis_size("gy")
+    at_x = lax.axis_index("gx")
+    at_y = lax.axis_index("gy")
+    mesh_ids = pl.DeviceIdType.MESH
+
+    def device(step_y, step_x):
+        return (lax.rem(at_x + step_x + 4 * count_x, count_x), lax.rem(at_y + step_y + 4 * count_y, count_y))
+
+    barrier = pltpu.get_barrier_semaphore()
+    for step_y, step_x in offsets:
+        pl.semaphore_signal(barrier, 1, device_id=device(step_y, step_x), device_id_type=mesh_ids)
+    pl.semaphore_wait(barrier, count)
+    copies = []
+    for slot, (step_y, step_x) in enumerate(offsets):
+        copy = pltpu.make_async_remote_copy(
+            src_ref=pieces[slot],
+            dst_ref=land[slot],
+            send_sem=send_sem.at[slot],
+            recv_sem=recv_sem.at[slot],
+            device_id=device(-step_y, -step_x),
+            device_id_type=mesh_ids,
+        )
+        copy.start()
+        copies.append(copy)
+    for copy in copies:
+        copy.wait()
+    for slot in range(count):
+        got[slot][...] = land[slot][...]
+
+
+def segments(width, size):
+    below, above = [], []
+    remaining, distance = width, 1
+    while remaining > 0:
+        take = min(remaining, size)
+        below.insert(0, (-distance, size - take, size))
+        above.append((distance, 0, take))
+        remaining -= take
+        distance += 1
+    return below + [(0, 0, size)] + above
+
+
+def padded_at_once(cells, width, tag):
+    rows, cols = cells.shape[2], cells.shape[3]
+    runs_y, runs_x = segments(width, rows), segments(width, cols)
+    pieces, offsets = [], []
+    for step_y, first_y, last_y in runs_y:
+        for step_x, first_x, last_x in runs_x:
+            if (step_y, step_x) != (0, 0):
+                pieces.append(cells[:, :, first_y:last_y, first_x:last_x])
+                offsets.append((step_y, step_x))
+    vmem = pl.BlockSpec(memory_space=pltpu.VMEM)
+    shapes = [jax.ShapeDtypeStruct(piece.shape, jnp.float32) for piece in pieces]
+    got = pl.pallas_call(
+        lambda *refs: halo_kernel(offsets, *refs),
+        out_shape=shapes,
+        in_specs=[vmem] * len(pieces),
+        out_specs=[vmem] * len(pieces),
+        scratch_shapes=[pltpu.VMEM(shape.shape, jnp.float32) for shape in shapes]
+        + [pltpu.SemaphoreType.DMA((len(pieces),)), pltpu.SemaphoreType.DMA((len(pieces),))],
+        compiler_params=pltpu.CompilerParams(collective_id=tag, has_side_effects=True),
+    )(*pieces)
+    received = iter(got)
+    bands = []
+    for step_y, _, _ in runs_y:
+        band = [cells if (step_y, step_x) == (0, 0) else next(received) for step_x, _, _ in runs_x]
+        bands.append(jnp.concatenate(band, axis=3))
+    return jnp.concatenate(bands, axis=2)
 
 
 def padded(cells, width):
@@ -237,13 +312,13 @@
     pre_0, pre_0_halo = chebyshev(ops_0, source_0, 5, None, None, spreads[0])
     resid_0 = crop(source_0, 5, 0) - ops_0.operate(crop(pre_0, pre_0_halo, 1), 1)
 
-    wide_1 = padded(jnp.concatenate([restrict(resid_0), fields_1], 0), 7)
+    wide_1 = padded_at_once(jnp.concatenate([restrict(resid_0), fields_1], 0), 7, 2)
     ops_1 = Level(coefficients(wide_1[2:], 1)[0], 7, 1)
     source_1 = wide_1[:2]
     pre_1, pre_1_halo = chebyshev(ops_1, source_1, 7, None, None, spreads[1])
     resid_1 = crop(source_1, 7, 0) - ops_1.operate(crop(pre_1, pre_1_halo, 1), 1)
 
-    wide_2 = padded(jnp.concatenate([restrict(resid_1), fields_2], 0), 8)
+    wide_2 = padded_at_once(jnp.concatenate([restrict(resid_1), fields_2], 0), 8, 3)
     ops_2 = Level(coefficients(wide_2[2:], 2)[0], 8, 2)
     source_2 = wide_2[:2]
     first_2, first_2_halo = chebyshev(ops_2, source_2, 8, None, None, spreads[2])

time: 99.9 us -> 113 us (1.13)
  the two profiles are of different devices: /device:TPU:0 before, /device:TPU:1 now
where the time goes in v7:
time: 113 us; the launch traced here: 112 us
  Pallas kernels  51.2 us (45%)
  other arithmetic  32.7 us (29%)
  starting transfers between devices  10.7 us (9%)
  between operations  8.04 us (7%)
  local copies, waits for them, and re-layouts  7.08 us (6%)
  matrix products  2.06 us (2%)
    pallas_call x2, Pallas kernels, padded_at_once(): pl.pallas_call(lambda *refs: halo_kernel(offsets, *refs), out_shape=shape...  30.2 us
    pallas_call x2, Pallas kernels, gather_axis(): pl.pallas_call(lambda *refs: gather_kernel(axis, *refs), out_shape=jax.Sh...  20.9 us
    ppermute x2, starting transfers between devices, padded_along(): lax.ppermute(head, axis, [((i + distance) % count, i) for i in range(coun...  10.7 us
    add x12, other arithmetic, chebyshev(): iterate = crop(iterate, halo + 1, halo) + update  4.39 us
    concatenate x5, other arithmetic, padded_at_once(): bands.append(jnp.concatenate(band, axis=3))  4.35 us
    slice x30, local copies, waits for them, and re-layouts, shrunk_neighbours(): along_z = jnp.roll(centre, 1, 1) + jnp.roll(centre, -1, 1)  3.45 us
    add x17, other arithmetic, operate(): first = coeff[0] * centre[0] + coeff[1] * centre[1]  3.15 us
    reduce_max x2, other arithmetic, global_max(): block = jnp.max(gather_axis(block, axis, tag), axis=0)  2.3 us
  transfers between devices with their start and end apart: 4, of which 0 were waited for; matrix products, arithmetic and copies ran while one was open for 12% of the time, Pallas kernels for 19%

profile of v7, /device:TPU:1, one launch (start us, length us, event | category | flops | bytes accessed | tf_op | source)
XLA Modules:
  0.0 111.7 jit_solution(8236562831659551999)
XLA Ops:
  0.0 1.1 pad_maximum_fusion.6
  1.3 3.2 %collective-permute-start.1 = (f32[6,8,16,6]{3,2,1,0:T(8,128)S(1)}, f32[6,8,16,6]{3,2,1,0:T(8,128)S(1)}, u32[]{:S(2)}, u32[]{:S(2)}) collective-permute-start(f32[6,8,16,6]{3,2,1,0:T(8,128)S(1)} %get-tuple-element.134), channel_id=1, source_target_pairs={{32,0},{64,32},{96,64},{128,96},{160,128},{192,160},{224,192},{0,2... | collective-permute-start | bytes 55304 | tf_op jit(solution)/shard_map/ppermute | solution.py:25
  4.6 0.7 fusion.153
  5.5 0.6 iota_shift-right-logical_fusion.2
  6.1 0.6 iota_shift-right-logical_fusion.3
  6.7 0.6 broadcast_add_fusion.2
  7.3 0.5 compare_and_fusion.2
  7.8 0.6 iota_shift-right-logical_fusion.6
  8.4 0.6 iota_shift-right-logical_fusion.7
  9.0 0.6 broadcast_add_fusion.5
  9.6 0.6 compare_and_fusion
  11.5 0.4 fusion.151
  12.2 0.8 fusion.239
  13.4 0.7 fusion.341
  16.8 0.6 select_select_fusion.8.refs_0_
  17.4 0.5 fusion.354
  18.4 7.5 %collective-permute-start.3 = (f32[6,8,6,140]{3,2,1,0:T(8,128)S(1)}, f32[6,8,6,140]{3,2,1,0:T(8,128)S(1)}, u32[]{:S(2)}, u32[]{:S(2)}) collective-permute-start(f32[6,8,6,140]{3,2,1,0:T(8,128)S(1)} %get-tuple-element.96), channel_id=1, source_target_pairs={{1,0},{2,1},{3,2},{4,3},{5,4},{6,5},{7,6},{8,7},{9,8},{10,9},{11,1... | collective-permute-start | bytes 483848 | tf_op jit(solution)/shard_map/ppermute | solution.py:25
  25.9 0.6 compare_and_fusion.8
  26.6 8.4 %shard_map.208 = f32[8,8,128]{2,1,0:T(8,128)} custom-call(f32[8,128]{1,0:T(8,128)} %select_select_fusion.8.refs_0_), custom_call_target="tpu_custom_call" | custom-call | tf_op jit(solution)/shard_map/pallas_call | solution.py:173
  35.0 1.4 %reduce_max.78.refs_0_ = f32[8,128]{1,0:T(8,128)} reduce(f32[8,8,128]{2,1,0:T(8,128)} %shard_map.208, f32[]{:T(128)} %constant.322.clone.1), dimensions={0}, to_apply=%region_6.7 | reduce | flops 7168 | bytes 36868 | tf_op jit(solution)/shard_map/reduce_max | solution.py:190
  36.4 12.5 %shard_map.209 = f32[32,8,128]{2,1,0:T(8,128)} custom-call(f32[8,128]{1,0:T(8,128)} %reduce_max.78.refs_0_), custom_call_target="tpu_custom_call" | custom-call | tf_op jit(solution)/shard_map/pallas_call | solution.py:173
  48.9 0.9 reduce_max.79
  49.8 0.7 fusion.425
  54.7 0.8 fusion.11
  55.9 0.4 fusion.66
  56.3 0.6 slice_add_fusion.12
  56.9 0.4 fusion.64
  57.6 0.7 fusion.32
  59.7 0.8 pad_maximum_fusion.8
  60.5 0.7 fusion.95
  61.2 0.7 fusion.100
  61.9 16.0 %shard_map.210 = (f32[6,4,7,7]{3,2,1,0:T(8,128)}, f32[6,4,7,64]{3,2,1,0:T(8,128)}, f32[6,4,7,7]{3,2,1,0:T(8,128)}, f32[6,4,8,7]{3,2,1,0:T(8,128)}, f32[6,4,8,7]{...) custom-call(f32[6,4,7,7]{3,2,1,0:T(8,128)} %get-tuple-element.174.refs_0_, ...), custom_call_target="tpu_custom_call" | custom-call | tf_op jit(solution)/shard_map/pallas_call | solution.py:89
  78.0 1.5 %maximum_maximum_fusion = f32[6,4,22,78]{3,2,1,0:T(8,128)S(1)} fusion(f32[6,4,7,7]{3,2,1,0:T(8,128)} %get-tuple-element.38, f32[6,4,7,64]{3,2,1,0:T(8,128)} %get-tuple-element.37, f32[6,4,7,7]{3,2,1,0:T(8,128)} %get-tuple-element.36, f32[6,4,8,7]{3,2,1,0:T(8,128)} %get-tuple-element.35, f32[4,4,8,64]{3,2,1,0:T(8,128)S(1)} %bitcast.67, ...), kind=kLoop, calls=%fused_computation.90 | loop fusion | flops 370656 | bytes 329472 | tf_op jit(solution)/shard_map/concatenate | solution.py:103
  81.8 0.7 fusion.246
  82.5 0.6 pad_maximum_fusion.9.refs_1_.refs_4_.refs_9_.refs_12_
  83.1 14.2 %shard_map.211 = (f32[6,2,4,8]{3,2,1,0:T(4,128)}, f32[6,2,4,32]{3,2,1,0:T(4,128)}, f32[6,2,4,8]{3,2,1,0:T(4,128)}, f32[6,2,4,8]{3,2,1,0:T(4,128)}, f32[6,2,4,32]...) custom-call(f32[6,2,4,8]{3,2,1,0:T(4,128)} %get-tuple-element.234.re, ...), custom_call_target="tpu_custom_call" | custom-call | tf_op jit(solution)/shard_map/pallas_call | solution.py:89
  97.3 0.8 pad_maximum_fusion.19
  98.2 0.9 pad_maximum_fusion.17
  99.1 0.9 pad_maximum_fusion.18
  100.0 0.9 pad_maximum_fusion.20
  100.9 0.9 pad_maximum_fusion.21
  106.3 0.6 slice.2093
  106.8 0.7 copy.44
  107.6 0.4 fusion.62
  108.3 0.6 slice_add_fusion.7
  108.9 0.4 fusion.60
  109.7 0.7 slice_add_fusion.4
  110.8 0.9 fusion.74
  (190 shorter events, 12.1 us)
Async XLA Ops:
  0.0 4.5 %copy-start = (f32[2,8,16,128]{3,2,1,0:T(8,128)S(1)}, f32[2,8,16,128]{3,2,1,0:T(8,128)}, u32[]{:S(2)}) copy-start(f32[2,8,16,128]{3,2,1,0:T(8,128)} %param.22) | copy-start | bytes 393220
  0.0 4.5 %copy-start.1 = (f32[8,16,128]{2,1,0:T(8,128)S(1)}, f32[8,16,128]{2,1,0:T(8,128)}, u32[]{:S(2)}) copy-start(f32[8,16,128]{2,1,0:T(8,128)} %param.25) | copy-start | bytes 196612
  0.0 4.6 %copy-start.2 = (f32[8,16,128]{2,1,0:T(8,128)S(1)}, f32[8,16,128]{2,1,0:T(8,128)}, u32[]{:S(2)}) copy-start(f32[8,16,128]{2,1,0:T(8,128)} %param.24) | copy-start | bytes 196612
  1.3 16.7 %collective-permute-start.1 = (f32[6,8,16,6]{3,2,1,0:T(8,128)S(1)}, f32[6,8,16,6]{3,2,1,0:T(8,128)S(1)}, u32[]{:S(2)}, u32[]{:S(2)}) collective-permute-start(f32[6,8,16,6]{3,2,1,0:T(8,128)S(1)} %get-tuple-element.134), channel_id=1, source_target_pairs={{32,0},{64,32},{96,64},{128,96},{160,128},{192,160},{224,192},{0,2... | collective-permute-start | bytes 55304 | tf_op jit(solution)/shard_map/ppermute | solution.py:25
  4.5 13.4 %collective-permute-start = (f32[6,8,16,6]{3,2,1,0:T(8,128)S(1)}, f32[6,8,16,6]{3,2,1,0:T(8,128)S(1)}, u32[]{:S(2)}, u32[]{:S(2)}) collective-permute-start(f32[6,8,16,6]{3,2,1,0:T(8,128)S(1)} %get-tuple-element.133), channel_id=1, source_target_pairs={{0,32},{32,64},{64,96},{96,128},{128,160},{160,192},{192,224},{224... | collective-permute-start | bytes 55304 | tf_op jit(solution)/shard_map/ppermute | solution.py:24
  5.4 7.6 %copy-start.21 = (s32[64]{0:T(128)}, s32[64]{0:T(128)S(1)}, u32[]{:S(2)}) copy-start(s32[64]{0:T(128)S(1)} %get-tuple-element.248) | copy-start | bytes 772
  5.4 7.6 %copy-start.23 = (s32[64]{0:T(128)}, s32[64]{0:T(128)S(1)}, u32[]{:S(2)}) copy-start(s32[64]{0:T(128)S(1)} %get-tuple-element.249) | copy-start | bytes 772
  5.4 7.6 %copy-start.35 = (pred[64]{0:T(512)(128)(4,1)}, pred[64]{0:T(512)(128)(4,1)S(1)}, u32[]{:S(2)}) copy-start(pred[64]{0:T(512)(128)(4,1)S(1)} %compare_and_fusion.4) | copy-start | bytes 196
  11.9 6.0 %copy-start.3 = (f32[2,8,16,128]{3,2,1,0:T(8,128)S(1)}, f32[2,8,16,128]{3,2,1,0:T(8,128)}, u32[]{:S(2)}) copy-start(f32[2,8,16,128]{3,2,1,0:T(8,128)} %param.23) | copy-start | bytes 393220
  18.4 34.9 %collective-permute-start.3 = (f32[6,8,6,140]{3,2,1,0:T(8,128)S(1)}, f32[6,8,6,140]{3,2,1,0:T(8,128)S(1)}, u32[]{:S(2)}, u32[]{:S(2)}) collective-permute-start(f32[6,8,6,140]{3,2,1,0:T(8,128)S(1)} %get-tuple-element.96), channel_id=1, source_target_pairs={{1,0},{2,1},{3,2},{4,3},{5,4},{6,5},{7,6},{8,7},{9,8},{10,9},{11,1... | collective-permute-start | bytes 483848 | tf_op jit(solution)/shard_map/ppermute | solution.py:25
  25.9 27.4 %collective-permute-start.2 = (f32[6,8,6,140]{3,2,1,0:T(8,128)S(1)}, f32[6,8,6,140]{3,2,1,0:T(8,128)S(1)}, u32[]{:S(2)}, u32[]{:S(2)}) collective-permute-start(f32[6,8,6,140]{3,2,1,0:T(8,128)S(1)} %get-tuple-element.95), channel_id=1, source_target_pairs={{0,1},{1,2},{2,3},{3,4},{4,5},{5,6},{6,7},{7,8},{8,9},{9,10},{10,1... | collective-permute-start | bytes 483848 | tf_op jit(solution)/shard_map/ppermute | solution.py:24
  54.0 0.7 copy-start.12
  58.4 1.1 copy-start.15
  58.4 1.1 copy-start.16
  58.4 1.1 copy-start.17
  58.4 1.1 copy-start.18
  58.4 1.1 copy-start.19
  58.4 1.1 copy-start.20
  58.4 1.1 copy-start.33
  58.4 1.1 copy-start.34
  58.4 1.1 copy-start.38
  78.0 2.0 %copy-start.13 = (f32[2]{0:T(128)S(1)}, f32[2]{0:T(128)}, u32[]{:S(2)}) copy-start(f32[2]{0:T(128)} %constant.335.clone) | copy-start | bytes 28
  80.1 1.1 copy-start.22
  80.1 1.1 copy-start.24
  80.2 1.1 copy-start.36
  80.2 1.4 %copy-start.25 = (s32[64]{0:T(128)S(1)}, s32[64]{0:T(128)}, u32[]{:S(2)}) copy-start(s32[64]{0:T(128)} %get-tuple-element.270) | copy-start | bytes 772
  80.2 1.4 %copy-start.26 = (s32[64]{0:T(128)S(1)}, s32[64]{0:T(128)}, u32[]{:S(2)}) copy-start(s32[64]{0:T(128)} %get-tuple-element.271) | copy-start | bytes 772
  80.2 1.4 %copy-start.27 = (s32[64]{0:T(128)S(1)}, s32[64]{0:T(128)}, u32[]{:S(2)}) copy-start(s32[64]{0:T(128)} %get-tuple-element.272) | copy-start | bytes 772
  80.2 1.4 %copy-start.28 = (s32[64]{0:T(128)S(1)}, s32[64]{0:T(128)}, u32[]{:S(2)}) copy-start(s32[64]{0:T(128)} %get-tuple-element.273) | copy-start | bytes 772
  80.2 1.4 %copy-start.29 = (s32[64]{0:T(128)S(1)}, s32[64]{0:T(128)}, u32[]{:S(2)}) copy-start(s32[64]{0:T(128)} %get-tuple-element.274) | copy-start | bytes 772
  80.2 1.4 %copy-start.30 = (s32[64]{0:T(128)S(1)}, s32[64]{0:T(128)}, u32[]{:S(2)}) copy-start(s32[64]{0:T(128)} %get-tuple-element.275) | copy-start | bytes 772
  80.2 1.4 %copy-start.31 = (pred[64]{0:T(512)(128)(4,1)S(1)}, pred[64]{0:T(512)(128)(4,1)}, u32[]{:S(2)}) copy-start(pred[64]{0:T(512)(128)(4,1)} %get-tuple-element.268) | copy-start | bytes 196
  80.2 1.4 %copy-start.32 = (pred[64]{0:T(512)(128)(4,1)S(1)}, pred[64]{0:T(512)(128)(4,1)}, u32[]{:S(2)}) copy-start(pred[64]{0:T(512)(128)(4,1)} %get-tuple-element.269) | copy-start | bytes 196
  80.2 1.4 %copy-start.37 = (pred[64]{0:T(512)(128)(4,1)S(1)}, pred[64]{0:T(512)(128)(4,1)}, u32[]{:S(2)}) copy-start(pred[64]{0:T(512)(128)(4,1)} %compare_and_fusion.8) | copy-start | bytes 196
  80.8 21.3 %copy-start.14 = (f32[2]{0:T(128)S(1)}, f32[2]{0:T(128)}, u32[]{:S(2)}) copy-start(f32[2]{0:T(128)} %constant.336.clone) | copy-start | bytes 28
  99.9 3.1 %copy-start.4 = (f32[6,2,4,8]{3,2,1,0:T(4,128)S(1)}, f32[6,2,4,8]{3,2,1,0:T(4,128)}, u32[]{:S(2)}) copy-start(f32[6,2,4,8]{3,2,1,0:T(4,128)} %get-tuple-element.42) | copy-start | bytes 4612
  99.9 3.1 %copy-start.5 = (f32[6,2,4,32]{3,2,1,0:T(4,128)S(1)}, f32[6,2,4,32]{3,2,1,0:T(4,128)}, u32[]{:S(2)}) copy-start(f32[6,2,4,32]{3,2,1,0:T(4,128)} %get-tuple-element.43) | copy-start | bytes 18436
  99.9 3.1 %copy-start.6 = (f32[6,2,4,8]{3,2,1,0:T(4,128)S(1)}, f32[6,2,4,8]{3,2,1,0:T(4,128)}, u32[]{:S(2)}) copy-start(f32[6,2,4,8]{3,2,1,0:T(4,128)} %get-tuple-element.44) | copy-start | bytes 4612
  100.0 3.1 %copy-start.7 = (f32[6,2,4,8]{3,2,1,0:T(4,128)S(1)}, f32[6,2,4,8]{3,2,1,0:T(4,128)}, u32[]{:S(2)}) copy-start(f32[6,2,4,8]{3,2,1,0:T(4,128)} %get-tuple-element.45) | copy-start | bytes 4612
  100.0 3.1 %copy-start.8 = (f32[6,2,4,8]{3,2,1,0:T(4,128)S(1)}, f32[6,2,4,8]{3,2,1,0:T(4,128)}, u32[]{:S(2)}) copy-start(f32[6,2,4,8]{3,2,1,0:T(4,128)} %get-tuple-element.46) | copy-start | bytes 4612
  100.0 3.1 %copy-start.9 = (f32[6,2,4,8]{3,2,1,0:T(4,128)S(1)}, f32[6,2,4,8]{3,2,1,0:T(4,128)}, u32[]{:S(2)}) copy-start(f32[6,2,4,8]{3,2,1,0:T(4,128)} %get-tuple-element.47) | copy-start | bytes 4612
  100.0 3.1 %copy-start.10 = (f32[6,2,4,32]{3,2,1,0:T(4,128)S(1)}, f32[6,2,4,32]{3,2,1,0:T(4,128)}, u32[]{:S(2)}) copy-start(f32[6,2,4,32]{3,2,1,0:T(4,128)} %get-tuple-element.48) | copy-start | bytes 18436
  100.0 3.1 %copy-start.11 = (f32[6,2,4,8]{3,2,1,0:T(4,128)S(1)}, f32[6,2,4,8]{3,2,1,0:T(4,128)}, u32[]{:S(2)}) copy-start(f32[6,2,4,8]{3,2,1,0:T(4,128)} %get-tuple-element.49) | copy-start | bytes 4612

commit v8 on v6

--- a/solution.py
+++ b/solution.py
@@ -1,3 +1,4 @@
+import numpy as np
 import jax
 import jax.numpy as jnp
 from jax import lax
@@ -119,11 +120,10 @@
 def restrict(field):
     lead, depth, rows, cols = field.shape
     count = lead * depth * rows
-    pick_x = (lax.broadcasted_iota(jnp.int32, (cols, cols // 2), 0) // 2
-              == lax.broadcasted_iota(jnp.int32, (cols, cols // 2), 1)).astype(jnp.float32)
-    row = lax.broadcasted_iota(jnp.int32, (count // 4, count), 1)
+    pick_x = (np.arange(cols)[:, None] // 2 == np.arange(cols // 2)[None, :]).astype(np.float32)
+    row = np.arange(count)
     target = ((row // (depth * rows)) * (depth // 2) + (row // rows) % depth // 2) * (rows // 2) + row % rows // 2
-    pick_rows = (lax.broadcasted_iota(jnp.int32, (count // 4, count), 0) == target).astype(jnp.float32)
+    pick_rows = (np.arange(count // 4)[:, None] == target[None, :]).astype(np.float32)
     pairs = jnp.dot(field.reshape(count, cols), pick_x, precision=lax.Precision.HIGHEST)
     blocks = jnp.dot(pick_rows, pairs, precision=lax.Precision.HIGHEST)
     return (blocks * 0.125).reshape(lead, depth // 2, rows // 2, cols // 2)

time: 99.9 us -> 95.7 us (0.958)
  other arithmetic: 22 us -> 17.7 us
    sub x4 -> x0, other arithmetic: 1.2 us -> none  [restrict(): row // rows]
    div x10 -> x0, other arithmetic: 1.2 us -> none  [the longest x4 0.59 us: restrict(): row // rows]
    and x10 -> x0, other arithmetic: 1.16 us -> none  [the longest x3 0.6 us: restrict(): row % rows // 2]
  transfers between devices with their start and end apart: 14 -> 14, of which waited for: 7 -> 8; matrix products, arithmetic and copies ran while one was open for 11% -> 7% of each run, Pallas kernels for 21% -> 22%
where the time goes in v8:
time: 95.7 us; the launch traced here: 95.3 us
  starting transfers between devices  22.7 us (24%)
  Pallas kernels  20.7 us (22%)
  waiting for transfers between devices  17.8 us (19%)
  other arithmetic  17.7 us (18%)
  between operations  7.29 us (8%)
  local copies, waits for them, and re-layouts  7.06 us (7%)
  matrix products  2.02 us (2%)
    ppermute x7, starting transfers between devices, padded_along(): lax.ppermute(head, axis, [((i + distance) % count, i) for i in range(coun...  21.7 us
    pallas_call x2, Pallas kernels, gather_axis(): pl.pallas_call(lambda *refs: gather_kernel(axis, *refs), out_shape=jax.Sh...  20.7 us
    ppermute x7, waiting for transfers between devices, padded_along(): lax.ppermute(tail, axis, [(i, (i + distance) % count) for i in range(coun...  12.4 us
    ppermute x7, waiting for transfers between devices, padded_along(): lax.ppermute(head, axis, [((i + distance) % count, i) for i in range(coun...  5.38 us
    add x12, other arithmetic, chebyshev(): iterate = crop(iterate, halo + 1, halo) + update  4.35 us
    slice x30, local copies, waits for them, and re-layouts, shrunk_neighbours(): along_z = jnp.roll(centre, 1, 1) + jnp.roll(centre, -1, 1)  3.45 us
    add x17, other arithmetic, operate(): first = coeff[0] * centre[0] + coeff[1] * centre[1]  3.15 us
    reduce_max x2, other arithmetic, global_max(): block = jnp.max(gather_axis(block, axis, tag), axis=0)  2.3 us
  transfers between devices with their start and end apart: 14, of which 8 were waited for; matrix products, arithmetic and copies ran while one was open for 7% of the time, Pallas kernels for 22%

profile of v8, /device:TPU:0, one launch (start us, length us, event | category | flops | bytes accessed | tf_op | source)
XLA Modules:
  0.0 95.3 jit_solution(16049209449961131001)
XLA Ops:
  0.0 1.1 %pad_maximum_fusion.6 = f32[6,8,16,128]{3,2,1,0:T(8,128)S(1)} fusion(f32[2,8,16,128]{3,2,1,0:T(8,128)} %param.31, f32[1,8,16,128]{3,2,1,0:T(8,128)} %bitcast.86, f32[1,8,16,128]{3,2,1,0:T(8,128)} %bitcast.89, f32[2,8,16,128]{3,2,1,0:T(8,128)} %param.30), kind=kLoop, calls=%fused_computation.66 | loop fusion | flops 294912 | bytes 786432 | tf_op jit(solution)/shard_map/concatenate | solution.py:218
  1.3 0.5 collective-permute-start.1
  1.9 0.6 fusion.107
  3.8 0.4 fusion.233
  4.2 0.4 convolution_multiply_fusion.1
  4.6 0.7 fusion.167
  5.7 0.7 fusion.188
  9.0 0.6 select_select_fusion.refs_0_
  9.6 0.7 collective-permute-done
  10.2 0.4 pad_maximum_fusion.1
  10.7 8.4 %collective-permute-start.3 = (f32[6,8,6,140]{3,2,1,0:T(8,128)S(1)}, f32[6,8,6,140]{3,2,1,0:T(8,128)S(1)}, u32[]{:S(2)}, u32[]{:S(2)}) collective-permute-start(f32[6,8,6,140]{3,2,1,0:T(8,128)S(1)} %get-tuple-element.52), channel_id=1, source_target_pairs={{1,0},{2,1},{3,2},{4,3},{5,4},{6,5},{7,6},{8,7},{9,8},{10,9},{11,1... | collective-permute-start | bytes 483848 | tf_op jit(solution)/shard_map/ppermute | solution.py:26
  19.2 6.8 %shard_map.280 = f32[8,8,128]{2,1,0:T(8,128)} custom-call(f32[8,128]{1,0:T(8,128)} %select_select_fusion.refs_0_), custom_call_target="tpu_custom_call" | custom-call | tf_op jit(solution)/shard_map/pallas_call | solution.py:99
  26.0 1.4 %reduce_max.78.refs_0_ = f32[8,128]{1,0:T(8,128)} reduce(f32[8,8,128]{2,1,0:T(8,128)} %shard_map.280, f32[]{:T(128)} %constant.31.clone.1), dimensions={0}, to_apply=%region_6.7 | reduce | flops 7168 | bytes 36868 | tf_op jit(solution)/shard_map/reduce_max | solution.py:116
  27.3 13.9 %shard_map.281 = f32[32,8,128]{2,1,0:T(8,128)} custom-call(f32[8,128]{1,0:T(8,128)} %reduce_max.78.refs_0_), custom_call_target="tpu_custom_call" | custom-call | tf_op jit(solution)/shard_map/pallas_call | solution.py:99
  41.3 0.9 reduce_max.79
  42.2 0.7 fusion.232
  44.1 0.4 fusion.42
  44.6 0.3 fusion.199
  44.9 0.4 subtract_bitcast_fusion
  45.3 0.8 fusion.12
  46.2 0.2 fusion.202
  46.4 0.4 fusion.54
  46.9 0.6 slice_add_fusion.12
  47.5 0.4 fusion.52
  48.0 0.2 fusion.212
  48.2 0.7 fusion.33
  49.8 0.3 fusion.235
  50.7 0.3 collective-permute-start.4
  51.0 1.9 %collective-permute-done.5 = f32[6,4,8,7]{3,2,1,0:T(8,128)S(1)} collective-permute-done((f32[6,4,8,7]{3,2,1,0:T(8,128)S(1)}, f32[6,4,8,7]{3,2,1,0:T(8,128)S(1)}, u32[]{:S(2)}, u32[]{:S(2)}) %collective-permute-start.5) | collective-permute-done | bytes 5408 | tf_op jit(solution)/shard_map/ppermute | solution.py:26
  52.9 3.0 %collective-permute-done.4 = f32[6,4,8,7]{3,2,1,0:T(8,128)S(1)} collective-permute-done((f32[6,4,8,7]{3,2,1,0:T(8,128)S(1)}, f32[6,4,8,7]{3,2,1,0:T(8,128)S(1)}, u32[]{:S(2)}, u32[]{:S(2)}) %collective-permute-start.4) | collective-permute-done | bytes 5408 | tf_op jit(solution)/shard_map/ppermute | solution.py:25
  56.1 4.5 %collective-permute-start.7 = (f32[6,4,7,78]{3,2,1,0:T(8,128)S(1)}, f32[6,4,7,78]{3,2,1,0:T(8,128)S(1)}, u32[]{:S(2)}, u32[]{:S(2)}) collective-permute-start(f32[6,4,7,78]{3,2,1,0:T(8,128)S(1)} %get-tuple-element.130), channel_id=1, source_target_pairs={{1,0},{2,1},{3,2},{4,3},{5,4},{6,5},{7,6},{8,7},{9,8},{10,9},{11,1... | collective-permute-start | bytes 157256 | tf_op jit(solution)/shard_map/ppermute | solution.py:26
  61.4 1.4 %collective-permute-done.7 = f32[6,4,7,78]{3,2,1,0:T(8,128)S(1)} collective-permute-done((f32[6,4,7,78]{3,2,1,0:T(8,128)S(1)}, f32[6,4,7,78]{3,2,1,0:T(8,128)S(1)}, u32[]{:S(2)}, u32[]{:S(2)}) %collective-permute-start.7) | collective-permute-done | bytes 52448 | tf_op jit(solution)/shard_map/ppermute | solution.py:26
  62.8 5.7 %collective-permute-done.6 = f32[6,4,7,78]{3,2,1,0:T(8,128)S(1)} collective-permute-done((f32[6,4,7,78]{3,2,1,0:T(8,128)S(1)}, f32[6,4,7,78]{3,2,1,0:T(8,128)S(1)}, u32[]{:S(2)}, u32[]{:S(2)}) %collective-permute-start.6) | collective-permute-done | bytes 52448 | tf_op jit(solution)/shard_map/ppermute | solution.py:25
  70.8 0.5 collective-permute-start.8
  71.3 1.0 %collective-permute-done.9 = f32[6,2,4,8]{3,2,1,0:T(4,128)S(1)} collective-permute-done((f32[6,2,4,8]{3,2,1,0:T(4,128)S(1)}, f32[6,2,4,8]{3,2,1,0:T(4,128)S(1)}, u32[]{:S(2)}, u32[]{:S(2)}) %collective-permute-start.9) | collective-permute-done | bytes 1568 | tf_op jit(solution)/shard_map/ppermute | solution.py:26
  72.3 3.0 %collective-permute-done.8 = f32[6,2,4,8]{3,2,1,0:T(4,128)S(1)} collective-permute-done((f32[6,2,4,8]{3,2,1,0:T(4,128)S(1)}, f32[6,2,4,8]{3,2,1,0:T(4,128)S(1)}, u32[]{:S(2)}, u32[]{:S(2)}) %collective-permute-start.8) | collective-permute-done | bytes 1568 | tf_op jit(solution)/shard_map/ppermute | solution.py:25
  75.6 5.3 %collective-permute-start.12 = (f32[6,2,4,48]{3,2,1,0:T(4,128)S(1)}, f32[6,2,4,48]{3,2,1,0:T(4,128)S(1)}, u32[]{:S(2)}, u32[]{:S(2)}) collective-permute-start(f32[6,2,4,48]{3,2,1,0:T(4,128)S(1)} %pad_maximum_fusion.17), channel_id=1, source_target_pairs={{1,0},{2,1},{3,2},{4,3},{5,4},{6,5},{7,6},{8,7},{9,8},{10,9},{11,1... | collective-permute-start | bytes 27656 | tf_op jit(solution)/shard_map/ppermute | solution.py:26
  80.9 2.8 %collective-permute-start.13 = (f32[6,2,4,48]{3,2,1,0:T(4,128)S(1)}, f32[6,2,4,48]{3,2,1,0:T(4,128)S(1)}, u32[]{:S(2)}, u32[]{:S(2)}) collective-permute-start(f32[6,2,4,48]{3,2,1,0:T(4,128)S(1)} %pad_maximum_fusion.17), channel_id=1, source_target_pairs={{2,0},{3,1},{4,2},{5,3},{6,4},{7,5},{8,6},{9,7},{10,8},{11,9},{12,... | collective-permute-start | bytes 27656 | tf_op jit(solution)/shard_map/ppermute | solution.py:26
  84.7 1.1 %collective-permute-done.13 = f32[6,2,4,48]{3,2,1,0:T(4,128)S(1)} collective-permute-done((f32[6,2,4,48]{3,2,1,0:T(4,128)S(1)}, f32[6,2,4,48]{3,2,1,0:T(4,128)S(1)}, u32[]{:S(2)}, u32[]{:S(2)}) %collective-permute-start.13) | collective-permute-done | bytes 9248 | tf_op jit(solution)/shard_map/ppermute | solution.py:26
  89.7 0.3 copy.51
  90.1 0.3 slice.2057
  90.4 0.7 copy.54
  91.2 0.4 fusion.50
  91.7 0.2 fusion.208
  91.9 0.6 slice_add_fusion.7
  92.5 0.4 fusion.48
  93.3 0.7 slice_add_fusion.4
  94.4 0.9 fusion.62
  (132 shorter events, 10.0 us)
Async XLA Ops:
  0.0 1.9 %copy-start = (f32[2,8,16,128]{3,2,1,0:T(8,128)S(1)}, f32[2,8,16,128]{3,2,1,0:T(8,128)}, u32[]{:S(2)}) copy-start(f32[2,8,16,128]{3,2,1,0:T(8,128)} %param.30) | copy-start | bytes 393220
  0.0 1.9 %copy-start.1 = (f32[8,16,128]{2,1,0:T(8,128)S(1)}, f32[8,16,128]{2,1,0:T(8,128)}, u32[]{:S(2)}) copy-start(f32[8,16,128]{2,1,0:T(8,128)} %param.33) | copy-start | bytes 196612
  0.0 1.9 %copy-start.2 = (f32[8,16,128]{2,1,0:T(8,128)S(1)}, f32[8,16,128]{2,1,0:T(8,128)}, u32[]{:S(2)}) copy-start(f32[8,16,128]{2,1,0:T(8,128)} %param.32) | copy-start | bytes 196612
  0.0 3.8 %copy-start.4 = (f32[128,64]{1,0:T(8,128)S(1)}, f32[128,64]{1,0:T(8,128)}, u32[]{:S(2)}) copy-start(f32[128,64]{1,0:T(8,128)} %constant.21.clone) | copy-start | bytes 98308
  1.1 3.1 %copy-start.6 = (f32[128,512]{1,0:T(8,128)S(1)}, f32[128,512]{1,0:T(8,128)}, u32[]{:S(2)}) copy-start(f32[128,512]{1,0:T(8,128)} %constant.22.clone) | copy-start | bytes 786436
  1.1 4.2 %copy-start.7 = (f32[64,32]{1,0:T(8,128)S(1)}, f32[64,32]{1,0:T(8,128)}, u32[]{:S(2)}) copy-start(f32[64,32]{1,0:T(8,128)} %constant.23.clone) | copy-start | bytes 24580
  1.1 4.4 %copy-start.12 = (f32[32,128]{1,0:T(8,128)S(1)}, f32[32,128]{1,0:T(8,128)}, u32[]{:S(2)}) copy-start(f32[32,128]{1,0:T(8,128)} %constant.24.clone) | copy-start | bytes 49156
  1.2 9.1 %copy-start.3 = (f32[2,8,16,128]{3,2,1,0:T(8,128)S(1)}, f32[2,8,16,128]{3,2,1,0:T(8,128)}, u32[]{:S(2)}) copy-start(f32[2,8,16,128]{3,2,1,0:T(8,128)} %param.31) | copy-start | bytes 393220
  1.3 8.2 %collective-permute-start.1 = (f32[6,8,16,6]{3,2,1,0:T(8,128)S(1)}, f32[6,8,16,6]{3,2,1,0:T(8,128)S(1)}, u32[]{:S(2)}, u32[]{:S(2)}) collective-permute-start(f32[6,8,16,6]{3,2,1,0:T(8,128)S(1)} %get-tuple-element.90), channel_id=1, source_target_pairs={{32,0},{64,32},{96,64},{128,96},{160,128},{192,160},{224,192},{0,2... | collective-permute-start | bytes 55304 | tf_op jit(solution)/shard_map/ppermute | solution.py:26
  1.8 8.4 %collective-permute-start = (f32[6,8,16,6]{3,2,1,0:T(8,128)S(1)}, f32[6,8,16,6]{3,2,1,0:T(8,128)S(1)}, u32[]{:S(2)}, u32[]{:S(2)}) collective-permute-start(f32[6,8,16,6]{3,2,1,0:T(8,128)S(1)} %get-tuple-element.89), channel_id=1, source_target_pairs={{0,32},{32,64},{64,96},{96,128},{128,160},{160,192},{192,224},{224... | collective-permute-start | bytes 55304 | tf_op jit(solution)/shard_map/ppermute | solution.py:25
  10.7 33.1 %collective-permute-start.3 = (f32[6,8,6,140]{3,2,1,0:T(8,128)S(1)}, f32[6,8,6,140]{3,2,1,0:T(8,128)S(1)}, u32[]{:S(2)}, u32[]{:S(2)}) collective-permute-start(f32[6,8,6,140]{3,2,1,0:T(8,128)S(1)} %get-tuple-element.52), channel_id=1, source_target_pairs={{1,0},{2,1},{3,2},{4,3},{5,4},{6,5},{7,6},{8,7},{9,8},{10,9},{11,1... | collective-permute-start | bytes 483848 | tf_op jit(solution)/shard_map/ppermute | solution.py:26
  19.1 24.8 %collective-permute-start.2 = (f32[6,8,6,140]{3,2,1,0:T(8,128)S(1)}, f32[6,8,6,140]{3,2,1,0:T(8,128)S(1)}, u32[]{:S(2)}, u32[]{:S(2)}) collective-permute-start(f32[6,8,6,140]{3,2,1,0:T(8,128)S(1)} %get-tuple-element.51), channel_id=1, source_target_pairs={{0,1},{1,2},{2,3},{3,4},{4,5},{5,6},{6,7},{7,8},{8,9},{9,10},{10,1... | collective-permute-start | bytes 483848 | tf_op jit(solution)/shard_map/ppermute | solution.py:25
  44.6 0.7 copy-start.10
  48.9 0.8 copy-start.5
  49.0 1.1 %copy-start.9 = (f32[64,256]{1,0:T(8,128)S(1)}, f32[64,256]{1,0:T(8,128)}, u32[]{:S(2)}) copy-start(f32[64,256]{1,0:T(8,128)} %constant.26.clone) | copy-start | bytes 196612
  50.5 2.4 %collective-permute-start.5 = (f32[6,4,8,7]{3,2,1,0:T(8,128)S(1)}, f32[6,4,8,7]{3,2,1,0:T(8,128)S(1)}, u32[]{:S(2)}, u32[]{:S(2)}) collective-permute-start(f32[6,4,8,7]{3,2,1,0:T(8,128)S(1)} %get-tuple-element.132), channel_id=1, source_target_pairs={{32,0},{64,32},{96,64},{128,96},{160,128},{192,160},{224,192},{0,2... | collective-permute-start | bytes 16136 | tf_op jit(solution)/shard_map/ppermute | solution.py:26
  50.7 18.4 %copy-start.11 = (f32[2]{0:T(128)S(1)}, f32[2]{0:T(128)}, u32[]{:S(2)}) copy-start(f32[2]{0:T(128)} %constant.84.clone) | copy-start | bytes 28
  50.7 5.3 %collective-permute-start.4 = (f32[6,4,8,7]{3,2,1,0:T(8,128)S(1)}, f32[6,4,8,7]{3,2,1,0:T(8,128)S(1)}, u32[]{:S(2)}, u32[]{:S(2)}) collective-permute-start(f32[6,4,8,7]{3,2,1,0:T(8,128)S(1)} %get-tuple-element.131), channel_id=1, source_target_pairs={{0,32},{32,64},{64,96},{96,128},{128,160},{160,192},{192,224},{224... | collective-permute-start | bytes 16136 | tf_op jit(solution)/shard_map/ppermute | solution.py:25
  56.1 6.7 %collective-permute-start.7 = (f32[6,4,7,78]{3,2,1,0:T(8,128)S(1)}, f32[6,4,7,78]{3,2,1,0:T(8,128)S(1)}, u32[]{:S(2)}, u32[]{:S(2)}) collective-permute-start(f32[6,4,7,78]{3,2,1,0:T(8,128)S(1)} %get-tuple-element.130), channel_id=1, source_target_pairs={{1,0},{2,1},{3,2},{4,3},{5,4},{6,5},{7,6},{8,7},{9,8},{10,9},{11,1... | collective-permute-start | bytes 157256 | tf_op jit(solution)/shard_map/ppermute | solution.py:26
  60.6 7.9 %collective-permute-start.6 = (f32[6,4,7,78]{3,2,1,0:T(8,128)S(1)}, f32[6,4,7,78]{3,2,1,0:T(8,128)S(1)}, u32[]{:S(2)}, u32[]{:S(2)}) collective-permute-start(f32[6,4,7,78]{3,2,1,0:T(8,128)S(1)} %get-tuple-element.129), channel_id=1, source_target_pairs={{0,1},{1,2},{2,3},{3,4},{4,5},{5,6},{6,7},{7,8},{8,9},{9,10},{10,1... | collective-permute-start | bytes 157256 | tf_op jit(solution)/shard_map/ppermute | solution.py:25
  69.3 1.0 %copy-start.8 = (f32[64,32]{1,0:T(8,128)S(1)}, f32[64,32]{1,0:T(8,128)}, u32[]{:S(2)}) copy-start(f32[64,32]{1,0:T(8,128)} %constant.23.clone) | copy-start | bytes 24580
  69.3 1.2 %copy-start.14 = (f32[16,64]{1,0:T(8,128)S(1)}, f32[16,64]{1,0:T(8,128)}, u32[]{:S(2)}) copy-start(f32[16,64]{1,0:T(8,128)} %constant.85.clone) | copy-start | bytes 12292
  69.7 16.4 %copy-start.13 = (f32[2]{0:T(128)S(1)}, f32[2]{0:T(128)}, u32[]{:S(2)}) copy-start(f32[2]{0:T(128)} %constant.86.clone) | copy-start | bytes 28
  70.8 1.5 %collective-permute-start.9 = (f32[6,2,4,8]{3,2,1,0:T(4,128)S(1)}, f32[6,2,4,8]{3,2,1,0:T(4,128)S(1)}, u32[]{:S(2)}, u32[]{:S(2)}) collective-permute-start(f32[6,2,4,8]{3,2,1,0:T(4,128)S(1)} %get-tuple-element.186), channel_id=1, source_target_pairs={{32,0},{64,32},{96,64},{128,96},{160,128},{192,160},{224,192},{0,2... | collective-permute-start | bytes 4616 | tf_op jit(solution)/shard_map/ppermute | solution.py:26
  70.8 4.5 %collective-permute-start.8 = (f32[6,2,4,8]{3,2,1,0:T(4,128)S(1)}, f32[6,2,4,8]{3,2,1,0:T(4,128)S(1)}, u32[]{:S(2)}, u32[]{:S(2)}) collective-permute-start(f32[6,2,4,8]{3,2,1,0:T(4,128)S(1)} %get-tuple-element.185), channel_id=1, source_target_pairs={{0,32},{32,64},{64,96},{96,128},{128,160},{160,192},{192,224},{224... | collective-permute-start | bytes 4616 | tf_op jit(solution)/shard_map/ppermute | solution.py:25
  75.4 9.3 %collective-permute-start.10 = (f32[6,2,4,48]{3,2,1,0:T(4,128)S(1)}, f32[6,2,4,48]{3,2,1,0:T(4,128)S(1)}, u32[]{:S(2)}, u32[]{:S(2)}) collective-permute-start(f32[6,2,4,48]{3,2,1,0:T(4,128)S(1)} %pad_maximum_fusion.17), channel_id=1, source_target_pairs={{0,2},{1,3},{2,4},{3,5},{4,6},{5,7},{6,8},{7,9},{8,10},{9,11},{10,... | collective-permute-start | bytes 27656 | tf_op jit(solution)/shard_map/ppermute | solution.py:25
  75.5 9.2 %collective-permute-start.11 = (f32[6,2,4,48]{3,2,1,0:T(4,128)S(1)}, f32[6,2,4,48]{3,2,1,0:T(4,128)S(1)}, u32[]{:S(2)}, u32[]{:S(2)}) collective-permute-start(f32[6,2,4,48]{3,2,1,0:T(4,128)S(1)} %pad_maximum_fusion.17), channel_id=1, source_target_pairs={{0,1},{1,2},{2,3},{3,4},{4,5},{5,6},{6,7},{7,8},{8,9},{9,10},{10,1... | collective-permute-start | bytes 27656 | tf_op jit(solution)/shard_map/ppermute | solution.py:25
  75.6 9.1 %collective-permute-start.12 = (f32[6,2,4,48]{3,2,1,0:T(4,128)S(1)}, f32[6,2,4,48]{3,2,1,0:T(4,128)S(1)}, u32[]{:S(2)}, u32[]{:S(2)}) collective-permute-start(f32[6,2,4,48]{3,2,1,0:T(4,128)S(1)} %pad_maximum_fusion.17), channel_id=1, source_target_pairs={{1,0},{2,1},{3,2},{4,3},{5,4},{6,5},{7,6},{8,7},{9,8},{10,9},{11,1... | collective-permute-start | bytes 27656 | tf_op jit(solution)/shard_map/ppermute | solution.py:26
  80.9 4.8 %collective-permute-start.13 = (f32[6,2,4,48]{3,2,1,0:T(4,128)S(1)}, f32[6,2,4,48]{3,2,1,0:T(4,128)S(1)}, u32[]{:S(2)}, u32[]{:S(2)}) collective-permute-start(f32[6,2,4,48]{3,2,1,0:T(4,128)S(1)} %pad_maximum_fusion.17), channel_id=1, source_target_pairs={{2,0},{3,1},{4,2},{5,3},{6,4},{7,5},{8,6},{9,7},{10,8},{11,9},{12,... | collective-permute-start | bytes 27656 | tf_op jit(solution)/shard_map/ppermute | solution.py:26

commit v9 on v8

--- a/solution.py
+++ b/solution.py
@@ -27,6 +27,45 @@
         remaining -= take
         distance += 1
     return jnp.concatenate(below + [cells] + above, axis=dim)
+
+
+def segments(width, size):
+    below, above = [], []
+    remaining, distance = width, 1
+    while remaining > 0:
+        take = min(remaining, size)
+        below.insert(0, (-distance, size - take, size))
+        above.append((distance, 0, take))
+        remaining -= take
+        distance += 1
+    return below + [(0, 0, size)] + above
+
+
+def padded_at_once(cells, width):
+    rows, cols = cells.shape[2], cells.shape[3]
+    count_x = lax.axis_size("gx")
+    count_y = lax.axis_size("gy")
+    runs_y, runs_x = segments(width, rows), segments(width, cols)
+    bands = []
+    for step_y, first_y, last_y in runs_y:
+        band = []
+        for step_x, first_x, last_x in runs_x:
+            if (step_y, step_x) == (0, 0):
+                band.append(cells)
+                continue
+            piece = cells[:, :, first_y:last_y, first_x:last_x]
+            if step_y == 0:
+                pairs = [(i, (i - step_x) % count_x) for i in range(count_x)]
+                band.append(lax.ppermute(piece, "gx", pairs))
+            elif step_x == 0:
+                pairs = [(i, (i - step_y) % count_y) for i in range(count_y)]
+                band.append(lax.ppermute(piece, "gy", pairs))
+            else:
+                pairs = [(i * count_y + j, ((i - step_x) % count_x) * count_y + (j - step_y) % count_y)
+                         for i in range(count_x) for j in range(count_y)]
+                band.append(lax.ppermute(piece, ("gx", "gy"), pairs))
+        bands.append(jnp.concatenate(band, axis=3))
+    return jnp.concatenate(bands, axis=2)
 
 
 def padded(cells, width):
@@ -215,11 +254,9 @@
     for level, level_fields in enumerate((fields, fields_1, fields_2)):
         _, first, second = coefficients(level_fields, level)
         local = jnp.where(lane == level, jnp.maximum(jnp.max(first), jnp.max(second)), local)
-    wide_x = padded_along(jnp.concatenate([fields, previous], 0), 6, "gx", 3)
-    local, wide_x = lax.optimization_barrier((local, wide_x))
+    wide = padded_at_once(jnp.concatenate([fields, previous], 0), 6)
     spreads = global_max(local)[0]
 
-    wide = padded_along(wide_x, 6, "gy", 2)
     ops_0 = Level(coefficients(crop(wide[:4], 6, 5), 0)[0], 5, 0)
     state_w = wide[:2]
     substrate, catalyst = crop(state_w[0], 6, 5), crop(state_w[1], 6, 5)
@@ -237,7 +274,7 @@
     pre_0, pre_0_halo = chebyshev(ops_0, source_0, 5, None, None, spreads[0])
     resid_0 = crop(source_0, 5, 0) - ops_0.operate(crop(pre_0, pre_0_halo, 1), 1)
 
-    wide_1 = padded(jnp.concatenate([restrict(resid_0), fields_1], 0), 7)
+    wide_1 = padded_at_once(jnp.concatenate([restrict(resid_0), fields_1], 0), 7)
     ops_1 = Level(coefficients(wide_1[2:], 1)[0], 7, 1)
     source_1 = wide_1[:2]
     pre_1, pre_1_halo = chebyshev(ops_1, source_1, 7, None, None, spreads[1])

time: 95.7 us -> 117 us (1.22)
  starting transfers between devices: 22.7 us -> 33.9 us
  waiting for transfers between devices: 17.8 us -> 27.2 us
  other arithmetic: 17.7 us -> 19.5 us
    ppermute x0 -> x16, starting transfers between devices: none -> 23.9 us  [the longest x8 18.2 us: padded_at_once(): band.append(lax.ppermute(piece, ('gx', 'gy'), pairs))]
    ppermute x0 -> x16, waiting for transfers between devices: none -> 21.6 us  [the longest x8 21.6 us: padded_at_once(): band.append(lax.ppermute(piece, ('gx', 'gy'), pairs))]
    ppermute x7 -> x3, starting transfers between devices: 21.7 us -> 9.86 us  [padded_along(): lax.ppermute(head, axis, [((i + distance) % count, i) for i in range(coun...]
    ppermute x7 -> x3, waiting for transfers between devices: 12.4 us -> 2.95 us  [padded_along(): lax.ppermute(tail, axis, [(i, (i + distance) % count) for i in range(coun...]
    ppermute x7 -> x3, waiting for transfers between devices: 5.38 us -> 2.58 us  [padded_along(): lax.ppermute(head, axis, [((i + distance) % count, i) for i in range(coun...]
    concatenate x2 -> x6, other arithmetic: 1.2 us -> 3.82 us  [the longest x2 2.53 us: padded_at_once(): return jnp.concatenate(bands, axis=2)]
    slice x30 -> x31, local copies, waits for them, and re-layouts: 3.45 us -> 3.55 us  [shrunk_neighbours(): along_z = jnp.roll(centre, 1, 1) + jnp.roll(centre, -1, 1)]
  transfers between devices with their start and end apart: 14 -> 22, of which waited for: 8 -> 7; matrix products, arithmetic and copies ran while one was open for 7% -> 6% of each run, Pallas kernels for 22% -> 17%
where the time goes in v9:
time: 117 us
  starting transfers between devices  33.9 us (29%)
  waiting for transfers between devices  27.2 us (23%)
  Pallas kernels  19.6 us (17%)
  other arithmetic  19.5 us (17%)
  between operations  7.59 us (6%)
  local copies, waits for them, and re-layouts  7.07 us (6%)
  matrix products  2.03 us (2%)
    ppermute x8, waiting for transfers between devices, padded_at_once(): band.append(lax.ppermute(piece, ('gx', 'gy'), pairs))  21.6 us
    pallas_call x2, Pallas kernels, gather_axis(): pl.pallas_call(lambda *refs: gather_kernel(axis, *refs), out_shape=jax.Sh...  19.6 us
    ppermute x8, starting transfers between devices, padded_at_once(): band.append(lax.ppermute(piece, ('gx', 'gy'), pairs))  18.2 us
    ppermute x3, starting transfers between devices, padded_along(): lax.ppermute(head, axis, [((i + distance) % count, i) for i in range(coun...  9.86 us
    add x12, other arithmetic, chebyshev(): iterate = crop(iterate, halo + 1, halo) + update  4.36 us
    ppermute x4, starting transfers between devices, padded_at_once(): band.append(lax.ppermute(piece, 'gy', pairs))  4.13 us
    slice x31, local copies, waits for them, and re-layouts, shrunk_neighbours(): along_z = jnp.roll(centre, 1, 1) + jnp.roll(centre, -1, 1)  3.55 us
    add x17, other arithmetic, operate(): first = coeff[0] * centre[0] + coeff[1] * centre[1]  3.15 us
  transfers between devices with their start and end apart: 22, of which 7 were waited for; matrix products, arithmetic and copies ran while one was open for 6% of the time, Pallas kernels for 17%

profile of v9, /device:TPU:0, one launch (start us, length us, event | category | flops | bytes accessed | tf_op | source)
XLA Modules:
  0.0 116.9 jit_solution(9490037300634000107)
XLA Ops:
  0.0 1.1 pad_maximum_fusion
  1.3 8.3 %collective-permute-start.7 = (f32[6,8,6,6]{3,2,1,0:T(8,128)S(1)}, f32[6,8,6,6]{3,2,1,0:T(8,128)S(1)}, u32[]{:S(2)}, u32[]{:S(2)}) collective-permute-start(f32[6,8,6,6]{3,2,1,0:T(8,128)S(1)} %get-tuple-element.87), channel_id=1, source_target_pairs={{0,255},{1,224},{2,225},{3,226},{4,227},{5,228},{6,229},{7,230},{8... | collective-permute-start | bytes 20744 | tf_op jit(solution)/shard_map/ppermute | solution.py:66
  9.6 1.1 collective-permute-start.6
  10.7 3.9 %collective-permute-start.2 = (f32[6,8,6,6]{3,2,1,0:T(8,128)S(1)}, f32[6,8,6,6]{3,2,1,0:T(8,128)}, u32[]{:S(2)}, u32[]{:S(2)}) collective-permute-start(f32[6,8,6,6]{3,2,1,0:T(8,128)S(1)} %get-tuple-element.88), channel_id=1, source_target_pairs={{0,225},{1,226},{2,227},{3,228},{4,229},{5,230},{6,231},{7,232},{8... | collective-permute-start | bytes 20744 | tf_op jit(solution)/shard_map/ppermute | solution.py:66
  14.6 1.0 collective-permute-start.1
  15.8 0.7 fusion.111
  17.9 0.4 fusion.238
  18.3 0.4 convolution_multiply_fusion.1
  18.7 0.8 fusion.171
  19.9 0.7 fusion.192
  23.2 0.6 select_select_fusion.refs_0_
  23.8 6.6 %shard_map.280 = f32[8,8,128]{2,1,0:T(8,128)} custom-call(f32[8,128]{1,0:T(8,128)} %select_select_fusion.refs_0_), custom_call_target="tpu_custom_call" | custom-call | tf_op jit(solution)/shard_map/pallas_call | solution.py:138
  30.4 1.4 %reduce_max.78.refs_0_ = f32[8,128]{1,0:T(8,128)} reduce(f32[8,8,128]{2,1,0:T(8,128)} %shard_map.280, f32[]{:T(128)} %constant.35.clone.1), dimensions={0}, to_apply=%region_6.7 | reduce | flops 7168 | bytes 36868 | tf_op jit(solution)/shard_map/reduce_max | solution.py:155
  31.8 13.0 %shard_map.281 = f32[32,8,128]{2,1,0:T(8,128)} custom-call(f32[8,128]{1,0:T(8,128)} %reduce_max.78.refs_0_), custom_call_target="tpu_custom_call" | custom-call | tf_op jit(solution)/shard_map/pallas_call | solution.py:138
  44.8 0.9 reduce_max.79
  45.8 0.5 collective-permute-start.3
  46.3 1.0 collective-permute-start
  47.3 0.7 fusion.237
  48.9 9.7 %collective-permute-done = f32[6,8,6,6]{3,2,1,0:T(8,128)S(1)} collective-permute-done((f32[6,8,6,6]{3,2,1,0:T(8,128)S(1)}, f32[6,8,6,6]{3,2,1,0:T(8,128)S(1)}, u32[]{:S(2)}, u32[]{:S(2)}) %collective-permute-start) | collective-permute-done | bytes 6944 | tf_op jit(solution)/shard_map/ppermute | solution.py:66
  58.6 2.2 %maximum_maximum_fusion = f32[6,8,28,140]{3,2,1,0:T(8,128)S(1)} fusion(f32[6,8,6,6]{3,2,1,0:T(8,128)S(1)} %collective-permute-done.7, f32[6,8,6,128]{3,2,1,0:T(8,128)} %collective-permute-done.6, f32[6,8,6,6]{3,2,1,0:T(8,128)} %collective-permute-done.5, f32[6,8,16,6]{3,2,1,0:T(8,128)S(1)} %collective-permute-done.4, f32[2,8,16,128]{3,2,1,0:T(8,128)S(1)} %copy-done.3, ...), kind=kLoop, calls=%fused_computation | loop fusion | flops 2069760 | bytes 1505280 | tf_op jit(solution)/shard_map/concatenate | solution.py:68
  60.8 0.4 fusion.39
  61.7 0.4 subtract_bitcast_fusion
  62.1 0.8 fusion.9
  63.2 0.4 fusion.51
  63.6 0.6 slice_add_fusion.12
  64.3 0.4 fusion.49
  65.0 0.7 fusion.30
  67.1 1.2 %collective-permute-start.15 = (f32[6,4,7,7]{3,2,1,0:T(8,128)S(1)}, f32[6,4,7,7]{3,2,1,0:T(8,128)S(1)}, u32[]{:S(2)}, u32[]{:S(2)}) collective-permute-start(f32[6,4,7,7]{3,2,1,0:T(8,128)S(1)} %get-tuple-element.134), channel_id=1, source_target_pairs={{0,255},{1,224},{2,225},{3,226},{4,227},{5,228},{6,229},{7,230},{8... | collective-permute-start | bytes 14120 | tf_op jit(solution)/shard_map/ppermute | solution.py:66
  68.4 1.3 %collective-permute-start.14 = (f32[6,4,7,64]{3,2,1,0:T(8,128)S(1)}, f32[6,4,7,64]{3,2,1,0:T(8,128)S(1)}, u32[]{:S(2)}, u32[]{:S(2)}) collective-permute-start(f32[6,4,7,64]{3,2,1,0:T(8,128)S(1)} %get-tuple-element.136), channel_id=1, source_target_pairs={{0,31},{1,0},{2,1},{3,2},{4,3},{5,4},{6,5},{7,6},{8,7},{9,8},{10,9... | collective-permute-start | bytes 129032 | tf_op jit(solution)/shard_map/ppermute | solution.py:62
  69.6 0.8 collective-permute-start.13
  70.5 3.0 %collective-permute-start.10 = (f32[6,4,7,7]{3,2,1,0:T(8,128)S(1)}, f32[6,4,7,7]{3,2,1,0:T(8,128)S(1)}, u32[]{:S(2)}, u32[]{:S(2)}) collective-permute-start(f32[6,4,7,7]{3,2,1,0:T(8,128)S(1)} %get-tuple-element.132), channel_id=1, source_target_pairs={{0,225},{1,226},{2,227},{3,228},{4,229},{5,230},{6,231},{7,232},{8... | collective-permute-start | bytes 14120 | tf_op jit(solution)/shard_map/ppermute | solution.py:66
  73.5 0.7 collective-permute-start.9
  74.6 1.3 %collective-permute-done.13 = f32[6,4,7,7]{3,2,1,0:T(8,128)S(1)} collective-permute-done((f32[6,4,7,7]{3,2,1,0:T(8,128)S(1)}, f32[6,4,7,7]{3,2,1,0:T(8,128)S(1)}, u32[]{:S(2)}, u32[]{:S(2)}) %collective-permute-start.13) | collective-permute-done | bytes 4736 | tf_op jit(solution)/shard_map/ppermute | solution.py:66
  75.9 0.8 collective-permute-start.11
  76.7 1.2 %collective-permute-done.10 = f32[6,4,7,7]{3,2,1,0:T(8,128)S(1)} collective-permute-done((f32[6,4,7,7]{3,2,1,0:T(8,128)S(1)}, f32[6,4,7,7]{3,2,1,0:T(8,128)S(1)}, u32[]{:S(2)}, u32[]{:S(2)}) %collective-permute-start.10) | collective-permute-done | bytes 4736 | tf_op jit(solution)/shard_map/ppermute | solution.py:66
  78.8 9.5 %collective-permute-done.8 = f32[6,4,7,7]{3,2,1,0:T(8,128)S(1)} collective-permute-done((f32[6,4,7,7]{3,2,1,0:T(8,128)S(1)}, f32[6,4,7,7]{3,2,1,0:T(8,128)S(1)}, u32[]{:S(2)}, u32[]{:S(2)}) %collective-permute-start.8) | collective-permute-done | bytes 4736 | tf_op jit(solution)/shard_map/ppermute | solution.py:66
  90.7 1.7 %collective-permute-start.17 = (f32[6,2,4,8]{3,2,1,0:T(4,128)S(1)}, f32[6,2,4,8]{3,2,1,0:T(4,128)S(1)}, u32[]{:S(2)}, u32[]{:S(2)}) collective-permute-start(f32[6,2,4,8]{3,2,1,0:T(4,128)S(1)} %get-tuple-element.192), channel_id=1, source_target_pairs={{32,0},{64,32},{96,64},{128,96},{160,128},{192,160},{224,192},{0,2... | collective-permute-start | bytes 4616 | tf_op jit(solution)/shard_map/ppermute | solution.py:26
  92.4 1.5 %collective-permute-done.17 = f32[6,2,4,8]{3,2,1,0:T(4,128)S(1)} collective-permute-done((f32[6,2,4,8]{3,2,1,0:T(4,128)S(1)}, f32[6,2,4,8]{3,2,1,0:T(4,128)S(1)}, u32[]{:S(2)}, u32[]{:S(2)}) %collective-permute-start.17) | collective-permute-done | bytes 1568 | tf_op jit(solution)/shard_map/ppermute | solution.py:26
  93.9 2.9 %collective-permute-done.16 = f32[6,2,4,8]{3,2,1,0:T(4,128)S(1)} collective-permute-done((f32[6,2,4,8]{3,2,1,0:T(4,128)S(1)}, f32[6,2,4,8]{3,2,1,0:T(4,128)S(1)}, u32[]{:S(2)}, u32[]{:S(2)}) %collective-permute-start.16) | collective-permute-done | bytes 1568 | tf_op jit(solution)/shard_map/ppermute | solution.py:25
  97.1 5.3 %collective-permute-start.20 = (f32[6,2,4,48]{3,2,1,0:T(4,128)S(1)}, f32[6,2,4,48]{3,2,1,0:T(4,128)S(1)}, u32[]{:S(2)}, u32[]{:S(2)}) collective-permute-start(f32[6,2,4,48]{3,2,1,0:T(4,128)S(1)} %pad_maximum_fusion.9), channel_id=1, source_target_pairs={{1,0},{2,1},{3,2},{4,3},{5,4},{6,5},{7,6},{8,7},{9,8},{10,9},{11,1... | collective-permute-start | bytes 27656 | tf_op jit(solution)/shard_map/ppermute | solution.py:26
  102.5 2.8 %collective-permute-start.21 = (f32[6,2,4,48]{3,2,1,0:T(4,128)S(1)}, f32[6,2,4,48]{3,2,1,0:T(4,128)S(1)}, u32[]{:S(2)}, u32[]{:S(2)}) collective-permute-start(f32[6,2,4,48]{3,2,1,0:T(4,128)S(1)} %pad_maximum_fusion.9), channel_id=1, source_target_pairs={{2,0},{3,1},{4,2},{5,3},{6,4},{7,5},{8,6},{9,7},{10,8},{11,9},{12,... | collective-permute-start | bytes 27656 | tf_op jit(solution)/shard_map/ppermute | solution.py:26
  106.2 1.1 collective-permute-done.21
  112.0 0.7 copy.54
  112.8 0.4 fusion.47
  113.5 0.6 slice_add_fusion.7
  114.1 0.4 fusion.45
  114.9 0.7 slice_add_fusion.4
  116.0 0.9 fusion.59
  (147 shorter events, 11.9 us)
Async XLA Ops:
  1.2 14.5 %copy-start = (f32[2,8,16,128]{3,2,1,0:T(8,128)S(1)}, f32[2,8,16,128]{3,2,1,0:T(8,128)}, u32[]{:S(2)}) copy-start(f32[2,8,16,128]{3,2,1,0:T(8,128)} %param.30) | copy-start | bytes 393220
  1.3 14.5 %copy-start.1 = (f32[8,16,128]{2,1,0:T(8,128)S(1)}, f32[8,16,128]{2,1,0:T(8,128)}, u32[]{:S(2)}) copy-start(f32[8,16,128]{2,1,0:T(8,128)} %param.33) | copy-start | bytes 196612
  1.3 14.5 %copy-start.2 = (f32[8,16,128]{2,1,0:T(8,128)S(1)}, f32[8,16,128]{2,1,0:T(8,128)}, u32[]{:S(2)}) copy-start(f32[8,16,128]{2,1,0:T(8,128)} %param.32) | copy-start | bytes 196612
  1.3 16.6 %copy-start.4 = (f32[128,64]{1,0:T(8,128)S(1)}, f32[128,64]{1,0:T(8,128)}, u32[]{:S(2)}) copy-start(f32[128,64]{1,0:T(8,128)} %constant.21.clone) | copy-start | bytes 98308
  1.3 44.4 %collective-permute-start.7 = (f32[6,8,6,6]{3,2,1,0:T(8,128)S(1)}, f32[6,8,6,6]{3,2,1,0:T(8,128)S(1)}, u32[]{:S(2)}, u32[]{:S(2)}) collective-permute-start(f32[6,8,6,6]{3,2,1,0:T(8,128)S(1)} %get-tuple-element.87), channel_id=1, source_target_pairs={{0,255},{1,224},{2,225},{3,226},{4,227},{5,228},{6,229},{7,230},{8... | collective-permute-start | bytes 20744 | tf_op jit(solution)/shard_map/ppermute | solution.py:66
  9.6 8.7 %copy-start.5 = (f32[128,512]{1,0:T(8,128)S(1)}, f32[128,512]{1,0:T(8,128)}, u32[]{:S(2)}) copy-start(f32[128,512]{1,0:T(8,128)} %constant.22.clone) | copy-start | bytes 786436
  9.6 49.0 %collective-permute-start.6 = (f32[6,8,6,128]{3,2,1,0:T(8,128)S(1)}, f32[6,8,6,128]{3,2,1,0:T(8,128)}, u32[]{:S(2)}, u32[]{:S(2)}) collective-permute-start(f32[6,8,6,128]{3,2,1,0:T(8,128)S(1)} %get-tuple-element.90), channel_id=1, source_target_pairs={{0,31},{1,0},{2,1},{3,2},{4,3},{5,4},{6,5},{7,6},{8,7},{9,8},{10,9... | collective-permute-start | bytes 442376 | tf_op jit(solution)/shard_map/ppermute | solution.py:62
  10.7 35.0 %collective-permute-start.5 = (f32[6,8,6,6]{3,2,1,0:T(8,128)S(1)}, f32[6,8,6,6]{3,2,1,0:T(8,128)}, u32[]{:S(2)}, u32[]{:S(2)}) collective-permute-start(f32[6,8,6,6]{3,2,1,0:T(8,128)S(1)} %get-tuple-element.86), channel_id=1, source_target_pairs={{0,63},{1,32},{2,33},{3,34},{4,35},{5,36},{6,37},{7,38},{8,39},{9,... | collective-permute-start | bytes 20744 | tf_op jit(solution)/shard_map/ppermute | solution.py:66
  10.7 35.5 %collective-permute-start.2 = (f32[6,8,6,6]{3,2,1,0:T(8,128)S(1)}, f32[6,8,6,6]{3,2,1,0:T(8,128)}, u32[]{:S(2)}, u32[]{:S(2)}) collective-permute-start(f32[6,8,6,6]{3,2,1,0:T(8,128)S(1)} %get-tuple-element.88), channel_id=1, source_target_pairs={{0,225},{1,226},{2,227},{3,228},{4,229},{5,230},{6,231},{7,232},{8... | collective-permute-start | bytes 20744 | tf_op jit(solution)/shard_map/ppermute | solution.py:66
  14.6 5.0 %copy-start.6 = (f32[64,32]{1,0:T(8,128)S(1)}, f32[64,32]{1,0:T(8,128)}, u32[]{:S(2)}) copy-start(f32[64,32]{1,0:T(8,128)} %constant.23.clone) | copy-start | bytes 24580
  14.6 5.2 %copy-start.11 = (f32[32,128]{1,0:T(8,128)S(1)}, f32[32,128]{1,0:T(8,128)}, u32[]{:S(2)}) copy-start(f32[32,128]{1,0:T(8,128)} %constant.24.clone) | copy-start | bytes 49156
  14.6 44.0 %collective-permute-start.1 = (f32[6,8,6,128]{3,2,1,0:T(8,128)S(1)}, f32[6,8,6,128]{3,2,1,0:T(8,128)}, u32[]{:S(2)}, u32[]{:S(2)}) collective-permute-start(f32[6,8,6,128]{3,2,1,0:T(8,128)S(1)} %get-tuple-element.89), channel_id=1, source_target_pairs={{0,1},{1,2},{2,3},{3,4},{4,5},{5,6},{6,7},{7,8},{8,9},{9,10},{10,1... | collective-permute-start | bytes 442376 | tf_op jit(solution)/shard_map/ppermute | solution.py:62
  15.8 42.8 %copy-start.3 = (f32[2,8,16,128]{3,2,1,0:T(8,128)S(1)}, f32[2,8,16,128]{3,2,1,0:T(8,128)}, u32[]{:S(2)}) copy-start(f32[2,8,16,128]{3,2,1,0:T(8,128)} %param.31) | copy-start | bytes 393220
  45.7 12.9 %collective-permute-start.4 = (f32[6,8,16,6]{3,2,1,0:T(8,128)S(1)}, f32[6,8,16,6]{3,2,1,0:T(8,128)S(1)}, u32[]{:S(2)}, u32[]{:S(2)}) collective-permute-start(f32[6,8,16,6]{3,2,1,0:T(8,128)S(1)} %get-tuple-element.92), channel_id=1, source_target_pairs={{0,224},{32,0},{64,32},{96,64},{128,96},{160,128},{192,160},{224,1... | collective-permute-start | bytes 55304 | tf_op jit(solution)/shard_map/ppermute | solution.py:59
  45.8 12.8 %collective-permute-start.3 = (f32[6,8,16,6]{3,2,1,0:T(8,128)S(1)}, f32[6,8,16,6]{3,2,1,0:T(8,128)S(1)}, u32[]{:S(2)}, u32[]{:S(2)}) collective-permute-start(f32[6,8,16,6]{3,2,1,0:T(8,128)S(1)} %get-tuple-element.91), channel_id=1, source_target_pairs={{0,32},{32,64},{64,96},{96,128},{128,160},{160,192},{192,224},{224... | collective-permute-start | bytes 55304 | tf_op jit(solution)/shard_map/ppermute | solution.py:59
  46.3 12.3 %collective-permute-start = (f32[6,8,6,6]{3,2,1,0:T(8,128)S(1)}, f32[6,8,6,6]{3,2,1,0:T(8,128)S(1)}, u32[]{:S(2)}, u32[]{:S(2)}) collective-permute-start(f32[6,8,6,6]{3,2,1,0:T(8,128)S(1)} %get-tuple-element.85), channel_id=1, source_target_pairs={{0,33},{1,34},{2,35},{3,36},{4,37},{5,38},{6,39},{7,40},{8,41},{9,... | collective-permute-start | bytes 20744 | tf_op jit(solution)/shard_map/ppermute | solution.py:66
  61.4 0.7 copy-start.8
  65.7 0.9 copy-start.7
  67.1 21.9 %copy-start.10 = (f32[2]{0:T(128)S(1)}, f32[2]{0:T(128)}, u32[]{:S(2)}) copy-start(f32[2]{0:T(128)} %constant.84.clone) | copy-start | bytes 28
  67.1 7.2 %collective-permute-start.15 = (f32[6,4,7,7]{3,2,1,0:T(8,128)S(1)}, f32[6,4,7,7]{3,2,1,0:T(8,128)S(1)}, u32[]{:S(2)}, u32[]{:S(2)}) collective-permute-start(f32[6,4,7,7]{3,2,1,0:T(8,128)S(1)} %get-tuple-element.134), channel_id=1, source_target_pairs={{0,255},{1,224},{2,225},{3,226},{4,227},{5,228},{6,229},{7,230},{8... | collective-permute-start | bytes 14120 | tf_op jit(solution)/shard_map/ppermute | solution.py:66
  68.4 19.9 %collective-permute-start.14 = (f32[6,4,7,64]{3,2,1,0:T(8,128)S(1)}, f32[6,4,7,64]{3,2,1,0:T(8,128)S(1)}, u32[]{:S(2)}, u32[]{:S(2)}) collective-permute-start(f32[6,4,7,64]{3,2,1,0:T(8,128)S(1)} %get-tuple-element.136), channel_id=1, source_target_pairs={{0,31},{1,0},{2,1},{3,2},{4,3},{5,4},{6,5},{7,6},{8,7},{9,8},{10,9... | collective-permute-start | bytes 129032 | tf_op jit(solution)/shard_map/ppermute | solution.py:62
  69.6 6.2 %collective-permute-start.13 = (f32[6,4,7,7]{3,2,1,0:T(8,128)S(1)}, f32[6,4,7,7]{3,2,1,0:T(8,128)S(1)}, u32[]{:S(2)}, u32[]{:S(2)}) collective-permute-start(f32[6,4,7,7]{3,2,1,0:T(8,128)S(1)} %get-tuple-element.133), channel_id=1, source_target_pairs={{0,63},{1,32},{2,33},{3,34},{4,35},{5,36},{6,37},{7,38},{8,39},{9,... | collective-permute-start | bytes 14120 | tf_op jit(solution)/shard_map/ppermute | solution.py:66
  70.5 7.4 %collective-permute-start.10 = (f32[6,4,7,7]{3,2,1,0:T(8,128)S(1)}, f32[6,4,7,7]{3,2,1,0:T(8,128)S(1)}, u32[]{:S(2)}, u32[]{:S(2)}) collective-permute-start(f32[6,4,7,7]{3,2,1,0:T(8,128)S(1)} %get-tuple-element.132), channel_id=1, source_target_pairs={{0,225},{1,226},{2,227},{3,228},{4,229},{5,230},{6,231},{7,232},{8... | collective-permute-start | bytes 14120 | tf_op jit(solution)/shard_map/ppermute | solution.py:66
  73.5 14.8 %collective-permute-start.9 = (f32[6,4,7,64]{3,2,1,0:T(8,128)S(1)}, f32[6,4,7,64]{3,2,1,0:T(8,128)S(1)}, u32[]{:S(2)}, u32[]{:S(2)}) collective-permute-start(f32[6,4,7,64]{3,2,1,0:T(8,128)S(1)} %get-tuple-element.135), channel_id=1, source_target_pairs={{0,1},{1,2},{2,3},{3,4},{4,5},{5,6},{6,7},{7,8},{8,9},{9,10},{10,1... | collective-permute-start | bytes 129032 | tf_op jit(solution)/shard_map/ppermute | solution.py:62
  74.3 13.9 %collective-permute-start.12 = (f32[6,4,8,7]{3,2,1,0:T(8,128)S(1)}, f32[6,4,8,7]{3,2,1,0:T(8,128)S(1)}, u32[]{:S(2)}, u32[]{:S(2)}) collective-permute-start(f32[6,4,8,7]{3,2,1,0:T(8,128)S(1)} %get-tuple-element.138), channel_id=1, source_target_pairs={{0,224},{32,0},{64,32},{96,64},{128,96},{160,128},{192,160},{224,1... | collective-permute-start | bytes 16136 | tf_op jit(solution)/shard_map/ppermute | solution.py:59
  75.9 12.4 %collective-permute-start.11 = (f32[6,4,8,7]{3,2,1,0:T(8,128)S(1)}, f32[6,4,8,7]{3,2,1,0:T(8,128)S(1)}, u32[]{:S(2)}, u32[]{:S(2)}) collective-permute-start(f32[6,4,8,7]{3,2,1,0:T(8,128)S(1)} %get-tuple-element.137), channel_id=1, source_target_pairs={{0,32},{32,64},{64,96},{96,128},{128,160},{160,192},{192,224},{224... | collective-permute-start | bytes 16136 | tf_op jit(solution)/shard_map/ppermute | solution.py:59
  77.8 10.4 %collective-permute-start.8 = (f32[6,4,7,7]{3,2,1,0:T(8,128)S(1)}, f32[6,4,7,7]{3,2,1,0:T(8,128)S(1)}, u32[]{:S(2)}, u32[]{:S(2)}) collective-permute-start(f32[6,4,7,7]{3,2,1,0:T(8,128)S(1)} %get-tuple-element.131), channel_id=1, source_target_pairs={{0,33},{1,34},{2,35},{3,36},{4,37},{5,38},{6,39},{7,40},{8,41},{9,... | collective-permute-start | bytes 14120 | tf_op jit(solution)/shard_map/ppermute | solution.py:66
  89.2 1.2 %copy-start.13 = (f32[16,64]{1,0:T(8,128)S(1)}, f32[16,64]{1,0:T(8,128)}, u32[]{:S(2)}) copy-start(f32[16,64]{1,0:T(8,128)} %constant.85.clone) | copy-start | bytes 12292
  89.6 18.0 %copy-start.12 = (f32[2]{0:T(128)S(1)}, f32[2]{0:T(128)}, u32[]{:S(2)}) copy-start(f32[2]{0:T(128)} %constant.86.clone) | copy-start | bytes 28
  90.7 3.2 %collective-permute-start.17 = (f32[6,2,4,8]{3,2,1,0:T(4,128)S(1)}, f32[6,2,4,8]{3,2,1,0:T(4,128)S(1)}, u32[]{:S(2)}, u32[]{:S(2)}) collective-permute-start(f32[6,2,4,8]{3,2,1,0:T(4,128)S(1)} %get-tuple-element.192), channel_id=1, source_target_pairs={{32,0},{64,32},{96,64},{128,96},{160,128},{192,160},{224,192},{0,2... | collective-permute-start | bytes 4616 | tf_op jit(solution)/shard_map/ppermute | solution.py:26
  92.4 4.5 %collective-permute-start.16 = (f32[6,2,4,8]{3,2,1,0:T(4,128)S(1)}, f32[6,2,4,8]{3,2,1,0:T(4,128)S(1)}, u32[]{:S(2)}, u32[]{:S(2)}) collective-permute-start(f32[6,2,4,8]{3,2,1,0:T(4,128)S(1)} %get-tuple-element.191), channel_id=1, source_target_pairs={{0,32},{32,64},{64,96},{96,128},{128,160},{160,192},{192,224},{224... | collective-permute-start | bytes 4616 | tf_op jit(solution)/shard_map/ppermute | solution.py:25
  97.0 9.3 %collective-permute-start.18 = (f32[6,2,4,48]{3,2,1,0:T(4,128)S(1)}, f32[6,2,4,48]{3,2,1,0:T(4,128)S(1)}, u32[]{:S(2)}, u32[]{:S(2)}) collective-permute-start(f32[6,2,4,48]{3,2,1,0:T(4,128)S(1)} %pad_maximum_fusion.9), channel_id=1, source_target_pairs={{0,2},{1,3},{2,4},{3,5},{4,6},{5,7},{6,8},{7,9},{8,10},{9,11},{10,... | collective-permute-start | bytes 27656 | tf_op jit(solution)/shard_map/ppermute | solution.py:25
  97.1 9.2 %collective-permute-start.19 = (f32[6,2,4,48]{3,2,1,0:T(4,128)S(1)}, f32[6,2,4,48]{3,2,1,0:T(4,128)S(1)}, u32[]{:S(2)}, u32[]{:S(2)}) collective-permute-start(f32[6,2,4,48]{3,2,1,0:T(4,128)S(1)} %pad_maximum_fusion.9), channel_id=1, source_target_pairs={{0,1},{1,2},{2,3},{3,4},{4,5},{5,6},{6,7},{7,8},{8,9},{9,10},{10,1... | collective-permute-start | bytes 27656 | tf_op jit(solution)/shard_map/ppermute | solution.py:25
  97.1 9.1 %collective-permute-start.20 = (f32[6,2,4,48]{3,2,1,0:T(4,128)S(1)}, f32[6,2,4,48]{3,2,1,0:T(4,128)S(1)}, u32[]{:S(2)}, u32[]{:S(2)}) collective-permute-start(f32[6,2,4,48]{3,2,1,0:T(4,128)S(1)} %pad_maximum_fusion.9), channel_id=1, source_target_pairs={{1,0},{2,1},{3,2},{4,3},{5,4},{6,5},{7,6},{8,7},{9,8},{10,9},{11,1... | collective-permute-start | bytes 27656 | tf_op jit(solution)/shard_map/ppermute | solution.py:26
  102.5 4.8 %collective-permute-start.21 = (f32[6,2,4,48]{3,2,1,0:T(4,128)S(1)}, f32[6,2,4,48]{3,2,1,0:T(4,128)S(1)}, u32[]{:S(2)}, u32[]{:S(2)}) collective-permute-start(f32[6,2,4,48]{3,2,1,0:T(4,128)S(1)} %pad_maximum_fusion.9), channel_id=1, source_target_pairs={{2,0},{3,1},{4,2},{5,3},{6,4},{7,5},{8,6},{9,7},{10,8},{11,9},{12,... | collective-permute-start | bytes 27656 | tf_op jit(solution)/shard_map/ppermute | solution.py:26
  112.8 0.8 copy-start.9

commit v10 on v8

--- a/solution.py
+++ b/solution.py
@@ -49,72 +49,100 @@
     return along_x + along_y + along_z
 
 
-def gather_kernel(axis, value, out, land, send_sem, recv_sem, own_sem):
-    count = lax.axis_size(axis)
-    me = lax.axis_index(axis)
-    other = lax.axis_index("gy" if axis == "gx" else "gx")
+def spread_kernel(value, out, land_x, land_y, send_x, recv_x, send_y, recv_y, own_x, own_y):
+    count_x = lax.axis_size("gx")
+    count_y = lax.axis_size("gy")
+    at_x = lax.axis_index("gx")
+    at_y = lax.axis_index("gy")
     mesh_ids = pl.DeviceIdType.MESH
-
-    def device(index):
-        return (index, other) if axis == "gx" else (other, index)
-
     barrier = pltpu.get_barrier_semaphore()
-    for step in range(1, count):
-        pl.semaphore_signal(barrier, 1, device_id=device(lax.rem(me + step, count)),
+    for step in range(1, count_x):
+        pl.semaphore_signal(barrier, 1, device_id=(lax.rem(at_x + step, count_x), at_y),
                             device_id_type=mesh_ids)
-    pl.semaphore_wait(barrier, count - 1)
+    for step in range(1, count_y):
+        pl.semaphore_signal(barrier, 1, device_id=(at_x, lax.rem(at_y + step, count_y)),
+                            device_id_type=mesh_ids)
+    pl.semaphore_wait(barrier, count_x + count_y - 2)
+
     copies = []
-    for step in range(1, count):
+    for step in range(1, count_x):
         copy = pltpu.make_async_remote_copy(
             src_ref=value,
-            dst_ref=land.at[me],
-            send_sem=send_sem.at[step],
-            recv_sem=recv_sem.at[me],
-            device_id=device(lax.rem(me + step, count)),
+            dst_ref=land_x.at[at_x],
+            send_sem=send_x.at[step],
+            recv_sem=recv_x.at[at_x],
+            device_id=(lax.rem(at_x + step, count_x), at_y),
             device_id_type=mesh_ids,
         )
         copy.start()
         copies.append(copy)
-    own = pltpu.make_async_copy(value, land.at[me], own_sem)
+    own = pltpu.make_async_copy(value, land_x.at[at_x], own_x)
     own.start()
-    for step in range(1, count):
+    for step in range(1, count_x):
         copies[step - 1].wait_send()
-        source = lax.rem(me + count - step, count)
+        source = lax.rem(at_x + count_x - step, count_x)
         pltpu.make_async_remote_copy(
             src_ref=value,
-            dst_ref=land.at[source],
-            send_sem=send_sem.at[step],
-            recv_sem=recv_sem.at[source],
-            device_id=device(source),
+            dst_ref=land_x.at[source],
+            send_sem=send_x.at[step],
+            recv_sem=recv_x.at[source],
+            device_id=(source, at_y),
             device_id_type=mesh_ids,
         ).wait_recv()
     own.wait()
-    out[...] = land[...]
-
-
-def gather_axis(block, axis, tag):
-    count = lax.axis_size(axis)
+
+    rows = land_x.at[:, pl.ds(0, 1), :]
+    copies = []
+    for step in range(1, count_y):
+        copy = pltpu.make_async_remote_copy(
+            src_ref=rows,
+            dst_ref=land_y.at[at_y],
+            send_sem=send_y.at[step],
+            recv_sem=recv_y.at[at_y],
+            device_id=(at_x, lax.rem(at_y + step, count_y)),
+            device_id_type=mesh_ids,
+        )
+        copy.start()
+        copies.append(copy)
+    own = pltpu.make_async_copy(rows, land_y.at[at_y], own_y)
+    own.start()
+    for step in range(1, count_y):
+        copies[step - 1].wait_send()
+        source = lax.rem(at_y + count_y - step, count_y)
+        pltpu.make_async_remote_copy(
+            src_ref=rows,
+            dst_ref=land_y.at[source],
+            send_sem=send_y.at[step],
+            recv_sem=recv_y.at[source],
+            device_id=(at_x, source),
+            device_id_type=mesh_ids,
+        ).wait_recv()
+    own.wait()
+    best = jnp.max(land_y[...], axis=(0, 1))
+    out[...] = jnp.broadcast_to(best, out.shape)
+
+
+def global_max(block):
+    count_x = lax.axis_size("gx")
+    count_y = lax.axis_size("gy")
     vmem = pl.BlockSpec(memory_space=pltpu.VMEM)
-    shape = (count,) + block.shape
     return pl.pallas_call(
-        lambda *refs: gather_kernel(axis, *refs),
-        out_shape=jax.ShapeDtypeStruct(shape, jnp.float32),
+        spread_kernel,
+        out_shape=jax.ShapeDtypeStruct(block.shape, jnp.float32),
         in_specs=[vmem],
         out_specs=vmem,
         scratch_shapes=[
-            pltpu.VMEM(shape, jnp.float32),
-            pltpu.SemaphoreType.DMA((count,)),
-            pltpu.SemaphoreType.DMA((count,)),
+            pltpu.VMEM((count_x,) + block.shape, jnp.float32),
+            pltpu.VMEM((count_y, count_x, 1, block.shape[1]), jnp.float32),
+            pltpu.SemaphoreType.DMA((count_x,)),
+            pltpu.SemaphoreType.DMA((count_x,)),
+            pltpu.SemaphoreType.DMA((count_y,)),
+            pltpu.SemaphoreType.DMA((count_y,)),
+            pltpu.SemaphoreType.DMA(()),
             pltpu.SemaphoreType.DMA(()),
         ],
-        compiler_params=pltpu.CompilerParams(collective_id=tag, has_side_effects=True),
+        compiler_params=pltpu.CompilerParams(collective_id=0, has_side_effects=True),
     )(block)
-
-
-def global_max(block):
-    for tag, axis in enumerate(("gx", "gy")):
-        block = jnp.max(gather_axis(block, axis, tag), axis=0)
-    return block
 
 
 def restrict(field):

time: 95.7 us -> 90.8 us (0.949)
  Pallas kernels: 20.7 us -> 17.3 us
  other arithmetic: 17.7 us -> 15.5 us
    pallas_call x2 -> x1, Pallas kernels: 20.7 us -> 17.3 us  [global_max(): pl.pallas_call(spread_kernel, out_shape=jax.ShapeDtypeStruct(block.shape,...]
    reduce_max x2 -> x0, other arithmetic: 2.3 us -> none  [global_max(): block = jnp.max(gather_axis(block, axis, tag), axis=0)]
  transfers between devices with their start and end apart: 14 -> 14, of which waited for: 8 -> 8; matrix products, arithmetic and copies ran while one was open for 7% -> 6% of each run, Pallas kernels for 22% -> 19%
where the time goes in v10:
time: 90.8 us; the launch traced here: 90.5 us
  starting transfers between devices  22.9 us (25%)
  waiting for transfers between devices  17.9 us (20%)
  Pallas kernels  17.3 us (19%)
  other arithmetic  15.5 us (17%)
  local copies, waits for them, and re-layouts  7.6 us (8%)
  between operations  7.31 us (8%)
  matrix products  2.02 us (2%)
    ppermute x7, starting transfers between devices, padded_along(): lax.ppermute(head, axis, [((i + distance) % count, i) for i in range(coun...  22.2 us
    pallas_call x1, Pallas kernels, global_max(): pl.pallas_call(spread_kernel, out_shape=jax.ShapeDtypeStruct(block.shape,...  17.3 us
    ppermute x7, waiting for transfers between devices, padded_along(): lax.ppermute(tail, axis, [(i, (i + distance) % count) for i in range(coun...  12.2 us
    ppermute x7, waiting for transfers between devices, padded_along(): lax.ppermute(head, axis, [((i + distance) % count, i) for i in range(coun...  5.67 us
    add x12, other arithmetic, chebyshev(): iterate = crop(iterate, halo + 1, halo) + update  4.36 us
    slice x30, local copies, waits for them, and re-layouts, shrunk_neighbours(): along_z = jnp.roll(centre, 1, 1) + jnp.roll(centre, -1, 1)  3.45 us
    add x17, other arithmetic, operate(): first = coeff[0] * centre[0] + coeff[1] * centre[1]  3.15 us
    reduce_max x3, other arithmetic, body(): jnp.max(second)  2.13 us
  transfers between devices with their start and end apart: 14, of which 8 were waited for; matrix products, arithmetic and copies ran while one was open for 6% of the time, Pallas kernels for 19%

profile of v10, /device:TPU:0, one launch (start us, length us, event | category | flops | bytes accessed | tf_op | source)
XLA Modules:
  0.0 90.5 jit_solution(10209090149489553275)
XLA Ops:
  0.0 1.1 %pad_maximum_fusion.6 = f32[6,8,16,128]{3,2,1,0:T(8,128)S(1)} fusion(f32[2,8,16,128]{3,2,1,0:T(8,128)} %param.31, f32[1,8,16,128]{3,2,1,0:T(8,128)} %bitcast.86, f32[1,8,16,128]{3,2,1,0:T(8,128)} %bitcast.89, f32[2,8,16,128]{3,2,1,0:T(8,128)} %param.30), kind=kLoop, calls=%fused_computation.66 | loop fusion | flops 294912 | bytes 786432 | tf_op jit(solution)/shard_map/concatenate | solution.py:246
  1.3 0.5 collective-permute-start.1
  1.9 0.7 fusion.107
  4.0 0.4 fusion.233
  4.4 0.4 convolution_multiply_fusion.1
  4.8 0.8 fusion.167
  6.0 0.6 fusion.188
  9.2 0.6 select_select_fusion.value
  9.8 0.5 collective-permute-done
  10.2 0.4 pad_maximum_fusion.1
  10.7 8.4 %collective-permute-start.3 = (f32[6,8,6,140]{3,2,1,0:T(8,128)S(1)}, f32[6,8,6,140]{3,2,1,0:T(8,128)S(1)}, u32[]{:S(2)}, u32[]{:S(2)}) collective-permute-start(f32[6,8,6,140]{3,2,1,0:T(8,128)S(1)} %get-tuple-element.52), channel_id=1, source_target_pairs={{1,0},{2,1},{3,2},{4,3},{5,4},{6,5},{7,6},{8,7},{9,8},{10,9},{11,1... | collective-permute-start | bytes 483848 | tf_op jit(solution)/shard_map/ppermute | solution.py:26
  19.2 17.3 %shard_map.280 = f32[8,128]{1,0:T(8,128)} custom-call(f32[8,128]{1,0:T(8,128)} %select_select_fusion.value), custom_call_target="tpu_custom_call" | custom-call | tf_op jit(solution)/shard_map/pallas_call | solution.py:129
  36.5 1.4 %fusion.232 = (f32[1,1]{1,0:T(1,128)}, f32[1,1]{1,0:T(1,128)}, f32[1,1]{1,0:T(1,128)}) fusion(f32[8,128]{1,0:T(8,128)} %shard_map.280), kind=kLoop, calls=%fused_computation.401 | loop fusion | bytes 24 | tf_op jit(solution)/shard_map/slice | solution.py:277
  38.8 0.2 pad_maximum_fusion
  39.0 0.4 fusion.42
  39.5 0.3 fusion.199
  39.8 0.4 subtract_bitcast_fusion
  40.2 0.8 fusion.12
  41.1 0.2 fusion.202
  41.4 0.4 fusion.54
  41.8 0.6 slice_add_fusion.12
  42.4 0.4 fusion.52
  42.9 0.2 fusion.212
  43.1 0.7 fusion.33
  44.3 0.2 fusion.67
  44.5 0.3 fusion.235
  45.2 1.8 %collective-permute-start.5 = (f32[6,4,8,7]{3,2,1,0:T(8,128)S(1)}, f32[6,4,8,7]{3,2,1,0:T(8,128)S(1)}, u32[]{:S(2)}, u32[]{:S(2)}) collective-permute-start(f32[6,4,8,7]{3,2,1,0:T(8,128)S(1)} %get-tuple-element.132), channel_id=1, source_target_pairs={{32,0},{64,32},{96,64},{128,96},{160,128},{192,160},{224,192},{0,2... | collective-permute-start | bytes 16136 | tf_op jit(solution)/shard_map/ppermute | solution.py:26
  47.1 2.2 %collective-permute-done.5 = f32[6,4,8,7]{3,2,1,0:T(8,128)S(1)} collective-permute-done((f32[6,4,8,7]{3,2,1,0:T(8,128)S(1)}, f32[6,4,8,7]{3,2,1,0:T(8,128)S(1)}, u32[]{:S(2)}, u32[]{:S(2)}) %collective-permute-start.5) | collective-permute-done | bytes 5408 | tf_op jit(solution)/shard_map/ppermute | solution.py:26
  49.3 3.0 %collective-permute-done.4 = f32[6,4,8,7]{3,2,1,0:T(8,128)S(1)} collective-permute-done((f32[6,4,8,7]{3,2,1,0:T(8,128)S(1)}, f32[6,4,8,7]{3,2,1,0:T(8,128)S(1)}, u32[]{:S(2)}, u32[]{:S(2)}) %collective-permute-start.4) | collective-permute-done | bytes 5408 | tf_op jit(solution)/shard_map/ppermute | solution.py:25
  52.5 3.3 %collective-permute-start.7 = (f32[6,4,7,78]{3,2,1,0:T(8,128)S(1)}, f32[6,4,7,78]{3,2,1,0:T(8,128)S(1)}, u32[]{:S(2)}, u32[]{:S(2)}) collective-permute-start(f32[6,4,7,78]{3,2,1,0:T(8,128)S(1)} %get-tuple-element.130), channel_id=1, source_target_pairs={{1,0},{2,1},{3,2},{4,3},{5,4},{6,5},{7,6},{8,7},{9,8},{10,9},{11,1... | collective-permute-start | bytes 157256 | tf_op jit(solution)/shard_map/ppermute | solution.py:26
  56.6 1.4 %collective-permute-done.7 = f32[6,4,7,78]{3,2,1,0:T(8,128)S(1)} collective-permute-done((f32[6,4,7,78]{3,2,1,0:T(8,128)S(1)}, f32[6,4,7,78]{3,2,1,0:T(8,128)S(1)}, u32[]{:S(2)}, u32[]{:S(2)}) %collective-permute-start.7) | collective-permute-done | bytes 52448 | tf_op jit(solution)/shard_map/ppermute | solution.py:26
  58.0 5.7 %collective-permute-done.6 = f32[6,4,7,78]{3,2,1,0:T(8,128)S(1)} collective-permute-done((f32[6,4,7,78]{3,2,1,0:T(8,128)S(1)}, f32[6,4,7,78]{3,2,1,0:T(8,128)S(1)}, u32[]{:S(2)}, u32[]{:S(2)}) %collective-permute-start.6) | collective-permute-done | bytes 52448 | tf_op jit(solution)/shard_map/ppermute | solution.py:25
  66.0 0.5 collective-permute-start.8
  66.5 1.0 %collective-permute-done.9 = f32[6,2,4,8]{3,2,1,0:T(4,128)S(1)} collective-permute-done((f32[6,2,4,8]{3,2,1,0:T(4,128)S(1)}, f32[6,2,4,8]{3,2,1,0:T(4,128)S(1)}, u32[]{:S(2)}, u32[]{:S(2)}) %collective-permute-start.9) | collective-permute-done | bytes 1568 | tf_op jit(solution)/shard_map/ppermute | solution.py:26
  67.5 3.0 %collective-permute-done.8 = f32[6,2,4,8]{3,2,1,0:T(4,128)S(1)} collective-permute-done((f32[6,2,4,8]{3,2,1,0:T(4,128)S(1)}, f32[6,2,4,8]{3,2,1,0:T(4,128)S(1)}, u32[]{:S(2)}, u32[]{:S(2)}) %collective-permute-start.8) | collective-permute-done | bytes 1568 | tf_op jit(solution)/shard_map/ppermute | solution.py:25
  70.7 5.3 %collective-permute-start.12 = (f32[6,2,4,48]{3,2,1,0:T(4,128)S(1)}, f32[6,2,4,48]{3,2,1,0:T(4,128)S(1)}, u32[]{:S(2)}, u32[]{:S(2)}) collective-permute-start(f32[6,2,4,48]{3,2,1,0:T(4,128)S(1)} %pad_maximum_fusion.17), channel_id=1, source_target_pairs={{1,0},{2,1},{3,2},{4,3},{5,4},{6,5},{7,6},{8,7},{9,8},{10,9},{11,1... | collective-permute-start | bytes 27656 | tf_op jit(solution)/shard_map/ppermute | solution.py:26
  76.1 2.8 %collective-permute-start.13 = (f32[6,2,4,48]{3,2,1,0:T(4,128)S(1)}, f32[6,2,4,48]{3,2,1,0:T(4,128)S(1)}, u32[]{:S(2)}, u32[]{:S(2)}) collective-permute-start(f32[6,2,4,48]{3,2,1,0:T(4,128)S(1)} %pad_maximum_fusion.17), channel_id=1, source_target_pairs={{2,0},{3,1},{4,2},{5,3},{6,4},{7,5},{8,6},{9,7},{10,8},{11,9},{12,... | collective-permute-start | bytes 27656 | tf_op jit(solution)/shard_map/ppermute | solution.py:26
  79.8 1.1 %collective-permute-done.13 = f32[6,2,4,48]{3,2,1,0:T(4,128)S(1)} collective-permute-done((f32[6,2,4,48]{3,2,1,0:T(4,128)S(1)}, f32[6,2,4,48]{3,2,1,0:T(4,128)S(1)}, u32[]{:S(2)}, u32[]{:S(2)}) %collective-permute-start.13) | collective-permute-done | bytes 9248 | tf_op jit(solution)/shard_map/ppermute | solution.py:26
  84.9 0.3 copy.51
  85.2 0.3 slice.2057
  85.6 0.7 copy.54
  86.3 0.4 fusion.50
  86.8 0.2 fusion.208
  87.1 0.6 slice_add_fusion.7
  87.7 0.4 fusion.48
  88.2 0.2 fusion.206
  88.4 0.7 slice_add_fusion.4
  89.6 1.0 %fusion.62 = f32[2,8,16,128]{3,2,1,0:T(8,128)} fusion(f32[2,8,18,130]{3,2,1,0:T(8,128)S(1)} %get-tuple-element.16, f32[2,8,18,130]{3,2,1,0:T(8,128)S(1)} %get-tuple-element.15, f32[1,8,16,128]{3,2,1,0:T(8,128)S(1)} %get-tuple-element.94, f32[1,8,16,128]{3,2,1,0:T(8,128)S(1)} %get-tuple-element.98, f32[2,1,16,128]{3,2,1,0:T(8,128)S(1)} %get-tuple-element.62, ...), kind=kLoop, calls=%fused_computation.120 | loop fusion | flops 557056 | bytes 1572880 | tf_op jit(solution)/shard_map/add | solution.py:231
  (125 shorter events, 8.8 us)
Async XLA Ops:
  0.0 1.9 %copy-start = (f32[2,8,16,128]{3,2,1,0:T(8,128)S(1)}, f32[2,8,16,128]{3,2,1,0:T(8,128)}, u32[]{:S(2)}) copy-start(f32[2,8,16,128]{3,2,1,0:T(8,128)} %param.30) | copy-start | bytes 393220
  0.0 1.9 %copy-start.1 = (f32[8,16,128]{2,1,0:T(8,128)S(1)}, f32[8,16,128]{2,1,0:T(8,128)}, u32[]{:S(2)}) copy-start(f32[8,16,128]{2,1,0:T(8,128)} %param.33) | copy-start | bytes 196612
  0.0 1.9 %copy-start.2 = (f32[8,16,128]{2,1,0:T(8,128)S(1)}, f32[8,16,128]{2,1,0:T(8,128)}, u32[]{:S(2)}) copy-start(f32[8,16,128]{2,1,0:T(8,128)} %param.32) | copy-start | bytes 196612
  0.0 4.0 %copy-start.4 = (f32[128,64]{1,0:T(8,128)S(1)}, f32[128,64]{1,0:T(8,128)}, u32[]{:S(2)}) copy-start(f32[128,64]{1,0:T(8,128)} %constant.21.clone) | copy-start | bytes 98308
  1.1 3.3 %copy-start.5 = (f32[128,512]{1,0:T(8,128)S(1)}, f32[128,512]{1,0:T(8,128)}, u32[]{:S(2)}) copy-start(f32[128,512]{1,0:T(8,128)} %constant.22.clone) | copy-start | bytes 786436
  1.1 4.5 %copy-start.6 = (f32[64,32]{1,0:T(8,128)S(1)}, f32[64,32]{1,0:T(8,128)}, u32[]{:S(2)}) copy-start(f32[64,32]{1,0:T(8,128)} %constant.23.clone) | copy-start | bytes 24580
  1.1 4.7 %copy-start.10 = (f32[32,128]{1,0:T(8,128)S(1)}, f32[32,128]{1,0:T(8,128)}, u32[]{:S(2)}) copy-start(f32[32,128]{1,0:T(8,128)} %constant.24.clone) | copy-start | bytes 49156
  1.2 9.1 %copy-start.3 = (f32[2,8,16,128]{3,2,1,0:T(8,128)S(1)}, f32[2,8,16,128]{3,2,1,0:T(8,128)}, u32[]{:S(2)}) copy-start(f32[2,8,16,128]{3,2,1,0:T(8,128)} %param.31) | copy-start | bytes 393220
  1.3 8.4 %collective-permute-start.1 = (f32[6,8,16,6]{3,2,1,0:T(8,128)S(1)}, f32[6,8,16,6]{3,2,1,0:T(8,128)S(1)}, u32[]{:S(2)}, u32[]{:S(2)}) collective-permute-start(f32[6,8,16,6]{3,2,1,0:T(8,128)S(1)} %get-tuple-element.90), channel_id=1, source_target_pairs={{32,0},{64,32},{96,64},{128,96},{160,128},{192,160},{224,192},{0,2... | collective-permute-start | bytes 55304 | tf_op jit(solution)/shard_map/ppermute | solution.py:26
  1.8 8.4 %collective-permute-start = (f32[6,8,16,6]{3,2,1,0:T(8,128)S(1)}, f32[6,8,16,6]{3,2,1,0:T(8,128)S(1)}, u32[]{:S(2)}, u32[]{:S(2)}) collective-permute-start(f32[6,8,16,6]{3,2,1,0:T(8,128)S(1)} %get-tuple-element.89), channel_id=1, source_target_pairs={{0,32},{32,64},{64,96},{96,128},{128,160},{160,192},{192,224},{224... | collective-permute-start | bytes 55304 | tf_op jit(solution)/shard_map/ppermute | solution.py:25
  10.7 28.0 %collective-permute-start.3 = (f32[6,8,6,140]{3,2,1,0:T(8,128)S(1)}, f32[6,8,6,140]{3,2,1,0:T(8,128)S(1)}, u32[]{:S(2)}, u32[]{:S(2)}) collective-permute-start(f32[6,8,6,140]{3,2,1,0:T(8,128)S(1)} %get-tuple-element.52), channel_id=1, source_target_pairs={{1,0},{2,1},{3,2},{4,3},{5,4},{6,5},{7,6},{8,7},{9,8},{10,9},{11,1... | collective-permute-start | bytes 483848 | tf_op jit(solution)/shard_map/ppermute | solution.py:26
  19.1 19.7 %collective-permute-start.2 = (f32[6,8,6,140]{3,2,1,0:T(8,128)S(1)}, f32[6,8,6,140]{3,2,1,0:T(8,128)S(1)}, u32[]{:S(2)}, u32[]{:S(2)}) collective-permute-start(f32[6,8,6,140]{3,2,1,0:T(8,128)S(1)} %get-tuple-element.51), channel_id=1, source_target_pairs={{0,1},{1,2},{2,3},{3,4},{4,5},{5,6},{6,7},{7,8},{8,9},{9,10},{10,1... | collective-permute-start | bytes 483848 | tf_op jit(solution)/shard_map/ppermute | solution.py:25
  39.5 0.7 copy-start.8
  43.9 0.9 %copy-start.7 = (f32[64,256]{1,0:T(8,128)S(1)}, f32[64,256]{1,0:T(8,128)}, u32[]{:S(2)}) copy-start(f32[64,256]{1,0:T(8,128)} %constant.26.clone) | copy-start | bytes 196612
  45.2 4.1 %collective-permute-start.5 = (f32[6,4,8,7]{3,2,1,0:T(8,128)S(1)}, f32[6,4,8,7]{3,2,1,0:T(8,128)S(1)}, u32[]{:S(2)}, u32[]{:S(2)}) collective-permute-start(f32[6,4,8,7]{3,2,1,0:T(8,128)S(1)} %get-tuple-element.132), channel_id=1, source_target_pairs={{32,0},{64,32},{96,64},{128,96},{160,128},{192,160},{224,192},{0,2... | collective-permute-start | bytes 16136 | tf_op jit(solution)/shard_map/ppermute | solution.py:26
  47.1 17.2 %copy-start.9 = (f32[2]{0:T(128)S(1)}, f32[2]{0:T(128)}, u32[]{:S(2)}) copy-start(f32[2]{0:T(128)} %constant.84.clone) | copy-start | bytes 28
  47.1 5.3 %collective-permute-start.4 = (f32[6,4,8,7]{3,2,1,0:T(8,128)S(1)}, f32[6,4,8,7]{3,2,1,0:T(8,128)S(1)}, u32[]{:S(2)}, u32[]{:S(2)}) collective-permute-start(f32[6,4,8,7]{3,2,1,0:T(8,128)S(1)} %get-tuple-element.131), channel_id=1, source_target_pairs={{0,32},{32,64},{64,96},{96,128},{128,160},{160,192},{192,224},{224... | collective-permute-start | bytes 16136 | tf_op jit(solution)/shard_map/ppermute | solution.py:25
  52.5 5.5 %collective-permute-start.7 = (f32[6,4,7,78]{3,2,1,0:T(8,128)S(1)}, f32[6,4,7,78]{3,2,1,0:T(8,128)S(1)}, u32[]{:S(2)}, u32[]{:S(2)}) collective-permute-start(f32[6,4,7,78]{3,2,1,0:T(8,128)S(1)} %get-tuple-element.130), channel_id=1, source_target_pairs={{1,0},{2,1},{3,2},{4,3},{5,4},{6,5},{7,6},{8,7},{9,8},{10,9},{11,1... | collective-permute-start | bytes 157256 | tf_op jit(solution)/shard_map/ppermute | solution.py:26
  55.8 7.9 %collective-permute-start.6 = (f32[6,4,7,78]{3,2,1,0:T(8,128)S(1)}, f32[6,4,7,78]{3,2,1,0:T(8,128)S(1)}, u32[]{:S(2)}, u32[]{:S(2)}) collective-permute-start(f32[6,4,7,78]{3,2,1,0:T(8,128)S(1)} %get-tuple-element.129), channel_id=1, source_target_pairs={{0,1},{1,2},{2,3},{3,4},{4,5},{5,6},{6,7},{7,8},{8,9},{9,10},{10,1... | collective-permute-start | bytes 157256 | tf_op jit(solution)/shard_map/ppermute | solution.py:25
  64.5 1.2 %copy-start.12 = (f32[16,64]{1,0:T(8,128)S(1)}, f32[16,64]{1,0:T(8,128)}, u32[]{:S(2)}) copy-start(f32[16,64]{1,0:T(8,128)} %constant.85.clone) | copy-start | bytes 12292
  64.9 16.4 %copy-start.11 = (f32[2]{0:T(128)S(1)}, f32[2]{0:T(128)}, u32[]{:S(2)}) copy-start(f32[2]{0:T(128)} %constant.86.clone) | copy-start | bytes 28
  66.0 1.5 %collective-permute-start.9 = (f32[6,2,4,8]{3,2,1,0:T(4,128)S(1)}, f32[6,2,4,8]{3,2,1,0:T(4,128)S(1)}, u32[]{:S(2)}, u32[]{:S(2)}) collective-permute-start(f32[6,2,4,8]{3,2,1,0:T(4,128)S(1)} %get-tuple-element.186), channel_id=1, source_target_pairs={{32,0},{64,32},{96,64},{128,96},{160,128},{192,160},{224,192},{0,2... | collective-permute-start | bytes 4616 | tf_op jit(solution)/shard_map/ppermute | solution.py:26
  66.0 4.5 %collective-permute-start.8 = (f32[6,2,4,8]{3,2,1,0:T(4,128)S(1)}, f32[6,2,4,8]{3,2,1,0:T(4,128)S(1)}, u32[]{:S(2)}, u32[]{:S(2)}) collective-permute-start(f32[6,2,4,8]{3,2,1,0:T(4,128)S(1)} %get-tuple-element.185), channel_id=1, source_target_pairs={{0,32},{32,64},{64,96},{96,128},{128,160},{160,192},{192,224},{224... | collective-permute-start | bytes 4616 | tf_op jit(solution)/shard_map/ppermute | solution.py:25
  70.6 9.3 %collective-permute-start.10 = (f32[6,2,4,48]{3,2,1,0:T(4,128)S(1)}, f32[6,2,4,48]{3,2,1,0:T(4,128)S(1)}, u32[]{:S(2)}, u32[]{:S(2)}) collective-permute-start(f32[6,2,4,48]{3,2,1,0:T(4,128)S(1)} %pad_maximum_fusion.17), channel_id=1, source_target_pairs={{0,2},{1,3},{2,4},{3,5},{4,6},{5,7},{6,8},{7,9},{8,10},{9,11},{10,... | collective-permute-start | bytes 27656 | tf_op jit(solution)/shard_map/ppermute | solution.py:25
  70.6 9.2 %collective-permute-start.11 = (f32[6,2,4,48]{3,2,1,0:T(4,128)S(1)}, f32[6,2,4,48]{3,2,1,0:T(4,128)S(1)}, u32[]{:S(2)}, u32[]{:S(2)}) collective-permute-start(f32[6,2,4,48]{3,2,1,0:T(4,128)S(1)} %pad_maximum_fusion.17), channel_id=1, source_target_pairs={{0,1},{1,2},{2,3},{3,4},{4,5},{5,6},{6,7},{7,8},{8,9},{9,10},{10,1... | collective-permute-start | bytes 27656 | tf_op jit(solution)/shard_map/ppermute | solution.py:25
  70.7 9.1 %collective-permute-start.12 = (f32[6,2,4,48]{3,2,1,0:T(4,128)S(1)}, f32[6,2,4,48]{3,2,1,0:T(4,128)S(1)}, u32[]{:S(2)}, u32[]{:S(2)}) collective-permute-start(f32[6,2,4,48]{3,2,1,0:T(4,128)S(1)} %pad_maximum_fusion.17), channel_id=1, source_target_pairs={{1,0},{2,1},{3,2},{4,3},{5,4},{6,5},{7,6},{8,7},{9,8},{10,9},{11,1... | collective-permute-start | bytes 27656 | tf_op jit(solution)/shard_map/ppermute | solution.py:26
  76.1 4.8 %collective-permute-start.13 = (f32[6,2,4,48]{3,2,1,0:T(4,128)S(1)}, f32[6,2,4,48]{3,2,1,0:T(4,128)S(1)}, u32[]{:S(2)}, u32[]{:S(2)}) collective-permute-start(f32[6,2,4,48]{3,2,1,0:T(4,128)S(1)} %pad_maximum_fusion.17), channel_id=1, source_target_pairs={{2,0},{3,1},{4,2},{5,3},{6,4},{7,5},{8,6},{9,7},{10,8},{11,9},{12,... | collective-permute-start | bytes 27656 | tf_op jit(solution)/shard_map/ppermute | solution.py:26

commit v11 on v10

--- a/solution.py
+++ b/solution.py
@@ -49,7 +49,8 @@
     return along_x + along_y + along_z
 
 
-def spread_kernel(value, out, land_x, land_y, send_x, recv_x, send_y, recv_y, own_x, own_y):
+def spread_kernel(width, value, cells, out, below, above, land_x, land_y, send_x, recv_x,
+                  send_y, recv_y, own_x, own_y, land_below, land_above, send_halo, recv_halo):
     count_x = lax.axis_size("gx")
     count_y = lax.axis_size("gy")
     at_x = lax.axis_index("gx")
@@ -63,6 +64,20 @@
         pl.semaphore_signal(barrier, 1, device_id=(at_x, lax.rem(at_y + step, count_y)),
                             device_id_type=mesh_ids)
     pl.semaphore_wait(barrier, count_x + count_y - 2)
+
+    rows_in = cells.shape[2]
+    halo = []
+    for slot, (first, target, step) in enumerate(((rows_in - width, land_below, 1), (0, land_above, -1))):
+        copy = pltpu.make_async_remote_copy(
+            src_ref=cells.at[:, :, pl.ds(first, width), :],
+            dst_ref=target,
+            send_sem=send_halo.at[slot],
+            recv_sem=recv_halo.at[slot],
+            device_id=(at_x, lax.rem(at_y + step + count_y, count_y)),
+            device_id_type=mesh_ids,
+        )
+        copy.start()
+        halo.append(copy)
 
     copies = []
     for step in range(1, count_x):
@@ -120,17 +135,26 @@
     own.wait()
     best = jnp.max(land_y[...], axis=(0, 1))
     out[...] = jnp.broadcast_to(best, out.shape)
-
-
-def global_max(block):
+    for copy in halo:
+        copy.wait()
+    below[...] = land_below[...]
+    above[...] = land_above[...]
+
+
+def global_max(block, cells, width):
     count_x = lax.axis_size("gx")
     count_y = lax.axis_size("gy")
     vmem = pl.BlockSpec(memory_space=pltpu.VMEM)
-    return pl.pallas_call(
-        spread_kernel,
-        out_shape=jax.ShapeDtypeStruct(block.shape, jnp.float32),
-        in_specs=[vmem],
-        out_specs=vmem,
+    face = cells.shape[:2] + (width,) + cells.shape[3:]
+    spreads, below, above = pl.pallas_call(
+        lambda *refs: spread_kernel(width, *refs),
+        out_shape=(
+            jax.ShapeDtypeStruct(block.shape, jnp.float32),
+            jax.ShapeDtypeStruct(face, jnp.float32),
+            jax.ShapeDtypeStruct(face, jnp.float32),
+        ),
+        in_specs=[vmem, vmem],
+        out_specs=(vmem, vmem, vmem),
         scratch_shapes=[
             pltpu.VMEM((count_x,) + block.shape, jnp.float32),
             pltpu.VMEM((count_y, count_x, 1, block.shape[1]), jnp.float32),
@@ -140,9 +164,14 @@
             pltpu.SemaphoreType.DMA((count_y,)),
             pltpu.SemaphoreType.DMA(()),
             pltpu.SemaphoreType.DMA(()),
+            pltpu.VMEM(face, jnp.float32),
+            pltpu.VMEM(face, jnp.float32),
+            pltpu.SemaphoreType.DMA((2,)),
+            pltpu.SemaphoreType.DMA((2,)),
         ],
         compiler_params=pltpu.CompilerParams(collective_id=0, has_side_effects=True),
-    )(block)
+    )(block, cells)
+    return spreads, jnp.concatenate([below, cells, above], axis=2)
 
 
 def restrict(field):
@@ -243,11 +272,10 @@
     for level, level_fields in enumerate((fields, fields_1, fields_2)):
         _, first, second = coefficients(level_fields, level)
         local = jnp.where(lane == level, jnp.maximum(jnp.max(first), jnp.max(second)), local)
-    wide_x = padded_along(jnp.concatenate([fields, previous], 0), 6, "gx", 3)
-    local, wide_x = lax.optimization_barrier((local, wide_x))
-    spreads = global_max(local)[0]
-
-    wide = padded_along(wide_x, 6, "gy", 2)
+    spread_block, wide_y = global_max(local, jnp.concatenate([fields, previous], 0), 6)
+    spreads = spread_block[0]
+    wide = padded_along(wide_y, 6, "gx", 3)
+
     ops_0 = Level(coefficients(crop(wide[:4], 6, 5), 0)[0], 5, 0)
     state_w = wide[:2]
     substrate, catalyst = crop(state_w[0], 6, 5), crop(state_w[1], 6, 5)

time: 90.8 us -> 94.8 us (1.044)
  starting transfers between devices: 22.9 us -> 14.6 us
  Pallas kernels: 17.3 us -> 21.1 us
  other arithmetic: 15.5 us -> 18.6 us
  local copies, waits for them, and re-layouts: 7.6 us -> 9.65 us
  matrix products: 2.02 us -> 3.81 us
  waiting for transfers between devices: 17.9 us -> 19.4 us
    ppermute x7 -> x6, starting transfers between devices: 22.2 us -> 13.1 us  [padded_along(): lax.ppermute(head, axis, [((i + distance) % count, i) for i in range(coun...]
    pallas_call x1, Pallas kernels: 17.3 us -> 21.1 us  [global_max(): pl.pallas_call(lambda *refs: spread_kernel(width, *refs), out_shape=(jax....]
    ppermute x7 -> x6, waiting for transfers between devices: 12.2 us -> 14.3 us  [padded_along(): lax.ppermute(tail, axis, [(i, (i + distance) % count) for i in range(coun...]
    reduce_max x3, other arithmetic: 2.13 us -> 3.14 us  [body(): jnp.max(second)]
    concatenate x1, other arithmetic: 0.02 us -> 1 us  [body(): fields = jnp.concatenate([state, feed[None], kill[None]], 0)]
    dot_general x4, matrix products: 0.87 us -> 1.83 us  [restrict(): blocks = jnp.dot(pick_rows, pairs, precision=lax.Precision.HIGHEST)]
    concatenate x1 -> x2, other arithmetic: 1.1 us -> 1.93 us  [the longest x1 1.14 us: global_max(): return (spreads, jnp.concatenate([below, cells, above], axis=2))]
    ppermute x7 -> x6, waiting for transfers between devices: 5.67 us -> 5.07 us  [padded_along(): lax.ppermute(head, axis, [((i + distance) % count, i) for i in range(coun...]
  transfers between devices with their start and end apart: 14 -> 12, of which waited for: 8 -> 8; matrix products, arithmetic and copies ran while one was open for 6% -> 3% of each run, Pallas kernels for 19% -> 0%
where the time goes in v11:
time: 94.8 us; the launch traced here: 94.4 us
  Pallas kernels  21.1 us (22%)
  waiting for transfers between devices  19.4 us (20%)
  other arithmetic  18.6 us (20%)
  starting transfers between devices  14.6 us (15%)
  local copies, waits for them, and re-layouts  9.65 us (10%)
  between operations  7.34 us (8%)
  matrix products  3.81 us (4%)
    pallas_call x1, Pallas kernels, global_max(): pl.pallas_call(lambda *refs: spread_kernel(width, *refs), out_shape=(jax....  21.1 us
    ppermute x6, waiting for transfers between devices, padded_along(): lax.ppermute(tail, axis, [(i, (i + distance) % count) for i in range(coun...  14.3 us
    ppermute x6, starting transfers between devices, padded_along(): lax.ppermute(head, axis, [((i + distance) % count, i) for i in range(coun...  13.1 us
    ppermute x6, waiting for transfers between devices, padded_along(): lax.ppermute(head, axis, [((i + distance) % count, i) for i in range(coun...  5.07 us
    add x12, other arithmetic, chebyshev(): iterate = crop(iterate, halo + 1, halo) + update  4.36 us
    slice x31, local copies, waits for them, and re-layouts, shrunk_neighbours(): along_z = jnp.roll(centre, 1, 1) + jnp.roll(centre, -1, 1)  3.55 us
    add x17, other arithmetic, operate(): first = coeff[0] * centre[0] + coeff[1] * centre[1]  3.15 us
    reduce_max x3, other arithmetic, body(): jnp.max(second)  3.14 us
  transfers between devices with their start and end apart: 12, of which 8 were waited for; matrix products, arithmetic and copies ran while one was open for 3% of the time, Pallas kernels for 0%

profile of v11, /device:TPU:0, one launch (start us, length us, event | category | flops | bytes accessed | tf_op | source)
XLA Modules:
  0.0 94.4 jit_solution(17178030177501327546)
XLA Ops:
  0.0 1.7 %fusion.104 = (f32[]{:T(128)}, f32[]{:T(128)}) fusion(f32[8,16,128]{2,1,0:T(8,128)} %param.33, f32[8,16,128]{2,1,0:T(8,128)} %param.32, f32[2,8,16,128]{3,2,1,0:T(8,128)} %param.30), kind=kLoop, calls=%fused_computation.200 | loop fusion | flops 262142 | bytes 262152 | tf_op jit(solution)/shard_map/reduce_max | solution.py:274
  3.1 1.0 %pad_maximum_fusion.4 = f32[4,8,16,128]{3,2,1,0:T(8,128)S(1)} fusion(f32[1,8,16,128]{3,2,1,0:T(8,128)} %bitcast.79, f32[1,8,16,128]{3,2,1,0:T(8,128)} %bitcast.83, f32[2,8,16,128]{3,2,1,0:T(8,128)} %param.30), kind=kLoop, calls=%fused_computation.83 | loop fusion | flops 131072 | bytes 524288 | tf_op jit(solution)/shard_map/concatenate | solution.py:267
  4.1 1.3 %fusion.230 = f32[512,64]{0,1:T(8,128)S(1)} fusion(f32[512,128]{1,0:T(8,128)S(1)} %bitcast.90, f32[128,64]{1,0:T(8,128)} %constant.21.clone), kind=kOutput, calls=%fused_computation.396 | convolution fusion | flops 50331648 | bytes 425984 | tf_op jit(solution)/shard_map/dot_general | solution.py:184
  5.4 1.3 %convolution_multiply_fusion.1 = f32[64,128]{1,0:T(8,128)S(1)} fusion(f32[512,64]{0,1:T(8,128)S(1)} %fusion.230, f32[128,512]{1,0:T(8,128)} %constant.22.clone), kind=kOutput, calls=%fused_computation.3 | convolution fusion | flops 50339840 | bytes 425984 | tf_op jit(solution)/shard_map/dot_general | solution.py:185
  6.7 0.8 fusion.164
  7.9 0.6 fusion.185
  8.5 0.8 pad_maximum_fusion.2.refs_1_
  11.8 0.6 select_select_fusion.refs_0_
  12.4 21.1 %shard_map.280 = (f32[8,128]{1,0:T(8,128)}, f32[6,8,6,128]{3,2,1,0:T(8,128)}, f32[6,8,6,128]{3,2,1,0:T(8,128)}) custom-call(f32[8,128]{1,0:T(8,128)} %select_select_fusion.refs_0_, f32[6,8,16,128]{3,2,1,0:T(8,128)} %pad_maximum_fusion.2.refs_1_), custom_call_target="tpu_custom_call" | custom-call | tf_op jit(solution)/shard_map/pallas_call | solution.py:149
  33.5 1.1 %pad_maximum_fusion.1 = f32[6,8,28,128]{3,2,1,0:T(8,128)S(1)} fusion(f32[6,8,6,128]{3,2,1,0:T(8,128)} %get-tuple-element.9, f32[2,8,16,128]{3,2,1,0:T(8,128)S(1)} %copy-done.3, f32[1,8,16,128]{3,2,1,0:T(8,128)S(1)} %bitcast.81, f32[1,8,16,128]{3,2,1,0:T(8,128)S(1)} %bitcast.85, f32[2,8,16,128]{3,2,1,0:T(8,128)S(1)} %copy-done, ...), kind=kLoop, calls=%fused_computation.6 | loop fusion | flops 860160 | bytes 1376256 | tf_op jit(solution)/shard_map/concatenate | solution.py:174
  34.7 0.3 fusion.198
  35.0 0.4 copy.48
  35.5 0.4 copy.47
  36.0 0.4 collective-permute-start
  36.4 1.4 %fusion.229 = (f32[1,1]{1,0:T(1,128)}, f32[1,1]{1,0:T(1,128)}, f32[1,1]{1,0:T(1,128)}) fusion(f32[8,128]{1,0:T(8,128)} %get-tuple-element.10), kind=kLoop, calls=%fused_computation.395 | loop fusion | bytes 24 | tf_op jit(solution)/shard_map/slice | solution.py:305
  38.7 0.4 copy.50
  39.2 2.6 %collective-permute-done = f32[6,8,28,6]{2,1,3,0:T(8,128)S(1)} collective-permute-done((f32[6,8,28,6]{2,1,3,0:T(8,128)S(1)}, f32[6,8,28,6]{2,1,3,0:T(8,128)S(1)}, u32[]{:S(2)}, u32[]{:S(2)}) %collective-permute-start) | collective-permute-done | bytes 32288 | tf_op jit(solution)/shard_map/ppermute | solution.py:25
  41.7 0.4 copy.49
  42.2 0.9 pad_maximum_fusion
  43.1 0.4 fusion.39
  43.7 0.3 fusion.197
  44.0 0.4 subtract_bitcast_fusion
  44.3 0.8 fusion.9
  45.5 0.4 fusion.51
  45.9 0.6 slice_add_fusion.12
  46.5 0.4 fusion.49
  47.3 0.7 fusion.30
  48.8 0.3 fusion.232
  49.5 0.5 collective-permute-start.2
  50.0 1.7 %collective-permute-done.3 = f32[6,4,8,7]{3,2,1,0:T(8,128)S(1)} collective-permute-done((f32[6,4,8,7]{3,2,1,0:T(8,128)S(1)}, f32[6,4,8,7]{3,2,1,0:T(8,128)S(1)}, u32[]{:S(2)}, u32[]{:S(2)}) %collective-permute-start.3) | collective-permute-done | bytes 5408 | tf_op jit(solution)/shard_map/ppermute | solution.py:26
  51.7 3.1 %collective-permute-done.2 = f32[6,4,8,7]{3,2,1,0:T(8,128)S(1)} collective-permute-done((f32[6,4,8,7]{3,2,1,0:T(8,128)S(1)}, f32[6,4,8,7]{3,2,1,0:T(8,128)S(1)}, u32[]{:S(2)}, u32[]{:S(2)}) %collective-permute-start.2) | collective-permute-done | bytes 5408 | tf_op jit(solution)/shard_map/ppermute | solution.py:25
  55.0 4.7 %collective-permute-start.5 = (f32[6,4,7,78]{3,2,1,0:T(8,128)S(1)}, f32[6,4,7,78]{3,2,1,0:T(8,128)S(1)}, u32[]{:S(2)}, u32[]{:S(2)}) collective-permute-start(f32[6,4,7,78]{3,2,1,0:T(8,128)S(1)} %get-tuple-element.132), channel_id=1, source_target_pairs={{1,0},{2,1},{3,2},{4,3},{5,4},{6,5},{7,6},{8,7},{9,8},{10,9},{11,1... | collective-permute-start | bytes 157256 | tf_op jit(solution)/shard_map/ppermute | solution.py:26
  60.6 1.3 %collective-permute-done.5 = f32[6,4,7,78]{3,2,1,0:T(8,128)S(1)} collective-permute-done((f32[6,4,7,78]{3,2,1,0:T(8,128)S(1)}, f32[6,4,7,78]{3,2,1,0:T(8,128)S(1)}, u32[]{:S(2)}, u32[]{:S(2)}) %collective-permute-start.5) | collective-permute-done | bytes 52448 | tf_op jit(solution)/shard_map/ppermute | solution.py:26
  61.9 5.7 %collective-permute-done.4 = f32[6,4,7,78]{3,2,1,0:T(8,128)S(1)} collective-permute-done((f32[6,4,7,78]{3,2,1,0:T(8,128)S(1)}, f32[6,4,7,78]{3,2,1,0:T(8,128)S(1)}, u32[]{:S(2)}, u32[]{:S(2)}) %collective-permute-start.4) | collective-permute-done | bytes 52448 | tf_op jit(solution)/shard_map/ppermute | solution.py:25
  69.9 0.5 collective-permute-start.6
  70.4 1.0 %collective-permute-done.7 = f32[6,2,4,8]{3,2,1,0:T(4,128)S(1)} collective-permute-done((f32[6,2,4,8]{3,2,1,0:T(4,128)S(1)}, f32[6,2,4,8]{3,2,1,0:T(4,128)S(1)}, u32[]{:S(2)}, u32[]{:S(2)}) %collective-permute-start.7) | collective-permute-done | bytes 1568 | tf_op jit(solution)/shard_map/ppermute | solution.py:26
  71.4 3.0 %collective-permute-done.6 = f32[6,2,4,8]{3,2,1,0:T(4,128)S(1)} collective-permute-done((f32[6,2,4,8]{3,2,1,0:T(4,128)S(1)}, f32[6,2,4,8]{3,2,1,0:T(4,128)S(1)}, u32[]{:S(2)}, u32[]{:S(2)}) %collective-permute-start.6) | collective-permute-done | bytes 1568 | tf_op jit(solution)/shard_map/ppermute | solution.py:25
  74.7 5.3 %collective-permute-start.10 = (f32[6,2,4,48]{3,2,1,0:T(4,128)S(1)}, f32[6,2,4,48]{3,2,1,0:T(4,128)S(1)}, u32[]{:S(2)}, u32[]{:S(2)}) collective-permute-start(f32[6,2,4,48]{3,2,1,0:T(4,128)S(1)} %pad_maximum_fusion.13), channel_id=1, source_target_pairs={{1,0},{2,1},{3,2},{4,3},{5,4},{6,5},{7,6},{8,7},{9,8},{10,9},{11,1... | collective-permute-start | bytes 27656 | tf_op jit(solution)/shard_map/ppermute | solution.py:26
  80.0 2.8 %collective-permute-start.11 = (f32[6,2,4,48]{3,2,1,0:T(4,128)S(1)}, f32[6,2,4,48]{3,2,1,0:T(4,128)S(1)}, u32[]{:S(2)}, u32[]{:S(2)}) collective-permute-start(f32[6,2,4,48]{3,2,1,0:T(4,128)S(1)} %pad_maximum_fusion.13), channel_id=1, source_target_pairs={{2,0},{3,1},{4,2},{5,3},{6,4},{7,5},{8,6},{9,7},{10,8},{11,9},{12,... | collective-permute-start | bytes 27656 | tf_op jit(solution)/shard_map/ppermute | solution.py:26
  83.8 1.1 %collective-permute-done.11 = f32[6,2,4,48]{3,2,1,0:T(4,128)S(1)} collective-permute-done((f32[6,2,4,48]{3,2,1,0:T(4,128)S(1)}, f32[6,2,4,48]{3,2,1,0:T(4,128)S(1)}, u32[]{:S(2)}, u32[]{:S(2)}) %collective-permute-start.11) | collective-permute-done | bytes 9248 | tf_op jit(solution)/shard_map/ppermute | solution.py:26
  88.8 0.3 copy.57
  89.2 0.3 slice.2051
  89.5 0.7 copy.60
  90.3 0.4 fusion.47
  91.0 0.6 slice_add_fusion.7
  91.7 0.4 fusion.45
  92.4 0.7 slice_add_fusion.4
  93.5 0.9 fusion.59
  (127 shorter events, 10.2 us)
Async XLA Ops:
  0.0 7.5 %copy-start.7 = (f32[64,32]{1,0:T(8,128)S(1)}, f32[64,32]{1,0:T(8,128)}, u32[]{:S(2)}) copy-start(f32[64,32]{1,0:T(8,128)} %constant.23.clone) | copy-start | bytes 24580
  0.0 7.7 %copy-start.11 = (f32[32,128]{1,0:T(8,128)S(1)}, f32[32,128]{1,0:T(8,128)}, u32[]{:S(2)}) copy-start(f32[32,128]{1,0:T(8,128)} %constant.24.clone) | copy-start | bytes 49156
  0.0 8.5 %copy-start.1 = (f32[8,16,128]{2,1,0:T(8,128)S(1)}, f32[8,16,128]{2,1,0:T(8,128)}, u32[]{:S(2)}) copy-start(f32[8,16,128]{2,1,0:T(8,128)} %param.33) | copy-start | bytes 196612
  0.0 8.5 %copy-start.2 = (f32[8,16,128]{2,1,0:T(8,128)S(1)}, f32[8,16,128]{2,1,0:T(8,128)}, u32[]{:S(2)}) copy-start(f32[8,16,128]{2,1,0:T(8,128)} %param.32) | copy-start | bytes 196612
  0.0 8.5 %copy-start = (f32[2,8,16,128]{3,2,1,0:T(8,128)S(1)}, f32[2,8,16,128]{3,2,1,0:T(8,128)}, u32[]{:S(2)}) copy-start(f32[2,8,16,128]{3,2,1,0:T(8,128)} %param.30) | copy-start | bytes 393220
  0.0 8.5 %copy-start.3 = (f32[2,8,16,128]{3,2,1,0:T(8,128)S(1)}, f32[2,8,16,128]{3,2,1,0:T(8,128)}, u32[]{:S(2)}) copy-start(f32[2,8,16,128]{3,2,1,0:T(8,128)} %param.31) | copy-start | bytes 393220
  35.4 6.8 %copy-start.4 = (f32[6,8,6,128]{3,2,1,0:T(8,128)S(1)}, f32[6,8,6,128]{3,2,1,0:T(8,128)}, u32[]{:S(2)}) copy-start(f32[6,8,6,128]{3,2,1,0:T(8,128)} %get-tuple-element.8) | copy-start | bytes 442372
  35.4 6.8 %copy-start.5 = (f32[6,8,6,128]{3,2,1,0:T(8,128)S(1)}, f32[6,8,6,128]{3,2,1,0:T(8,128)}, u32[]{:S(2)}) copy-start(f32[6,8,6,128]{3,2,1,0:T(8,128)} %get-tuple-element.9) | copy-start | bytes 442372
  35.4 3.3 %collective-permute-start.1 = (f32[6,8,28,6]{2,1,3,0:T(8,128)S(1)}, f32[6,8,28,6]{2,1,3,0:T(8,128)S(1)}, u32[]{:S(2)}, u32[]{:S(2)}) collective-permute-start(f32[6,8,28,6]{2,1,3,0:T(8,128)S(1)} %copy.48), channel_id=1, source_target_pairs={{32,0},{64,32},{96,64},{128,96},{160,128},{192,160},{224,192},{0,2... | collective-permute-start | bytes 96776 | tf_op jit(solution)/shard_map/ppermute | solution.py:26
  36.0 5.8 %collective-permute-start = (f32[6,8,28,6]{2,1,3,0:T(8,128)S(1)}, f32[6,8,28,6]{2,1,3,0:T(8,128)S(1)}, u32[]{:S(2)}, u32[]{:S(2)}) collective-permute-start(f32[6,8,28,6]{2,1,3,0:T(8,128)S(1)} %copy.47), channel_id=1, source_target_pairs={{0,32},{32,64},{64,96},{96,128},{128,160},{160,192},{192,224},{224... | collective-permute-start | bytes 96776 | tf_op jit(solution)/shard_map/ppermute | solution.py:25
  43.6 0.7 copy-start.9
  48.0 0.8 copy-start.6
  48.0 1.1 %copy-start.8 = (f32[64,256]{1,0:T(8,128)S(1)}, f32[64,256]{1,0:T(8,128)}, u32[]{:S(2)}) copy-start(f32[64,256]{1,0:T(8,128)} %constant.26.clone) | copy-start | bytes 196612
  49.5 2.2 %collective-permute-start.3 = (f32[6,4,8,7]{3,2,1,0:T(8,128)S(1)}, f32[6,4,8,7]{3,2,1,0:T(8,128)S(1)}, u32[]{:S(2)}, u32[]{:S(2)}) collective-permute-start(f32[6,4,8,7]{3,2,1,0:T(8,128)S(1)} %get-tuple-element.134), channel_id=1, source_target_pairs={{32,0},{64,32},{96,64},{128,96},{160,128},{192,160},{224,192},{0,2... | collective-permute-start | bytes 16136 | tf_op jit(solution)/shard_map/ppermute | solution.py:26
  49.5 18.7 %copy-start.10 = (f32[2]{0:T(128)S(1)}, f32[2]{0:T(128)}, u32[]{:S(2)}) copy-start(f32[2]{0:T(128)} %constant.84.clone) | copy-start | bytes 28
  49.5 5.3 %collective-permute-start.2 = (f32[6,4,8,7]{3,2,1,0:T(8,128)S(1)}, f32[6,4,8,7]{3,2,1,0:T(8,128)S(1)}, u32[]{:S(2)}, u32[]{:S(2)}) collective-permute-start(f32[6,4,8,7]{3,2,1,0:T(8,128)S(1)} %get-tuple-element.133), channel_id=1, source_target_pairs={{0,32},{32,64},{64,96},{96,128},{128,160},{160,192},{192,224},{224... | collective-permute-start | bytes 16136 | tf_op jit(solution)/shard_map/ppermute | solution.py:25
  55.0 6.9 %collective-permute-start.5 = (f32[6,4,7,78]{3,2,1,0:T(8,128)S(1)}, f32[6,4,7,78]{3,2,1,0:T(8,128)S(1)}, u32[]{:S(2)}, u32[]{:S(2)}) collective-permute-start(f32[6,4,7,78]{3,2,1,0:T(8,128)S(1)} %get-tuple-element.132), channel_id=1, source_target_pairs={{1,0},{2,1},{3,2},{4,3},{5,4},{6,5},{7,6},{8,7},{9,8},{10,9},{11,1... | collective-permute-start | bytes 157256 | tf_op jit(solution)/shard_map/ppermute | solution.py:26
  59.7 7.9 %collective-permute-start.4 = (f32[6,4,7,78]{3,2,1,0:T(8,128)S(1)}, f32[6,4,7,78]{3,2,1,0:T(8,128)S(1)}, u32[]{:S(2)}, u32[]{:S(2)}) collective-permute-start(f32[6,4,7,78]{3,2,1,0:T(8,128)S(1)} %get-tuple-element.131), channel_id=1, source_target_pairs={{0,1},{1,2},{2,3},{3,4},{4,5},{5,6},{6,7},{7,8},{8,9},{9,10},{10,1... | collective-permute-start | bytes 157256 | tf_op jit(solution)/shard_map/ppermute | solution.py:25
  68.4 1.2 %copy-start.13 = (f32[16,64]{1,0:T(8,128)S(1)}, f32[16,64]{1,0:T(8,128)}, u32[]{:S(2)}) copy-start(f32[16,64]{1,0:T(8,128)} %constant.85.clone) | copy-start | bytes 12292
  68.8 16.4 %copy-start.12 = (f32[2]{0:T(128)S(1)}, f32[2]{0:T(128)}, u32[]{:S(2)}) copy-start(f32[2]{0:T(128)} %constant.86.clone) | copy-start | bytes 28
  69.9 1.5 %collective-permute-start.7 = (f32[6,2,4,8]{3,2,1,0:T(4,128)S(1)}, f32[6,2,4,8]{3,2,1,0:T(4,128)S(1)}, u32[]{:S(2)}, u32[]{:S(2)}) collective-permute-start(f32[6,2,4,8]{3,2,1,0:T(4,128)S(1)} %get-tuple-element.188), channel_id=1, source_target_pairs={{32,0},{64,32},{96,64},{128,96},{160,128},{192,160},{224,192},{0,2... | collective-permute-start | bytes 4616 | tf_op jit(solution)/shard_map/ppermute | solution.py:26
  69.9 4.5 %collective-permute-start.6 = (f32[6,2,4,8]{3,2,1,0:T(4,128)S(1)}, f32[6,2,4,8]{3,2,1,0:T(4,128)S(1)}, u32[]{:S(2)}, u32[]{:S(2)}) collective-permute-start(f32[6,2,4,8]{3,2,1,0:T(4,128)S(1)} %get-tuple-element.187), channel_id=1, source_target_pairs={{0,32},{32,64},{64,96},{96,128},{128,160},{160,192},{192,224},{224... | collective-permute-start | bytes 4616 | tf_op jit(solution)/shard_map/ppermute | solution.py:25
  74.5 9.3 %collective-permute-start.8 = (f32[6,2,4,48]{3,2,1,0:T(4,128)S(1)}, f32[6,2,4,48]{3,2,1,0:T(4,128)S(1)}, u32[]{:S(2)}, u32[]{:S(2)}) collective-permute-start(f32[6,2,4,48]{3,2,1,0:T(4,128)S(1)} %pad_maximum_fusion.13), channel_id=1, source_target_pairs={{0,2},{1,3},{2,4},{3,5},{4,6},{5,7},{6,8},{7,9},{8,10},{9,11},{10,... | collective-permute-start | bytes 27656 | tf_op jit(solution)/shard_map/ppermute | solution.py:25
  74.6 9.2 %collective-permute-start.9 = (f32[6,2,4,48]{3,2,1,0:T(4,128)S(1)}, f32[6,2,4,48]{3,2,1,0:T(4,128)S(1)}, u32[]{:S(2)}, u32[]{:S(2)}) collective-permute-start(f32[6,2,4,48]{3,2,1,0:T(4,128)S(1)} %pad_maximum_fusion.13), channel_id=1, source_target_pairs={{0,1},{1,2},{2,3},{3,4},{4,5},{5,6},{6,7},{7,8},{8,9},{9,10},{10,1... | collective-permute-start | bytes 27656 | tf_op jit(solution)/shard_map/ppermute | solution.py:25
  74.7 9.1 %collective-permute-start.10 = (f32[6,2,4,48]{3,2,1,0:T(4,128)S(1)}, f32[6,2,4,48]{3,2,1,0:T(4,128)S(1)}, u32[]{:S(2)}, u32[]{:S(2)}) collective-permute-start(f32[6,2,4,48]{3,2,1,0:T(4,128)S(1)} %pad_maximum_fusion.13), channel_id=1, source_target_pairs={{1,0},{2,1},{3,2},{4,3},{5,4},{6,5},{7,6},{8,7},{9,8},{10,9},{11,1... | collective-permute-start | bytes 27656 | tf_op jit(solution)/shard_map/ppermute | solution.py:26
  80.0 4.8 %collective-permute-start.11 = (f32[6,2,4,48]{3,2,1,0:T(4,128)S(1)}, f32[6,2,4,48]{3,2,1,0:T(4,128)S(1)}, u32[]{:S(2)}, u32[]{:S(2)}) collective-permute-start(f32[6,2,4,48]{3,2,1,0:T(4,128)S(1)} %pad_maximum_fusion.13), channel_id=1, source_target_pairs={{2,0},{3,1},{4,2},{5,3},{6,4},{7,5},{8,6},{9,7},{10,8},{11,9},{12,... | collective-permute-start | bytes 27656 | tf_op jit(solution)/shard_map/ppermute | solution.py:26

commit v12 on v10

--- a/solution.py
+++ b/solution.py
@@ -243,11 +243,11 @@
     for level, level_fields in enumerate((fields, fields_1, fields_2)):
         _, first, second = coefficients(level_fields, level)
         local = jnp.where(lane == level, jnp.maximum(jnp.max(first), jnp.max(second)), local)
-    wide_x = padded_along(jnp.concatenate([fields, previous], 0), 6, "gx", 3)
+    wide_x = padded_along(jnp.concatenate([fields, previous], 0), 6, "gy", 2)
     local, wide_x = lax.optimization_barrier((local, wide_x))
     spreads = global_max(local)[0]
 
-    wide = padded_along(wide_x, 6, "gy", 2)
+    wide = padded_along(wide_x, 6, "gx", 3)
     ops_0 = Level(coefficients(crop(wide[:4], 6, 5), 0)[0], 5, 0)
     state_w = wide[:2]
     substrate, catalyst = crop(state_w[0], 6, 5), crop(state_w[1], 6, 5)

time: 90.8 us -> 93 us (1.024)
  local copies, waits for them, and re-layouts: 7.6 us -> 9.87 us
  starting transfers between devices: 22.9 us -> 21.9 us
    ppermute x7, starting transfers between devices: 22.2 us -> 20.7 us  [padded_along(): lax.ppermute(head, axis, [((i + distance) % count, i) for i in range(coun...]
    ppermute x7, waiting for transfers between devices: 12.2 us -> 13.5 us  [padded_along(): lax.ppermute(tail, axis, [(i, (i + distance) % count) for i in range(coun...]
  transfers between devices with their start and end apart: 14 -> 14, of which waited for: 8 -> 8; matrix products, arithmetic and copies ran while one was open for 6% -> 7% of each run, Pallas kernels for 19% -> 18%
where the time goes in v12:
time: 93 us; the launch traced here: 92.7 us
  starting transfers between devices  21.9 us (24%)
  waiting for transfers between devices  18.6 us (20%)
  Pallas kernels  17.1 us (18%)
  other arithmetic  15.8 us (17%)
  local copies, waits for them, and re-layouts  9.87 us (11%)
  between operations  7.39 us (8%)
  matrix products  2.02 us (2%)
    ppermute x7, starting transfers between devices, padded_along(): lax.ppermute(head, axis, [((i + distance) % count, i) for i in range(coun...  20.7 us
    pallas_call x1, Pallas kernels, global_max(): pl.pallas_call(spread_kernel, out_shape=jax.ShapeDtypeStruct(block.shape,...  17.1 us
    ppermute x7, waiting for transfers between devices, padded_along(): lax.ppermute(tail, axis, [(i, (i + distance) % count) for i in range(coun...  13.5 us
    ppermute x7, waiting for transfers between devices, padded_along(): lax.ppermute(head, axis, [((i + distance) % count, i) for i in range(coun...  5.12 us
    add x12, other arithmetic, chebyshev(): iterate = crop(iterate, halo + 1, halo) + update  4.37 us
    slice x30, local copies, waits for them, and re-layouts, shrunk_neighbours(): along_z = jnp.roll(centre, 1, 1) + jnp.roll(centre, -1, 1)  3.45 us
    add x17, other arithmetic, operate(): first = coeff[0] * centre[0] + coeff[1] * centre[1]  3.18 us
    reduce_max x3, other arithmetic, body(): jnp.max(second)  2.16 us
  transfers between devices with their start and end apart: 14, of which 8 were waited for; matrix products, arithmetic and copies ran while one was open for 7% of the time, Pallas kernels for 18%

profile of v12, /device:TPU:0, one launch (start us, length us, event | category | flops | bytes accessed | tf_op | source)
XLA Modules:
  0.0 92.7 jit_solution(8435765365120688536)
XLA Ops:
  0.0 1.1 %pad_maximum_fusion.6 = f32[6,8,16,128]{3,2,1,0:T(8,128)S(1)} fusion(f32[2,8,16,128]{3,2,1,0:T(8,128)} %param.31, f32[1,8,16,128]{3,2,1,0:T(8,128)} %bitcast.86, f32[1,8,16,128]{3,2,1,0:T(8,128)} %bitcast.89, f32[2,8,16,128]{3,2,1,0:T(8,128)} %param.30), kind=kLoop, calls=%fused_computation.66 | loop fusion | flops 294912 | bytes 786432 | tf_op jit(solution)/shard_map/concatenate | solution.py:246
  1.2 6.7 %collective-permute-start.1 = (f32[6,8,6,128]{3,2,1,0:T(8,128)S(1)}, f32[6,8,6,128]{3,2,1,0:T(8,128)S(1)}, u32[]{:S(2)}, u32[]{:S(2)}) collective-permute-start(f32[6,8,6,128]{3,2,1,0:T(8,128)S(1)} %get-tuple-element.90), channel_id=1, source_target_pairs={{1,0},{2,1},{3,2},{4,3},{5,4},{6,5},{7,6},{8,7},{9,8},{10,9},{11,1... | collective-permute-start | bytes 442376 | tf_op jit(solution)/shard_map/ppermute | solution.py:26
  7.9 0.7 fusion.107
  8.6 0.4 fusion.233
  9.1 0.4 convolution_multiply_fusion.1
  9.5 0.8 fusion.167
  12.0 0.7 fusion.188
  15.2 0.6 select_select_fusion.value
  15.8 1.7 %collective-permute-done = f32[6,8,6,128]{3,2,1,0:T(8,128)S(1)} collective-permute-done((f32[6,8,6,128]{3,2,1,0:T(8,128)S(1)}, f32[6,8,6,128]{3,2,1,0:T(8,128)S(1)}, u32[]{:S(2)}, u32[]{:S(2)}) %collective-permute-start) | collective-permute-done | bytes 147488 | tf_op jit(solution)/shard_map/ppermute | solution.py:25
  17.7 0.3 fusion.200
  18.0 0.4 copy.54
  18.4 1.0 %collective-permute-start.3 = (f32[6,8,28,6]{2,1,3,0:T(8,128)S(1)}, f32[6,8,28,6]{2,1,3,0:T(8,128)S(1)}, u32[]{:S(2)}, u32[]{:S(2)}) collective-permute-start(f32[6,8,28,6]{2,1,3,0:T(8,128)S(1)} %copy.54), channel_id=1, source_target_pairs={{32,0},{64,32},{96,64},{128,96},{160,128},{192,160},{224,192},{0,2... | collective-permute-start | bytes 96776 | tf_op jit(solution)/shard_map/ppermute | solution.py:26
  19.4 0.4 copy.53
  19.8 17.1 %shard_map.280 = f32[8,128]{1,0:T(8,128)} custom-call(f32[8,128]{1,0:T(8,128)} %select_select_fusion.value), custom_call_target="tpu_custom_call" | custom-call | tf_op jit(solution)/shard_map/pallas_call | solution.py:129
  37.0 1.4 %fusion.232 = (f32[1,1]{1,0:T(1,128)}, f32[1,1]{1,0:T(1,128)}, f32[1,1]{1,0:T(1,128)}) fusion(f32[8,128]{1,0:T(8,128)} %shard_map.280), kind=kLoop, calls=%fused_computation.401 | loop fusion | bytes 24 | tf_op jit(solution)/shard_map/slice | solution.py:277
  39.3 0.4 copy.56
  39.8 0.4 copy.55
  40.2 0.7 pad_maximum_fusion
  40.9 0.4 fusion.42
  41.3 0.3 fusion.199
  41.7 0.4 subtract_bitcast_fusion
  42.0 0.9 fusion.12
  43.2 0.4 fusion.54
  43.7 0.6 slice_add_fusion.12
  44.3 0.4 fusion.52
  44.8 0.2 fusion.212
  45.0 0.7 fusion.33
  46.6 0.3 fusion.235
  47.3 0.5 collective-permute-start.4
  47.8 1.7 %collective-permute-done.5 = f32[6,4,8,7]{3,2,1,0:T(8,128)S(1)} collective-permute-done((f32[6,4,8,7]{3,2,1,0:T(8,128)S(1)}, f32[6,4,8,7]{3,2,1,0:T(8,128)S(1)}, u32[]{:S(2)}, u32[]{:S(2)}) %collective-permute-start.5) | collective-permute-done | bytes 5408 | tf_op jit(solution)/shard_map/ppermute | solution.py:26
  49.5 3.1 %collective-permute-done.4 = f32[6,4,8,7]{3,2,1,0:T(8,128)S(1)} collective-permute-done((f32[6,4,8,7]{3,2,1,0:T(8,128)S(1)}, f32[6,4,8,7]{3,2,1,0:T(8,128)S(1)}, u32[]{:S(2)}, u32[]{:S(2)}) %collective-permute-start.4) | collective-permute-done | bytes 5408 | tf_op jit(solution)/shard_map/ppermute | solution.py:25
  52.8 4.8 %collective-permute-start.7 = (f32[6,4,7,78]{3,2,1,0:T(8,128)S(1)}, f32[6,4,7,78]{3,2,1,0:T(8,128)S(1)}, u32[]{:S(2)}, u32[]{:S(2)}) collective-permute-start(f32[6,4,7,78]{3,2,1,0:T(8,128)S(1)} %get-tuple-element.130), channel_id=1, source_target_pairs={{1,0},{2,1},{3,2},{4,3},{5,4},{6,5},{7,6},{8,7},{9,8},{10,9},{11,1... | collective-permute-start | bytes 157256 | tf_op jit(solution)/shard_map/ppermute | solution.py:26
  58.5 1.3 %collective-permute-done.7 = f32[6,4,7,78]{3,2,1,0:T(8,128)S(1)} collective-permute-done((f32[6,4,7,78]{3,2,1,0:T(8,128)S(1)}, f32[6,4,7,78]{3,2,1,0:T(8,128)S(1)}, u32[]{:S(2)}, u32[]{:S(2)}) %collective-permute-start.7) | collective-permute-done | bytes 52448 | tf_op jit(solution)/shard_map/ppermute | solution.py:26
  59.8 5.7 %collective-permute-done.6 = f32[6,4,7,78]{3,2,1,0:T(8,128)S(1)} collective-permute-done((f32[6,4,7,78]{3,2,1,0:T(8,128)S(1)}, f32[6,4,7,78]{3,2,1,0:T(8,128)S(1)}, u32[]{:S(2)}, u32[]{:S(2)}) %collective-permute-start.6) | collective-permute-done | bytes 52448 | tf_op jit(solution)/shard_map/ppermute | solution.py:25
  67.8 0.5 collective-permute-start.8
  68.3 1.0 %collective-permute-done.9 = f32[6,2,4,8]{3,2,1,0:T(4,128)S(1)} collective-permute-done((f32[6,2,4,8]{3,2,1,0:T(4,128)S(1)}, f32[6,2,4,8]{3,2,1,0:T(4,128)S(1)}, u32[]{:S(2)}, u32[]{:S(2)}) %collective-permute-start.9) | collective-permute-done | bytes 1568 | tf_op jit(solution)/shard_map/ppermute | solution.py:26
  69.3 3.0 %collective-permute-done.8 = f32[6,2,4,8]{3,2,1,0:T(4,128)S(1)} collective-permute-done((f32[6,2,4,8]{3,2,1,0:T(4,128)S(1)}, f32[6,2,4,8]{3,2,1,0:T(4,128)S(1)}, u32[]{:S(2)}, u32[]{:S(2)}) %collective-permute-start.8) | collective-permute-done | bytes 1568 | tf_op jit(solution)/shard_map/ppermute | solution.py:25
  72.6 5.3 %collective-permute-start.12 = (f32[6,2,4,48]{3,2,1,0:T(4,128)S(1)}, f32[6,2,4,48]{3,2,1,0:T(4,128)S(1)}, u32[]{:S(2)}, u32[]{:S(2)}) collective-permute-start(f32[6,2,4,48]{3,2,1,0:T(4,128)S(1)} %pad_maximum_fusion.17), channel_id=1, source_target_pairs={{1,0},{2,1},{3,2},{4,3},{5,4},{6,5},{7,6},{8,7},{9,8},{10,9},{11,1... | collective-permute-start | bytes 27656 | tf_op jit(solution)/shard_map/ppermute | solution.py:26
  77.9 2.8 %collective-permute-start.13 = (f32[6,2,4,48]{3,2,1,0:T(4,128)S(1)}, f32[6,2,4,48]{3,2,1,0:T(4,128)S(1)}, u32[]{:S(2)}, u32[]{:S(2)}) collective-permute-start(f32[6,2,4,48]{3,2,1,0:T(4,128)S(1)} %pad_maximum_fusion.17), channel_id=1, source_target_pairs={{2,0},{3,1},{4,2},{5,3},{6,4},{7,5},{8,6},{9,7},{10,8},{11,9},{12,... | collective-permute-start | bytes 27656 | tf_op jit(solution)/shard_map/ppermute | solution.py:26
  81.7 1.1 %collective-permute-done.13 = f32[6,2,4,48]{3,2,1,0:T(4,128)S(1)} collective-permute-done((f32[6,2,4,48]{3,2,1,0:T(4,128)S(1)}, f32[6,2,4,48]{3,2,1,0:T(4,128)S(1)}, u32[]{:S(2)}, u32[]{:S(2)}) %collective-permute-start.13) | collective-permute-done | bytes 9248 | tf_op jit(solution)/shard_map/ppermute | solution.py:26
  86.7 0.3 copy.63
  87.1 0.3 slice.2057
  87.5 0.7 copy.66
  88.5 0.4 fusion.50
  89.2 0.6 slice_add_fusion.7
  89.9 0.4 fusion.48
  90.6 0.7 slice_add_fusion.4
  91.7 1.0 %fusion.62 = f32[2,8,16,128]{3,2,1,0:T(8,128)} fusion(f32[2,8,18,130]{3,2,1,0:T(8,128)S(1)} %get-tuple-element.16, f32[2,8,18,130]{3,2,1,0:T(8,128)S(1)} %get-tuple-element.15, f32[1,8,16,128]{3,2,1,0:T(8,128)S(1)} %get-tuple-element.94, f32[1,8,16,128]{3,2,1,0:T(8,128)S(1)} %get-tuple-element.98, f32[2,1,16,128]{3,2,1,0:T(8,128)S(1)} %get-tuple-element.62, ...), kind=kLoop, calls=%fused_computation.120 | loop fusion | flops 557056 | bytes 1572880 | tf_op jit(solution)/shard_map/add | solution.py:231
  (143 shorter events, 10.2 us)
Async XLA Ops:
  0.0 8.6 %copy-start.8 = (f32[128,64]{1,0:T(8,128)S(1)}, f32[128,64]{1,0:T(8,128)}, u32[]{:S(2)}) copy-start(f32[128,64]{1,0:T(8,128)} %constant.21.clone) | copy-start | bytes 98308
  0.0 9.1 %copy-start.10 = (f32[128,512]{1,0:T(8,128)S(1)}, f32[128,512]{1,0:T(8,128)}, u32[]{:S(2)}) copy-start(f32[128,512]{1,0:T(8,128)} %constant.22.clone) | copy-start | bytes 786436
  0.0 7.9 %copy-start.4 = (f32[2,8,16,128]{3,2,1,0:T(8,128)S(1)}, f32[2,8,16,128]{3,2,1,0:T(8,128)}, u32[]{:S(2)}) copy-start(f32[2,8,16,128]{3,2,1,0:T(8,128)} %param.30) | copy-start | bytes 393220
  0.0 7.9 %copy-start.5 = (f32[8,16,128]{2,1,0:T(8,128)S(1)}, f32[8,16,128]{2,1,0:T(8,128)}, u32[]{:S(2)}) copy-start(f32[8,16,128]{2,1,0:T(8,128)} %param.33) | copy-start | bytes 196612
  0.0 7.9 %copy-start.6 = (f32[8,16,128]{2,1,0:T(8,128)S(1)}, f32[8,16,128]{2,1,0:T(8,128)}, u32[]{:S(2)}) copy-start(f32[8,16,128]{2,1,0:T(8,128)} %param.32) | copy-start | bytes 196612
  0.0 11.6 %copy-start.11 = (f32[64,32]{1,0:T(8,128)S(1)}, f32[64,32]{1,0:T(8,128)}, u32[]{:S(2)}) copy-start(f32[64,32]{1,0:T(8,128)} %constant.23.clone) | copy-start | bytes 24580
  1.1 10.7 %copy-start.17 = (f32[32,128]{1,0:T(8,128)S(1)}, f32[32,128]{1,0:T(8,128)}, u32[]{:S(2)}) copy-start(f32[32,128]{1,0:T(8,128)} %constant.24.clone) | copy-start | bytes 49156
  1.2 16.4 %copy-start.7 = (f32[2,8,16,128]{3,2,1,0:T(8,128)S(1)}, f32[2,8,16,128]{3,2,1,0:T(8,128)}, u32[]{:S(2)}) copy-start(f32[2,8,16,128]{3,2,1,0:T(8,128)} %param.31) | copy-start | bytes 393220
  1.2 14.6 %collective-permute-start.1 = (f32[6,8,6,128]{3,2,1,0:T(8,128)S(1)}, f32[6,8,6,128]{3,2,1,0:T(8,128)S(1)}, u32[]{:S(2)}, u32[]{:S(2)}) collective-permute-start(f32[6,8,6,128]{3,2,1,0:T(8,128)S(1)} %get-tuple-element.90), channel_id=1, source_target_pairs={{1,0},{2,1},{3,2},{4,3},{5,4},{6,5},{7,6},{8,7},{9,8},{10,9},{11,1... | collective-permute-start | bytes 442376 | tf_op jit(solution)/shard_map/ppermute | solution.py:26
  7.9 9.7 %collective-permute-start = (f32[6,8,6,128]{3,2,1,0:T(8,128)S(1)}, f32[6,8,6,128]{3,2,1,0:T(8,128)S(1)}, u32[]{:S(2)}, u32[]{:S(2)}) collective-permute-start(f32[6,8,6,128]{3,2,1,0:T(8,128)S(1)} %get-tuple-element.89), channel_id=1, source_target_pairs={{0,1},{1,2},{2,3},{3,4},{4,5},{5,6},{6,7},{7,8},{8,9},{9,10},{10,1... | collective-permute-start | bytes 442376 | tf_op jit(solution)/shard_map/ppermute | solution.py:25
  18.4 20.9 %collective-permute-start.3 = (f32[6,8,28,6]{2,1,3,0:T(8,128)S(1)}, f32[6,8,28,6]{2,1,3,0:T(8,128)S(1)}, u32[]{:S(2)}, u32[]{:S(2)}) collective-permute-start(f32[6,8,28,6]{2,1,3,0:T(8,128)S(1)} %copy.54), channel_id=1, source_target_pairs={{32,0},{64,32},{96,64},{128,96},{160,128},{192,160},{224,192},{0,2... | collective-permute-start | bytes 96776 | tf_op jit(solution)/shard_map/ppermute | solution.py:26
  19.8 19.9 %collective-permute-start.2 = (f32[6,8,28,6]{2,1,3,0:T(8,128)S(1)}, f32[6,8,28,6]{2,1,3,0:T(8,128)S(1)}, u32[]{:S(2)}, u32[]{:S(2)}) collective-permute-start(f32[6,8,28,6]{2,1,3,0:T(8,128)S(1)} %copy.53), channel_id=1, source_target_pairs={{0,32},{32,64},{64,96},{96,128},{128,160},{160,192},{192,224},{224... | collective-permute-start | bytes 96776 | tf_op jit(solution)/shard_map/ppermute | solution.py:25
  41.2 4.5 %copy-start = (f32[1,8,26,138]{3,2,1,0:T(8,128)}, f32[1,8,26,138]{3,2,1,0:T(8,128)S(1)}, u32[]{:S(2)}) copy-start(f32[1,8,26,138]{3,2,1,0:T(8,128)S(1)} %get-tuple-element.40) | copy-start | bytes 344452
  41.2 4.5 %copy-start.2 = (f32[1,8,26,138]{3,2,1,0:T(8,128)}, f32[1,8,26,138]{3,2,1,0:T(8,128)S(1)}, u32[]{:S(2)}) copy-start(f32[1,8,26,138]{3,2,1,0:T(8,128)S(1)} %get-tuple-element.41) | copy-start | bytes 344452
  41.3 0.7 copy-start.14
  45.8 0.8 copy-start.9
  45.8 1.1 %copy-start.13 = (f32[64,256]{1,0:T(8,128)S(1)}, f32[64,256]{1,0:T(8,128)}, u32[]{:S(2)}) copy-start(f32[64,256]{1,0:T(8,128)} %constant.26.clone) | copy-start | bytes 196612
  47.3 2.2 %collective-permute-start.5 = (f32[6,4,8,7]{3,2,1,0:T(8,128)S(1)}, f32[6,4,8,7]{3,2,1,0:T(8,128)S(1)}, u32[]{:S(2)}, u32[]{:S(2)}) collective-permute-start(f32[6,4,8,7]{3,2,1,0:T(8,128)S(1)} %get-tuple-element.132), channel_id=1, source_target_pairs={{32,0},{64,32},{96,64},{128,96},{160,128},{192,160},{224,192},{0,2... | collective-permute-start | bytes 16136 | tf_op jit(solution)/shard_map/ppermute | solution.py:26
  47.3 18.8 %copy-start.16 = (f32[2]{0:T(128)S(1)}, f32[2]{0:T(128)}, u32[]{:S(2)}) copy-start(f32[2]{0:T(128)} %constant.84.clone) | copy-start | bytes 28
  47.3 5.3 %collective-permute-start.4 = (f32[6,4,8,7]{3,2,1,0:T(8,128)S(1)}, f32[6,4,8,7]{3,2,1,0:T(8,128)S(1)}, u32[]{:S(2)}, u32[]{:S(2)}) collective-permute-start(f32[6,4,8,7]{3,2,1,0:T(8,128)S(1)} %get-tuple-element.131), channel_id=1, source_target_pairs={{0,32},{32,64},{64,96},{96,128},{128,160},{160,192},{192,224},{224... | collective-permute-start | bytes 16136 | tf_op jit(solution)/shard_map/ppermute | solution.py:25
  52.8 7.0 %collective-permute-start.7 = (f32[6,4,7,78]{3,2,1,0:T(8,128)S(1)}, f32[6,4,7,78]{3,2,1,0:T(8,128)S(1)}, u32[]{:S(2)}, u32[]{:S(2)}) collective-permute-start(f32[6,4,7,78]{3,2,1,0:T(8,128)S(1)} %get-tuple-element.130), channel_id=1, source_target_pairs={{1,0},{2,1},{3,2},{4,3},{5,4},{6,5},{7,6},{8,7},{9,8},{10,9},{11,1... | collective-permute-start | bytes 157256 | tf_op jit(solution)/shard_map/ppermute | solution.py:26
  57.6 7.9 %collective-permute-start.6 = (f32[6,4,7,78]{3,2,1,0:T(8,128)S(1)}, f32[6,4,7,78]{3,2,1,0:T(8,128)S(1)}, u32[]{:S(2)}, u32[]{:S(2)}) collective-permute-start(f32[6,4,7,78]{3,2,1,0:T(8,128)S(1)} %get-tuple-element.129), channel_id=1, source_target_pairs={{0,1},{1,2},{2,3},{3,4},{4,5},{5,6},{6,7},{7,8},{8,9},{9,10},{10,1... | collective-permute-start | bytes 157256 | tf_op jit(solution)/shard_map/ppermute | solution.py:25
  66.3 1.0 %copy-start.12 = (f32[64,32]{1,0:T(8,128)S(1)}, f32[64,32]{1,0:T(8,128)}, u32[]{:S(2)}) copy-start(f32[64,32]{1,0:T(8,128)} %constant.23.clone) | copy-start | bytes 24580
  66.3 1.2 %copy-start.19 = (f32[16,64]{1,0:T(8,128)S(1)}, f32[16,64]{1,0:T(8,128)}, u32[]{:S(2)}) copy-start(f32[16,64]{1,0:T(8,128)} %constant.85.clone) | copy-start | bytes 12292
  66.7 16.4 %copy-start.18 = (f32[2]{0:T(128)S(1)}, f32[2]{0:T(128)}, u32[]{:S(2)}) copy-start(f32[2]{0:T(128)} %constant.86.clone) | copy-start | bytes 28
  67.8 1.5 %collective-permute-start.9 = (f32[6,2,4,8]{3,2,1,0:T(4,128)S(1)}, f32[6,2,4,8]{3,2,1,0:T(4,128)S(1)}, u32[]{:S(2)}, u32[]{:S(2)}) collective-permute-start(f32[6,2,4,8]{3,2,1,0:T(4,128)S(1)} %get-tuple-element.186), channel_id=1, source_target_pairs={{32,0},{64,32},{96,64},{128,96},{160,128},{192,160},{224,192},{0,2... | collective-permute-start | bytes 4616 | tf_op jit(solution)/shard_map/ppermute | solution.py:26
  67.8 4.5 %collective-permute-start.8 = (f32[6,2,4,8]{3,2,1,0:T(4,128)S(1)}, f32[6,2,4,8]{3,2,1,0:T(4,128)S(1)}, u32[]{:S(2)}, u32[]{:S(2)}) collective-permute-start(f32[6,2,4,8]{3,2,1,0:T(4,128)S(1)} %get-tuple-element.185), channel_id=1, source_target_pairs={{0,32},{32,64},{64,96},{96,128},{128,160},{160,192},{192,224},{224... | collective-permute-start | bytes 4616 | tf_op jit(solution)/shard_map/ppermute | solution.py:25
  72.4 9.3 %collective-permute-start.10 = (f32[6,2,4,48]{3,2,1,0:T(4,128)S(1)}, f32[6,2,4,48]{3,2,1,0:T(4,128)S(1)}, u32[]{:S(2)}, u32[]{:S(2)}) collective-permute-start(f32[6,2,4,48]{3,2,1,0:T(4,128)S(1)} %pad_maximum_fusion.17), channel_id=1, source_target_pairs={{0,2},{1,3},{2,4},{3,5},{4,6},{5,7},{6,8},{7,9},{8,10},{9,11},{10,... | collective-permute-start | bytes 27656 | tf_op jit(solution)/shard_map/ppermute | solution.py:25
  72.5 9.2 %collective-permute-start.11 = (f32[6,2,4,48]{3,2,1,0:T(4,128)S(1)}, f32[6,2,4,48]{3,2,1,0:T(4,128)S(1)}, u32[]{:S(2)}, u32[]{:S(2)}) collective-permute-start(f32[6,2,4,48]{3,2,1,0:T(4,128)S(1)} %pad_maximum_fusion.17), channel_id=1, source_target_pairs={{0,1},{1,2},{2,3},{3,4},{4,5},{5,6},{6,7},{7,8},{8,9},{9,10},{10,1... | collective-permute-start | bytes 27656 | tf_op jit(solution)/shard_map/ppermute | solution.py:25
  72.6 9.1 %collective-permute-start.12 = (f32[6,2,4,48]{3,2,1,0:T(4,128)S(1)}, f32[6,2,4,48]{3,2,1,0:T(4,128)S(1)}, u32[]{:S(2)}, u32[]{:S(2)}) collective-permute-start(f32[6,2,4,48]{3,2,1,0:T(4,128)S(1)} %pad_maximum_fusion.17), channel_id=1, source_target_pairs={{1,0},{2,1},{3,2},{4,3},{5,4},{6,5},{7,6},{8,7},{9,8},{10,9},{11,1... | collective-permute-start | bytes 27656 | tf_op jit(solution)/shard_map/ppermute | solution.py:26
  77.9 4.8 %collective-permute-start.13 = (f32[6,2,4,48]{3,2,1,0:T(4,128)S(1)}, f32[6,2,4,48]{3,2,1,0:T(4,128)S(1)}, u32[]{:S(2)}, u32[]{:S(2)}) collective-permute-start(f32[6,2,4,48]{3,2,1,0:T(4,128)S(1)} %pad_maximum_fusion.17), channel_id=1, source_target_pairs={{2,0},{3,1},{4,2},{5,3},{6,4},{7,5},{8,6},{9,7},{10,8},{11,9},{12,... | collective-permute-start | bytes 27656 | tf_op jit(solution)/shard_map/ppermute | solution.py:26
  87.5 1.0 %copy-start.1 = (f32[1,8,26,138]{3,2,1,0:T(8,128)S(1)}, f32[1,8,26,138]{3,2,1,0:T(8,128)}, u32[]{:S(2)}) copy-start(f32[1,8,26,138]{3,2,1,0:T(8,128)} %copy-done) | copy-start | bytes 344452
  87.5 1.0 %copy-start.3 = (f32[1,8,26,138]{3,2,1,0:T(8,128)S(1)}, f32[1,8,26,138]{3,2,1,0:T(8,128)}, u32[]{:S(2)}) copy-start(f32[1,8,26,138]{3,2,1,0:T(8,128)} %copy-done.2) | copy-start | bytes 344452
  88.5 0.7 copy-start.15

commit v13 on v8

--- a/solution.py
+++ b/solution.py
@@ -49,24 +49,12 @@
     return along_x + along_y + along_z
 
 
-def gather_kernel(axis, value, out, land, send_sem, recv_sem, own_sem):
-    count = lax.axis_size(axis)
-    me = lax.axis_index(axis)
-    other = lax.axis_index("gy" if axis == "gx" else "gx")
+def gather_rows(source, land, send_sem, recv_sem, own_sem, device, count, me):
     mesh_ids = pl.DeviceIdType.MESH
-
-    def device(index):
-        return (index, other) if axis == "gx" else (other, index)
-
-    barrier = pltpu.get_barrier_semaphore()
-    for step in range(1, count):
-        pl.semaphore_signal(barrier, 1, device_id=device(lax.rem(me + step, count)),
-                            device_id_type=mesh_ids)
-    pl.semaphore_wait(barrier, count - 1)
     copies = []
     for step in range(1, count):
         copy = pltpu.make_async_remote_copy(
-            src_ref=value,
+            src_ref=source,
             dst_ref=land.at[me],
             send_sem=send_sem.at[step],
             recv_sem=recv_sem.at[me],
@@ -75,46 +63,75 @@
         )
         copy.start()
         copies.append(copy)
-    own = pltpu.make_async_copy(value, land.at[me], own_sem)
+    own = pltpu.make_async_copy(source, land.at[me], own_sem)
     own.start()
     for step in range(1, count):
         copies[step - 1].wait_send()
-        source = lax.rem(me + count - step, count)
+        sender = lax.rem(me + count - step, count)
         pltpu.make_async_remote_copy(
-            src_ref=value,
-            dst_ref=land.at[source],
+            src_ref=source,
+            dst_ref=land.at[sender],
             send_sem=send_sem.at[step],
-            recv_sem=recv_sem.at[source],
-            device_id=device(source),
+            recv_sem=recv_sem.at[sender],
+            device_id=device(sender),
             device_id_type=mesh_ids,
         ).wait_recv()
     own.wait()
-    out[...] = land[...]
-
-
-def gather_axis(block, axis, tag):
-    count = lax.axis_size(axis)
+
+
+def spread_kernel(inner, value, out, land_x, land_z, land_y, send_x, recv_x, send_z, recv_z,
+                  send_y, recv_y, own_x, own_z, own_y):
+    count_x = lax.axis_size("gx")
+    count_y = lax.axis_size("gy")
+    outer = count_y // inner
+    at_x = lax.axis_index("gx")
+    at_y = lax.axis_index("gy")
+    group, place = at_y // inner, lax.rem(at_y, inner)
+    mesh_ids = pl.DeviceIdType.MESH
+    along_x = lambda index: (index, at_y)
+    along_z = lambda index: (at_x, group * inner + index)
+    along_y = lambda index: (at_x, index * inner + place)
+    barrier = pltpu.get_barrier_semaphore()
+    for count, me, device in ((count_x, at_x, along_x), (inner, place, along_z), (outer, group, along_y)):
+        for step in range(1, count):
+            pl.semaphore_signal(barrier, 1, device_id=device(lax.rem(me + step, count)),
+                                device_id_type=mesh_ids)
+    pl.semaphore_wait(barrier, count_x + inner + outer - 3)
+    gather_rows(value, land_x, send_x, recv_x, own_x, along_x, count_x, at_x)
+    gather_rows(land_x.at[:, pl.ds(0, 1), :], land_z, send_z, recv_z, own_z, along_z, inner, place)
+    gather_rows(land_z, land_y, send_y, recv_y, own_y, along_y, outer, group)
+    best = jnp.max(land_y[...], axis=(0, 1, 2))
+    out[...] = jnp.broadcast_to(best, out.shape)
+
+
+def global_max(block):
+    count_x = lax.axis_size("gx")
+    count_y = lax.axis_size("gy")
+    inner = 8 if count_y % 8 == 0 else count_y
+    outer = count_y // inner
     vmem = pl.BlockSpec(memory_space=pltpu.VMEM)
-    shape = (count,) + block.shape
+    lanes = block.shape[1]
     return pl.pallas_call(
-        lambda *refs: gather_kernel(axis, *refs),
-        out_shape=jax.ShapeDtypeStruct(shape, jnp.float32),
+        lambda *refs: spread_kernel(inner, *refs),
+        out_shape=jax.ShapeDtypeStruct(block.shape, jnp.float32),
         in_specs=[vmem],
         out_specs=vmem,
         scratch_shapes=[
-            pltpu.VMEM(shape, jnp.float32),
-            pltpu.SemaphoreType.DMA((count,)),
-            pltpu.SemaphoreType.DMA((count,)),
+            pltpu.VMEM((count_x,) + block.shape, jnp.float32),
+            pltpu.VMEM((inner, count_x, 1, lanes), jnp.float32),
+            pltpu.VMEM((outer, inner, count_x, 1, lanes), jnp.float32),
+            pltpu.SemaphoreType.DMA((count_x,)),
+            pltpu.SemaphoreType.DMA((count_x,)),
+            pltpu.SemaphoreType.DMA((inner,)),
+            pltpu.SemaphoreType.DMA((inner,)),
+            pltpu.SemaphoreType.DMA((outer,)),
+            pltpu.SemaphoreType.DMA((outer,)),
+            pltpu.SemaphoreType.DMA(()),
+            pltpu.SemaphoreType.DMA(()),
             pltpu.SemaphoreType.DMA(()),
         ],
-        compiler_params=pltpu.CompilerParams(collective_id=tag, has_side_effects=True),
+        compiler_params=pltpu.CompilerParams(collective_id=0, has_side_effects=True),
     )(block)
-
-
-def global_max(block):
-    for tag, axis in enumerate(("gx", "gy")):
-        block = jnp.max(gather_axis(block, axis, tag), axis=0)
-    return block
 
 
 def restrict(field):

time: 95.7 us -> 88.2 us (0.922)
  Pallas kernels: 20.7 us -> 17.6 us
  other arithmetic: 17.7 us -> 15.5 us
  waiting for transfers between devices: 17.8 us -> 16.3 us
  starting transfers between devices: 22.7 us -> 21.6 us
    pallas_call x2 -> x1, Pallas kernels: 20.7 us -> 17.6 us  [global_max(): pl.pallas_call(lambda *refs: spread_kernel(inner, *refs), out_shape=jax.S...]
    ppermute x7, starting transfers between devices: 21.7 us -> 18.8 us  [padded_along(): lax.ppermute(head, axis, [((i + distance) % count, i) for i in range(coun...]
    reduce_max x2 -> x0, other arithmetic: 2.3 us -> none  [global_max(): block = jnp.max(gather_axis(block, axis, tag), axis=0)]
    ppermute x7, waiting for transfers between devices: 12.4 us -> 10.3 us  [padded_along(): lax.ppermute(tail, axis, [(i, (i + distance) % count) for i in range(coun...]
    ppermute x7, starting transfers between devices: 1 us -> 2.78 us  [padded_along(): lax.ppermute(tail, axis, [(i, (i + distance) % count) for i in range(coun...]
  transfers between devices with their start and end apart: 14 -> 14, of which waited for: 8 -> 8; matrix products, arithmetic and copies ran while one was open for 7% -> 6% of each run, Pallas kernels for 22% -> 20%
where the time goes in v13:
time: 88.2 us; the launch traced here: 88 us
  starting transfers between devices  21.6 us (24%)
  Pallas kernels  17.6 us (20%)
  waiting for transfers between devices  16.3 us (18%)
  other arithmetic  15.5 us (18%)
  local copies, waits for them, and re-layouts  7.6 us (9%)
  between operations  7.3 us (8%)
  matrix products  2.02 us (2%)
    ppermute x7, starting transfers between devices, padded_along(): lax.ppermute(head, axis, [((i + distance) % count, i) for i in range(coun...  18.8 us
    pallas_call x1, Pallas kernels, global_max(): pl.pallas_call(lambda *refs: spread_kernel(inner, *refs), out_shape=jax.S...  17.6 us
    ppermute x7, waiting for transfers between devices, padded_along(): lax.ppermute(tail, axis, [(i, (i + distance) % count) for i in range(coun...  10.3 us
    ppermute x7, waiting for transfers between devices, padded_along(): lax.ppermute(head, axis, [((i + distance) % count, i) for i in range(coun...  6.05 us
    add x12, other arithmetic, chebyshev(): iterate = crop(iterate, halo + 1, halo) + update  4.36 us
    slice x30, local copies, waits for them, and re-layouts, shrunk_neighbours(): along_z = jnp.roll(centre, 1, 1) + jnp.roll(centre, -1, 1)  3.45 us
    add x17, other arithmetic, operate(): first = coeff[0] * centre[0] + coeff[1] * centre[1]  3.15 us
    ppermute x7, starting transfers between devices, padded_along(): lax.ppermute(tail, axis, [(i, (i + distance) % count) for i in range(coun...  2.78 us
  transfers between devices with their start and end apart: 14, of which 8 were waited for; matrix products, arithmetic and copies ran while one was open for 6% of the time, Pallas kernels for 20%

profile of v13, /device:TPU:0, one launch (start us, length us, event | category | flops | bytes accessed | tf_op | source)
XLA Modules:
  0.0 88.0 jit_solution(5087702874804589282)
XLA Ops:
  0.0 1.1 %pad_maximum_fusion.6 = f32[6,8,16,128]{3,2,1,0:T(8,128)S(1)} fusion(f32[2,8,16,128]{3,2,1,0:T(8,128)} %param.31, f32[1,8,16,128]{3,2,1,0:T(8,128)} %bitcast.86, f32[1,8,16,128]{3,2,1,0:T(8,128)} %bitcast.89, f32[2,8,16,128]{3,2,1,0:T(8,128)} %param.30), kind=kLoop, calls=%fused_computation.66 | loop fusion | flops 294912 | bytes 786432 | tf_op jit(solution)/shard_map/concatenate | solution.py:235
  1.3 0.5 collective-permute-start.1
  1.9 0.7 fusion.107
  4.0 0.4 fusion.233
  4.4 0.4 convolution_multiply_fusion.1
  4.8 0.8 fusion.167
  6.0 0.6 fusion.188
  9.2 0.6 select_select_fusion.refs_0_
  9.8 0.5 collective-permute-done
  10.2 0.4 pad_maximum_fusion.1
  10.7 8.4 %collective-permute-start.3 = (f32[6,8,6,140]{3,2,1,0:T(8,128)S(1)}, f32[6,8,6,140]{3,2,1,0:T(8,128)S(1)}, u32[]{:S(2)}, u32[]{:S(2)}) collective-permute-start(f32[6,8,6,140]{3,2,1,0:T(8,128)S(1)} %get-tuple-element.52), channel_id=1, source_target_pairs={{1,0},{2,1},{3,2},{4,3},{5,4},{6,5},{7,6},{8,7},{9,8},{10,9},{11,1... | collective-permute-start | bytes 483848 | tf_op jit(solution)/shard_map/ppermute | solution.py:26
  19.2 17.6 %shard_map.280 = f32[8,128]{1,0:T(8,128)} custom-call(f32[8,128]{1,0:T(8,128)} %select_select_fusion.refs_0_), custom_call_target="tpu_custom_call" | custom-call | tf_op jit(solution)/shard_map/pallas_call | solution.py:114
  36.8 1.4 %fusion.232 = (f32[1,1]{1,0:T(1,128)}, f32[1,1]{1,0:T(1,128)}, f32[1,1]{1,0:T(1,128)}) fusion(f32[8,128]{1,0:T(8,128)} %shard_map.280), kind=kLoop, calls=%fused_computation.401 | loop fusion | bytes 24 | tf_op jit(solution)/shard_map/slice | solution.py:266
  39.4 0.4 fusion.42
  39.8 0.3 fusion.199
  40.2 0.4 subtract_bitcast_fusion
  40.5 0.8 fusion.12
  41.5 0.2 fusion.202
  41.7 0.4 fusion.54
  42.1 0.6 slice_add_fusion.12
  42.8 0.4 fusion.52
  43.3 0.2 fusion.212
  43.5 0.7 fusion.33
  44.9 0.3 fusion.235
  45.6 1.7 %collective-permute-start.5 = (f32[6,4,8,7]{3,2,1,0:T(8,128)S(1)}, f32[6,4,8,7]{3,2,1,0:T(8,128)S(1)}, u32[]{:S(2)}, u32[]{:S(2)}) collective-permute-start(f32[6,4,8,7]{3,2,1,0:T(8,128)S(1)} %get-tuple-element.132), channel_id=1, source_target_pairs={{32,0},{64,32},{96,64},{128,96},{160,128},{192,160},{224,192},{0,2... | collective-permute-start | bytes 16136 | tf_op jit(solution)/shard_map/ppermute | solution.py:26
  47.3 2.2 %collective-permute-done.5 = f32[6,4,8,7]{3,2,1,0:T(8,128)S(1)} collective-permute-done((f32[6,4,8,7]{3,2,1,0:T(8,128)S(1)}, f32[6,4,8,7]{3,2,1,0:T(8,128)S(1)}, u32[]{:S(2)}, u32[]{:S(2)}) %collective-permute-start.5) | collective-permute-done | bytes 5408 | tf_op jit(solution)/shard_map/ppermute | solution.py:26
  49.5 3.0 %collective-permute-done.4 = f32[6,4,8,7]{3,2,1,0:T(8,128)S(1)} collective-permute-done((f32[6,4,8,7]{3,2,1,0:T(8,128)S(1)}, f32[6,4,8,7]{3,2,1,0:T(8,128)S(1)}, u32[]{:S(2)}, u32[]{:S(2)}) %collective-permute-start.4) | collective-permute-done | bytes 5408 | tf_op jit(solution)/shard_map/ppermute | solution.py:25
  52.7 0.5 collective-permute-start.7
  53.2 1.6 %collective-permute-start.6 = (f32[6,4,7,78]{3,2,1,0:T(8,128)S(1)}, f32[6,4,7,78]{3,2,1,0:T(8,128)S(1)}, u32[]{:S(2)}, u32[]{:S(2)}) collective-permute-start(f32[6,4,7,78]{3,2,1,0:T(8,128)S(1)} %get-tuple-element.129), channel_id=1, source_target_pairs={{0,1},{1,2},{2,3},{3,4},{4,5},{5,6},{6,7},{7,8},{8,9},{9,10},{10,1... | collective-permute-start | bytes 157256 | tf_op jit(solution)/shard_map/ppermute | solution.py:25
  55.6 1.8 %collective-permute-done.7 = f32[6,4,7,78]{3,2,1,0:T(8,128)S(1)} collective-permute-done((f32[6,4,7,78]{3,2,1,0:T(8,128)S(1)}, f32[6,4,7,78]{3,2,1,0:T(8,128)S(1)}, u32[]{:S(2)}, u32[]{:S(2)}) %collective-permute-start.7) | collective-permute-done | bytes 52448 | tf_op jit(solution)/shard_map/ppermute | solution.py:26
  57.4 3.8 %collective-permute-done.6 = f32[6,4,7,78]{3,2,1,0:T(8,128)S(1)} collective-permute-done((f32[6,4,7,78]{3,2,1,0:T(8,128)S(1)}, f32[6,4,7,78]{3,2,1,0:T(8,128)S(1)}, u32[]{:S(2)}, u32[]{:S(2)}) %collective-permute-start.6) | collective-permute-done | bytes 52448 | tf_op jit(solution)/shard_map/ppermute | solution.py:25
  63.4 0.5 collective-permute-start.8
  63.9 1.0 %collective-permute-done.9 = f32[6,2,4,8]{3,2,1,0:T(4,128)S(1)} collective-permute-done((f32[6,2,4,8]{3,2,1,0:T(4,128)S(1)}, f32[6,2,4,8]{3,2,1,0:T(4,128)S(1)}, u32[]{:S(2)}, u32[]{:S(2)}) %collective-permute-start.9) | collective-permute-done | bytes 1568 | tf_op jit(solution)/shard_map/ppermute | solution.py:26
  64.9 3.0 %collective-permute-done.8 = f32[6,2,4,8]{3,2,1,0:T(4,128)S(1)} collective-permute-done((f32[6,2,4,8]{3,2,1,0:T(4,128)S(1)}, f32[6,2,4,8]{3,2,1,0:T(4,128)S(1)}, u32[]{:S(2)}, u32[]{:S(2)}) %collective-permute-start.8) | collective-permute-done | bytes 1568 | tf_op jit(solution)/shard_map/ppermute | solution.py:25
  68.1 0.6 collective-permute-start.11
  68.7 4.8 %collective-permute-start.12 = (f32[6,2,4,48]{3,2,1,0:T(4,128)S(1)}, f32[6,2,4,48]{3,2,1,0:T(4,128)S(1)}, u32[]{:S(2)}, u32[]{:S(2)}) collective-permute-start(f32[6,2,4,48]{3,2,1,0:T(4,128)S(1)} %pad_maximum_fusion.17), channel_id=1, source_target_pairs={{1,0},{2,1},{3,2},{4,3},{5,4},{6,5},{7,6},{8,7},{9,8},{10,9},{11,1... | collective-permute-start | bytes 27656 | tf_op jit(solution)/shard_map/ppermute | solution.py:26
  73.5 2.8 %collective-permute-start.13 = (f32[6,2,4,48]{3,2,1,0:T(4,128)S(1)}, f32[6,2,4,48]{3,2,1,0:T(4,128)S(1)}, u32[]{:S(2)}, u32[]{:S(2)}) collective-permute-start(f32[6,2,4,48]{3,2,1,0:T(4,128)S(1)} %pad_maximum_fusion.17), channel_id=1, source_target_pairs={{2,0},{3,1},{4,2},{5,3},{6,4},{7,5},{8,6},{9,7},{10,8},{11,9},{12,... | collective-permute-start | bytes 27656 | tf_op jit(solution)/shard_map/ppermute | solution.py:26
  77.3 1.1 %collective-permute-done.13 = f32[6,2,4,48]{3,2,1,0:T(4,128)S(1)} collective-permute-done((f32[6,2,4,48]{3,2,1,0:T(4,128)S(1)}, f32[6,2,4,48]{3,2,1,0:T(4,128)S(1)}, u32[]{:S(2)}, u32[]{:S(2)}) %collective-permute-start.13) | collective-permute-done | bytes 9248 | tf_op jit(solution)/shard_map/ppermute | solution.py:26
  82.3 0.3 copy.51
  82.7 0.3 slice.2057
  83.0 0.7 copy.54
  83.8 0.4 fusion.50
  84.3 0.2 fusion.208
  84.5 0.6 slice_add_fusion.7
  85.1 0.4 fusion.48
  85.6 0.2 fusion.206
  85.9 0.7 slice_add_fusion.4
  87.0 1.0 %fusion.62 = f32[2,8,16,128]{3,2,1,0:T(8,128)} fusion(f32[2,8,18,130]{3,2,1,0:T(8,128)S(1)} %get-tuple-element.16, f32[2,8,18,130]{3,2,1,0:T(8,128)S(1)} %get-tuple-element.15, f32[1,8,16,128]{3,2,1,0:T(8,128)S(1)} %get-tuple-element.94, f32[1,8,16,128]{3,2,1,0:T(8,128)S(1)} %get-tuple-element.98, f32[2,1,16,128]{3,2,1,0:T(8,128)S(1)} %get-tuple-element.62, ...), kind=kLoop, calls=%fused_computation.120 | loop fusion | flops 557056 | bytes 1572880 | tf_op jit(solution)/shard_map/add | solution.py:220
  (125 shorter events, 9.2 us)
Async XLA Ops:
  0.0 1.9 %copy-start = (f32[2,8,16,128]{3,2,1,0:T(8,128)S(1)}, f32[2,8,16,128]{3,2,1,0:T(8,128)}, u32[]{:S(2)}) copy-start(f32[2,8,16,128]{3,2,1,0:T(8,128)} %param.30) | copy-start | bytes 393220
  0.0 1.9 %copy-start.1 = (f32[8,16,128]{2,1,0:T(8,128)S(1)}, f32[8,16,128]{2,1,0:T(8,128)}, u32[]{:S(2)}) copy-start(f32[8,16,128]{2,1,0:T(8,128)} %param.33) | copy-start | bytes 196612
  0.0 1.9 %copy-start.2 = (f32[8,16,128]{2,1,0:T(8,128)S(1)}, f32[8,16,128]{2,1,0:T(8,128)}, u32[]{:S(2)}) copy-start(f32[8,16,128]{2,1,0:T(8,128)} %param.32) | copy-start | bytes 196612
  0.0 4.0 %copy-start.4 = (f32[128,64]{1,0:T(8,128)S(1)}, f32[128,64]{1,0:T(8,128)}, u32[]{:S(2)}) copy-start(f32[128,64]{1,0:T(8,128)} %constant.21.clone) | copy-start | bytes 98308
  1.1 3.3 %copy-start.5 = (f32[128,512]{1,0:T(8,128)S(1)}, f32[128,512]{1,0:T(8,128)}, u32[]{:S(2)}) copy-start(f32[128,512]{1,0:T(8,128)} %constant.22.clone) | copy-start | bytes 786436
  1.1 4.5 %copy-start.6 = (f32[64,32]{1,0:T(8,128)S(1)}, f32[64,32]{1,0:T(8,128)}, u32[]{:S(2)}) copy-start(f32[64,32]{1,0:T(8,128)} %constant.23.clone) | copy-start | bytes 24580
  1.1 4.7 %copy-start.10 = (f32[32,128]{1,0:T(8,128)S(1)}, f32[32,128]{1,0:T(8,128)}, u32[]{:S(2)}) copy-start(f32[32,128]{1,0:T(8,128)} %constant.24.clone) | copy-start | bytes 49156
  1.2 9.1 %copy-start.3 = (f32[2,8,16,128]{3,2,1,0:T(8,128)S(1)}, f32[2,8,16,128]{3,2,1,0:T(8,128)}, u32[]{:S(2)}) copy-start(f32[2,8,16,128]{3,2,1,0:T(8,128)} %param.31) | copy-start | bytes 393220
  1.3 8.4 %collective-permute-start.1 = (f32[6,8,16,6]{3,2,1,0:T(8,128)S(1)}, f32[6,8,16,6]{3,2,1,0:T(8,128)S(1)}, u32[]{:S(2)}, u32[]{:S(2)}) collective-permute-start(f32[6,8,16,6]{3,2,1,0:T(8,128)S(1)} %get-tuple-element.90), channel_id=1, source_target_pairs={{32,0},{64,32},{96,64},{128,96},{160,128},{192,160},{224,192},{0,2... | collective-permute-start | bytes 55304 | tf_op jit(solution)/shard_map/ppermute | solution.py:26
  1.8 8.4 %collective-permute-start = (f32[6,8,16,6]{3,2,1,0:T(8,128)S(1)}, f32[6,8,16,6]{3,2,1,0:T(8,128)S(1)}, u32[]{:S(2)}, u32[]{:S(2)}) collective-permute-start(f32[6,8,16,6]{3,2,1,0:T(8,128)S(1)} %get-tuple-element.89), channel_id=1, source_target_pairs={{0,32},{32,64},{64,96},{96,128},{128,160},{160,192},{192,224},{224... | collective-permute-start | bytes 55304 | tf_op jit(solution)/shard_map/ppermute | solution.py:25
  10.7 28.4 %collective-permute-start.3 = (f32[6,8,6,140]{3,2,1,0:T(8,128)S(1)}, f32[6,8,6,140]{3,2,1,0:T(8,128)S(1)}, u32[]{:S(2)}, u32[]{:S(2)}) collective-permute-start(f32[6,8,6,140]{3,2,1,0:T(8,128)S(1)} %get-tuple-element.52), channel_id=1, source_target_pairs={{1,0},{2,1},{3,2},{4,3},{5,4},{6,5},{7,6},{8,7},{9,8},{10,9},{11,1... | collective-permute-start | bytes 483848 | tf_op jit(solution)/shard_map/ppermute | solution.py:26
  19.1 20.0 %collective-permute-start.2 = (f32[6,8,6,140]{3,2,1,0:T(8,128)S(1)}, f32[6,8,6,140]{3,2,1,0:T(8,128)S(1)}, u32[]{:S(2)}, u32[]{:S(2)}) collective-permute-start(f32[6,8,6,140]{3,2,1,0:T(8,128)S(1)} %get-tuple-element.51), channel_id=1, source_target_pairs={{0,1},{1,2},{2,3},{3,4},{4,5},{5,6},{6,7},{7,8},{8,9},{9,10},{10,1... | collective-permute-start | bytes 483848 | tf_op jit(solution)/shard_map/ppermute | solution.py:25
  39.8 0.7 copy-start.8
  44.2 0.9 %copy-start.7 = (f32[64,256]{1,0:T(8,128)S(1)}, f32[64,256]{1,0:T(8,128)}, u32[]{:S(2)}) copy-start(f32[64,256]{1,0:T(8,128)} %constant.26.clone) | copy-start | bytes 196612
  45.6 3.9 %collective-permute-start.5 = (f32[6,4,8,7]{3,2,1,0:T(8,128)S(1)}, f32[6,4,8,7]{3,2,1,0:T(8,128)S(1)}, u32[]{:S(2)}, u32[]{:S(2)}) collective-permute-start(f32[6,4,8,7]{3,2,1,0:T(8,128)S(1)} %get-tuple-element.132), channel_id=1, source_target_pairs={{32,0},{64,32},{96,64},{128,96},{160,128},{192,160},{224,192},{0,2... | collective-permute-start | bytes 16136 | tf_op jit(solution)/shard_map/ppermute | solution.py:26
  47.3 14.4 %copy-start.9 = (f32[2]{0:T(128)S(1)}, f32[2]{0:T(128)}, u32[]{:S(2)}) copy-start(f32[2]{0:T(128)} %constant.84.clone) | copy-start | bytes 28
  47.3 5.3 %collective-permute-start.4 = (f32[6,4,8,7]{3,2,1,0:T(8,128)S(1)}, f32[6,4,8,7]{3,2,1,0:T(8,128)S(1)}, u32[]{:S(2)}, u32[]{:S(2)}) collective-permute-start(f32[6,4,8,7]{3,2,1,0:T(8,128)S(1)} %get-tuple-element.131), channel_id=1, source_target_pairs={{0,32},{32,64},{64,96},{96,128},{128,160},{160,192},{192,224},{224... | collective-permute-start | bytes 16136 | tf_op jit(solution)/shard_map/ppermute | solution.py:25
  52.7 4.7 %collective-permute-start.7 = (f32[6,4,7,78]{3,2,1,0:T(8,128)S(1)}, f32[6,4,7,78]{3,2,1,0:T(8,128)S(1)}, u32[]{:S(2)}, u32[]{:S(2)}) collective-permute-start(f32[6,4,7,78]{3,2,1,0:T(8,128)S(1)} %get-tuple-element.130), channel_id=1, source_target_pairs={{1,0},{2,1},{3,2},{4,3},{5,4},{6,5},{7,6},{8,7},{9,8},{10,9},{11,1... | collective-permute-start | bytes 157256 | tf_op jit(solution)/shard_map/ppermute | solution.py:26
  53.2 7.9 %collective-permute-start.6 = (f32[6,4,7,78]{3,2,1,0:T(8,128)S(1)}, f32[6,4,7,78]{3,2,1,0:T(8,128)S(1)}, u32[]{:S(2)}, u32[]{:S(2)}) collective-permute-start(f32[6,4,7,78]{3,2,1,0:T(8,128)S(1)} %get-tuple-element.129), channel_id=1, source_target_pairs={{0,1},{1,2},{2,3},{3,4},{4,5},{5,6},{6,7},{7,8},{8,9},{9,10},{10,1... | collective-permute-start | bytes 157256 | tf_op jit(solution)/shard_map/ppermute | solution.py:25
  62.0 1.2 %copy-start.12 = (f32[16,64]{1,0:T(8,128)S(1)}, f32[16,64]{1,0:T(8,128)}, u32[]{:S(2)}) copy-start(f32[16,64]{1,0:T(8,128)} %constant.85.clone) | copy-start | bytes 12292
  62.3 16.4 %copy-start.11 = (f32[2]{0:T(128)S(1)}, f32[2]{0:T(128)}, u32[]{:S(2)}) copy-start(f32[2]{0:T(128)} %constant.86.clone) | copy-start | bytes 28
  63.4 1.5 %collective-permute-start.9 = (f32[6,2,4,8]{3,2,1,0:T(4,128)S(1)}, f32[6,2,4,8]{3,2,1,0:T(4,128)S(1)}, u32[]{:S(2)}, u32[]{:S(2)}) collective-permute-start(f32[6,2,4,8]{3,2,1,0:T(4,128)S(1)} %get-tuple-element.186), channel_id=1, source_target_pairs={{32,0},{64,32},{96,64},{128,96},{160,128},{192,160},{224,192},{0,2... | collective-permute-start | bytes 4616 | tf_op jit(solution)/shard_map/ppermute | solution.py:26
  63.4 4.5 %collective-permute-start.8 = (f32[6,2,4,8]{3,2,1,0:T(4,128)S(1)}, f32[6,2,4,8]{3,2,1,0:T(4,128)S(1)}, u32[]{:S(2)}, u32[]{:S(2)}) collective-permute-start(f32[6,2,4,8]{3,2,1,0:T(4,128)S(1)} %get-tuple-element.185), channel_id=1, source_target_pairs={{0,32},{32,64},{64,96},{96,128},{128,160},{160,192},{192,224},{224... | collective-permute-start | bytes 4616 | tf_op jit(solution)/shard_map/ppermute | solution.py:25
  68.0 9.3 %collective-permute-start.10 = (f32[6,2,4,48]{3,2,1,0:T(4,128)S(1)}, f32[6,2,4,48]{3,2,1,0:T(4,128)S(1)}, u32[]{:S(2)}, u32[]{:S(2)}) collective-permute-start(f32[6,2,4,48]{3,2,1,0:T(4,128)S(1)} %pad_maximum_fusion.17), channel_id=1, source_target_pairs={{0,2},{1,3},{2,4},{3,5},{4,6},{5,7},{6,8},{7,9},{8,10},{9,11},{10,... | collective-permute-start | bytes 27656 | tf_op jit(solution)/shard_map/ppermute | solution.py:25
  68.1 9.2 %collective-permute-start.11 = (f32[6,2,4,48]{3,2,1,0:T(4,128)S(1)}, f32[6,2,4,48]{3,2,1,0:T(4,128)S(1)}, u32[]{:S(2)}, u32[]{:S(2)}) collective-permute-start(f32[6,2,4,48]{3,2,1,0:T(4,128)S(1)} %pad_maximum_fusion.17), channel_id=1, source_target_pairs={{0,1},{1,2},{2,3},{3,4},{4,5},{5,6},{6,7},{7,8},{8,9},{9,10},{10,1... | collective-permute-start | bytes 27656 | tf_op jit(solution)/shard_map/ppermute | solution.py:25
  68.7 8.6 %collective-permute-start.12 = (f32[6,2,4,48]{3,2,1,0:T(4,128)S(1)}, f32[6,2,4,48]{3,2,1,0:T(4,128)S(1)}, u32[]{:S(2)}, u32[]{:S(2)}) collective-permute-start(f32[6,2,4,48]{3,2,1,0:T(4,128)S(1)} %pad_maximum_fusion.17), channel_id=1, source_target_pairs={{1,0},{2,1},{3,2},{4,3},{5,4},{6,5},{7,6},{8,7},{9,8},{10,9},{11,1... | collective-permute-start | bytes 27656 | tf_op jit(solution)/shard_map/ppermute | solution.py:26
  73.5 4.8 %collective-permute-start.13 = (f32[6,2,4,48]{3,2,1,0:T(4,128)S(1)}, f32[6,2,4,48]{3,2,1,0:T(4,128)S(1)}, u32[]{:S(2)}, u32[]{:S(2)}) collective-permute-start(f32[6,2,4,48]{3,2,1,0:T(4,128)S(1)} %pad_maximum_fusion.17), channel_id=1, source_target_pairs={{2,0},{3,1},{4,2},{5,3},{6,4},{7,5},{8,6},{9,7},{10,8},{11,9},{12,... | collective-permute-start | bytes 27656 | tf_op jit(solution)/shard_map/ppermute | solution.py:26

commit v14 on v13

--- a/solution.py
+++ b/solution.py
@@ -79,57 +79,57 @@
     own.wait()
 
 
-def spread_kernel(inner, value, out, land_x, land_z, land_y, send_x, recv_x, send_z, recv_z,
-                  send_y, recv_y, own_x, own_z, own_y):
+def spread_kernel(pair, inner, value, out, land_c, land_x, land_z, land_y, send_c, recv_c,
+                  send_x, recv_x, send_z, recv_z, send_y, recv_y, own_c, own_x, own_z, own_y):
     count_x = lax.axis_size("gx")
     count_y = lax.axis_size("gy")
-    outer = count_y // inner
+    chips, outer = count_x // pair, count_y // inner
     at_x = lax.axis_index("gx")
     at_y = lax.axis_index("gy")
+    chip, core = at_x // pair, lax.rem(at_x, pair)
     group, place = at_y // inner, lax.rem(at_y, inner)
     mesh_ids = pl.DeviceIdType.MESH
-    along_x = lambda index: (index, at_y)
+    along_c = lambda index: (chip * pair + index, at_y)
+    along_x = lambda index: (index * pair + core, at_y)
     along_z = lambda index: (at_x, group * inner + index)
     along_y = lambda index: (at_x, index * inner + place)
+    stages = ((pair, core, along_c), (chips, chip, along_x), (inner, place, along_z), (outer, group, along_y))
     barrier = pltpu.get_barrier_semaphore()
-    for count, me, device in ((count_x, at_x, along_x), (inner, place, along_z), (outer, group, along_y)):
+    for count, me, device in stages:
         for step in range(1, count):
             pl.semaphore_signal(barrier, 1, device_id=device(lax.rem(me + step, count)),
                                 device_id_type=mesh_ids)
-    pl.semaphore_wait(barrier, count_x + inner + outer - 3)
-    gather_rows(value, land_x, send_x, recv_x, own_x, along_x, count_x, at_x)
-    gather_rows(land_x.at[:, pl.ds(0, 1), :], land_z, send_z, recv_z, own_z, along_z, inner, place)
+    pl.semaphore_wait(barrier, pair + chips + inner + outer - 4)
+    gather_rows(value, land_c, send_c, recv_c, own_c, along_c, pair, core)
+    gather_rows(land_c.at[:, pl.ds(0, 1), :], land_x, send_x, recv_x, own_x, along_x, chips, chip)
+    gather_rows(land_x, land_z, send_z, recv_z, own_z, along_z, inner, place)
     gather_rows(land_z, land_y, send_y, recv_y, own_y, along_y, outer, group)
-    best = jnp.max(land_y[...], axis=(0, 1, 2))
+    best = jnp.max(land_y[...], axis=(0, 1, 2, 3))
     out[...] = jnp.broadcast_to(best, out.shape)
 
 
 def global_max(block):
     count_x = lax.axis_size("gx")
     count_y = lax.axis_size("gy")
+    pair = 2 if count_x % 2 == 0 else 1
     inner = 8 if count_y % 8 == 0 else count_y
-    outer = count_y // inner
+    chips, outer = count_x // pair, count_y // inner
     vmem = pl.BlockSpec(memory_space=pltpu.VMEM)
     lanes = block.shape[1]
+    semaphores = []
+    for count in (pair, chips, inner, outer):
+        semaphores += [pltpu.SemaphoreType.DMA((count,)), pltpu.SemaphoreType.DMA((count,))]
     return pl.pallas_call(
-        lambda *refs: spread_kernel(inner, *refs),
+        lambda *refs: spread_kernel(pair, inner, *refs),
         out_shape=jax.ShapeDtypeStruct(block.shape, jnp.float32),
         in_specs=[vmem],
         out_specs=vmem,
         scratch_shapes=[
-            pltpu.VMEM((count_x,) + block.shape, jnp.float32),
-            pltpu.VMEM((inner, count_x, 1, lanes), jnp.float32),
-            pltpu.VMEM((outer, inner, count_x, 1, lanes), jnp.float32),
-            pltpu.SemaphoreType.DMA((count_x,)),
-            pltpu.SemaphoreType.DMA((count_x,)),
-            pltpu.SemaphoreType.DMA((inner,)),
-            pltpu.SemaphoreType.DMA((inner,)),
-            pltpu.SemaphoreType.DMA((outer,)),
-            pltpu.SemaphoreType.DMA((outer,)),
-            pltpu.SemaphoreType.DMA(()),
-            pltpu.SemaphoreType.DMA(()),
-            pltpu.SemaphoreType.DMA(()),
-        ],
+            pltpu.VMEM((pair,) + block.shape, jnp.float32),
+            pltpu.VMEM((chips, pair, 1, lanes), jnp.float32),
+            pltpu.VMEM((inner, chips, pair, 1, lanes), jnp.float32),
+            pltpu.VMEM((outer, inner, chips, pair, 1, lanes), jnp.float32),
+        ] + semaphores + [pltpu.SemaphoreType.DMA(())] * 4,
         compiler_params=pltpu.CompilerParams(collective_id=0, has_side_effects=True),
     )(block)
 

time: 88.2 us -> 89.3 us (1.012)
  starting transfers between devices: 21.6 us -> 20.4 us
  Pallas kernels: 17.6 us -> 18.8 us
  waiting for transfers between devices: 16.3 us -> 17.4 us
    ppermute x7, starting transfers between devices: 2.78 us -> 1.18 us  [padded_along(): lax.ppermute(tail, axis, [(i, (i + distance) % count) for i in range(coun...]
    ppermute x7, waiting for transfers between devices: 10.3 us -> 11.7 us  [padded_along(): lax.ppermute(tail, axis, [(i, (i + distance) % count) for i in range(coun...]
    pallas_call x1, Pallas kernels: 17.6 us -> 18.8 us  [global_max(): pl.pallas_call(lambda *refs: spread_kernel(pair, inner, *refs), out_shape...]
  transfers between devices with their start and end apart: 14 -> 14, of which waited for: 8 -> 8; matrix products, arithmetic and copies ran while one was open for 6% -> 6% of each run, Pallas kernels for 20% -> 21%
where the time goes in v14:
time: 89.3 us; the launch traced here: 89.1 us
  starting transfers between devices  20.4 us (23%)
  Pallas kernels  18.8 us (21%)
  waiting for transfers between devices  17.4 us (19%)
  other arithmetic  15.5 us (17%)
  local copies, waits for them, and re-layouts  7.6 us (9%)
  between operations  7.31 us (8%)
  matrix products  2.02 us (2%)
    ppermute x7, starting transfers between devices, padded_along(): lax.ppermute(head, axis, [((i + distance) % count, i) for i in range(coun...  19.2 us
    pallas_call x1, Pallas kernels, global_max(): pl.pallas_call(lambda *refs: spread_kernel(pair, inner, *refs), out_shape...  18.8 us
    ppermute x7, waiting for transfers between devices, padded_along(): lax.ppermute(tail, axis, [(i, (i + distance) % count) for i in range(coun...  11.7 us
    ppermute x7, waiting for transfers between devices, padded_along(): lax.ppermute(head, axis, [((i + distance) % count, i) for i in range(coun...  5.71 us
    add x12, other arithmetic, chebyshev(): iterate = crop(iterate, halo + 1, halo) + update  4.36 us
    slice x30, local copies, waits for them, and re-layouts, shrunk_neighbours(): along_z = jnp.roll(centre, 1, 1) + jnp.roll(centre, -1, 1)  3.45 us
    add x17, other arithmetic, operate(): first = coeff[0] * centre[0] + coeff[1] * centre[1]  3.15 us
    reduce_max x3, other arithmetic, body(): jnp.max(second)  2.13 us
  transfers between devices with their start and end apart: 14, of which 8 were waited for; matrix products, arithmetic and copies ran while one was open for 6% of the time, Pallas kernels for 21%

profile of v14, /device:TPU:0, one launch (start us, length us, event | category | flops | bytes accessed | tf_op | source)
XLA Modules:
  0.0 89.1 jit_solution(11378549542489930315)
XLA Ops:
  0.0 1.1 %pad_maximum_fusion.6 = f32[6,8,16,128]{3,2,1,0:T(8,128)S(1)} fusion(f32[2,8,16,128]{3,2,1,0:T(8,128)} %param.31, f32[1,8,16,128]{3,2,1,0:T(8,128)} %bitcast.86, f32[1,8,16,128]{3,2,1,0:T(8,128)} %bitcast.89, f32[2,8,16,128]{3,2,1,0:T(8,128)} %param.30), kind=kLoop, calls=%fused_computation.66 | loop fusion | flops 294912 | bytes 786432 | tf_op jit(solution)/shard_map/concatenate | solution.py:235
  1.3 0.5 collective-permute-start.1
  1.9 0.7 fusion.107
  4.0 0.4 fusion.233
  4.4 0.4 convolution_multiply_fusion.1
  4.8 0.8 fusion.167
  6.0 0.6 fusion.188
  9.2 0.6 select_select_fusion.refs_0_
  9.8 0.5 collective-permute-done
  10.2 0.4 pad_maximum_fusion.1
  10.7 8.4 %collective-permute-start.3 = (f32[6,8,6,140]{3,2,1,0:T(8,128)S(1)}, f32[6,8,6,140]{3,2,1,0:T(8,128)S(1)}, u32[]{:S(2)}, u32[]{:S(2)}) collective-permute-start(f32[6,8,6,140]{3,2,1,0:T(8,128)S(1)} %get-tuple-element.52), channel_id=1, source_target_pairs={{1,0},{2,1},{3,2},{4,3},{5,4},{6,5},{7,6},{8,7},{9,8},{10,9},{11,1... | collective-permute-start | bytes 483848 | tf_op jit(solution)/shard_map/ppermute | solution.py:26
  19.2 18.8 %shard_map.280 = f32[8,128]{1,0:T(8,128)} custom-call(f32[8,128]{1,0:T(8,128)} %select_select_fusion.refs_0_), custom_call_target="tpu_custom_call" | custom-call | tf_op jit(solution)/shard_map/pallas_call | solution.py:122
  38.0 1.4 %fusion.232 = (f32[1,1]{1,0:T(1,128)}, f32[1,1]{1,0:T(1,128)}, f32[1,1]{1,0:T(1,128)}) fusion(f32[8,128]{1,0:T(8,128)} %shard_map.280), kind=kLoop, calls=%fused_computation.401 | loop fusion | bytes 24 | tf_op jit(solution)/shard_map/slice | solution.py:266
  40.3 0.2 pad_maximum_fusion
  40.6 0.4 fusion.42
  41.0 0.3 fusion.199
  41.4 0.4 subtract_bitcast_fusion
  41.7 0.8 fusion.12
  42.7 0.2 fusion.202
  42.9 0.4 fusion.54
  43.3 0.6 slice_add_fusion.12
  44.0 0.4 fusion.52
  44.5 0.2 fusion.212
  44.7 0.7 fusion.33
  45.8 0.2 fusion.67
  46.1 0.3 fusion.235
  47.0 0.3 collective-permute-start.4
  47.3 1.9 %collective-permute-done.5 = f32[6,4,8,7]{3,2,1,0:T(8,128)S(1)} collective-permute-done((f32[6,4,8,7]{3,2,1,0:T(8,128)S(1)}, f32[6,4,8,7]{3,2,1,0:T(8,128)S(1)}, u32[]{:S(2)}, u32[]{:S(2)}) %collective-permute-start.5) | collective-permute-done | bytes 5408 | tf_op jit(solution)/shard_map/ppermute | solution.py:26
  49.2 3.0 %collective-permute-done.4 = f32[6,4,8,7]{3,2,1,0:T(8,128)S(1)} collective-permute-done((f32[6,4,8,7]{3,2,1,0:T(8,128)S(1)}, f32[6,4,8,7]{3,2,1,0:T(8,128)S(1)}, u32[]{:S(2)}, u32[]{:S(2)}) %collective-permute-start.4) | collective-permute-done | bytes 5408 | tf_op jit(solution)/shard_map/ppermute | solution.py:25
  52.4 2.0 %collective-permute-start.7 = (f32[6,4,7,78]{3,2,1,0:T(8,128)S(1)}, f32[6,4,7,78]{3,2,1,0:T(8,128)S(1)}, u32[]{:S(2)}, u32[]{:S(2)}) collective-permute-start(f32[6,4,7,78]{3,2,1,0:T(8,128)S(1)} %get-tuple-element.130), channel_id=1, source_target_pairs={{1,0},{2,1},{3,2},{4,3},{5,4},{6,5},{7,6},{8,7},{9,8},{10,9},{11,1... | collective-permute-start | bytes 157256 | tf_op jit(solution)/shard_map/ppermute | solution.py:26
  55.3 1.8 %collective-permute-done.7 = f32[6,4,7,78]{3,2,1,0:T(8,128)S(1)} collective-permute-done((f32[6,4,7,78]{3,2,1,0:T(8,128)S(1)}, f32[6,4,7,78]{3,2,1,0:T(8,128)S(1)}, u32[]{:S(2)}, u32[]{:S(2)}) %collective-permute-start.7) | collective-permute-done | bytes 52448 | tf_op jit(solution)/shard_map/ppermute | solution.py:26
  57.0 5.2 %collective-permute-done.6 = f32[6,4,7,78]{3,2,1,0:T(8,128)S(1)} collective-permute-done((f32[6,4,7,78]{3,2,1,0:T(8,128)S(1)}, f32[6,4,7,78]{3,2,1,0:T(8,128)S(1)}, u32[]{:S(2)}, u32[]{:S(2)}) %collective-permute-start.6) | collective-permute-done | bytes 52448 | tf_op jit(solution)/shard_map/ppermute | solution.py:25
  64.6 0.5 collective-permute-start.8
  65.0 1.0 %collective-permute-done.9 = f32[6,2,4,8]{3,2,1,0:T(4,128)S(1)} collective-permute-done((f32[6,2,4,8]{3,2,1,0:T(4,128)S(1)}, f32[6,2,4,8]{3,2,1,0:T(4,128)S(1)}, u32[]{:S(2)}, u32[]{:S(2)}) %collective-permute-start.9) | collective-permute-done | bytes 1568 | tf_op jit(solution)/shard_map/ppermute | solution.py:26
  66.1 3.0 %collective-permute-done.8 = f32[6,2,4,8]{3,2,1,0:T(4,128)S(1)} collective-permute-done((f32[6,2,4,8]{3,2,1,0:T(4,128)S(1)}, f32[6,2,4,8]{3,2,1,0:T(4,128)S(1)}, u32[]{:S(2)}, u32[]{:S(2)}) %collective-permute-start.8) | collective-permute-done | bytes 1568 | tf_op jit(solution)/shard_map/ppermute | solution.py:25
  69.3 5.3 %collective-permute-start.12 = (f32[6,2,4,48]{3,2,1,0:T(4,128)S(1)}, f32[6,2,4,48]{3,2,1,0:T(4,128)S(1)}, u32[]{:S(2)}, u32[]{:S(2)}) collective-permute-start(f32[6,2,4,48]{3,2,1,0:T(4,128)S(1)} %pad_maximum_fusion.17), channel_id=1, source_target_pairs={{1,0},{2,1},{3,2},{4,3},{5,4},{6,5},{7,6},{8,7},{9,8},{10,9},{11,1... | collective-permute-start | bytes 27656 | tf_op jit(solution)/shard_map/ppermute | solution.py:26
  74.6 2.8 %collective-permute-start.13 = (f32[6,2,4,48]{3,2,1,0:T(4,128)S(1)}, f32[6,2,4,48]{3,2,1,0:T(4,128)S(1)}, u32[]{:S(2)}, u32[]{:S(2)}) collective-permute-start(f32[6,2,4,48]{3,2,1,0:T(4,128)S(1)} %pad_maximum_fusion.17), channel_id=1, source_target_pairs={{2,0},{3,1},{4,2},{5,3},{6,4},{7,5},{8,6},{9,7},{10,8},{11,9},{12,... | collective-permute-start | bytes 27656 | tf_op jit(solution)/shard_map/ppermute | solution.py:26
  78.4 1.1 %collective-permute-done.13 = f32[6,2,4,48]{3,2,1,0:T(4,128)S(1)} collective-permute-done((f32[6,2,4,48]{3,2,1,0:T(4,128)S(1)}, f32[6,2,4,48]{3,2,1,0:T(4,128)S(1)}, u32[]{:S(2)}, u32[]{:S(2)}) %collective-permute-start.13) | collective-permute-done | bytes 9248 | tf_op jit(solution)/shard_map/ppermute | solution.py:26
  83.4 0.3 copy.51
  83.8 0.3 slice.2057
  84.2 0.7 copy.54
  84.9 0.4 fusion.50
  85.4 0.2 fusion.208
  85.6 0.6 slice_add_fusion.7
  86.3 0.4 fusion.48
  86.8 0.2 fusion.206
  87.0 0.7 slice_add_fusion.4
  88.1 1.0 %fusion.62 = f32[2,8,16,128]{3,2,1,0:T(8,128)} fusion(f32[2,8,18,130]{3,2,1,0:T(8,128)S(1)} %get-tuple-element.16, f32[2,8,18,130]{3,2,1,0:T(8,128)S(1)} %get-tuple-element.15, f32[1,8,16,128]{3,2,1,0:T(8,128)S(1)} %get-tuple-element.94, f32[1,8,16,128]{3,2,1,0:T(8,128)S(1)} %get-tuple-element.98, f32[2,1,16,128]{3,2,1,0:T(8,128)S(1)} %get-tuple-element.62, ...), kind=kLoop, calls=%fused_computation.120 | loop fusion | flops 557056 | bytes 1572880 | tf_op jit(solution)/shard_map/add | solution.py:220
  (125 shorter events, 9.1 us)
Async XLA Ops:
  0.0 1.9 %copy-start = (f32[2,8,16,128]{3,2,1,0:T(8,128)S(1)}, f32[2,8,16,128]{3,2,1,0:T(8,128)}, u32[]{:S(2)}) copy-start(f32[2,8,16,128]{3,2,1,0:T(8,128)} %param.30) | copy-start | bytes 393220
  0.0 1.9 %copy-start.1 = (f32[8,16,128]{2,1,0:T(8,128)S(1)}, f32[8,16,128]{2,1,0:T(8,128)}, u32[]{:S(2)}) copy-start(f32[8,16,128]{2,1,0:T(8,128)} %param.33) | copy-start | bytes 196612
  0.0 1.9 %copy-start.2 = (f32[8,16,128]{2,1,0:T(8,128)S(1)}, f32[8,16,128]{2,1,0:T(8,128)}, u32[]{:S(2)}) copy-start(f32[8,16,128]{2,1,0:T(8,128)} %param.32) | copy-start | bytes 196612
  0.0 4.0 %copy-start.4 = (f32[128,64]{1,0:T(8,128)S(1)}, f32[128,64]{1,0:T(8,128)}, u32[]{:S(2)}) copy-start(f32[128,64]{1,0:T(8,128)} %constant.21.clone) | copy-start | bytes 98308
  1.1 3.3 %copy-start.5 = (f32[128,512]{1,0:T(8,128)S(1)}, f32[128,512]{1,0:T(8,128)}, u32[]{:S(2)}) copy-start(f32[128,512]{1,0:T(8,128)} %constant.22.clone) | copy-start | bytes 786436
  1.1 4.5 %copy-start.6 = (f32[64,32]{1,0:T(8,128)S(1)}, f32[64,32]{1,0:T(8,128)}, u32[]{:S(2)}) copy-start(f32[64,32]{1,0:T(8,128)} %constant.23.clone) | copy-start | bytes 24580
  1.1 4.7 %copy-start.10 = (f32[32,128]{1,0:T(8,128)S(1)}, f32[32,128]{1,0:T(8,128)}, u32[]{:S(2)}) copy-start(f32[32,128]{1,0:T(8,128)} %constant.24.clone) | copy-start | bytes 49156
  1.2 9.1 %copy-start.3 = (f32[2,8,16,128]{3,2,1,0:T(8,128)S(1)}, f32[2,8,16,128]{3,2,1,0:T(8,128)}, u32[]{:S(2)}) copy-start(f32[2,8,16,128]{3,2,1,0:T(8,128)} %param.31) | copy-start | bytes 393220
  1.3 8.4 %collective-permute-start.1 = (f32[6,8,16,6]{3,2,1,0:T(8,128)S(1)}, f32[6,8,16,6]{3,2,1,0:T(8,128)S(1)}, u32[]{:S(2)}, u32[]{:S(2)}) collective-permute-start(f32[6,8,16,6]{3,2,1,0:T(8,128)S(1)} %get-tuple-element.90), channel_id=1, source_target_pairs={{32,0},{64,32},{96,64},{128,96},{160,128},{192,160},{224,192},{0,2... | collective-permute-start | bytes 55304 | tf_op jit(solution)/shard_map/ppermute | solution.py:26
  1.8 8.4 %collective-permute-start = (f32[6,8,16,6]{3,2,1,0:T(8,128)S(1)}, f32[6,8,16,6]{3,2,1,0:T(8,128)S(1)}, u32[]{:S(2)}, u32[]{:S(2)}) collective-permute-start(f32[6,8,16,6]{3,2,1,0:T(8,128)S(1)} %get-tuple-element.89), channel_id=1, source_target_pairs={{0,32},{32,64},{64,96},{96,128},{128,160},{160,192},{192,224},{224... | collective-permute-start | bytes 55304 | tf_op jit(solution)/shard_map/ppermute | solution.py:25
  10.7 29.6 %collective-permute-start.3 = (f32[6,8,6,140]{3,2,1,0:T(8,128)S(1)}, f32[6,8,6,140]{3,2,1,0:T(8,128)S(1)}, u32[]{:S(2)}, u32[]{:S(2)}) collective-permute-start(f32[6,8,6,140]{3,2,1,0:T(8,128)S(1)} %get-tuple-element.52), channel_id=1, source_target_pairs={{1,0},{2,1},{3,2},{4,3},{5,4},{6,5},{7,6},{8,7},{9,8},{10,9},{11,1... | collective-permute-start | bytes 483848 | tf_op jit(solution)/shard_map/ppermute | solution.py:26
  19.1 21.2 %collective-permute-start.2 = (f32[6,8,6,140]{3,2,1,0:T(8,128)S(1)}, f32[6,8,6,140]{3,2,1,0:T(8,128)S(1)}, u32[]{:S(2)}, u32[]{:S(2)}) collective-permute-start(f32[6,8,6,140]{3,2,1,0:T(8,128)S(1)} %get-tuple-element.51), channel_id=1, source_target_pairs={{0,1},{1,2},{2,3},{3,4},{4,5},{5,6},{6,7},{7,8},{8,9},{9,10},{10,1... | collective-permute-start | bytes 483848 | tf_op jit(solution)/shard_map/ppermute | solution.py:25
  41.0 0.7 copy-start.8
  45.4 0.9 %copy-start.7 = (f32[64,256]{1,0:T(8,128)S(1)}, f32[64,256]{1,0:T(8,128)}, u32[]{:S(2)}) copy-start(f32[64,256]{1,0:T(8,128)} %constant.26.clone) | copy-start | bytes 196612
  46.8 2.4 %collective-permute-start.5 = (f32[6,4,8,7]{3,2,1,0:T(8,128)S(1)}, f32[6,4,8,7]{3,2,1,0:T(8,128)S(1)}, u32[]{:S(2)}, u32[]{:S(2)}) collective-permute-start(f32[6,4,8,7]{3,2,1,0:T(8,128)S(1)} %get-tuple-element.132), channel_id=1, source_target_pairs={{32,0},{64,32},{96,64},{128,96},{160,128},{192,160},{224,192},{0,2... | collective-permute-start | bytes 16136 | tf_op jit(solution)/shard_map/ppermute | solution.py:26
  47.0 15.9 %copy-start.9 = (f32[2]{0:T(128)S(1)}, f32[2]{0:T(128)}, u32[]{:S(2)}) copy-start(f32[2]{0:T(128)} %constant.84.clone) | copy-start | bytes 28
  47.0 5.3 %collective-permute-start.4 = (f32[6,4,8,7]{3,2,1,0:T(8,128)S(1)}, f32[6,4,8,7]{3,2,1,0:T(8,128)S(1)}, u32[]{:S(2)}, u32[]{:S(2)}) collective-permute-start(f32[6,4,8,7]{3,2,1,0:T(8,128)S(1)} %get-tuple-element.131), channel_id=1, source_target_pairs={{0,32},{32,64},{64,96},{96,128},{128,160},{160,192},{192,224},{224... | collective-permute-start | bytes 16136 | tf_op jit(solution)/shard_map/ppermute | solution.py:25
  52.4 4.7 %collective-permute-start.7 = (f32[6,4,7,78]{3,2,1,0:T(8,128)S(1)}, f32[6,4,7,78]{3,2,1,0:T(8,128)S(1)}, u32[]{:S(2)}, u32[]{:S(2)}) collective-permute-start(f32[6,4,7,78]{3,2,1,0:T(8,128)S(1)} %get-tuple-element.130), channel_id=1, source_target_pairs={{1,0},{2,1},{3,2},{4,3},{5,4},{6,5},{7,6},{8,7},{9,8},{10,9},{11,1... | collective-permute-start | bytes 157256 | tf_op jit(solution)/shard_map/ppermute | solution.py:26
  54.3 7.9 %collective-permute-start.6 = (f32[6,4,7,78]{3,2,1,0:T(8,128)S(1)}, f32[6,4,7,78]{3,2,1,0:T(8,128)S(1)}, u32[]{:S(2)}, u32[]{:S(2)}) collective-permute-start(f32[6,4,7,78]{3,2,1,0:T(8,128)S(1)} %get-tuple-element.129), channel_id=1, source_target_pairs={{0,1},{1,2},{2,3},{3,4},{4,5},{5,6},{6,7},{7,8},{8,9},{9,10},{10,1... | collective-permute-start | bytes 157256 | tf_op jit(solution)/shard_map/ppermute | solution.py:25
  63.1 1.2 %copy-start.12 = (f32[16,64]{1,0:T(8,128)S(1)}, f32[16,64]{1,0:T(8,128)}, u32[]{:S(2)}) copy-start(f32[16,64]{1,0:T(8,128)} %constant.85.clone) | copy-start | bytes 12292
  63.4 16.4 %copy-start.11 = (f32[2]{0:T(128)S(1)}, f32[2]{0:T(128)}, u32[]{:S(2)}) copy-start(f32[2]{0:T(128)} %constant.86.clone) | copy-start | bytes 28
  64.5 1.5 %collective-permute-start.9 = (f32[6,2,4,8]{3,2,1,0:T(4,128)S(1)}, f32[6,2,4,8]{3,2,1,0:T(4,128)S(1)}, u32[]{:S(2)}, u32[]{:S(2)}) collective-permute-start(f32[6,2,4,8]{3,2,1,0:T(4,128)S(1)} %get-tuple-element.186), channel_id=1, source_target_pairs={{32,0},{64,32},{96,64},{128,96},{160,128},{192,160},{224,192},{0,2... | collective-permute-start | bytes 4616 | tf_op jit(solution)/shard_map/ppermute | solution.py:26
  64.6 4.5 %collective-permute-start.8 = (f32[6,2,4,8]{3,2,1,0:T(4,128)S(1)}, f32[6,2,4,8]{3,2,1,0:T(4,128)S(1)}, u32[]{:S(2)}, u32[]{:S(2)}) collective-permute-start(f32[6,2,4,8]{3,2,1,0:T(4,128)S(1)} %get-tuple-element.185), channel_id=1, source_target_pairs={{0,32},{32,64},{64,96},{96,128},{128,160},{160,192},{192,224},{224... | collective-permute-start | bytes 4616 | tf_op jit(solution)/shard_map/ppermute | solution.py:25
  69.1 9.3 %collective-permute-start.10 = (f32[6,2,4,48]{3,2,1,0:T(4,128)S(1)}, f32[6,2,4,48]{3,2,1,0:T(4,128)S(1)}, u32[]{:S(2)}, u32[]{:S(2)}) collective-permute-start(f32[6,2,4,48]{3,2,1,0:T(4,128)S(1)} %pad_maximum_fusion.17), channel_id=1, source_target_pairs={{0,2},{1,3},{2,4},{3,5},{4,6},{5,7},{6,8},{7,9},{8,10},{9,11},{10,... | collective-permute-start | bytes 27656 | tf_op jit(solution)/shard_map/ppermute | solution.py:25
  69.2 9.2 %collective-permute-start.11 = (f32[6,2,4,48]{3,2,1,0:T(4,128)S(1)}, f32[6,2,4,48]{3,2,1,0:T(4,128)S(1)}, u32[]{:S(2)}, u32[]{:S(2)}) collective-permute-start(f32[6,2,4,48]{3,2,1,0:T(4,128)S(1)} %pad_maximum_fusion.17), channel_id=1, source_target_pairs={{0,1},{1,2},{2,3},{3,4},{4,5},{5,6},{6,7},{7,8},{8,9},{9,10},{10,1... | collective-permute-start | bytes 27656 | tf_op jit(solution)/shard_map/ppermute | solution.py:25
  69.3 9.1 %collective-permute-start.12 = (f32[6,2,4,48]{3,2,1,0:T(4,128)S(1)}, f32[6,2,4,48]{3,2,1,0:T(4,128)S(1)}, u32[]{:S(2)}, u32[]{:S(2)}) collective-permute-start(f32[6,2,4,48]{3,2,1,0:T(4,128)S(1)} %pad_maximum_fusion.17), channel_id=1, source_target_pairs={{1,0},{2,1},{3,2},{4,3},{5,4},{6,5},{7,6},{8,7},{9,8},{10,9},{11,1... | collective-permute-start | bytes 27656 | tf_op jit(solution)/shard_map/ppermute | solution.py:26
  74.6 4.8 %collective-permute-start.13 = (f32[6,2,4,48]{3,2,1,0:T(4,128)S(1)}, f32[6,2,4,48]{3,2,1,0:T(4,128)S(1)}, u32[]{:S(2)}, u32[]{:S(2)}) collective-permute-start(f32[6,2,4,48]{3,2,1,0:T(4,128)S(1)} %pad_maximum_fusion.17), channel_id=1, source_target_pairs={{2,0},{3,1},{4,2},{5,3},{6,4},{7,5},{8,6},{9,7},{10,8},{11,9},{12,... | collective-permute-start | bytes 27656 | tf_op jit(solution)/shard_map/ppermute | solution.py:26

commit v15 on v13

--- a/solution.py
+++ b/solution.py
@@ -97,8 +97,8 @@
             pl.semaphore_signal(barrier, 1, device_id=device(lax.rem(me + step, count)),
                                 device_id_type=mesh_ids)
     pl.semaphore_wait(barrier, count_x + inner + outer - 3)
-    gather_rows(value, land_x, send_x, recv_x, own_x, along_x, count_x, at_x)
-    gather_rows(land_x.at[:, pl.ds(0, 1), :], land_z, send_z, recv_z, own_z, along_z, inner, place)
+    gather_rows(value.at[pl.ds(0, 1), :], land_x, send_x, recv_x, own_x, along_x, count_x, at_x)
+    gather_rows(land_x, land_z, send_z, recv_z, own_z, along_z, inner, place)
     gather_rows(land_z, land_y, send_y, recv_y, own_y, along_y, outer, group)
     best = jnp.max(land_y[...], axis=(0, 1, 2))
     out[...] = jnp.broadcast_to(best, out.shape)
@@ -117,7 +117,7 @@
         in_specs=[vmem],
         out_specs=vmem,
         scratch_shapes=[
-            pltpu.VMEM((count_x,) + block.shape, jnp.float32),
+            pltpu.VMEM((count_x, 1, lanes), jnp.float32),
             pltpu.VMEM((inner, count_x, 1, lanes), jnp.float32),
             pltpu.VMEM((outer, inner, count_x, 1, lanes), jnp.float32),
             pltpu.SemaphoreType.DMA((count_x,)),

time: 88.2 us -> 88.2 us (level)
  no operation moved by 1% of the time
where the time goes in v15:
time: 88.2 us; the launch traced here: 87.9 us
  starting transfers between devices  21.8 us (25%)
  Pallas kernels  17.5 us (20%)
  waiting for transfers between devices  16.1 us (18%)
  other arithmetic  15.5 us (18%)
  local copies, waits for them, and re-layouts  7.6 us (9%)
  between operations  7.3 us (8%)
  matrix products  2.02 us (2%)
    ppermute x7, starting transfers between devices, padded_along(): lax.ppermute(head, axis, [((i + distance) % count, i) for i in range(coun...  18.6 us
    pallas_call x1, Pallas kernels, global_max(): pl.pallas_call(lambda *refs: spread_kernel(inner, *refs), out_shape=jax.S...  17.5 us
    ppermute x7, waiting for transfers between devices, padded_along(): lax.ppermute(tail, axis, [(i, (i + distance) % count) for i in range(coun...  10.1 us
    ppermute x7, waiting for transfers between devices, padded_along(): lax.ppermute(head, axis, [((i + distance) % count, i) for i in range(coun...  6.05 us
    add x12, other arithmetic, chebyshev(): iterate = crop(iterate, halo + 1, halo) + update  4.36 us
    slice x30, local copies, waits for them, and re-layouts, shrunk_neighbours(): along_z = jnp.roll(centre, 1, 1) + jnp.roll(centre, -1, 1)  3.45 us
    ppermute x7, starting transfers between devices, padded_along(): lax.ppermute(tail, axis, [(i, (i + distance) % count) for i in range(coun...  3.2 us
    add x17, other arithmetic, operate(): first = coeff[0] * centre[0] + coeff[1] * centre[1]  3.15 us
  transfers between devices with their start and end apart: 14, of which 8 were waited for; matrix products, arithmetic and copies ran while one was open for 6% of the time, Pallas kernels for 20%

profile of v15, /device:TPU:0, one launch (start us, length us, event | category | flops | bytes accessed | tf_op | source)
XLA Modules:
  0.0 87.9 jit_solution(8287334203615294635)
XLA Ops:
  0.0 1.1 %pad_maximum_fusion.6 = f32[6,8,16,128]{3,2,1,0:T(8,128)S(1)} fusion(f32[2,8,16,128]{3,2,1,0:T(8,128)} %param.31, f32[1,8,16,128]{3,2,1,0:T(8,128)} %bitcast.86, f32[1,8,16,128]{3,2,1,0:T(8,128)} %bitcast.89, f32[2,8,16,128]{3,2,1,0:T(8,128)} %param.30), kind=kLoop, calls=%fused_computation.66 | loop fusion | flops 294912 | bytes 786432 | tf_op jit(solution)/shard_map/concatenate | solution.py:235
  1.3 0.5 collective-permute-start.1
  1.9 0.7 fusion.107
  4.0 0.4 fusion.233
  4.4 0.4 convolution_multiply_fusion.1
  4.8 0.8 fusion.167
  6.0 0.6 fusion.188
  9.2 0.6 select_select_fusion.refs_0_
  9.8 0.5 collective-permute-done
  10.2 0.4 pad_maximum_fusion.1
  10.7 8.4 %collective-permute-start.3 = (f32[6,8,6,140]{3,2,1,0:T(8,128)S(1)}, f32[6,8,6,140]{3,2,1,0:T(8,128)S(1)}, u32[]{:S(2)}, u32[]{:S(2)}) collective-permute-start(f32[6,8,6,140]{3,2,1,0:T(8,128)S(1)} %get-tuple-element.52), channel_id=1, source_target_pairs={{1,0},{2,1},{3,2},{4,3},{5,4},{6,5},{7,6},{8,7},{9,8},{10,9},{11,1... | collective-permute-start | bytes 483848 | tf_op jit(solution)/shard_map/ppermute | solution.py:26
  19.2 17.5 %shard_map.280 = f32[8,128]{1,0:T(8,128)} custom-call(f32[8,128]{1,0:T(8,128)} %select_select_fusion.refs_0_), custom_call_target="tpu_custom_call" | custom-call | tf_op jit(solution)/shard_map/pallas_call | solution.py:114
  36.7 1.4 %fusion.232 = (f32[1,1]{1,0:T(1,128)}, f32[1,1]{1,0:T(1,128)}, f32[1,1]{1,0:T(1,128)}) fusion(f32[8,128]{1,0:T(8,128)} %shard_map.280), kind=kLoop, calls=%fused_computation.401 | loop fusion | bytes 24 | tf_op jit(solution)/shard_map/slice | solution.py:266
  39.2 0.4 fusion.42
  39.7 0.3 fusion.199
  40.0 0.4 subtract_bitcast_fusion
  40.4 0.8 fusion.12
  41.3 0.2 fusion.202
  41.6 0.4 fusion.54
  42.0 0.6 slice_add_fusion.12
  42.6 0.4 fusion.52
  43.1 0.2 fusion.212
  43.4 0.7 fusion.33
  44.5 0.2 fusion.67
  44.8 0.3 fusion.235
  45.4 2.0 %collective-permute-start.5 = (f32[6,4,8,7]{3,2,1,0:T(8,128)S(1)}, f32[6,4,8,7]{3,2,1,0:T(8,128)S(1)}, u32[]{:S(2)}, u32[]{:S(2)}) collective-permute-start(f32[6,4,8,7]{3,2,1,0:T(8,128)S(1)} %get-tuple-element.132), channel_id=1, source_target_pairs={{32,0},{64,32},{96,64},{128,96},{160,128},{192,160},{224,192},{0,2... | collective-permute-start | bytes 16136 | tf_op jit(solution)/shard_map/ppermute | solution.py:26
  47.4 2.2 %collective-permute-done.5 = f32[6,4,8,7]{3,2,1,0:T(8,128)S(1)} collective-permute-done((f32[6,4,8,7]{3,2,1,0:T(8,128)S(1)}, f32[6,4,8,7]{3,2,1,0:T(8,128)S(1)}, u32[]{:S(2)}, u32[]{:S(2)}) %collective-permute-start.5) | collective-permute-done | bytes 5408 | tf_op jit(solution)/shard_map/ppermute | solution.py:26
  49.6 3.0 %collective-permute-done.4 = f32[6,4,8,7]{3,2,1,0:T(8,128)S(1)} collective-permute-done((f32[6,4,8,7]{3,2,1,0:T(8,128)S(1)}, f32[6,4,8,7]{3,2,1,0:T(8,128)S(1)}, u32[]{:S(2)}, u32[]{:S(2)}) %collective-permute-start.4) | collective-permute-done | bytes 5408 | tf_op jit(solution)/shard_map/ppermute | solution.py:25
  53.0 1.9 %collective-permute-start.6 = (f32[6,4,7,78]{3,2,1,0:T(8,128)S(1)}, f32[6,4,7,78]{3,2,1,0:T(8,128)S(1)}, u32[]{:S(2)}, u32[]{:S(2)}) collective-permute-start(f32[6,4,7,78]{3,2,1,0:T(8,128)S(1)} %get-tuple-element.129), channel_id=1, source_target_pairs={{0,1},{1,2},{2,3},{3,4},{4,5},{5,6},{6,7},{7,8},{8,9},{9,10},{10,1... | collective-permute-start | bytes 157256 | tf_op jit(solution)/shard_map/ppermute | solution.py:25
  55.8 1.8 %collective-permute-done.7 = f32[6,4,7,78]{3,2,1,0:T(8,128)S(1)} collective-permute-done((f32[6,4,7,78]{3,2,1,0:T(8,128)S(1)}, f32[6,4,7,78]{3,2,1,0:T(8,128)S(1)}, u32[]{:S(2)}, u32[]{:S(2)}) %collective-permute-start.7) | collective-permute-done | bytes 52448 | tf_op jit(solution)/shard_map/ppermute | solution.py:26
  57.5 3.6 %collective-permute-done.6 = f32[6,4,7,78]{3,2,1,0:T(8,128)S(1)} collective-permute-done((f32[6,4,7,78]{3,2,1,0:T(8,128)S(1)}, f32[6,4,7,78]{3,2,1,0:T(8,128)S(1)}, u32[]{:S(2)}, u32[]{:S(2)}) %collective-permute-start.6) | collective-permute-done | bytes 52448 | tf_op jit(solution)/shard_map/ppermute | solution.py:25
  63.4 0.5 collective-permute-start.8
  63.9 1.0 %collective-permute-done.9 = f32[6,2,4,8]{3,2,1,0:T(4,128)S(1)} collective-permute-done((f32[6,2,4,8]{3,2,1,0:T(4,128)S(1)}, f32[6,2,4,8]{3,2,1,0:T(4,128)S(1)}, u32[]{:S(2)}, u32[]{:S(2)}) %collective-permute-start.9) | collective-permute-done | bytes 1568 | tf_op jit(solution)/shard_map/ppermute | solution.py:26
  64.9 3.0 %collective-permute-done.8 = f32[6,2,4,8]{3,2,1,0:T(4,128)S(1)} collective-permute-done((f32[6,2,4,8]{3,2,1,0:T(4,128)S(1)}, f32[6,2,4,8]{3,2,1,0:T(4,128)S(1)}, u32[]{:S(2)}, u32[]{:S(2)}) %collective-permute-start.8) | collective-permute-done | bytes 1568 | tf_op jit(solution)/shard_map/ppermute | solution.py:25
  68.1 0.7 collective-permute-start.11
  68.7 4.8 %collective-permute-start.12 = (f32[6,2,4,48]{3,2,1,0:T(4,128)S(1)}, f32[6,2,4,48]{3,2,1,0:T(4,128)S(1)}, u32[]{:S(2)}, u32[]{:S(2)}) collective-permute-start(f32[6,2,4,48]{3,2,1,0:T(4,128)S(1)} %pad_maximum_fusion.17), channel_id=1, source_target_pairs={{1,0},{2,1},{3,2},{4,3},{5,4},{6,5},{7,6},{8,7},{9,8},{10,9},{11,1... | collective-permute-start | bytes 27656 | tf_op jit(solution)/shard_map/ppermute | solution.py:26
  73.5 2.8 %collective-permute-start.13 = (f32[6,2,4,48]{3,2,1,0:T(4,128)S(1)}, f32[6,2,4,48]{3,2,1,0:T(4,128)S(1)}, u32[]{:S(2)}, u32[]{:S(2)}) collective-permute-start(f32[6,2,4,48]{3,2,1,0:T(4,128)S(1)} %pad_maximum_fusion.17), channel_id=1, source_target_pairs={{2,0},{3,1},{4,2},{5,3},{6,4},{7,5},{8,6},{9,7},{10,8},{11,9},{12,... | collective-permute-start | bytes 27656 | tf_op jit(solution)/shard_map/ppermute | solution.py:26
  77.2 1.1 %collective-permute-done.13 = f32[6,2,4,48]{3,2,1,0:T(4,128)S(1)} collective-permute-done((f32[6,2,4,48]{3,2,1,0:T(4,128)S(1)}, f32[6,2,4,48]{3,2,1,0:T(4,128)S(1)}, u32[]{:S(2)}, u32[]{:S(2)}) %collective-permute-start.13) | collective-permute-done | bytes 9248 | tf_op jit(solution)/shard_map/ppermute | solution.py:26
  82.3 0.3 copy.51
  82.7 0.3 slice.2057
  83.0 0.7 copy.54
  83.7 0.4 fusion.50
  84.2 0.2 fusion.208
  84.5 0.6 slice_add_fusion.7
  85.1 0.4 fusion.48
  85.6 0.2 fusion.206
  85.8 0.7 slice_add_fusion.4
  87.0 1.0 %fusion.62 = f32[2,8,16,128]{3,2,1,0:T(8,128)} fusion(f32[2,8,18,130]{3,2,1,0:T(8,128)S(1)} %get-tuple-element.16, f32[2,8,18,130]{3,2,1,0:T(8,128)S(1)} %get-tuple-element.15, f32[1,8,16,128]{3,2,1,0:T(8,128)S(1)} %get-tuple-element.94, f32[1,8,16,128]{3,2,1,0:T(8,128)S(1)} %get-tuple-element.98, f32[2,1,16,128]{3,2,1,0:T(8,128)S(1)} %get-tuple-element.62, ...), kind=kLoop, calls=%fused_computation.120 | loop fusion | flops 557056 | bytes 1572880 | tf_op jit(solution)/shard_map/add | solution.py:220
  (125 shorter events, 9.2 us)
Async XLA Ops:
  0.0 1.9 %copy-start = (f32[2,8,16,128]{3,2,1,0:T(8,128)S(1)}, f32[2,8,16,128]{3,2,1,0:T(8,128)}, u32[]{:S(2)}) copy-start(f32[2,8,16,128]{3,2,1,0:T(8,128)} %param.30) | copy-start | bytes 393220
  0.0 1.9 %copy-start.1 = (f32[8,16,128]{2,1,0:T(8,128)S(1)}, f32[8,16,128]{2,1,0:T(8,128)}, u32[]{:S(2)}) copy-start(f32[8,16,128]{2,1,0:T(8,128)} %param.33) | copy-start | bytes 196612
  0.0 1.9 %copy-start.2 = (f32[8,16,128]{2,1,0:T(8,128)S(1)}, f32[8,16,128]{2,1,0:T(8,128)}, u32[]{:S(2)}) copy-start(f32[8,16,128]{2,1,0:T(8,128)} %param.32) | copy-start | bytes 196612
  0.0 4.0 %copy-start.4 = (f32[128,64]{1,0:T(8,128)S(1)}, f32[128,64]{1,0:T(8,128)}, u32[]{:S(2)}) copy-start(f32[128,64]{1,0:T(8,128)} %constant.21.clone) | copy-start | bytes 98308
  1.1 3.3 %copy-start.5 = (f32[128,512]{1,0:T(8,128)S(1)}, f32[128,512]{1,0:T(8,128)}, u32[]{:S(2)}) copy-start(f32[128,512]{1,0:T(8,128)} %constant.22.clone) | copy-start | bytes 786436
  1.1 4.5 %copy-start.6 = (f32[64,32]{1,0:T(8,128)S(1)}, f32[64,32]{1,0:T(8,128)}, u32[]{:S(2)}) copy-start(f32[64,32]{1,0:T(8,128)} %constant.23.clone) | copy-start | bytes 24580
  1.1 4.7 %copy-start.10 = (f32[32,128]{1,0:T(8,128)S(1)}, f32[32,128]{1,0:T(8,128)}, u32[]{:S(2)}) copy-start(f32[32,128]{1,0:T(8,128)} %constant.24.clone) | copy-start | bytes 49156
  1.2 9.1 %copy-start.3 = (f32[2,8,16,128]{3,2,1,0:T(8,128)S(1)}, f32[2,8,16,128]{3,2,1,0:T(8,128)}, u32[]{:S(2)}) copy-start(f32[2,8,16,128]{3,2,1,0:T(8,128)} %param.31) | copy-start | bytes 393220
  1.3 8.4 %collective-permute-start.1 = (f32[6,8,16,6]{3,2,1,0:T(8,128)S(1)}, f32[6,8,16,6]{3,2,1,0:T(8,128)S(1)}, u32[]{:S(2)}, u32[]{:S(2)}) collective-permute-start(f32[6,8,16,6]{3,2,1,0:T(8,128)S(1)} %get-tuple-element.90), channel_id=1, source_target_pairs={{32,0},{64,32},{96,64},{128,96},{160,128},{192,160},{224,192},{0,2... | collective-permute-start | bytes 55304 | tf_op jit(solution)/shard_map/ppermute | solution.py:26
  1.8 8.4 %collective-permute-start = (f32[6,8,16,6]{3,2,1,0:T(8,128)S(1)}, f32[6,8,16,6]{3,2,1,0:T(8,128)S(1)}, u32[]{:S(2)}, u32[]{:S(2)}) collective-permute-start(f32[6,8,16,6]{3,2,1,0:T(8,128)S(1)} %get-tuple-element.89), channel_id=1, source_target_pairs={{0,32},{32,64},{64,96},{96,128},{128,160},{160,192},{192,224},{224... | collective-permute-start | bytes 55304 | tf_op jit(solution)/shard_map/ppermute | solution.py:25
  10.7 28.3 %collective-permute-start.3 = (f32[6,8,6,140]{3,2,1,0:T(8,128)S(1)}, f32[6,8,6,140]{3,2,1,0:T(8,128)S(1)}, u32[]{:S(2)}, u32[]{:S(2)}) collective-permute-start(f32[6,8,6,140]{3,2,1,0:T(8,128)S(1)} %get-tuple-element.52), channel_id=1, source_target_pairs={{1,0},{2,1},{3,2},{4,3},{5,4},{6,5},{7,6},{8,7},{9,8},{10,9},{11,1... | collective-permute-start | bytes 483848 | tf_op jit(solution)/shard_map/ppermute | solution.py:26
  19.1 19.9 %collective-permute-start.2 = (f32[6,8,6,140]{3,2,1,0:T(8,128)S(1)}, f32[6,8,6,140]{3,2,1,0:T(8,128)S(1)}, u32[]{:S(2)}, u32[]{:S(2)}) collective-permute-start(f32[6,8,6,140]{3,2,1,0:T(8,128)S(1)} %get-tuple-element.51), channel_id=1, source_target_pairs={{0,1},{1,2},{2,3},{3,4},{4,5},{5,6},{6,7},{7,8},{8,9},{9,10},{10,1... | collective-permute-start | bytes 483848 | tf_op jit(solution)/shard_map/ppermute | solution.py:25
  39.7 0.7 copy-start.8
  44.1 0.9 %copy-start.7 = (f32[64,256]{1,0:T(8,128)S(1)}, f32[64,256]{1,0:T(8,128)}, u32[]{:S(2)}) copy-start(f32[64,256]{1,0:T(8,128)} %constant.26.clone) | copy-start | bytes 196612
  45.4 4.2 %collective-permute-start.5 = (f32[6,4,8,7]{3,2,1,0:T(8,128)S(1)}, f32[6,4,8,7]{3,2,1,0:T(8,128)S(1)}, u32[]{:S(2)}, u32[]{:S(2)}) collective-permute-start(f32[6,4,8,7]{3,2,1,0:T(8,128)S(1)} %get-tuple-element.132), channel_id=1, source_target_pairs={{32,0},{64,32},{96,64},{128,96},{160,128},{192,160},{224,192},{0,2... | collective-permute-start | bytes 16136 | tf_op jit(solution)/shard_map/ppermute | solution.py:26
  47.4 14.3 %copy-start.9 = (f32[2]{0:T(128)S(1)}, f32[2]{0:T(128)}, u32[]{:S(2)}) copy-start(f32[2]{0:T(128)} %constant.84.clone) | copy-start | bytes 28
  47.4 5.3 %collective-permute-start.4 = (f32[6,4,8,7]{3,2,1,0:T(8,128)S(1)}, f32[6,4,8,7]{3,2,1,0:T(8,128)S(1)}, u32[]{:S(2)}, u32[]{:S(2)}) collective-permute-start(f32[6,4,8,7]{3,2,1,0:T(8,128)S(1)} %get-tuple-element.131), channel_id=1, source_target_pairs={{0,32},{32,64},{64,96},{96,128},{128,160},{160,192},{192,224},{224... | collective-permute-start | bytes 16136 | tf_op jit(solution)/shard_map/ppermute | solution.py:25
  52.8 4.7 %collective-permute-start.7 = (f32[6,4,7,78]{3,2,1,0:T(8,128)S(1)}, f32[6,4,7,78]{3,2,1,0:T(8,128)S(1)}, u32[]{:S(2)}, u32[]{:S(2)}) collective-permute-start(f32[6,4,7,78]{3,2,1,0:T(8,128)S(1)} %get-tuple-element.130), channel_id=1, source_target_pairs={{1,0},{2,1},{3,2},{4,3},{5,4},{6,5},{7,6},{8,7},{9,8},{10,9},{11,1... | collective-permute-start | bytes 157256 | tf_op jit(solution)/shard_map/ppermute | solution.py:26
  53.0 8.1 %collective-permute-start.6 = (f32[6,4,7,78]{3,2,1,0:T(8,128)S(1)}, f32[6,4,7,78]{3,2,1,0:T(8,128)S(1)}, u32[]{:S(2)}, u32[]{:S(2)}) collective-permute-start(f32[6,4,7,78]{3,2,1,0:T(8,128)S(1)} %get-tuple-element.129), channel_id=1, source_target_pairs={{0,1},{1,2},{2,3},{3,4},{4,5},{5,6},{6,7},{7,8},{8,9},{9,10},{10,1... | collective-permute-start | bytes 157256 | tf_op jit(solution)/shard_map/ppermute | solution.py:25
  61.9 1.2 %copy-start.12 = (f32[16,64]{1,0:T(8,128)S(1)}, f32[16,64]{1,0:T(8,128)}, u32[]{:S(2)}) copy-start(f32[16,64]{1,0:T(8,128)} %constant.85.clone) | copy-start | bytes 12292
  62.3 16.4 %copy-start.11 = (f32[2]{0:T(128)S(1)}, f32[2]{0:T(128)}, u32[]{:S(2)}) copy-start(f32[2]{0:T(128)} %constant.86.clone) | copy-start | bytes 28
  63.4 1.5 %collective-permute-start.9 = (f32[6,2,4,8]{3,2,1,0:T(4,128)S(1)}, f32[6,2,4,8]{3,2,1,0:T(4,128)S(1)}, u32[]{:S(2)}, u32[]{:S(2)}) collective-permute-start(f32[6,2,4,8]{3,2,1,0:T(4,128)S(1)} %get-tuple-element.186), channel_id=1, source_target_pairs={{32,0},{64,32},{96,64},{128,96},{160,128},{192,160},{224,192},{0,2... | collective-permute-start | bytes 4616 | tf_op jit(solution)/shard_map/ppermute | solution.py:26
  63.4 4.5 %collective-permute-start.8 = (f32[6,2,4,8]{3,2,1,0:T(4,128)S(1)}, f32[6,2,4,8]{3,2,1,0:T(4,128)S(1)}, u32[]{:S(2)}, u32[]{:S(2)}) collective-permute-start(f32[6,2,4,8]{3,2,1,0:T(4,128)S(1)} %get-tuple-element.185), channel_id=1, source_target_pairs={{0,32},{32,64},{64,96},{96,128},{128,160},{160,192},{192,224},{224... | collective-permute-start | bytes 4616 | tf_op jit(solution)/shard_map/ppermute | solution.py:25
  68.0 9.3 %collective-permute-start.10 = (f32[6,2,4,48]{3,2,1,0:T(4,128)S(1)}, f32[6,2,4,48]{3,2,1,0:T(4,128)S(1)}, u32[]{:S(2)}, u32[]{:S(2)}) collective-permute-start(f32[6,2,4,48]{3,2,1,0:T(4,128)S(1)} %pad_maximum_fusion.17), channel_id=1, source_target_pairs={{0,2},{1,3},{2,4},{3,5},{4,6},{5,7},{6,8},{7,9},{8,10},{9,11},{10,... | collective-permute-start | bytes 27656 | tf_op jit(solution)/shard_map/ppermute | solution.py:25
  68.1 9.2 %collective-permute-start.11 = (f32[6,2,4,48]{3,2,1,0:T(4,128)S(1)}, f32[6,2,4,48]{3,2,1,0:T(4,128)S(1)}, u32[]{:S(2)}, u32[]{:S(2)}) collective-permute-start(f32[6,2,4,48]{3,2,1,0:T(4,128)S(1)} %pad_maximum_fusion.17), channel_id=1, source_target_pairs={{0,1},{1,2},{2,3},{3,4},{4,5},{5,6},{6,7},{7,8},{8,9},{9,10},{10,1... | collective-permute-start | bytes 27656 | tf_op jit(solution)/shard_map/ppermute | solution.py:25
  68.7 8.5 %collective-permute-start.12 = (f32[6,2,4,48]{3,2,1,0:T(4,128)S(1)}, f32[6,2,4,48]{3,2,1,0:T(4,128)S(1)}, u32[]{:S(2)}, u32[]{:S(2)}) collective-permute-start(f32[6,2,4,48]{3,2,1,0:T(4,128)S(1)} %pad_maximum_fusion.17), channel_id=1, source_target_pairs={{1,0},{2,1},{3,2},{4,3},{5,4},{6,5},{7,6},{8,7},{9,8},{10,9},{11,1... | collective-permute-start | bytes 27656 | tf_op jit(solution)/shard_map/ppermute | solution.py:26
  73.5 4.8 %collective-permute-start.13 = (f32[6,2,4,48]{3,2,1,0:T(4,128)S(1)}, f32[6,2,4,48]{3,2,1,0:T(4,128)S(1)}, u32[]{:S(2)}, u32[]{:S(2)}) collective-permute-start(f32[6,2,4,48]{3,2,1,0:T(4,128)S(1)} %pad_maximum_fusion.17), channel_id=1, source_target_pairs={{2,0},{3,1},{4,2},{5,3},{6,4},{7,5},{8,6},{9,7},{10,8},{11,9},{12,... | collective-permute-start | bytes 27656 | tf_op jit(solution)/shard_map/ppermute | solution.py:26

commit v16 on v15

--- a/solution.py
+++ b/solution.py
@@ -235,6 +235,8 @@
     wide_x = padded_along(jnp.concatenate([fields, previous], 0), 6, "gx", 3)
     local, wide_x = lax.optimization_barrier((local, wide_x))
     spreads = global_max(local)[0]
+    ops_1 = Level(coefficients(padded(fields_1, 7), 1)[0], 7, 1)
+    ops_2 = Level(coefficients(padded(fields_2, 8), 2)[0], 8, 2)
 
     wide = padded_along(wide_x, 6, "gy", 2)
     ops_0 = Level(coefficients(crop(wide[:4], 6, 5), 0)[0], 5, 0)
@@ -254,15 +256,11 @@
     pre_0, pre_0_halo = chebyshev(ops_0, source_0, 5, None, None, spreads[0])
     resid_0 = crop(source_0, 5, 0) - ops_0.operate(crop(pre_0, pre_0_halo, 1), 1)
 
-    wide_1 = padded(jnp.concatenate([restrict(resid_0), fields_1], 0), 7)
-    ops_1 = Level(coefficients(wide_1[2:], 1)[0], 7, 1)
-    source_1 = wide_1[:2]
+    source_1 = padded(restrict(resid_0), 7)
     pre_1, pre_1_halo = chebyshev(ops_1, source_1, 7, None, None, spreads[1])
     resid_1 = crop(source_1, 7, 0) - ops_1.operate(crop(pre_1, pre_1_halo, 1), 1)
 
-    wide_2 = padded(jnp.concatenate([restrict(resid_1), fields_2], 0), 8)
-    ops_2 = Level(coefficients(wide_2[2:], 2)[0], 8, 2)
-    source_2 = wide_2[:2]
+    source_2 = padded(restrict(resid_1), 8)
     first_2, first_2_halo = chebyshev(ops_2, source_2, 8, None, None, spreads[2])
     coarse_2, coarse_2_halo = chebyshev(ops_2, source_2, 8, first_2, first_2_halo, spreads[2])
 

time: 88.2 us -> 102 us (1.16)
  starting transfers between devices: 21.8 us -> 37.6 us
  waiting for transfers between devices: 16.1 us -> 13.3 us
  local copies, waits for them, and re-layouts: 7.6 us -> 10.1 us
  Pallas kernels: 17.5 us -> 15.2 us
    ppermute x7 -> x12, starting transfers between devices: 18.6 us -> 28.3 us  [padded_along(): lax.ppermute(head, axis, [((i + distance) % count, i) for i in range(coun...]
    ppermute x7 -> x12, starting transfers between devices: 3.2 us -> 9.27 us  [padded_along(): lax.ppermute(tail, axis, [(i, (i + distance) % count) for i in range(coun...]
    ppermute x7 -> x12, waiting for transfers between devices: 6.05 us -> 3.63 us  [padded_along(): lax.ppermute(head, axis, [((i + distance) % count, i) for i in range(coun...]
    pallas_call x1, Pallas kernels: 17.5 us -> 15.2 us  [global_max(): pl.pallas_call(lambda *refs: spread_kernel(inner, *refs), out_shape=jax.S...]
    concatenate x1 -> x2, local copies, waits for them, and re-layouts: 0.08 us -> 1.57 us  [padded_along(): return jnp.concatenate(below + [cells] + above, axis=dim)]
    concatenate x5 -> x8, other arithmetic: 0.99 us -> 2.05 us  [padded_along(): return jnp.concatenate(below + [cells] + above, axis=dim)]
    ppermute x7 -> x12, waiting for transfers between devices: 10.1 us -> 9.7 us  [padded_along(): lax.ppermute(tail, axis, [(i, (i + distance) % count) for i in range(coun...]
  transfers between devices with their start and end apart: 14 -> 24, of which waited for: 8 -> 7; matrix products, arithmetic and copies ran while one was open for 6% -> 17% of each run, Pallas kernels for 20% -> 15%
where the time goes in v16:
time: 102 us
  starting transfers between devices  37.6 us (37%)
  other arithmetic  16.3 us (16%)
  Pallas kernels  15.2 us (15%)
  waiting for transfers between devices  13.3 us (13%)
  local copies, waits for them, and re-layouts  10.1 us (10%)
  between operations  7.11 us (7%)
  matrix products  2.03 us (2%)
    ppermute x12, starting transfers between devices, padded_along(): lax.ppermute(head, axis, [((i + distance) % count, i) for i in range(coun...  28.3 us
    pallas_call x1, Pallas kernels, global_max(): pl.pallas_call(lambda *refs: spread_kernel(inner, *refs), out_shape=jax.S...  15.2 us
    ppermute x12, waiting for transfers between devices, padded_along(): lax.ppermute(tail, axis, [(i, (i + distance) % count) for i in range(coun...  9.7 us
    ppermute x12, starting transfers between devices, padded_along(): lax.ppermute(tail, axis, [(i, (i + distance) % count) for i in range(coun...  9.27 us
    add x12, other arithmetic, chebyshev(): iterate = crop(iterate, halo + 1, halo) + update  4.31 us
    ppermute x12, waiting for transfers between devices, padded_along(): lax.ppermute(head, axis, [((i + distance) % count, i) for i in range(coun...  3.63 us
    slice x30, local copies, waits for them, and re-layouts, shrunk_neighbours(): along_z = jnp.roll(centre, 1, 1) + jnp.roll(centre, -1, 1)  3.45 us
    add x17, other arithmetic, operate(): first = coeff[0] * centre[0] + coeff[1] * centre[1]  3.15 us
  transfers between devices with their start and end apart: 24, of which 7 were waited for; matrix products, arithmetic and copies ran while one was open for 17% of the time, Pallas kernels for 15%

profile of v16, /device:TPU:0, one launch (start us, length us, event | category | flops | bytes accessed | tf_op | source)
XLA Modules:
  0.0 101.6 jit_solution(8628803686173784474)
XLA Ops:
  0.0 1.1 %pad_maximum_fusion.6 = f32[6,8,16,128]{3,2,1,0:T(8,128)S(1)} fusion(f32[2,8,16,128]{3,2,1,0:T(8,128)} %param.31, f32[1,8,16,128]{3,2,1,0:T(8,128)} %bitcast.90, f32[1,8,16,128]{3,2,1,0:T(8,128)} %bitcast.93, f32[2,8,16,128]{3,2,1,0:T(8,128)} %param.30), kind=kLoop, calls=%fused_computation.66 | loop fusion | flops 294912 | bytes 786432 | tf_op jit(solution)/shard_map/concatenate | solution.py:235
  1.4 0.5 collective-permute-start.1
  1.9 0.4 fusion.240
  2.4 0.4 convolution_multiply_fusion.1
  2.9 2.9 %collective-permute-start.9 = (f32[4,4,8,7]{3,2,1,0:T(8,128)S(1)}, f32[4,4,8,7]{3,2,1,0:T(8,128)S(1)}, u32[]{:S(2)}, u32[]{:S(2)}) collective-permute-start(f32[4,4,8,7]{3,2,1,0:T(8,128)S(1)} %get-tuple-element.146), channel_id=1, source_target_pairs={{32,0},{64,32},{96,64},{128,96},{160,128},{192,160},{224,192},{0,2... | collective-permute-start | bytes 10760 | tf_op jit(solution)/shard_map/ppermute | solution.py:26
  6.4 0.5 collective-permute-start.18
  6.9 0.6 fusion.108
  7.5 0.8 fusion.169
  9.5 0.6 fusion.190
  12.5 0.6 select_select_fusion.refs_0_
  13.2 3.4 %collective-permute-start.20 = (f32[4,2,4,48]{3,2,1,0:T(4,128)S(1)}, f32[4,2,4,48]{3,2,1,0:T(4,128)}, u32[]{:S(2)}, u32[]{:S(2)}) collective-permute-start(f32[4,2,4,48]{3,2,1,0:T(4,128)S(1)} %pad_maximum_fusion.13), channel_id=1, source_target_pairs={{0,2},{1,3},{2,4},{3,5},{4,6},{5,7},{6,8},{7,9},{8,10},{9,11},{10,... | collective-permute-start | bytes 18440 | tf_op jit(solution)/shard_map/ppermute | solution.py:25
  16.6 1.9 %collective-permute-start.21 = (f32[4,2,4,48]{3,2,1,0:T(4,128)S(1)}, f32[4,2,4,48]{3,2,1,0:T(4,128)}, u32[]{:S(2)}, u32[]{:S(2)}) collective-permute-start(f32[4,2,4,48]{3,2,1,0:T(4,128)S(1)} %pad_maximum_fusion.13), channel_id=1, source_target_pairs={{0,1},{1,2},{2,3},{3,4},{4,5},{5,6},{6,7},{7,8},{8,9},{9,10},{10,1... | collective-permute-start | bytes 18440 | tf_op jit(solution)/shard_map/ppermute | solution.py:25
  18.5 7.8 %collective-permute-start.22 = (f32[4,2,4,48]{3,2,1,0:T(4,128)S(1)}, f32[4,2,4,48]{3,2,1,0:T(4,128)}, u32[]{:S(2)}, u32[]{:S(2)}) collective-permute-start(f32[4,2,4,48]{3,2,1,0:T(4,128)S(1)} %pad_maximum_fusion.13), channel_id=1, source_target_pairs={{1,0},{2,1},{3,2},{4,3},{5,4},{6,5},{7,6},{8,7},{9,8},{10,9},{11,1... | collective-permute-start | bytes 18440 | tf_op jit(solution)/shard_map/ppermute | solution.py:26
  26.5 0.4 pad_maximum_fusion.1
  27.0 1.1 %collective-permute-start.3 = (f32[6,8,6,140]{3,2,1,0:T(8,128)S(1)}, f32[6,8,6,140]{3,2,1,0:T(8,128)S(1)}, u32[]{:S(2)}, u32[]{:S(2)}) collective-permute-start(f32[6,8,6,140]{3,2,1,0:T(8,128)S(1)} %get-tuple-element.54), channel_id=1, source_target_pairs={{1,0},{2,1},{3,2},{4,3},{5,4},{6,5},{7,6},{8,7},{9,8},{10,9},{11,1... | collective-permute-start | bytes 483848 | tf_op jit(solution)/shard_map/ppermute | solution.py:26
  28.0 1.0 %collective-permute-start.2 = (f32[6,8,6,140]{3,2,1,0:T(8,128)S(1)}, f32[6,8,6,140]{3,2,1,0:T(8,128)S(1)}, u32[]{:S(2)}, u32[]{:S(2)}) collective-permute-start(f32[6,8,6,140]{3,2,1,0:T(8,128)S(1)} %get-tuple-element.53), channel_id=1, source_target_pairs={{0,1},{1,2},{2,3},{3,4},{4,5},{5,6},{6,7},{7,8},{8,9},{9,10},{10,1... | collective-permute-start | bytes 483848 | tf_op jit(solution)/shard_map/ppermute | solution.py:25
  29.1 0.7 fusion.228
  29.7 15.2 %shard_map.280 = f32[8,128]{1,0:T(8,128)} custom-call(f32[8,128]{1,0:T(8,128)} %select_select_fusion.refs_0_), custom_call_target="tpu_custom_call" | custom-call | tf_op jit(solution)/shard_map/pallas_call | solution.py:114
  44.9 1.4 %fusion.239 = (f32[1,1]{1,0:T(1,128)}, f32[1,1]{1,0:T(1,128)}, f32[1,1]{1,0:T(1,128)}) fusion(f32[8,128]{1,0:T(8,128)} %shard_map.280), kind=kLoop, calls=%fused_computation.401 | loop fusion | bytes 24 | tf_op jit(solution)/shard_map/slice | solution.py:264
  48.2 1.8 %collective-permute-start.11 = (f32[4,4,7,78]{3,2,1,0:T(8,128)}, f32[4,4,7,78]{3,2,1,0:T(8,128)}, u32[]{:S(2)}, u32[]{:S(2)}) collective-permute-start(f32[4,4,7,78]{3,2,1,0:T(8,128)} %get-tuple-element.144), channel_id=1, source_target_pairs={{1,0},{2,1},{3,2},{4,3},{5,4},{6,5},{7,6},{8,7},{9,8},{10,9},{11,1... | collective-permute-start | bytes 104840 | tf_op jit(solution)/shard_map/ppermute | solution.py:26
  50.5 0.4 fusion.42
  51.3 0.4 subtract_bitcast_fusion
  51.7 0.8 fusion.12
  52.9 0.4 fusion.54
  53.3 0.6 slice_add_fusion.12
  53.9 0.4 fusion.52
  54.7 0.7 fusion.33
  56.7 0.9 collective-permute-start.5
  57.9 1.0 pad_maximum_fusion.8
  59.2 3.3 %collective-permute-done.4 = f32[2,4,8,7]{3,2,1,0:T(8,128)S(1)} collective-permute-done((f32[2,4,8,7]{3,2,1,0:T(8,128)S(1)}, f32[2,4,8,7]{3,2,1,0:T(8,128)S(1)}, u32[]{:S(2)}, u32[]{:S(2)}) %collective-permute-start.4) | collective-permute-done | bytes 1824 | tf_op jit(solution)/shard_map/ppermute | solution.py:25
  62.5 4.8 %collective-permute-start.7 = (f32[2,4,7,78]{3,2,1,0:T(8,128)S(1)}, f32[2,4,7,78]{3,2,1,0:T(8,128)S(1)}, u32[]{:S(2)}, u32[]{:S(2)}) collective-permute-start(f32[2,4,7,78]{3,2,1,0:T(8,128)S(1)} %get-tuple-element.178), channel_id=1, source_target_pairs={{1,0},{2,1},{3,2},{4,3},{5,4},{6,5},{7,6},{8,7},{9,8},{10,9},{11,1... | collective-permute-start | bytes 52424 | tf_op jit(solution)/shard_map/ppermute | solution.py:26
  67.4 1.6 %collective-permute-done.7 = f32[2,4,7,78]{3,2,1,0:T(8,128)S(1)} collective-permute-done((f32[2,4,7,78]{3,2,1,0:T(8,128)S(1)}, f32[2,4,7,78]{3,2,1,0:T(8,128)S(1)}, u32[]{:S(2)}, u32[]{:S(2)}) %collective-permute-start.7) | collective-permute-done | bytes 17504 | tf_op jit(solution)/shard_map/ppermute | solution.py:26
  69.0 1.8 %collective-permute-start.23 = (f32[4,2,4,48]{3,2,1,0:T(4,128)S(1)}, f32[4,2,4,48]{3,2,1,0:T(4,128)S(1)}, u32[]{:S(2)}, u32[]{:S(2)}) collective-permute-start(f32[4,2,4,48]{3,2,1,0:T(4,128)S(1)} %pad_maximum_fusion.13), channel_id=1, source_target_pairs={{2,0},{3,1},{4,2},{5,3},{6,4},{7,5},{8,6},{9,7},{10,8},{11,9},{12,... | collective-permute-start | bytes 18440 | tf_op jit(solution)/shard_map/ppermute | solution.py:26
  70.8 3.9 %collective-permute-done.6 = f32[2,4,7,78]{3,2,1,0:T(8,128)S(1)} collective-permute-done((f32[2,4,7,78]{3,2,1,0:T(8,128)S(1)}, f32[2,4,7,78]{3,2,1,0:T(8,128)S(1)}, u32[]{:S(2)}, u32[]{:S(2)}) %collective-permute-start.6) | collective-permute-done | bytes 17504 | tf_op jit(solution)/shard_map/ppermute | solution.py:25
  76.7 0.5 collective-permute-start.12
  77.3 1.5 %concatenate.198 = f32[4,2,20,48]{3,2,1,0:T(8,128)S(1)} concatenate(f32[4,2,4,48]{3,2,1,0:T(4,128)} %collective-permute-done.20, f32[4,2,4,48]{3,2,1,0:T(4,128)} %collective-permute-done.21, f32[4,2,4,48]{3,2,1,0:T(4,128)S(1)} %pad_maximum_fusion.13, f32[4,2,4,48]{3,2,1,0:T(4,128)} %collective-permute-done.22, f32[4,2,4,48]{3,2,1,0:T(4,128)S(1)} %collective-permute-done.23), dimensions={2} | concatenate | bytes 61440 | tf_op jit(solution)/shard_map/concatenate | solution.py:29
  78.8 2.3 %collective-permute-done.12 = f32[2,2,4,8]{3,2,1,0:T(4,128)S(1)} collective-permute-done((f32[2,2,4,8]{3,2,1,0:T(4,128)S(1)}, f32[2,2,4,8]{3,2,1,0:T(4,128)S(1)}, u32[]{:S(2)}, u32[]{:S(2)}) %collective-permute-start.12) | collective-permute-done | bytes 544 | tf_op jit(solution)/shard_map/ppermute | solution.py:25
  81.2 1.6 %collective-permute-start.15 = (f32[2,2,4,48]{3,2,1,0:T(4,128)S(1)}, f32[2,2,4,48]{3,2,1,0:T(4,128)S(1)}, u32[]{:S(2)}, u32[]{:S(2)}) collective-permute-start(f32[2,2,4,48]{3,2,1,0:T(4,128)S(1)} %pad_maximum_fusion.14), channel_id=1, source_target_pairs={{0,1},{1,2},{2,3},{3,4},{4,5},{5,6},{6,7},{7,8},{8,9},{9,10},{10,1... | collective-permute-start | bytes 9224 | tf_op jit(solution)/shard_map/ppermute | solution.py:25
  82.8 4.7 %collective-permute-start.16 = (f32[2,2,4,48]{3,2,1,0:T(4,128)S(1)}, f32[2,2,4,48]{3,2,1,0:T(4,128)S(1)}, u32[]{:S(2)}, u32[]{:S(2)}) collective-permute-start(f32[2,2,4,48]{3,2,1,0:T(4,128)S(1)} %pad_maximum_fusion.14), channel_id=1, source_target_pairs={{1,0},{2,1},{3,2},{4,3},{5,4},{6,5},{7,6},{8,7},{9,8},{10,9},{11,1... | collective-permute-start | bytes 9224 | tf_op jit(solution)/shard_map/ppermute | solution.py:26
  87.5 1.9 %collective-permute-start.17 = (f32[2,2,4,48]{3,2,1,0:T(4,128)S(1)}, f32[2,2,4,48]{3,2,1,0:T(4,128)S(1)}, u32[]{:S(2)}, u32[]{:S(2)}) collective-permute-start(f32[2,2,4,48]{3,2,1,0:T(4,128)S(1)} %pad_maximum_fusion.14), channel_id=1, source_target_pairs={{2,0},{3,1},{4,2},{5,3},{6,4},{7,5},{8,6},{9,7},{10,8},{11,9},{12,... | collective-permute-start | bytes 9224 | tf_op jit(solution)/shard_map/ppermute | solution.py:26
  90.3 1.8 %collective-permute-done.17 = f32[2,2,4,48]{3,2,1,0:T(4,128)S(1)} collective-permute-done((f32[2,2,4,48]{3,2,1,0:T(4,128)S(1)}, f32[2,2,4,48]{3,2,1,0:T(4,128)S(1)}, u32[]{:S(2)}, u32[]{:S(2)}) %collective-permute-start.17) | collective-permute-done | bytes 3104 | tf_op jit(solution)/shard_map/ppermute | solution.py:26
  96.4 0.3 slice.2055
  96.7 0.7 copy.54
  97.5 0.4 fusion.50
  98.2 0.6 slice_add_fusion.7
  98.8 0.4 fusion.48
  99.6 0.7 slice_add_fusion.4
  100.7 1.0 fusion.62
  (156 shorter events, 12.1 us)
Async XLA Ops:
  0.0 1.9 %copy-start.4 = (f32[128,64]{1,0:T(8,128)S(1)}, f32[128,64]{1,0:T(8,128)}, u32[]{:S(2)}) copy-start(f32[128,64]{1,0:T(8,128)} %constant.21.clone) | copy-start | bytes 98308
  0.0 1.9 %copy-start = (f32[2,8,16,128]{3,2,1,0:T(8,128)S(1)}, f32[2,8,16,128]{3,2,1,0:T(8,128)}, u32[]{:S(2)}) copy-start(f32[2,8,16,128]{3,2,1,0:T(8,128)} %param.30) | copy-start | bytes 393220
  0.0 1.9 %copy-start.1 = (f32[8,16,128]{2,1,0:T(8,128)S(1)}, f32[8,16,128]{2,1,0:T(8,128)}, u32[]{:S(2)}) copy-start(f32[8,16,128]{2,1,0:T(8,128)} %param.33) | copy-start | bytes 196612
  0.0 1.9 %copy-start.2 = (f32[8,16,128]{2,1,0:T(8,128)S(1)}, f32[8,16,128]{2,1,0:T(8,128)}, u32[]{:S(2)}) copy-start(f32[8,16,128]{2,1,0:T(8,128)} %param.32) | copy-start | bytes 196612
  0.0 2.3 %copy-start.5 = (f32[128,512]{1,0:T(8,128)S(1)}, f32[128,512]{1,0:T(8,128)}, u32[]{:S(2)}) copy-start(f32[128,512]{1,0:T(8,128)} %constant.22.clone) | copy-start | bytes 786436
  1.1 4.7 %copy-start.8 = (f32[64,32]{1,0:T(8,128)S(1)}, f32[64,32]{1,0:T(8,128)}, u32[]{:S(2)}) copy-start(f32[64,32]{1,0:T(8,128)} %constant.23.clone) | copy-start | bytes 24580
  1.2 5.0 %copy-start.12 = (f32[32,128]{1,0:T(8,128)S(1)}, f32[32,128]{1,0:T(8,128)}, u32[]{:S(2)}) copy-start(f32[32,128]{1,0:T(8,128)} %constant.24.clone) | copy-start | bytes 49156
  1.3 25.1 %copy-start.3 = (f32[2,8,16,128]{3,2,1,0:T(8,128)S(1)}, f32[2,8,16,128]{3,2,1,0:T(8,128)}, u32[]{:S(2)}) copy-start(f32[2,8,16,128]{3,2,1,0:T(8,128)} %param.31) | copy-start | bytes 393220
  1.4 25.1 %collective-permute-start.1 = (f32[6,8,16,6]{3,2,1,0:T(8,128)S(1)}, f32[6,8,16,6]{3,2,1,0:T(8,128)S(1)}, u32[]{:S(2)}, u32[]{:S(2)}) collective-permute-start(f32[6,8,16,6]{3,2,1,0:T(8,128)S(1)} %get-tuple-element.92), channel_id=1, source_target_pairs={{32,0},{64,32},{96,64},{128,96},{160,128},{192,160},{224,192},{0,2... | collective-permute-start | bytes 55304 | tf_op jit(solution)/shard_map/ppermute | solution.py:26
  1.8 24.6 %collective-permute-start = (f32[6,8,16,6]{3,2,1,0:T(8,128)S(1)}, f32[6,8,16,6]{3,2,1,0:T(8,128)S(1)}, u32[]{:S(2)}, u32[]{:S(2)}) collective-permute-start(f32[6,8,16,6]{3,2,1,0:T(8,128)S(1)} %get-tuple-element.91), channel_id=1, source_target_pairs={{0,32},{32,64},{64,96},{96,128},{128,160},{160,192},{192,224},{224... | collective-permute-start | bytes 55304 | tf_op jit(solution)/shard_map/ppermute | solution.py:25
  2.9 13.7 %collective-permute-start.9 = (f32[4,4,8,7]{3,2,1,0:T(8,128)S(1)}, f32[4,4,8,7]{3,2,1,0:T(8,128)S(1)}, u32[]{:S(2)}, u32[]{:S(2)}) collective-permute-start(f32[4,4,8,7]{3,2,1,0:T(8,128)S(1)} %get-tuple-element.146), channel_id=1, source_target_pairs={{32,0},{64,32},{96,64},{128,96},{160,128},{192,160},{224,192},{0,2... | collective-permute-start | bytes 10760 | tf_op jit(solution)/shard_map/ppermute | solution.py:26
  6.3 6.8 %collective-permute-start.19 = (f32[4,2,4,8]{3,2,1,0:T(4,128)S(1)}, f32[4,2,4,8]{3,2,1,0:T(4,128)S(1)}, u32[]{:S(2)}, u32[]{:S(2)}) collective-permute-start(f32[4,2,4,8]{3,2,1,0:T(4,128)S(1)} %get-tuple-element.192), channel_id=1, source_target_pairs={{32,0},{64,32},{96,64},{128,96},{160,128},{192,160},{224,192},{0,2... | collective-permute-start | bytes 3080 | tf_op jit(solution)/shard_map/ppermute | solution.py:26
  6.4 6.8 %collective-permute-start.18 = (f32[4,2,4,8]{3,2,1,0:T(4,128)S(1)}, f32[4,2,4,8]{3,2,1,0:T(4,128)S(1)}, u32[]{:S(2)}, u32[]{:S(2)}) collective-permute-start(f32[4,2,4,8]{3,2,1,0:T(4,128)S(1)} %get-tuple-element.191), channel_id=1, source_target_pairs={{0,32},{32,64},{64,96},{96,128},{128,160},{160,192},{192,224},{224... | collective-permute-start | bytes 3080 | tf_op jit(solution)/shard_map/ppermute | solution.py:25
  13.2 5.4 %collective-permute-start.8 = (f32[4,4,8,7]{3,2,1,0:T(8,128)S(1)}, f32[4,4,8,7]{3,2,1,0:T(8,128)S(1)}, u32[]{:S(2)}, u32[]{:S(2)}) collective-permute-start(f32[4,4,8,7]{3,2,1,0:T(8,128)S(1)} %get-tuple-element.145), channel_id=1, source_target_pairs={{0,32},{32,64},{64,96},{96,128},{128,160},{160,192},{192,224},{224... | collective-permute-start | bytes 10760 | tf_op jit(solution)/shard_map/ppermute | solution.py:25
  13.2 63.5 %collective-permute-start.20 = (f32[4,2,4,48]{3,2,1,0:T(4,128)S(1)}, f32[4,2,4,48]{3,2,1,0:T(4,128)}, u32[]{:S(2)}, u32[]{:S(2)}) collective-permute-start(f32[4,2,4,48]{3,2,1,0:T(4,128)S(1)} %pad_maximum_fusion.13), channel_id=1, source_target_pairs={{0,2},{1,3},{2,4},{3,5},{4,6},{5,7},{6,8},{7,9},{8,10},{9,11},{10,... | collective-permute-start | bytes 18440 | tf_op jit(solution)/shard_map/ppermute | solution.py:25
  16.6 60.7 %collective-permute-start.21 = (f32[4,2,4,48]{3,2,1,0:T(4,128)S(1)}, f32[4,2,4,48]{3,2,1,0:T(4,128)}, u32[]{:S(2)}, u32[]{:S(2)}) collective-permute-start(f32[4,2,4,48]{3,2,1,0:T(4,128)S(1)} %pad_maximum_fusion.13), channel_id=1, source_target_pairs={{0,1},{1,2},{2,3},{3,4},{4,5},{5,6},{6,7},{7,8},{8,9},{9,10},{10,1... | collective-permute-start | bytes 18440 | tf_op jit(solution)/shard_map/ppermute | solution.py:25
  18.5 8.4 %copy-start.6 = (f32[4,4,8,7]{3,2,1,0:T(8,128)}, f32[4,4,8,7]{3,2,1,0:T(8,128)S(1)}, u32[]{:S(2)}) copy-start(f32[4,4,8,7]{3,2,1,0:T(8,128)S(1)} %collective-permute-done.8) | copy-start | bytes 10756
  18.5 58.7 %collective-permute-start.22 = (f32[4,2,4,48]{3,2,1,0:T(4,128)S(1)}, f32[4,2,4,48]{3,2,1,0:T(4,128)}, u32[]{:S(2)}, u32[]{:S(2)}) collective-permute-start(f32[4,2,4,48]{3,2,1,0:T(4,128)S(1)} %pad_maximum_fusion.13), channel_id=1, source_target_pairs={{1,0},{2,1},{3,2},{4,3},{5,4},{6,5},{7,6},{8,7},{9,8},{10,9},{11,1... | collective-permute-start | bytes 18440 | tf_op jit(solution)/shard_map/ppermute | solution.py:26
  27.0 21.2 %collective-permute-start.3 = (f32[6,8,6,140]{3,2,1,0:T(8,128)S(1)}, f32[6,8,6,140]{3,2,1,0:T(8,128)S(1)}, u32[]{:S(2)}, u32[]{:S(2)}) collective-permute-start(f32[6,8,6,140]{3,2,1,0:T(8,128)S(1)} %get-tuple-element.54), channel_id=1, source_target_pairs={{1,0},{2,1},{3,2},{4,3},{5,4},{6,5},{7,6},{8,7},{9,8},{10,9},{11,1... | collective-permute-start | bytes 483848 | tf_op jit(solution)/shard_map/ppermute | solution.py:26
  28.0 21.9 %collective-permute-start.2 = (f32[6,8,6,140]{3,2,1,0:T(8,128)S(1)}, f32[6,8,6,140]{3,2,1,0:T(8,128)S(1)}, u32[]{:S(2)}, u32[]{:S(2)}) collective-permute-start(f32[6,8,6,140]{3,2,1,0:T(8,128)S(1)} %get-tuple-element.53), channel_id=1, source_target_pairs={{0,1},{1,2},{2,3},{3,4},{4,5},{5,6},{6,7},{7,8},{8,9},{9,10},{10,1... | collective-permute-start | bytes 483848 | tf_op jit(solution)/shard_map/ppermute | solution.py:25
  48.2 8.6 %collective-permute-start.11 = (f32[4,4,7,78]{3,2,1,0:T(8,128)}, f32[4,4,7,78]{3,2,1,0:T(8,128)}, u32[]{:S(2)}, u32[]{:S(2)}) collective-permute-start(f32[4,4,7,78]{3,2,1,0:T(8,128)} %get-tuple-element.144), channel_id=1, source_target_pairs={{1,0},{2,1},{3,2},{4,3},{5,4},{6,5},{7,6},{8,7},{9,8},{10,9},{11,1... | collective-permute-start | bytes 104840 | tf_op jit(solution)/shard_map/ppermute | solution.py:26
  50.0 7.9 %collective-permute-start.10 = (f32[4,4,7,78]{3,2,1,0:T(8,128)}, f32[4,4,7,78]{3,2,1,0:T(8,128)}, u32[]{:S(2)}, u32[]{:S(2)}) collective-permute-start(f32[4,4,7,78]{3,2,1,0:T(8,128)} %get-tuple-element.143), channel_id=1, source_target_pairs={{0,1},{1,2},{2,3},{3,4},{4,5},{5,6},{6,7},{7,8},{8,9},{9,10},{10,1... | collective-permute-start | bytes 104840 | tf_op jit(solution)/shard_map/ppermute | solution.py:25
  51.0 0.7 copy-start.10
  55.4 1.0 copy-start.9
  55.4 2.5 %copy-start.7 = (f32[4,4,8,7]{3,2,1,0:T(8,128)S(1)}, f32[4,4,8,7]{3,2,1,0:T(8,128)}, u32[]{:S(2)}) copy-start(f32[4,4,8,7]{3,2,1,0:T(8,128)} %copy-done.6) | copy-start | bytes 10756
  56.0 19.1 %copy-start.11 = (f32[2]{0:T(128)S(1)}, f32[2]{0:T(128)}, u32[]{:S(2)}) copy-start(f32[2]{0:T(128)} %constant.84.clone) | copy-start | bytes 28
  56.7 2.5 %collective-permute-start.5 = (f32[2,4,8,7]{3,2,1,0:T(8,128)S(1)}, f32[2,4,8,7]{3,2,1,0:T(8,128)S(1)}, u32[]{:S(2)}, u32[]{:S(2)}) collective-permute-start(f32[2,4,8,7]{3,2,1,0:T(8,128)S(1)} %get-tuple-element.180), channel_id=1, source_target_pairs={{32,0},{64,32},{96,64},{128,96},{160,128},{192,160},{224,192},{0,2... | collective-permute-start | bytes 5384 | tf_op jit(solution)/shard_map/ppermute | solution.py:26
  57.9 4.6 %collective-permute-start.4 = (f32[2,4,8,7]{3,2,1,0:T(8,128)S(1)}, f32[2,4,8,7]{3,2,1,0:T(8,128)S(1)}, u32[]{:S(2)}, u32[]{:S(2)}) collective-permute-start(f32[2,4,8,7]{3,2,1,0:T(8,128)S(1)} %get-tuple-element.179), channel_id=1, source_target_pairs={{0,32},{32,64},{64,96},{96,128},{128,160},{160,192},{192,224},{224... | collective-permute-start | bytes 5384 | tf_op jit(solution)/shard_map/ppermute | solution.py:25
  62.5 6.4 %collective-permute-start.7 = (f32[2,4,7,78]{3,2,1,0:T(8,128)S(1)}, f32[2,4,7,78]{3,2,1,0:T(8,128)S(1)}, u32[]{:S(2)}, u32[]{:S(2)}) collective-permute-start(f32[2,4,7,78]{3,2,1,0:T(8,128)S(1)} %get-tuple-element.178), channel_id=1, source_target_pairs={{1,0},{2,1},{3,2},{4,3},{5,4},{6,5},{7,6},{8,7},{9,8},{10,9},{11,1... | collective-permute-start | bytes 52424 | tf_op jit(solution)/shard_map/ppermute | solution.py:26
  67.4 7.2 %collective-permute-start.6 = (f32[2,4,7,78]{3,2,1,0:T(8,128)S(1)}, f32[2,4,7,78]{3,2,1,0:T(8,128)S(1)}, u32[]{:S(2)}, u32[]{:S(2)}) collective-permute-start(f32[2,4,7,78]{3,2,1,0:T(8,128)S(1)} %get-tuple-element.177), channel_id=1, source_target_pairs={{0,1},{1,2},{2,3},{3,4},{4,5},{5,6},{6,7},{7,8},{8,9},{9,10},{10,1... | collective-permute-start | bytes 52424 | tf_op jit(solution)/shard_map/ppermute | solution.py:25
  69.0 8.3 %collective-permute-start.23 = (f32[4,2,4,48]{3,2,1,0:T(4,128)S(1)}, f32[4,2,4,48]{3,2,1,0:T(4,128)S(1)}, u32[]{:S(2)}, u32[]{:S(2)}) collective-permute-start(f32[4,2,4,48]{3,2,1,0:T(4,128)S(1)} %pad_maximum_fusion.13), channel_id=1, source_target_pairs={{2,0},{3,1},{4,2},{5,3},{6,4},{7,5},{8,6},{9,7},{10,8},{11,9},{12,... | collective-permute-start | bytes 18440 | tf_op jit(solution)/shard_map/ppermute | solution.py:26
  75.3 1.2 %copy-start.14 = (f32[16,64]{1,0:T(8,128)S(1)}, f32[16,64]{1,0:T(8,128)}, u32[]{:S(2)}) copy-start(f32[16,64]{1,0:T(8,128)} %constant.85.clone) | copy-start | bytes 12292
  75.6 16.7 %copy-start.13 = (f32[2]{0:T(128)S(1)}, f32[2]{0:T(128)}, u32[]{:S(2)}) copy-start(f32[2]{0:T(128)} %constant.86.clone) | copy-start | bytes 28
  76.7 2.0 %collective-permute-start.13 = (f32[2,2,4,8]{3,2,1,0:T(4,128)S(1)}, f32[2,2,4,8]{3,2,1,0:T(4,128)S(1)}, u32[]{:S(2)}, u32[]{:S(2)}) collective-permute-start(f32[2,2,4,8]{3,2,1,0:T(4,128)S(1)} %get-tuple-element.194), channel_id=1, source_target_pairs={{32,0},{64,32},{96,64},{128,96},{160,128},{192,160},{224,192},{0,2... | collective-permute-start | bytes 1544 | tf_op jit(solution)/shard_map/ppermute | solution.py:26
  76.7 4.3 %collective-permute-start.12 = (f32[2,2,4,8]{3,2,1,0:T(4,128)S(1)}, f32[2,2,4,8]{3,2,1,0:T(4,128)S(1)}, u32[]{:S(2)}, u32[]{:S(2)}) collective-permute-start(f32[2,2,4,8]{3,2,1,0:T(4,128)S(1)} %get-tuple-element.193), channel_id=1, source_target_pairs={{0,32},{32,64},{64,96},{96,128},{128,160},{160,192},{192,224},{224... | collective-permute-start | bytes 1544 | tf_op jit(solution)/shard_map/ppermute | solution.py:25
  81.1 9.1 %collective-permute-start.14 = (f32[2,2,4,48]{3,2,1,0:T(4,128)S(1)}, f32[2,2,4,48]{3,2,1,0:T(4,128)S(1)}, u32[]{:S(2)}, u32[]{:S(2)}) collective-permute-start(f32[2,2,4,48]{3,2,1,0:T(4,128)S(1)} %pad_maximum_fusion.14), channel_id=1, source_target_pairs={{0,2},{1,3},{2,4},{3,5},{4,6},{5,7},{6,8},{7,9},{8,10},{9,11},{10,... | collective-permute-start | bytes 9224 | tf_op jit(solution)/shard_map/ppermute | solution.py:25
  81.2 9.1 %collective-permute-start.15 = (f32[2,2,4,48]{3,2,1,0:T(4,128)S(1)}, f32[2,2,4,48]{3,2,1,0:T(4,128)S(1)}, u32[]{:S(2)}, u32[]{:S(2)}) collective-permute-start(f32[2,2,4,48]{3,2,1,0:T(4,128)S(1)} %pad_maximum_fusion.14), channel_id=1, source_target_pairs={{0,1},{1,2},{2,3},{3,4},{4,5},{5,6},{6,7},{7,8},{8,9},{9,10},{10,1... | collective-permute-start | bytes 9224 | tf_op jit(solution)/shard_map/ppermute | solution.py:25
  82.8 7.5 %collective-permute-start.16 = (f32[2,2,4,48]{3,2,1,0:T(4,128)S(1)}, f32[2,2,4,48]{3,2,1,0:T(4,128)S(1)}, u32[]{:S(2)}, u32[]{:S(2)}) collective-permute-start(f32[2,2,4,48]{3,2,1,0:T(4,128)S(1)} %pad_maximum_fusion.14), channel_id=1, source_target_pairs={{1,0},{2,1},{3,2},{4,3},{5,4},{6,5},{7,6},{8,7},{9,8},{10,9},{11,1... | collective-permute-start | bytes 9224 | tf_op jit(solution)/shard_map/ppermute | solution.py:26
  87.5 4.6 %collective-permute-start.17 = (f32[2,2,4,48]{3,2,1,0:T(4,128)S(1)}, f32[2,2,4,48]{3,2,1,0:T(4,128)S(1)}, u32[]{:S(2)}, u32[]{:S(2)}) collective-permute-start(f32[2,2,4,48]{3,2,1,0:T(4,128)S(1)} %pad_maximum_fusion.14), channel_id=1, source_target_pairs={{2,0},{3,1},{4,2},{5,3},{6,4},{7,5},{8,6},{9,7},{10,8},{11,9},{12,... | collective-permute-start | bytes 9224 | tf_op jit(solution)/shard_map/ppermute | solution.py:26
